TPU v7x, 32 devices: a whole 2x2x4 slice. The times are simulated.
32 devices in a mesh: fsdp: 8 (over z, y), tensor: 4 (over x, core).
Axes of the slice: x: 2, y: 2, z: 4, core: 2. Of those that a mesh axis runs over, the one named last changes fastest.
Arguments:
- block_input: bfloat16 [32768, 512], P(('fsdp', 'tensor')), may hold values from -6 to 6
- segments: int32 [32768], P('fsdp'), may hold values from 0 to 6, as said below
- ln_gain: bfloat16 [512], P('fsdp'), may hold values from 0.5 to 1.5
- ln_bias: bfloat16 [512], P('fsdp'), may hold values from -3 to 3
- b_real: bfloat16 [512, 256], P('fsdp', 'tensor'), may hold values from -0.1875 to 0.1875
- b_imag: bfloat16 [512, 256], P('fsdp', 'tensor'), may hold values from -0.1875 to 0.1875
- c_real: bfloat16 [512, 256], P('fsdp', 'tensor'), may hold values from -0.25 to 0.25
- c_imag: bfloat16 [512, 256], P('fsdp', 'tensor'), may hold values from -0.25 to 0.25
- nu_log: bfloat16 [256], P('fsdp'), may hold values from -9.1875 to -3
- theta_log: bfloat16 [256], P('fsdp'), may hold values from -4 to -1
- gamma_log: bfloat16 [256], P('fsdp'), may hold values from -0.5 to 0.5
- d_skip: bfloat16 [512], P('fsdp'), may hold values from -4 to 4
- w_value: bfloat16 [512, 512], P('fsdp', 'tensor'), may hold values from -0.25 to 0.25
- w_gate: bfloat16 [512, 512], P('fsdp', 'tensor'), may hold values from -0.25 to 0.25
- b_value: bfloat16 [512], P('fsdp'), may hold values from -3 to 3
- b_gate: bfloat16 [512], P('fsdp'), may hold values from -3 to 3
- out_grad: bfloat16 [32768, 512], P(('fsdp', 'tensor')), may hold values from -6 to 6
Outputs:
- mixed: bfloat16 [32768, 512], P(('fsdp', 'tensor'))
- input_grad: float32 [32768, 512], P(('fsdp', 'tensor'))
- ln_gain_grad: float32 [512], P('fsdp')
- ln_bias_grad: float32 [512], P('fsdp')
- b_real_grad: float32 [512, 256], P('fsdp', 'tensor')
- b_imag_grad: float32 [512, 256], P('fsdp', 'tensor')
- c_real_grad: float32 [512, 256], P('fsdp', 'tensor')
- c_imag_grad: float32 [512, 256], P('fsdp', 'tensor')
- nu_grad: float32 [256], P('fsdp')
- theta_grad: float32 [256], P('fsdp')
- gamma_grad: float32 [256], P('fsdp')
- skip_grad: float32 [512], P('fsdp')
- value_weight_grad: float32 [512, 512], P('fsdp', 'tensor')
- gate_weight_grad: float32 [512, 512], P('fsdp', 'tensor')
- value_bias_grad: float32 [512], P('fsdp')
- gate_bias_grad: float32 [512], P('fsdp')
Inputs may be any that keep to these rules, and one draw needn't show every extreme that they name: `segments`: in each sequence of 2048 tokens the document numbers start at 1, rise by one at each of 5 boundaries that lie in the first three quarters, and all of 1 to 6 occur; the last 1 to 512 tokens are padding with number 0.
All inputs are finite; a program needn't handle non-finite values.
Results may differ from a plain program's by a relative error of at most 0.02.
Values may be sent and summed in bfloat16 or wider, within the bound.
No kernel may reach another device: no remote copies, remote signals or barrier semaphores. Data moves between devices by JAX's collectives and lax.ppermute only.
A program may use at most 128 MiB of HBM per device.

v0:
```python
import math

import jax
import jax.numpy as jnp
from jax import lax
from jax.sharding import PartitionSpec as P

SEQ_LEN = 2048


norm_epsilon = 1e-05


def complex_product(left, right):
    half_width = left.shape[-1] // 2
    left_re = left[..., :half_width]
    left_im = left[..., half_width:]
    right_re = right[..., :half_width]
    right_im = right[..., half_width:]
    return jnp.concatenate(
        [left_re * right_re - left_im * right_im, left_re * right_im + left_im * right_re], axis=-1
    )


def linear_chain(earlier, later):
    return (complex_product(later[0], earlier[0]), complex_product(later[0], earlier[1]) + later[1])


def blocked_chain(decay, source, reverse):
    rows, width = source.shape
    block = math.gcd(rows, 16)
    count = rows // block
    decay_blocks = decay.reshape(count, block, width)
    source_blocks = source.reshape(count, block, width)
    order = list(range(block - 1, -1, -1)) if reverse else list(range(block))
    decay_parts = [None] * block
    local_parts = [None] * block
    running_decay = None
    running_local = None
    for place in order:
        decay_here = decay_blocks[:, place]
        source_here = source_blocks[:, place]
        if running_decay is None:
            running_decay = decay_here
            running_local = source_here
        else:
            running_decay, running_local = linear_chain(
                (running_decay, running_local), (decay_here, source_here)
            )
        decay_parts[place] = running_decay
        local_parts[place] = running_local
    decay_cum = jnp.stack(decay_parts, axis=1)
    local = jnp.stack(local_parts, axis=1)
    edge = 0 if reverse else block - 1
    _, carried = lax.associative_scan(
        linear_chain, (decay_parts[edge], local_parts[edge]), reverse=reverse, axis=0
    )
    zero_row = jnp.zeros((1, width), jnp.float32)
    if reverse:
        incoming = jnp.concatenate([carried[1:], zero_row], axis=0)
    else:
        incoming = jnp.concatenate([zero_row, carried[:-1]], axis=0)
    return (local + complex_product(decay_cum, incoming[:, None, :])).reshape(rows, width)


def state_params(nu_part, theta_part, gamma_part):
    modulus = jnp.exp(-jnp.exp(nu_part))
    rotation = jnp.exp(theta_part)
    return (
        modulus * jnp.cos(rotation),
        modulus * jnp.sin(rotation),
        jnp.exp(gamma_part) * jnp.sqrt(1.0 - modulus * modulus),
    )


def contract_rows(left, right):
    return lax.dot_general(
        left, right, (((0,), (0,)), ((), ())), preferred_element_type=jnp.float32
    )


def contract_cols(left, right):
    return lax.dot_general(
        left, right, (((1,), (1,)), ((), ())), preferred_element_type=jnp.float32
    )


def shards(
    block_input,
    segments,
    ln_gain,
    ln_bias,
    b_real,
    b_imag,
    c_real,
    c_imag,
    nu_log,
    theta_log,
    gamma_log,
    d_skip,
    w_value,
    w_gate,
    b_value,
    b_gate,
    out_grad,
):
    tensor_rank = lax.axis_index("tensor")
    (
        gain_all,
        shift_all,
        nu_all,
        theta_all,
        gamma_all,
        skip_all,
        value_bias_all,
        gate_bias_all,
        breal_all,
        bimag_all,
        creal_all,
        cimag_all,
        wvalue_all,
        wgate_all,
    ) = (
        lax.all_gather(ln_gain, "fsdp", axis=0, tiled=True),
        lax.all_gather(ln_bias, "fsdp", axis=0, tiled=True),
        lax.all_gather(nu_log, "fsdp", axis=0, tiled=True),
        lax.all_gather(theta_log, "fsdp", axis=0, tiled=True),
        lax.all_gather(gamma_log, "fsdp", axis=0, tiled=True),
        lax.all_gather(d_skip, "fsdp", axis=0, tiled=True),
        lax.all_gather(b_value, "fsdp", axis=0, tiled=True),
        lax.all_gather(b_gate, "fsdp", axis=0, tiled=True),
        lax.all_gather(b_real, "fsdp", axis=0, tiled=True),
        lax.all_gather(b_imag, "fsdp", axis=0, tiled=True),
        lax.all_gather(c_real, "fsdp", axis=0, tiled=True),
        lax.all_gather(c_imag, "fsdp", axis=0, tiled=True),
        lax.all_gather(w_value, "fsdp", axis=0, tiled=True),
        lax.all_gather(w_gate, "fsdp", axis=0, tiled=True),
    )
    row_count, feature_count = block_input.shape
    group_rows = segments.shape[0]
    state_count = b_real.shape[1]
    unit_count = w_value.shape[1]
    full_states = nu_all.shape[0]
    position = jnp.arange(group_rows)
    earlier_ids = jnp.concatenate([segments[:1], segments[:-1]])
    keep = jnp.where((position % SEQ_LEN > 0) & (segments == earlier_ids), 1.0, 0.0).astype(
        jnp.float32
    )[:, None]
    keep_next = jnp.concatenate([keep[1:], jnp.zeros((1, 1), jnp.float32)], axis=0)
    live = jnp.where(segments > 0, 1.0, 0.0).astype(jnp.float32)[:, None]
    row_live = lax.dynamic_slice_in_dim(live, tensor_rank * row_count, row_count, 0)
    gain = gain_all.astype(jnp.float32)
    shift = shift_all.astype(jnp.float32)
    skip = skip_all.astype(jnp.float32)
    inputs_wide = block_input.astype(jnp.float32)
    centred = inputs_wide - jnp.mean(inputs_wide, axis=1, keepdims=True)
    inverse_std = lax.rsqrt(jnp.mean(centred * centred, axis=1, keepdims=True) + norm_epsilon)
    standard = centred * inverse_std
    normed = (standard * gain + shift).astype(jnp.bfloat16)
    normed_group = lax.all_gather(normed, "tensor", axis=0, tiled=True)
    state_start = tensor_rank * state_count
    (decay_re, decay_im, gamma), params_back = jax.vjp(
        state_params,
        lax.dynamic_slice_in_dim(nu_all.astype(jnp.float32), state_start, state_count),
        lax.dynamic_slice_in_dim(theta_all.astype(jnp.float32), state_start, state_count),
        lax.dynamic_slice_in_dim(gamma_all.astype(jnp.float32), state_start, state_count),
    )
    rate_pair = jnp.concatenate([decay_re, decay_im])
    gamma_pair = jnp.concatenate([gamma, gamma])
    conj_sign = jnp.concatenate(
        [jnp.ones((state_count,), jnp.float32), -jnp.ones((state_count,), jnp.float32)]
    )
    input_pack = jnp.concatenate([breal_all, bimag_all], axis=1)
    output_pack = jnp.concatenate([creal_all, -cimag_all], axis=1)
    drive = jnp.dot(normed_group, input_pack, preferred_element_type=jnp.float32)
    decay = keep * rate_pair
    hidden = blocked_chain(decay, gamma_pair * live * drive, False)
    hidden_low = hidden.astype(jnp.bfloat16)
    state_total = lax.psum_scatter(
        contract_cols(hidden_low, output_pack), "tensor", scatter_dimension=0, tiled=True
    )
    normed_wide = normed.astype(jnp.float32)
    lru_out = state_total + skip * normed_wide
    activated, gelu_back = jax.vjp(jax.nn.gelu, lru_out)
    act = activated.astype(jnp.bfloat16)
    unit_start = tensor_rank * unit_count
    act_group = lax.all_gather(act, "tensor", axis=0, tiled=True)
    value_shift = lax.dynamic_slice_in_dim(
        value_bias_all.astype(jnp.float32), unit_start, unit_count
    )
    gate_shift = lax.dynamic_slice_in_dim(gate_bias_all.astype(jnp.float32), unit_start, unit_count)
    value = jnp.dot(act_group, wvalue_all, preferred_element_type=jnp.float32) + value_shift
    gate = jnp.dot(act_group, wgate_all, preferred_element_type=jnp.float32) + gate_shift
    opening = jax.nn.sigmoid(gate)
    gated_units = (value * opening).astype(jnp.bfloat16)
    gated_mine = lax.all_to_all(gated_units, "tensor", split_axis=0, concat_axis=1, tiled=True)
    mixed = (inputs_wide + row_live * gated_mine.astype(jnp.float32)).astype(jnp.bfloat16)
    cotangent = out_grad.astype(jnp.float32)
    gated_grad = (row_live * cotangent).astype(jnp.bfloat16)
    gated_grad_units = lax.all_to_all(
        gated_grad, "tensor", split_axis=1, concat_axis=0, tiled=True
    ).astype(jnp.float32)
    value_grad = (gated_grad_units * opening).astype(jnp.bfloat16)
    gate_grad = (gated_grad_units * value * opening * (1.0 - opening)).astype(jnp.bfloat16)
    value_weight_grad = contract_rows(act_group, value_grad)
    gate_weight_grad = contract_rows(act_group, gate_grad)
    value_bias_grad = lax.dynamic_update_slice(
        jnp.zeros((feature_count,), jnp.float32),
        jnp.sum(value_grad.astype(jnp.float32), axis=0),
        (unit_start,),
    )
    gate_bias_grad = lax.dynamic_update_slice(
        jnp.zeros((feature_count,), jnp.float32),
        jnp.sum(gate_grad.astype(jnp.float32), axis=0),
        (unit_start,),
    )
    act_grad = lax.psum_scatter(
        contract_cols(value_grad, wvalue_all) + contract_cols(gate_grad, wgate_all),
        "tensor",
        scatter_dimension=0,
        tiled=True,
    )
    lru_grad = gelu_back(act_grad)[0].astype(jnp.bfloat16)
    lru_grad_wide = lru_grad.astype(jnp.float32)
    skip_grad = jnp.sum(lru_grad_wide * normed_wide, axis=0)
    lru_grad_group = lax.all_gather(lru_grad, "tensor", axis=0, tiled=True)
    state_grad = jnp.dot(lru_grad_group, output_pack, preferred_element_type=jnp.float32)
    output_pack_grad = contract_rows(lru_grad_group, hidden_low)
    next_decay = keep_next * (rate_pair * conj_sign)
    total_grad = blocked_chain(next_decay, state_grad, True)
    rate_grad = jnp.sum(keep[1:] * complex_product(hidden[:-1] * conj_sign, total_grad[1:]), axis=0)
    gamma_terms = jnp.sum(live * drive * total_grad, axis=0)
    nu_part_grad, theta_part_grad, gamma_part_grad = params_back(
        (
            rate_grad[:state_count],
            rate_grad[state_count:],
            gamma_terms[:state_count] + gamma_terms[state_count:],
        )
    )
    empty_states = jnp.zeros((full_states,), jnp.float32)
    nu_grad = lax.dynamic_update_slice(empty_states, nu_part_grad, (state_start,))
    theta_grad = lax.dynamic_update_slice(empty_states, theta_part_grad, (state_start,))
    gamma_grad = lax.dynamic_update_slice(empty_states, gamma_part_grad, (state_start,))
    drive_grad = (gamma_pair * live * total_grad).astype(jnp.bfloat16)
    input_pack_grad = contract_rows(normed_group, drive_grad)
    state_part = lax.psum_scatter(
        contract_cols(drive_grad, input_pack).astype(jnp.bfloat16),
        "tensor",
        scatter_dimension=0,
        tiled=True,
    ).astype(jnp.float32)
    normed_grad = state_part + lru_grad_wide * skip
    standard_grad = normed_grad * gain
    gain_grad = jnp.sum(normed_grad * standard, axis=0)
    shift_grad = jnp.sum(normed_grad, axis=0)
    input_grad = cotangent + inverse_std * (
        standard_grad
        - jnp.mean(standard_grad, axis=1, keepdims=True)
        - standard * jnp.mean(standard_grad * standard, axis=1, keepdims=True)
    )
    summed = (
        lax.psum_scatter(gain_grad, "fsdp", scatter_dimension=0, tiled=True),
        lax.psum_scatter(shift_grad, "fsdp", scatter_dimension=0, tiled=True),
        lax.psum_scatter(nu_grad, "fsdp", scatter_dimension=0, tiled=True),
        lax.psum_scatter(theta_grad, "fsdp", scatter_dimension=0, tiled=True),
        lax.psum_scatter(gamma_grad, "fsdp", scatter_dimension=0, tiled=True),
        lax.psum_scatter(skip_grad, "fsdp", scatter_dimension=0, tiled=True),
        lax.psum_scatter(value_bias_grad, "fsdp", scatter_dimension=0, tiled=True),
        lax.psum_scatter(gate_bias_grad, "fsdp", scatter_dimension=0, tiled=True),
        lax.psum_scatter(input_pack_grad[:, :state_count], "fsdp", scatter_dimension=0, tiled=True),
        lax.psum_scatter(input_pack_grad[:, state_count:], "fsdp", scatter_dimension=0, tiled=True),
        lax.psum_scatter(
            output_pack_grad[:, :state_count], "fsdp", scatter_dimension=0, tiled=True
        ),
        lax.psum_scatter(
            -output_pack_grad[:, state_count:], "fsdp", scatter_dimension=0, tiled=True
        ),
        lax.psum_scatter(value_weight_grad, "fsdp", scatter_dimension=0, tiled=True),
        lax.psum_scatter(gate_weight_grad, "fsdp", scatter_dimension=0, tiled=True),
    )
    vectors = lax.psum(
        (summed[0], summed[1], summed[2], summed[3], summed[4], summed[5], summed[6], summed[7]),
        "tensor",
    )
    return (
        mixed,
        input_grad,
        vectors[0],
        vectors[1],
        summed[8],
        summed[9],
        summed[10],
        summed[11],
        vectors[2],
        vectors[3],
        vectors[4],
        vectors[5],
        summed[12],
        summed[13],
        vectors[6],
        vectors[7],
    )


def solution(mesh):
    in_specs = (
        P(("fsdp", "tensor"), None),
        P("fsdp"),
        P("fsdp"),
        P("fsdp"),
        P("fsdp", "tensor"),
        P("fsdp", "tensor"),
        P("fsdp", "tensor"),
        P("fsdp", "tensor"),
        P("fsdp"),
        P("fsdp"),
        P("fsdp"),
        P("fsdp"),
        P("fsdp", "tensor"),
        P("fsdp", "tensor"),
        P("fsdp"),
        P("fsdp"),
        P(("fsdp", "tensor"), None),
    )
    out_specs = (
        P(("fsdp", "tensor"), None),
        P(("fsdp", "tensor"), None),
        P("fsdp"),
        P("fsdp"),
        P("fsdp", "tensor"),
        P("fsdp", "tensor"),
        P("fsdp", "tensor"),
        P("fsdp", "tensor"),
        P("fsdp"),
        P("fsdp"),
        P("fsdp"),
        P("fsdp"),
        P("fsdp", "tensor"),
        P("fsdp", "tensor"),
        P("fsdp"),
        P("fsdp"),
    )
    return jax.shard_map(shards, mesh=mesh, in_specs=in_specs, out_specs=out_specs, check_vma=False)
```

profile of v0, /device:TPU:0, one launch (start us, length us, event | category | flops | bytes accessed | tf_op | source)
XLA Modules:
  0.0 1046.0 jit_solution(13006507848595677849)
XLA Ops:
  16.7 23.9 %all-reduce.52 = (bf16[512]{0:T(512)(128)(2,1)}, bf16[512]{0:T(512)(128)(2,1)}, bf16[256]{0:T(256)(128)(2,1)S(1)}, bf16[256]{0:T(256)(128)(2,1)S(1)}, bf16[512]{...) all-reduce(bf16[512]{0:T(512)(128)(2,1)S(1)} %dynamic-update-slice., ...), channel_id=1, replica_groups=mesh['fsdp'=8,'tensor'=4] {'fsdp'}, use_global_device_ids=true, to_apply=%add.40 | all-reduce | flops 3328 | bytes 13312
  48.2 30.5 %all_gather.60 = bf16[512,64]{1,0:T(8,128)(2,1)S(1)} all-gather(bf16[64,64]{1,0:T(8,128)(2,1)S(1)} %copy-done.229), channel_id=1, replica_groups=mesh['fsdp'=8,'tensor'=4] {'fsdp'}, dimensions={0}, use_global_device_ids=true | all-gather | bytes 73728 | tf_op jit(solution)/shard_map/all_gather | solution.py:135
  78.8 32.5 %all_gather.56 = bf16[512,64]{1,0:T(8,128)(2,1)} all-gather(bf16[64,64]{1,0:T(8,128)(2,1)S(1)} %copy-done.230), channel_id=1, replica_groups=mesh['fsdp'=8,'tensor'=4] {'fsdp'}, dimensions={0}, use_global_device_ids=true | all-gather | bytes 73728 | tf_op jit(solution)/shard_map/all_gather | solution.py:132
  111.3 32.5 %all_gather.57 = bf16[512,64]{1,0:T(8,128)(2,1)} all-gather(bf16[64,64]{1,0:T(8,128)(2,1)S(1)} %copy-done.231), channel_id=1, replica_groups=mesh['fsdp'=8,'tensor'=4] {'fsdp'}, dimensions={0}, use_global_device_ids=true | all-gather | bytes 73728 | tf_op jit(solution)/shard_map/all_gather | solution.py:133
  143.8 30.5 %all_gather.59 = bf16[512,64]{1,0:T(8,128)(2,1)S(1)} all-gather(bf16[64,64]{1,0:T(8,128)(2,1)S(1)} %copy-done.232), channel_id=1, replica_groups=mesh['fsdp'=8,'tensor'=4] {'fsdp'}, dimensions={0}, use_global_device_ids=true | all-gather | bytes 73728 | tf_op jit(solution)/shard_map/all_gather | solution.py:134
  175.2 2.7 broadcast_multiply_fusion
  190.7 5.0 multiply_multiply_fusion.3
  195.6 2.5 fusion.98
  214.3 2.6 copy.194
  216.9 6.0 stack.153
  225.3 4.6 fusion.39
  230.6 68.5 %reduce-scatter.18.cloned.1.call-done = f32[1024,512]{1,0:T(8,128)} async-done(((f32[4096,512]{1,0:T(8,128)}), f32[1024,512]{1,0:T(8,128)}) %reduce-scatter.18.cloned.1.call-update) | async-done | bytes 2097168 | tf_op jit(solution)/shard_map/reduce_scatter | solution.py:179
  299.1 3.5 multiply_convert_fusion.1
  302.7 2.6 copy_bitcast_fusion
  305.3 4.2 all-to-all-start.1
  309.7 30.6 %all_gather.63 = bf16[512,128]{1,0:T(8,128)(2,1)S(1)} all-gather(bf16[64,128]{1,0:T(8,128)(2,1)S(1)} %copy-done.233), channel_id=1, replica_groups=mesh['fsdp'=8,'tensor'=4] {'fsdp'}, dimensions={0}, use_global_device_ids=true | all-gather | bytes 147456 | tf_op jit(solution)/shard_map/all_gather | solution.py:136
  340.4 30.5 %all_gather.65 = bf16[512,128]{1,0:T(8,128)(2,1)S(1)} all-gather(bf16[64,128]{1,0:T(8,128)(2,1)S(1)} %copy-done.234), channel_id=1, replica_groups=mesh['fsdp'=8,'tensor'=4] {'fsdp'}, dimensions={0}, use_global_device_ids=true | all-gather | bytes 147456 | tf_op jit(solution)/shard_map/all_gather | solution.py:137
  370.9 4.8 convolution_add_fusion.2
  375.7 6.0 convert_reduce_fusion.1
  383.1 4.6 convolution_add_fusion
  387.7 73.0 %reduce-scatter.20.cloned.1.call-done = f32[1024,512]{1,0:T(8,128)} async-done(((f32[4096,512]{1,0:T(8,128)}), f32[1024,512]{1,0:T(8,128)}) %reduce-scatter.20.cloned.1.call-update) | async-done | bytes 2097168 | tf_op jit(solution)/shard_map/reduce_scatter | solution.py:217
  460.8 4.5 fusion.28
  465.5 2.5 fusion.97
  480.1 19.8 %all-gather.8.cloned.1.call-done = bf16[4096,512]{1,0:T(8,128)(2,1)} async-done(((bf16[1024,512]{1,0:T(8,128)(2,1)}), bf16[4096,512]{1,0:T(8,128)(2,1)}) %all-gather.8.cloned.1.call-update) | async-done | bytes 4194320 | tf_op jit(solution)/shard_map/all_gather | solution.py:226
  499.9 3.6 fusion.71
  503.5 2.4 fusion.96
  581.1 2.5 copy.229
  583.7 7.8 stack.171
  591.5 3.0 multiply_subtract_fusion.1
  598.2 3.0 convolution_convert_fusion
  602.6 4.5 fusion.108
  608.6 4.4 all-to-all-start
  614.1 4.5 fusion.109
  618.7 3.7 fusion.37
  623.3 6.8 multiply_subtract_fusion
  631.2 3.8 fusion.90
  637.0 2.9 fusion.30
  641.3 10.1 reduce-scatter.22.cloned.1.call-done
  651.4 2.9 fusion.15
  654.3 37.1 %all-reduce.50 = (f32[512]{0:T(512)S(1)}, f32[512]{0:T(512)S(1)}, f32[256]{0:T(256)S(1)}, f32[256]{0:T(256)S(1)}, f32[256]{0:T(256)S(1)}, /*index=5*/f32[512]{0:T(512)S(1)}, f32[512]{0:T(512)S(1)}, f32[512]{0:T(512)S(1)}) all-reduce(f32[512]{0:T(512)S(1)} %get-tuple-element.64, ...), channel_id=5, replica_groups=mesh['fsdp'=8,'tensor'=4] {'fsdp'}, use_global_device_ids=true, to_apply=%region_8.9.clone | all-reduce | flops 3328 | bytes 26624
  692.0 6.3 all-reduce.51
  698.3 3.8 convert_add_fusion.1
  702.1 14.7 %reduce-scatter.24.cloned.1.call-done = f32[64,128]{1,0:T(8,128)} async-done(((f32[512,128]{1,0:T(8,128)}), f32[64,128]{1,0:T(8,128)}) %reduce-scatter.24.cloned.1.call-update) | async-done | bytes 32784 | tf_op jit(solution)/shard_map/reduce_scatter | solution.py:278
  716.8 64.5 %reduce-scatter.26.cloned.1.call-done = f32[64,128]{1,0:T(8,128)} async-done(((f32[512,128]{1,0:T(8,128)}), f32[64,128]{1,0:T(8,128)}) %reduce-scatter.26.cloned.1.call-update) | async-done | bytes 32784 | tf_op jit(solution)/shard_map/reduce_scatter | solution.py:279
  781.4 64.5 %reduce-scatter.34.cloned.1.call-done = f32[64,64]{1,0:T(8,128)} async-done(((f32[512,64]{1,0:T(8,128)}), f32[64,64]{1,0:T(8,128)}) %reduce-scatter.34.cloned.1.call-update) | async-done | bytes 16400
  845.8 64.3 %reduce-scatter.32.cloned.1.call-done = f32[64,64]{1,0:T(8,128)} async-done(((f32[512,64]{1,0:T(8,128)}), f32[64,64]{1,0:T(8,128)}) %reduce-scatter.32.cloned.1.call-update) | async-done | bytes 16400
  910.2 64.5 %reduce-scatter.30.cloned.1.call-done = f32[64,64]{1,0:T(8,128)} async-done(((f32[512,64]{1,0:T(8,128)}), f32[64,64]{1,0:T(8,128)}) %reduce-scatter.30.cloned.1.call-update) | async-done | bytes 16400
  974.7 64.3 %reduce-scatter.28.cloned.1.call-done = f32[64,64]{1,0:T(8,128)} async-done(((f32[512,64]{1,0:T(8,128)}), f32[64,64]{1,0:T(8,128)}) %reduce-scatter.28.cloned.1.call-update) | async-done | bytes 16400
  (985 shorter events, 146.3 us)
Async XLA Ops:
  7.2 37.3 %copy-start = (bf16[1024,512]{1,0:T(8,128)(2,1)S(1)}, bf16[1024,512]{1,0:T(8,128)(2,1)}, u32[]{:S(2)}) copy-start(bf16[1024,512]{1,0:T(8,128)(2,1)} %param.17) | copy-start | bytes 3145732
  7.2 183.5 %all-gather.4.cloned.1.call-start = ((), (), s32[]{:S(2)}) async-start(), calls=%async_computation.11 | async-start | bytes 5242880 | tf_op jit(solution)/shard_map/all_gather | solution.py:160
  44.4 34.3 %copy-start.230 = (bf16[64,64]{1,0:T(8,128)(2,1)S(1)}, bf16[64,64]{1,0:T(8,128)(2,1)}, u32[]{:S(2)}) copy-start(bf16[64,64]{1,0:T(8,128)(2,1)} %param.21) | copy-start | bytes 24580
  44.4 66.8 %copy-start.231 = (bf16[64,64]{1,0:T(8,128)(2,1)S(1)}, bf16[64,64]{1,0:T(8,128)(2,1)}, u32[]{:S(2)}) copy-start(bf16[64,64]{1,0:T(8,128)(2,1)} %param.22) | copy-start | bytes 24580
  44.4 99.4 %copy-start.232 = (bf16[64,64]{1,0:T(8,128)(2,1)S(1)}, bf16[64,64]{1,0:T(8,128)(2,1)}, u32[]{:S(2)}) copy-start(bf16[64,64]{1,0:T(8,128)(2,1)} %param.23) | copy-start | bytes 24580
  44.4 130.7 %copy-start.249 = (f32[128]{0:T(128)S(1)}, f32[128]{0:T(128)}, u32[]{:S(2)}) copy-start(f32[128]{0:T(128)} %constant.70.clone.1) | copy-start | bytes 1540
  45.9 253.2 %reduce-scatter.18.cloned.1.call-start = ((), (), s32[]{:S(2)}) async-start(), calls=%async_computation.12 | async-start | bytes 10485760 | tf_op jit(solution)/shard_map/reduce_scatter | solution.py:179
  47.4 130.5 %copy-start.245 = (f32[256]{0:T(256)}, f32[256]{0:T(256)S(1)}, u32[]{:S(2)}) copy-start(f32[256]{0:T(256)S(1)} %convert_element_type.102) | copy-start | bytes 3076
  47.4 130.5 %copy-start.247 = (f32[256]{0:T(256)}, f32[256]{0:T(256)S(1)}, u32[]{:S(2)}) copy-start(f32[256]{0:T(256)S(1)} %convert_element_type.97) | copy-start | bytes 3076
  47.4 130.5 %copy-start.251 = (f32[256]{0:T(256)}, f32[256]{0:T(256)S(1)}, u32[]{:S(2)}) copy-start(f32[256]{0:T(256)S(1)} %convert_element_type.98) | copy-start | bytes 3076
  78.8 146.5 %copy-start.36 = (bf16[512,64]{1,0:T(8,128)(2,1)}, bf16[512,64]{1,0:T(8,128)(2,1)S(1)}, u32[]{:S(2)}) copy-start(bf16[512,64]{1,0:T(8,128)(2,1)S(1)} %neg.22) | copy-start | bytes 196612
  174.3 50.9 %copy-start.37 = (bf16[512,64]{1,0:T(8,128)(2,1)}, bf16[512,64]{1,0:T(8,128)(2,1)S(1)}, u32[]{:S(2)}) copy-start(bf16[512,64]{1,0:T(8,128)(2,1)S(1)} %all_gather.59) | copy-start | bytes 196612
  180.1 9.8 copy-start.38
  229.9 69.2 %copy-start.212 = (f32[1024]{0:T(1024)S(1)}, f32[1024]{0:T(1024)}, u32[]{:S(2)}) copy-start(f32[1024]{0:T(1024)} %copy-done.211) | copy-start | bytes 12292
  229.9 69.2 %copy-start.215 = (f32[1024]{0:T(1024)S(1)}, f32[1024]{0:T(1024)}, u32[]{:S(2)}) copy-start(f32[1024]{0:T(1024)} %copy-done.214) | copy-start | bytes 12292
  229.9 69.2 %copy-start.219 = (f32[512]{0:T(512)S(1)}, f32[512]{0:T(512)}, u32[]{:S(2)}) copy-start(f32[512]{0:T(512)} %copy-done.218) | copy-start | bytes 6148
  229.9 69.2 %copy-start.225 = (f32[512]{0:T(512)S(1)}, f32[512]{0:T(512)}, u32[]{:S(2)}) copy-start(f32[512]{0:T(512)} %copy-done.224) | copy-start | bytes 6148
  229.9 140.9 %all-gather.6.cloned.1.call-start = ((), (), s32[]{:S(2)}) async-start(), calls=%async_computation.13 | async-start | bytes 5242880 | tf_op jit(solution)/shard_map/all_gather | solution.py:187
  230.6 230.2 %copy-start.222 = (f32[512]{0:T(512)}, f32[512]{0:T(512)S(1)}, u32[]{:S(2)}) copy-start(f32[512]{0:T(512)S(1)} %convert_element_type.104) | copy-start | bytes 6148
  302.7 37.7 %copy-start.234 = (bf16[64,128]{1,0:T(8,128)(2,1)S(1)}, bf16[64,128]{1,0:T(8,128)(2,1)}, u32[]{:S(2)}) copy-start(bf16[64,128]{1,0:T(8,128)(2,1)} %param.30) | copy-start | bytes 49156
  305.3 70.4 %all-to-all-start.1 = ((bf16[1024,4,128]{2,0,1:T(8,128)(2,1)}), bf16[1024,4,128]{2,0,1:T(8,128)(2,1)}, u32[]{:S(2)}, u32[]{:S(2)}) async-start(bf16[1024,4,128]{2,0,1:T(8,128)(2,1)} %copy_bitcast_fusion), calls=%async_computation.2 | async-start | bytes 2097152 | tf_op jit(solution)/shard_map/all_to_all | solution.py:200
  309.5 151.3 %reduce-scatter.20.cloned.1.call-start = ((), (), s32[]{:S(2)}) async-start(), calls=%async_computation.14 | async-start | bytes 10485760 | tf_op jit(solution)/shard_map/reduce_scatter | solution.py:217
  387.7 112.3 %all-gather.8.cloned.1.call-start = ((), (), s32[]{:S(2)}) async-start(), calls=%async_computation.15 | async-start | bytes 5242880 | tf_op jit(solution)/shard_map/all_gather | solution.py:226
  465.3 186.1 %reduce-scatter.22.cloned.1.call-start = ((), (), s32[]{:S(2)}) async-start(), calls=%async_computation.16 | async-start | bytes 5242880 | tf_op jit(solution)/shard_map/reduce_scatter | solution.py:246
  469.5 9.8 copy-start.40
  469.5 9.8 copy-start.42
  512.0 21.8 %copy-start.102 = (f32[256,64]{1,0:T(8,128)}, f32[256,64]{1,0:T(8,128)S(1)}, u32[]{:S(2)}) copy-start(f32[256,64]{1,0:T(8,128)S(1)} %get-tuple-element.248) | copy-start | bytes 196612
  523.8 28.1 %copy-start.205 = (f32[127,128]{1,0:T(8,128)S(1)}, f32[127,128]{1,0:T(8,128)}, u32[]{:S(2)}) copy-start(f32[127,128]{1,0:T(8,128)} %slice.1920) | copy-start | bytes 195076
  534.3 20.2 %copy-start.210 = (f32[127,128]{1,0:T(8,128)S(1)}, f32[127,128]{1,0:T(8,128)}, u32[]{:S(2)}) copy-start(f32[127,128]{1,0:T(8,128)} %slice.2051) | copy-start | bytes 195076
  570.3 9.4 copy-start.65
  571.9 7.9 copy-start.63
  601.3 115.6 %reduce-scatter.24.cloned.1.call-start = ((), (), s32[]{:S(2)}) async-start(), calls=%async_computation.17 | async-start | bytes 294912 | tf_op jit(solution)/shard_map/reduce_scatter | solution.py:278
  608.6 89.7 %all-to-all-start = ((bf16[4,1024,128]{2,1,0:T(8,128)(2,1)}), bf16[4,1024,128]{2,1,0:T(8,128)(2,1)}, u32[]{:S(2)}, u32[]{:S(2)}) async-start(bf16[4,1024,128]{2,1,0:T(8,128)(2,1)} %bitcast.520), calls=%async_computation.1 | async-start | bytes 2097152 | tf_op jit(solution)/shard_map/all_to_all | solution.py:196
  613.0 168.3 %reduce-scatter.26.cloned.1.call-start = ((), (), s32[]{:S(2)}) async-start(), calls=%async_computation.18 | async-start | bytes 294912 | tf_op jit(solution)/shard_map/reduce_scatter | solution.py:279
  618.6 227.2 %reduce-scatter.34.cloned.1.call-start = ((), (), s32[]{:S(2)}) async-start(), calls=%async_computation.22 | async-start | bytes 294912
  623.3 286.9 %reduce-scatter.32.cloned.1.call-start = ((), (), s32[]{:S(2)}) async-start(), calls=%async_computation.21 | async-start | bytes 294912
  631.0 343.7 %reduce-scatter.30.cloned.1.call-start = ((), (), s32[]{:S(2)}) async-start(), calls=%async_computation.20 | async-start | bytes 294912
  636.8 402.2 %reduce-scatter.28.cloned.1.call-start = ((), (), s32[]{:S(2)}) async-start(), calls=%async_computation.19 | async-start | bytes 294912
  636.9 14.4 %copy-start.3 = (bf16[1024,512]{1,0:T(8,128)(2,1)S(1)}, bf16[1024,512]{1,0:T(8,128)(2,1)}, u32[]{:S(2)}) copy-start(bf16[1024,512]{1,0:T(8,128)(2,1)} %fusion.28) | copy-start | bytes 3145732
  636.9 14.4 %copy-start.213 = (f32[1024]{0:T(1024)S(1)}, f32[1024]{0:T(1024)}, u32[]{:S(2)}) copy-start(f32[1024]{0:T(1024)} %copy-done.211) | copy-start | bytes 12292
  636.9 14.4 %copy-start.216 = (f32[1024]{0:T(1024)S(1)}, f32[1024]{0:T(1024)}, u32[]{:S(2)}) copy-start(f32[1024]{0:T(1024)} %copy-done.214) | copy-start | bytes 12292
  636.9 14.4 %copy-start.220 = (f32[512]{0:T(512)S(1)}, f32[512]{0:T(512)}, u32[]{:S(2)}) copy-start(f32[512]{0:T(512)} %copy-done.218) | copy-start | bytes 6148
  636.9 14.4 %copy-start.223 = (f32[512]{0:T(512)S(1)}, f32[512]{0:T(512)}, u32[]{:S(2)}) copy-start(f32[512]{0:T(512)} %copy-done.222) | copy-start | bytes 6148
  637.0 14.4 %copy-start.226 = (f32[512]{0:T(512)S(1)}, f32[512]{0:T(512)}, u32[]{:S(2)}) copy-start(f32[512]{0:T(512)} %copy-done.224) | copy-start | bytes 6148
  639.8 14.4 %copy-start.241 = (f32[512]{0:T(512)S(1)}, f32[512]{0:T(512)}, u32[]{:S(2)}) copy-start(f32[512]{0:T(512)} %copy-done.240) | copy-start | bytes 6148
  639.9 14.4 %copy-start.243 = (f32[512]{0:T(512)S(1)}, f32[512]{0:T(512)}, u32[]{:S(2)}) copy-start(f32[512]{0:T(512)} %copy-done.242) | copy-start | bytes 6148
  639.9 58.4 %copy-start.8 = (bf16[1024,512]{1,0:T(8,128)(2,1)S(1)}, bf16[1024,512]{1,0:T(8,128)(2,1)}, u32[]{:S(2)}) copy-start(bf16[1024,512]{1,0:T(8,128)(2,1)} %param.33) | copy-start | bytes 3145732
  639.9 58.4 %copy-start.228 = (f32[1024]{0:T(1024)S(1)}, f32[1024]{0:T(1024)}, u32[]{:S(2)}) copy-start(f32[1024]{0:T(1024)} %copy-done.227) | copy-start | bytes 12292
  (224 other events, 563.0 us)
Sparse Core Ops, SparseCore 0:
  46.0 31.7 all-gather.3
  230.1 68.9 reduce-scatter.17
  302.7 45.2 all-gather.5
  387.8 72.9 reduce-scatter.19
  465.4 34.4 all-gather.7
  601.4 49.9 reduce-scatter.21
  655.6 61.1 reduce-scatter.23
  721.1 60.2 reduce-scatter.25
  785.6 60.1 reduce-scatter.33
  850.0 60.1 reduce-scatter.31
  914.4 60.1 reduce-scatter.29
  978.8 60.1 reduce-scatter.27
where the time goes:
time: 1050 us
  waiting for transfers between devices  509 us (48%)
  blocking collectives  255 us (24%)
  other arithmetic  114 us (11%)
  local copies, waits for them, and re-layouts  88.2 us (8%)
  matrix products  49.3 us (5%)
  between operations  21.5 us (2%)
    unnamed x16, waiting for transfers between devices  258 us
    reduce_scatter x1, waiting for transfers between devices, shards(): lax.psum_scatter(contract_cols(value_grad, wvalue_all) + contract_cols(ga...  73 us
    reduce_scatter x1, waiting for transfers between devices, shards(): lax.psum_scatter(contract_cols(hidden_low, output_pack), 'tensor', scatte...  68.5 us
    reduce_scatter x1, waiting for transfers between devices, shards(): lax.psum_scatter(gate_weight_grad, 'fsdp', scatter_dimension=0, tiled=True)  64.5 us
    unnamed x2, blocking collectives  61.1 us
    all_gather x1, blocking collectives, shards(): lax.all_gather(b_imag, 'fsdp', axis=0, tiled=True)  32.5 us
    all_gather x1, blocking collectives, shards(): lax.all_gather(b_real, 'fsdp', axis=0, tiled=True)  32.5 us
    all_gather x1, blocking collectives, shards(): lax.all_gather(w_value, 'fsdp', axis=0, tiled=True)  30.6 us
  transfers between devices with their start and end apart: 14, of which 10 were waited for; matrix products, arithmetic and copies ran while one was open for 8% of the time, Pallas kernels for 0%

commit v1 on v0

v1 whole, which is shorter than its diff:
```python
import functools
import math

import jax
import jax.numpy as jnp
from jax import lax
from jax.experimental import pallas as pl
from jax.experimental.pallas import tpu as pltpu
from jax.sharding import PartitionSpec as P

SEQ_LEN = 2048
LANES = 128
AXES = ("fsdp", "tensor")
norm_epsilon = 1e-05
GELU_SCALE = math.sqrt(2.0 / math.pi)
GELU_CUBE = 0.044715
F32 = jnp.float32
BF16 = jnp.bfloat16


def bit_reversed(value, bits):
    out = 0
    for _ in range(bits):
        out = out * 2 + value % 2
        value //= 2
    return out


def flip(value, bit, count):
    return lax.ppermute(value, AXES, [(i, i ^ (1 << bit)) for i in range(count)])


def dot(left, right, left_dim=1, right_dim=0):
    return lax.dot_general(
        left, right, (((left_dim,), (right_dim,)), ((), ())), preferred_element_type=F32
    )


def fold_rows(value):
    rows, width = value.shape
    return jnp.sum(value.reshape(rows // 8, 8, width), axis=0)


def wide(mask, width):
    return jnp.concatenate([mask] * (width // LANES), axis=1)


def regroup_matrix(states, shards):
    own = states // shards
    width = 2 * states
    source = lax.broadcasted_iota(jnp.int32, (width, width), 0)
    target = lax.broadcasted_iota(jnp.int32, (width, width), 1)
    shard = source // (2 * own)
    part = (source % (2 * own)) // own
    place = part * states + shard * own + source % own
    return jnp.where(place == target, 1.0, 0.0).astype(BF16)


class Plan:
    def __init__(self, mesh, rows, group_rows, features, states, units):
        self.fsdp = mesh.shape["fsdp"]
        self.tensor = mesh.shape["tensor"]
        self.count = self.fsdp * self.tensor
        self.bits = self.count.bit_length() - 1
        self.rows = rows
        self.features = features
        self.states = states
        self.units = units
        self.own_rows = features // self.fsdp
        self.pieces = SEQ_LEN // rows
        self.chunks = 16
        self.span = rows // self.chunks
        self.tile = 256

    def slot_owner(self, slot, me):
        owner = me ^ bit_reversed(slot, self.bits)
        return owner // self.tensor, owner % self.tensor


def groups_of(value):
    return [value[..., at : at + LANES] for at in range(0, value.shape[-1], LANES)]


def put_groups(ref, at, value):
    for place, part in enumerate(groups_of(value)):
        ref[place, at, :] = part


def take_groups(ref, at):
    return jnp.concatenate([ref[place, at, :] for place in range(ref.shape[0])], axis=1)


def scan_pass(plan, keep_ref, rate, start, reverse, visit):
    chunks, span = plan.chunks, plan.span
    rate_re = groups_of(jnp.broadcast_to(rate[0], (chunks, plan.states)))
    rate_im = groups_of(jnp.broadcast_to(rate[1], (chunks, plan.states)))

    def step(index, carried):
        place = span - 1 - index if reverse else index
        at = pl.ds(place, chunks, stride=span)
        return visit(at, keep_ref[at, :], rate_re, rate_im, carried)

    return lax.fori_loop(0, span, step, start, unroll=4)


def advance(source_ref, at, keep, rate_re, rate_im, now):
    half = len(rate_re)
    following = [None] * (2 * half)
    for place in range(half):
        pass_re = keep * rate_re[place]
        pass_im = keep * rate_im[place]
        now_re, now_im = now[place], now[half + place]
        following[place] = (source_ref[place, at, :] + pass_re * now_re) - pass_im * now_im
        following[half + place] = (source_ref[half + place, at, :] + pass_re * now_im) + pass_im * now_re
    return following


def local_ends(plan, source_ref, keep_ref, rate, reverse):
    zero = jnp.zeros((plan.chunks, LANES), F32)
    groups = 2 * plan.states // LANES

    def visit(at, keep, rate_re, rate_im, carried):
        now, hold = carried
        return advance(source_ref, at, keep, rate_re, rate_im, now), hold * keep

    now, hold = scan_pass(plan, keep_ref, rate, ([zero] * groups, zero + 1.0), reverse, visit)
    half = groups // 2
    return jnp.concatenate(now[:half], axis=1), jnp.concatenate(now[half:], axis=1), hold


def rate_power(rate, times):
    re, im = rate
    while times > 1:
        re, im = re * re - im * im, 2.0 * re * im
        times //= 2
    return re, im


def chunk_entries(plan, ends_re, ends_im, hold, rate, start, reverse):
    power = rate_power(rate, plan.span)
    order = list(range(plan.chunks))
    if reverse:
        order.reverse()
    now_re, now_im = start
    rows_re, rows_im = [None] * plan.chunks, [None] * plan.chunks
    held = wide(hold, plan.states)
    for chunk in order:
        rows_re[chunk], rows_im[chunk] = now_re, now_im
        at = slice(chunk, chunk + 1)
        pass_re, pass_im = held[at] * power[0], held[at] * power[1]
        now_re, now_im = (
            pass_re * now_re - pass_im * now_im + ends_re[at],
            pass_re * now_im + pass_im * now_re + ends_im[at],
        )
    return (
        jnp.concatenate(rows_re, axis=0),
        jnp.concatenate(rows_im, axis=0),
        jnp.concatenate([now_re, now_im], axis=1),
    )


def collect(plan, me, refs, out_ref, parts):
    slot = 0
    rows = plan.own_rows
    for ref in refs:
        for place in range(ref.shape[0]):
            band, shard = plan.slot_owner(slot, me)
            slot += 1
            block = ref[place].astype(out_ref.dtype)
            at = pl.ds(pl.multiple_of(band * rows, rows), rows)
            width = block.shape[1] // parts
            for part in range(parts):
                base = part * plan.tensor * width
                column = pl.multiple_of(base + shard * width, LANES)
                out_ref[at, pl.ds(column, width)] = block[:, part * width : (part + 1) * width]


def distribute(plan, me, full_ref, refs, parts):
    slot = 0
    rows = plan.own_rows
    for ref in refs:
        width = ref.shape[2] // parts
        for place in range(ref.shape[0]):
            band, shard = plan.slot_owner(slot, me)
            slot += 1
            at = pl.ds(pl.multiple_of(band * rows, rows), rows)
            for part in range(parts):
                base = part * plan.tensor * width
                column = pl.multiple_of(base + shard * width, LANES)
                ref[place, :, part * width : (part + 1) * width] = full_ref[
                    at, pl.ds(column, width)
                ].astype(ref.dtype)


def normal_rows(values, gain, shift):
    wide_values = values.astype(F32)
    centred = wide_values - jnp.mean(wide_values, axis=1, keepdims=True)
    inverse = lax.rsqrt(jnp.mean(centred * centred, axis=1, keepdims=True) + norm_epsilon)
    standard = centred * inverse
    return standard, inverse


def state_rates(vec_ref, states):
    nu = vec_ref[5:6, :states].astype(F32)
    theta = vec_ref[6:7, :states].astype(F32)
    scale = vec_ref[7:8, :states].astype(F32)
    speed = jnp.exp(nu)
    modulus = jnp.exp(-speed)
    rotation = jnp.exp(theta)
    rate = (modulus * jnp.cos(rotation), modulus * jnp.sin(rotation))
    rest = 1.0 - modulus * modulus
    gamma = jnp.exp(scale) * jnp.sqrt(rest)
    return rate, gamma, speed, modulus, rest, rotation


def enter_kernel(
    plan, me_ref, x_ref, b0_ref, b1_ref, vec_ref, keep_ref, live_ref,
    normed_ref, source_ref, carry_ref, input_map_ref, pack_ref,
):
    me = me_ref[0]
    states = plan.states
    collect(plan, me, (b0_ref, b1_ref), pack_ref, 1)
    input_map_ref[...] = dot(pack_ref[...].astype(BF16), regroup_matrix(states, plan.tensor)).astype(BF16)
    gain = vec_ref[0:1, :].astype(F32)
    shift = vec_ref[1:2, :].astype(F32)
    rate, gamma, *_ = state_rates(vec_ref, states)
    gamma_pair = jnp.concatenate([gamma, gamma], axis=1)

    def rows_step(index, _):
        at = pl.ds(pl.multiple_of(index * plan.tile, plan.tile), plan.tile)
        standard, inverse = normal_rows(x_ref[at, :], gain, shift)
        normed = (standard * gain + shift).astype(BF16)
        normed_ref[at, :] = normed
        drive = dot(normed, input_map_ref[...])
        put_groups(source_ref, at, drive * gamma_pair * wide(live_ref[at, :], 2 * states))
        return 0

    lax.fori_loop(0, plan.rows // plan.tile, rows_step, 0)
    ends_re, ends_im, hold = local_ends(plan, source_ref, keep_ref, rate, False)
    zero = jnp.zeros((1, states), F32)
    _, _, leaving = chunk_entries(plan, ends_re, ends_im, hold, rate, (zero, zero), False)
    carry_ref[...] = jnp.broadcast_to(leaving, carry_ref.shape)


def middle_kernel(
    plan, me_ref, x_ref, grad_ref, normed_ref, source_ref, carry_ref,
    c0_ref, c1_ref, w0_ref, w1_ref, vec_ref, keep_ref, next_ref, live_ref,
    mixed_ref, hidden_ref, lru_grad_ref, state_grad_ref, back_ref,
    cs_ref, ck_ref, ws_ref, wk_ref, sums_ref,
    pack_ref, wpack_ref, out_map_ref, act_ref, unit_grad_ref, full_ref, low_ref,
):
    me = me_ref[0]
    states, features = plan.states, plan.features
    collect(plan, me, (c0_ref, c1_ref), pack_ref, 1)
    collect(plan, me, (w0_ref, w1_ref), wpack_ref, 2)
    regroup = regroup_matrix(states, plan.tensor)
    sign = jnp.where(
        lax.broadcasted_iota(jnp.int32, (1, 2 * states), 1) < states, 1.0, -1.0
    )
    out_map_ref[...] = (dot(pack_ref[...].astype(BF16), regroup) * sign).astype(BF16)
    rate, *_ = state_rates(vec_ref, states)
    ends_re, ends_im, hold = local_ends(plan, source_ref, keep_ref, rate, False)
    start = (carry_ref[0:1, :states], carry_ref[0:1, states:])
    entry_re, entry_im, _ = chunk_entries(plan, ends_re, ends_im, hold, rate, start, False)

    def visit(at, keep, rate_re, rate_im, now):
        now = advance(source_ref, at, keep, rate_re, rate_im, now)
        for place, part in enumerate(now):
            hidden_ref[place, at, :] = part
        return now

    scan_pass(plan, keep_ref, rate, groups_of(entry_re) + groups_of(entry_im), False, visit)
    skip = vec_ref[2:3, :].astype(F32)
    biases = jnp.concatenate([vec_ref[3:4, :], vec_ref[4:5, :]], axis=1).astype(F32)
    sums_ref[...] = jnp.zeros_like(sums_ref)

    def rows_step(index, _):
        at = pl.ds(pl.multiple_of(index * plan.tile, plan.tile), plan.tile)
        low = take_groups(hidden_ref, at).astype(BF16)
        low_ref[at, :] = low
        normed = normed_ref[at, :].astype(F32)
        lru = dot(low, out_map_ref[...], 1, 1) + skip * normed
        square = lru * lru
        bent = jnp.tanh(GELU_SCALE * lru * (1.0 + GELU_CUBE * square))
        half = 0.5 * (1.0 + bent)
        act = (lru * half).astype(BF16)
        slope = half + (0.5 * GELU_SCALE) * lru * (1.0 - bent * bent) * (
            1.0 + (3.0 * GELU_CUBE) * square
        )
        act_ref[at, :] = act
        mapped = dot(act, wpack_ref[...].astype(BF16)) + biases
        value = mapped[:, :features]
        opening = 0.5 + 0.5 * jnp.tanh(0.5 * mapped[:, features:])
        live = wide(live_ref[at, :], features)
        gated = value * opening
        mixed_ref[at, :] = (
            x_ref[at, :].astype(F32) + live * gated.astype(BF16).astype(F32)
        ).astype(BF16)
        gated_grad = live * grad_ref[at, :].astype(F32)
        value_grad = gated_grad * opening
        gate_grad = value_grad * value * (1.0 - opening)
        sums_ref[8:16, :] += fold_rows(value_grad)
        sums_ref[16:24, :] += fold_rows(gate_grad)
        unit_grad = jnp.concatenate([value_grad, gate_grad], axis=1).astype(BF16)
        unit_grad_ref[at, :] = unit_grad
        act_grad = dot(unit_grad, wpack_ref[...].astype(BF16), 1, 1)
        lru_grad = act_grad * slope
        sums_ref[0:8, :] += fold_rows(lru_grad * normed)
        lru_grad = lru_grad.astype(BF16)
        lru_grad_ref[at, :] = lru_grad
        put_groups(state_grad_ref, at, dot(lru_grad, out_map_ref[...]))
        return 0

    lax.fori_loop(0, plan.rows // plan.tile, rows_step, 0)
    back_rate = (rate[0], -rate[1])
    ends_re, ends_im, hold = local_ends(plan, state_grad_ref, next_ref, back_rate, True)
    zero = jnp.zeros((1, states), F32)
    _, _, leaving = chunk_entries(plan, ends_re, ends_im, hold, back_rate, (zero, zero), True)
    back_ref[...] = jnp.broadcast_to(leaving, back_ref.shape)
    full_ref[...] = dot(act_ref[...], unit_grad_ref[...], 0, 0)
    distribute(plan, me, full_ref, (wk_ref, ws_ref), 2)
    out_grad = dot(lru_grad_ref[...], low_ref[...], 0, 0) * sign
    full_ref[:, : 2 * states] = dot(out_grad.astype(BF16), regroup, 1, 1)
    distribute(plan, me, full_ref, (ck_ref, cs_ref), 1)


def leave_kernel(
    plan, me_ref, x_ref, grad_ref, normed_ref, source_ref, carry_ref, hidden_ref,
    state_grad_ref, lru_grad_ref, input_map_ref, vec_ref, next_ref, live_ref, sums_ref,
    input_grad_ref, bs_ref, bk_ref, out_sums_ref,
    drive_grad_ref, low_ref, full_ref,
):
    me = me_ref[0]
    states, features, chunks = plan.states, plan.features, plan.chunks
    rate, gamma, speed, modulus, rest, rotation = state_rates(vec_ref, states)
    back_rate = (rate[0], -rate[1])
    ends_re, ends_im, hold = local_ends(plan, state_grad_ref, next_ref, back_rate, True)
    start = (carry_ref[0:1, :states], carry_ref[0:1, states:])
    entry_re, entry_im, _ = chunk_entries(plan, ends_re, ends_im, hold, back_rate, start, True)
    zero = jnp.zeros((chunks, LANES), F32)
    gamma_wide = groups_of(jnp.broadcast_to(gamma, (chunks, states)))
    half = states // LANES

    def visit(at, keep, rate_re, rate_im, carried):
        now, rate_sum_re, rate_sum_im, gamma_sum = carried
        live = live_ref[at, :]
        after = [None] * (2 * half)
        sums = ([], [], [])
        for place in range(half):
            other = half + place
            next_re, next_im = keep * now[place], keep * now[other]
            hidden_re, hidden_im = hidden_ref[place, at, :], hidden_ref[other, at, :]
            sums[0].append(rate_sum_re[place] + (hidden_re * next_re + hidden_im * next_im))
            sums[1].append(rate_sum_im[place] + (hidden_re * next_im - hidden_im * next_re))
            rate_a, rate_b = rate_re[place], rate_im[place]
            now_re = (state_grad_ref[place, at, :] + rate_a * next_re) - rate_b * next_im
            now_im = (state_grad_ref[other, at, :] + rate_a * next_im) + rate_b * next_re
            driven = source_ref[place, at, :] * now_re + source_ref[other, at, :] * now_im
            sums[2].append(gamma_sum[place] + driven)
            scale = gamma_wide[place] * live
            drive_grad_ref[place, at, :] = scale * now_re
            drive_grad_ref[other, at, :] = scale * now_im
            after[place], after[other] = now_re, now_im
        return after, *sums

    _, rate_sum_re, rate_sum_im, gamma_sum = scan_pass(
        plan,
        next_ref,
        back_rate,
        (groups_of(entry_re) + groups_of(entry_im), [zero] * half, [zero] * half, [zero] * half),
        True,
        visit,
    )

    def total(parts):
        return jnp.sum(jnp.concatenate(parts, axis=1), axis=0, keepdims=True)

    rate_sum_re, rate_sum_im, gamma_sum = total(rate_sum_re), total(rate_sum_im), total(gamma_sum)
    nu_grad = speed * (
        gamma_sum * modulus * modulus / rest - (rate_sum_re * rate[0] + rate_sum_im * rate[1])
    )
    theta_grad = rotation * (rate_sum_im * rate[0] - rate_sum_re * rate[1])
    gain = vec_ref[0:1, :].astype(F32)
    shift = vec_ref[1:2, :].astype(F32)
    skip = vec_ref[2:3, :].astype(F32)
    gain_sum = jnp.zeros((8, features), F32)

    def rows_step(index, sums):
        gain_sum, shift_sum = sums
        at = pl.ds(pl.multiple_of(index * plan.tile, plan.tile), plan.tile)
        low = take_groups(drive_grad_ref, at).astype(BF16)
        low_ref[at, :] = low
        normed_grad = dot(low, input_map_ref[...], 1, 1) + skip * lru_grad_ref[at, :].astype(F32)
        standard, inverse = normal_rows(x_ref[at, :], gain, shift)
        gain_sum += fold_rows(normed_grad * standard)
        shift_sum += fold_rows(normed_grad)
        scaled = normed_grad * gain
        input_grad_ref[at, :] = grad_ref[at, :].astype(F32) + inverse * (
            scaled
            - jnp.mean(scaled, axis=1, keepdims=True)
            - standard * jnp.mean(scaled * standard, axis=1, keepdims=True)
        )
        return gain_sum, shift_sum

    gain_sum, shift_sum = lax.fori_loop(
        0, plan.rows // plan.tile, rows_step, (gain_sum, gain_sum)
    )
    into = dot(normed_ref[...], low_ref[...], 0, 0)
    full_ref[...] = dot(into.astype(BF16), regroup_matrix(states, plan.tensor), 1, 1)
    distribute(plan, me, full_ref, (bk_ref, bs_ref), 1)
    out_sums_ref[...] = jnp.zeros_like(out_sums_ref)
    out_sums_ref[0:1, :] = jnp.sum(gain_sum, axis=0, keepdims=True)
    out_sums_ref[1:2, :] = jnp.sum(shift_sum, axis=0, keepdims=True)
    for place in range(3):
        out_sums_ref[2 + place : 3 + place, :] = jnp.sum(
            sums_ref[8 * place : 8 * place + 8, :], axis=0, keepdims=True
        )
    out_sums_ref[5:6, :states] = nu_grad
    out_sums_ref[6:7, :states] = theta_grad
    out_sums_ref[7:8, :states] = gamma_sum


def call(kernel, plan, outs, scratch, *args):
    whole = pl.BlockSpec(memory_space=pltpu.VMEM)
    return pl.pallas_call(
        functools.partial(kernel, plan),
        out_shape=outs,
        in_specs=[pl.BlockSpec(memory_space=pltpu.SMEM)] + [whole] * (len(args) - 1),
        out_specs=[whole] * len(outs),
        scratch_shapes=scratch,
        compiler_params=pltpu.CompilerParams(vmem_limit_bytes=48 * 1024 * 1024),
    )(*args)


def shape(dims, dtype=F32):
    return jax.ShapeDtypeStruct(dims, dtype)


def gather_blocks(plan, block, summed=None):
    held = block[None]
    tensor_bits = plan.tensor.bit_length() - 1
    for stage in range(plan.bits):
        bit = plan.bits - 1 - stage
        if summed is not None and bit >= tensor_bits:
            count = held.shape[0] * held.shape[1]
            joined = jnp.concatenate([held.reshape(count, -1), summed], axis=0)
            other = flip(joined, bit, plan.count)
            summed = summed + other[count:]
            other = other[:count].reshape(held.shape)
        else:
            other = flip(held, bit, plan.count)
        if stage == plan.bits - 1:
            return held, other, summed
        held = jnp.concatenate([held, other], axis=0)


def split_high_low(value):
    high = value.astype(BF16)
    return jnp.concatenate([high, (value - high.astype(F32)).astype(BF16)], axis=0)


def scatter_blocks(plan, keep, send, summed=None):
    for stage in range(plan.bits):
        if summed is not None:
            count = send.shape[0] * send.shape[1]
            pair = split_high_low(summed)
            other = flip(jnp.concatenate([send.reshape(count, -1), pair], axis=0), stage, plan.count)
            rows = summed.shape[0]
            tail = other[count:].astype(F32)
            summed = summed + (tail[:rows] + tail[rows:])
            other = other[:count].reshape(send.shape)
        else:
            other = flip(send, stage, plan.count)
        total = keep.astype(F32) + other.astype(F32)
        half = total.shape[0] // 2
        if half:
            keep, send = total[:half].astype(BF16), total[half:].astype(BF16)
    return total[0], summed


def shards(
    mesh,
    block_input,
    segments,
    ln_gain,
    ln_bias,
    b_real,
    b_imag,
    c_real,
    c_imag,
    nu_log,
    theta_log,
    gamma_log,
    d_skip,
    w_value,
    w_gate,
    b_value,
    b_gate,
    out_grad,
):
    band = lax.axis_index("fsdp")
    shard = lax.axis_index("tensor")
    rows, features = block_input.shape
    own = b_real.shape[1]
    plan = Plan(
        mesh, rows, segments.shape[0], features, own * mesh.shape["tensor"], w_value.shape[1]
    )
    states, half = plan.states, plan.count // 2
    me = (band * plan.tensor + shard).astype(jnp.int32).reshape(1)

    position = jnp.arange(segments.shape[0])
    earlier = jnp.concatenate([segments[:1], segments[:-1]])
    keep = jnp.where((position % SEQ_LEN > 0) & (segments == earlier), 1.0, 0.0).astype(F32)
    following = jnp.concatenate([keep[1:], jnp.zeros((1,), F32)])
    live = jnp.where(segments > 0, 1.0, 0.0).astype(F32)

    def mine(mask):
        part = lax.dynamic_slice_in_dim(mask, shard * rows, rows, 0)
        return jnp.broadcast_to(part[:, None], (rows, LANES))

    keep, following, live = mine(keep), mine(following), mine(live)

    def placed(vector):
        length = vector.shape[0] * plan.fsdp
        spread = jnp.tile(vector, plan.fsdp)
        spread = jnp.where(jnp.arange(length) // vector.shape[0] == band, spread, 0)
        return jnp.pad(spread, (0, features - length))

    vectors = jnp.stack(
        [
            placed(v)
            for v in (
                ln_gain, ln_bias, d_skip, b_value, b_gate, nu_log, theta_log, gamma_log,
            )
        ]
    )
    b0, b1, vectors = gather_blocks(
        plan, jnp.concatenate([b_real, b_imag], axis=1), vectors.reshape(-1, 2 * own)
    )
    vectors = vectors.reshape(8, features)
    c0, c1, _ = gather_blocks(plan, jnp.concatenate([c_real, c_imag], axis=1))
    w0, w1, _ = gather_blocks(plan, jnp.concatenate([w_value, w_gate], axis=1))

    pack_type = BF16 if plan.own_rows % 16 == 0 else F32
    normed, source, carry, input_map = call(
        enter_kernel,
        plan,
        [
            shape((rows, features), BF16),
            shape((2 * states // LANES, rows, LANES)),
            shape((8, 2 * states)),
            shape((features, 2 * states), BF16),
        ],
        [pltpu.VMEM((features, 2 * states), pack_type)],
        me, block_input, b0, b1, vectors, keep, live,
    )

    def pass_on(value, forward):
        pairs = []
        for first in range(0, plan.tensor, 2):
            pairs.append((first, first + 1) if forward else (first + 1, first))
        return lax.ppermute(value, "tensor", pairs)

    if plan.pieces == 2:
        carry = pass_on(carry, True)
    else:
        carry = jnp.zeros_like(carry)
    half_block = (half, plan.own_rows)
    (
        mixed, hidden, lru_grad, state_grad, back,
        c_send, c_keep, w_send, w_keep, sums,
    ) = call(
        middle_kernel,
        plan,
        [
            shape((rows, features), BF16),
            shape((2 * states // LANES, rows, LANES)),
            shape((rows, features), BF16),
            shape((2 * states // LANES, rows, LANES)),
            shape((8, 2 * states)),
            shape((*half_block, 2 * own), BF16),
            shape((*half_block, 2 * own), BF16),
            shape((*half_block, 2 * plan.units), BF16),
            shape((*half_block, 2 * plan.units), BF16),
            shape((24, features)),
        ],
        [
            pltpu.VMEM((features, 2 * states), pack_type),
            pltpu.VMEM((features, 2 * features), pack_type),
            pltpu.VMEM((features, 2 * states), BF16),
            pltpu.VMEM((rows, features), BF16),
            pltpu.VMEM((rows, 2 * features), BF16),
            pltpu.VMEM((features, 2 * features), F32),
            pltpu.VMEM((rows, 2 * states), BF16),
        ],
        me, block_input, out_grad, normed, source, carry,
        c0, c1, w0, w1, vectors, keep, following, live,
    )
    back = pass_on(back, False) if plan.pieces == 2 else jnp.zeros_like(back)
    w_mine, _ = scatter_blocks(plan, w_keep, w_send)
    c_mine, _ = scatter_blocks(plan, c_keep, c_send)
    input_grad, b_send, b_keep, vector_sums = call(
        leave_kernel,
        plan,
        [
            shape((rows, features)),
            shape((*half_block, 2 * own), BF16),
            shape((*half_block, 2 * own), BF16),
            shape((8, features)),
        ],
        [
            pltpu.VMEM((2 * states // LANES, rows, LANES), F32),
            pltpu.VMEM((rows, 2 * states), BF16),
            pltpu.VMEM((features, 2 * states), F32),
        ],
        me, block_input, out_grad, normed, source, back, hidden,
        state_grad, lru_grad, input_map, vectors, following, live, sums,
    )
    b_mine, vector_sums = scatter_blocks(plan, b_keep, b_send, vector_sums.reshape(-1, 2 * own))
    vector_sums = vector_sums.reshape(8, features)

    def vector(place, length):
        return lax.dynamic_slice(vector_sums[place], (band * length,), (length,))

    units = plan.units
    long, short = plan.own_rows, states // plan.fsdp
    return (
        mixed,
        input_grad,
        vector(0, long),
        vector(1, long),
        b_mine[:, :own],
        b_mine[:, own:],
        c_mine[:, :own],
        c_mine[:, own:],
        vector(5, short),
        vector(6, short),
        vector(7, short),
        vector(2, long),
        w_mine[:, :units],
        w_mine[:, units:],
        vector(3, long),
        vector(4, long),
    )


def solution(mesh):
    in_specs = (
        P(("fsdp", "tensor"), None),
        P("fsdp"),
        P("fsdp"),
        P("fsdp"),
        P("fsdp", "tensor"),
        P("fsdp", "tensor"),
        P("fsdp", "tensor"),
        P("fsdp", "tensor"),
        P("fsdp"),
        P("fsdp"),
        P("fsdp"),
        P("fsdp"),
        P("fsdp", "tensor"),
        P("fsdp", "tensor"),
        P("fsdp"),
        P("fsdp"),
        P(("fsdp", "tensor"), None),
    )
    out_specs = (
        P(("fsdp", "tensor"), None),
        P(("fsdp", "tensor"), None),
        P("fsdp"),
        P("fsdp"),
        P("fsdp", "tensor"),
        P("fsdp", "tensor"),
        P("fsdp", "tensor"),
        P("fsdp", "tensor"),
        P("fsdp"),
        P("fsdp"),
        P("fsdp"),
        P("fsdp"),
        P("fsdp", "tensor"),
        P("fsdp", "tensor"),
        P("fsdp"),
        P("fsdp"),
    )
    return jax.shard_map(
        functools.partial(shards, mesh),
        mesh=mesh,
        in_specs=in_specs,
        out_specs=out_specs,
        check_vma=False,
    )
```

time: 1050 us -> 154 us (0.15)
  waiting for transfers between devices: 509 us -> 33.5 us
  blocking collectives: 255 us -> 0 us
  other arithmetic: 114 us -> 8.79 us
  local copies, waits for them, and re-layouts: 88.2 us -> 18.6 us
  matrix products: 49.3 us -> 0 us
  Pallas kernels: 0 us -> 48.7 us
  starting transfers between devices: 9.53 us -> 41.5 us
  between operations: 21.5 us -> 1.24 us
    unnamed x16 -> x0, waiting for transfers between devices: 258 us -> none
    reduce_scatter x5 -> x0, waiting for transfers between devices: 231 us -> none  [the longest x1 73 us: shards(): lax.psum_scatter(contract_cols(value_grad, wvalue_all) + contract_cols(ga...]
    all_gather x6 -> x0, blocking collectives: 187 us -> none  [the longest x1 32.5 us: shards(): lax.all_gather(b_imag, 'fsdp', axis=0, tiled=True)]
    unnamed x2 -> x0, blocking collectives: 61.1 us -> none
    dot_general x12 -> x0, matrix products: 49.3 us -> none  [the longest x4 16.4 us: contract_rows(): lax.dot_general(left, right, (((0,), (0,)), ((), ())), preferred_element_...]
    pallas_call x0 -> x3, Pallas kernels: none -> 48.7 us  [call(): pl.pallas_call(functools.partial(kernel, plan), out_shape=outs, in_specs=...]
    ppermute x0 -> x32, starting transfers between devices: none -> 41.5 us  [the longest x30 38 us: flip(): return lax.ppermute(value, AXES, [(i, i ^ 1 << bit) for i in range(count)])]
    slice x115 -> x22, local copies, waits for them, and re-layouts: 44.4 us -> 4.37 us  [the longest x1 1.2 us: shards(): earlier = jnp.concatenate([segments[:1], segments[:-1]])]
  transfers between devices with their start and end apart: 14 -> 32, of which waited for: 10 -> 18; matrix products, arithmetic and copies ran while one was open for 8% -> 11% of each run, Pallas kernels for 0% -> 17%
where the time goes in v1:
time: 154 us; the launch traced here: 152 us
  Pallas kernels  48.7 us (32%)
  starting transfers between devices  41.5 us (27%)
  waiting for transfers between devices  33.5 us (22%)
  local copies, waits for them, and re-layouts  18.6 us (12%)
  other arithmetic  8.79 us (6%)
    pallas_call x3, Pallas kernels, call(): pl.pallas_call(functools.partial(kernel, plan), out_shape=outs, in_specs=...  48.7 us
    ppermute x30, starting transfers between devices, flip(): return lax.ppermute(value, AXES, [(i, i ^ 1 << bit) for i in range(count)])  38 us
    ppermute x30, waiting for transfers between devices, flip(): return lax.ppermute(value, AXES, [(i, i ^ 1 << bit) for i in range(count)])  32.3 us
    another operation x16, local copies, waits for them, and re-layouts, placed(): spread = jnp.tile(vector, plan.fsdp)  5.95 us
    dynamic_slice x8, local copies, waits for them, and re-layouts, vector(): return lax.dynamic_slice(vector_sums[place], (band * length,), (length,))  4.66 us
    ppermute x2, starting transfers between devices, pass_on(): return lax.ppermute(value, 'tensor', pairs)  3.49 us
  transfers between devices with their start and end apart: 32, of which 18 were waited for; matrix products, arithmetic and copies ran while one was open for 11% of the time, Pallas kernels for 17%

profile of v1, /device:TPU:0, one launch (start us, length us, event | category | flops | bytes accessed | tf_op | source)
XLA Modules:
  0.0 152.4 jit_solution(1166168944428391718)
XLA Ops:
  6.8 0.8 pad_maximum_fusion.16
  7.6 4.1 %collective-permute-start = (bf16[96,128]{1,0:T(8,128)(2,1)S(1)}, bf16[96,128]{1,0:T(8,128)(2,1)S(1)}, u32[]{:S(2)}, u32[]{:S(2)}) collective-permute-start(bf16[96,128]{1,0:T(8,128)(2,1)S(1)} %pad_maximum_fusion.16), channel_id=1, source_target_pairs={{0,16},{1,17},{2,18},{3,19},{4,20},{5,21},{6,22},{7,23},{8,24},{9,... | collective-permute-start | bytes 73736 | tf_op jit(solution)/shard_map/ppermute | solution.py:30
  11.7 0.8 constant_dynamic-update-slice_fusion.9
  13.3 2.9 %collective-permute-start.11 = (bf16[1,64,256]{2,1,0:T(8,128)(2,1)S(1)}, bf16[1,64,256]{2,1,0:T(8,128)(2,1)S(1)}, u32[]{:S(2)}, u32[]{:S(2)}) collective-permute-start(bf16[1,64,256]{2,1,0:T(8,128)(2,1)S(1)} %maximum_bitcast_fusion), channel_id=1, source_target_pairs={{0,16},{1,17},{2,18},{3,19},{4,20},{5,21},{6,22},{7,23},{8,24},{9,... | collective-permute-start | bytes 98312 | tf_op jit(solution)/shard_map/ppermute | solution.py:30
  16.2 0.8 constant_dynamic-update-slice_fusion.4
  17.0 0.7 constant_dynamic-update-slice_fusion.14
  17.8 1.2 slice.239
  19.0 1.5 fusion.15
  21.3 1.6 %collective-permute-start.7 = (bf16[2,64,128]{2,1,0:T(8,128)(2,1)S(1)}, bf16[2,64,128]{2,1,0:T(8,128)(2,1)S(1)}, u32[]{:S(2)}, u32[]{:S(2)}) collective-permute-start(bf16[2,64,128]{2,1,0:T(8,128)(2,1)S(1)} %pad_maximum_fusion.14), channel_id=1, source_target_pairs={{0,8},{1,9},{2,10},{3,11},{4,12},{5,13},{6,14},{7,15},{8,0},{9,1},... | collective-permute-start | bytes 98312 | tf_op jit(solution)/shard_map/ppermute | solution.py:30
  23.5 1.6 %collective-permute-start.12 = (bf16[2,64,256]{2,1,0:T(8,128)(2,1)S(1)}, bf16[2,64,256]{2,1,0:T(8,128)(2,1)S(1)}, u32[]{:S(2)}, u32[]{:S(2)}) collective-permute-start(bf16[2,64,256]{2,1,0:T(8,128)(2,1)S(1)} %pad_maximum_fusion.10), channel_id=1, source_target_pairs={{0,8},{1,9},{2,10},{3,11},{4,12},{5,13},{6,14},{7,15},{8,0},{9,1},... | collective-permute-start | bytes 196616 | tf_op jit(solution)/shard_map/ppermute | solution.py:30
  25.5 1.6 %collective-permute-start.8 = (bf16[4,64,128]{2,1,0:T(8,128)(2,1)S(1)}, bf16[4,64,128]{2,1,0:T(8,128)(2,1)S(1)}, u32[]{:S(2)}, u32[]{:S(2)}) collective-permute-start(bf16[4,64,128]{2,1,0:T(8,128)(2,1)S(1)} %pad_maximum_fusion.9), channel_id=1, source_target_pairs={{0,4},{1,5},{2,6},{3,7},{4,0},{5,1},{6,2},{7,3},{8,12},{9,13},{10,... | collective-permute-start | bytes 196616 | tf_op jit(solution)/shard_map/ppermute | solution.py:30
  27.2 1.5 collective-permute-start.2
  29.4 1.1 collective-permute-done.8
  30.5 1.6 %collective-permute-start.9 = (bf16[8,64,128]{2,1,0:T(8,128)(2,1)S(1)}, bf16[8,64,128]{2,1,0:T(8,128)(2,1)S(1)}, u32[]{:S(2)}, u32[]{:S(2)}) collective-permute-start(bf16[8,64,128]{2,1,0:T(8,128)(2,1)S(1)} %pad_maximum_fusion.4), channel_id=1, source_target_pairs={{0,2},{1,3},{2,0},{3,1},{4,6},{5,7},{6,4},{7,5},{8,10},{9,11},{10,... | collective-permute-start | bytes 393224 | tf_op jit(solution)/shard_map/ppermute | solution.py:30
  32.1 1.6 %collective-permute-done.13 = bf16[4,64,256]{2,1,0:T(8,128)(2,1)S(1)} collective-permute-done((bf16[4,64,256]{2,1,0:T(8,128)(2,1)S(1)}, bf16[4,64,256]{2,1,0:T(8,128)(2,1)S(1)}, u32[]{:S(2)}, u32[]{:S(2)}) %collective-permute-start.13) | collective-permute-done | bytes 131104 | tf_op jit(solution)/shard_map/ppermute | solution.py:30
  33.8 1.6 %collective-permute-start.14 = (bf16[8,64,256]{2,1,0:T(8,128)(2,1)S(1)}, bf16[8,64,256]{2,1,0:T(8,128)(2,1)S(1)}, u32[]{:S(2)}, u32[]{:S(2)}) collective-permute-start(bf16[8,64,256]{2,1,0:T(8,128)(2,1)S(1)} %pad_maximum_fusion.1), channel_id=1, source_target_pairs={{0,2},{1,3},{2,0},{3,1},{4,6},{5,7},{6,4},{7,5},{8,10},{9,11},{10,... | collective-permute-start | bytes 786440 | tf_op jit(solution)/shard_map/ppermute | solution.py:30
  36.0 5.8 %collective-permute-done.14 = bf16[8,64,256]{2,1,0:T(8,128)(2,1)S(1)} collective-permute-done((bf16[8,64,256]{2,1,0:T(8,128)(2,1)S(1)}, bf16[8,64,256]{2,1,0:T(8,128)(2,1)S(1)}, u32[]{:S(2)}, u32[]{:S(2)}) %collective-permute-start.14) | collective-permute-done | bytes 262176 | tf_op jit(solution)/shard_map/ppermute | solution.py:30
  41.8 1.3 collective-permute-done.3
  43.8 0.9 collective-permute-done.4.b1_ref
  45.2 6.0 %shard_map.288 = (bf16[1024,512]{1,0:T(8,128)(2,1)S(1)}, f32[4,1024,128]{2,1,0:T(8,128)}, f32[8,512]{1,0:T(8,128)S(1)}, bf16[512,512]{1,0:T(8,128)(2,1)S(1)}) custom-call(s32[1]{0:T(128)} %bitcast.me_ref, bf16[1024,512]{1,0:T(8,128)(2,1)S(1)} %copy-done, bf16[16,64,128]{2,1,0:T(8,128)(2,1)S(1)} %constant_dynamic-update-slice_fusion.b0_ref, ...), custom_call_target="tpu_custom_call" | custom-call | tf_op jit(solution)/shard_map/pallas_call | solution.py:425
  51.1 1.0 copy-done.3
  52.1 2.0 %collective-permute-start.5 = (f32[8,512]{1,0:T(8,128)S(1)}, f32[8,512]{1,0:T(8,128)S(1)}, u32[]{:S(2)}, u32[]{:S(2)}) collective-permute-start(f32[8,512]{1,0:T(8,128)S(1)} %get-tuple-element.36), channel_id=1, source_target_pairs={{0,1},{2,3},{4,5},{6,7},{8,9},{10,11},{12,13},{14,15},{16,17},{18,... | collective-permute-start | bytes 49160 | tf_op jit(solution)/shard_map/ppermute | solution.py:562
  55.2 22.9 %shard_map.289 = (bf16[1024,512]{1,0:T(8,128)(2,1)}, f32[4,1024,128]{2,1,0:T(8,128)}, bf16[1024,512]{1,0:T(8,128)(2,1)S(1)}, f32[4,1024,128]{2,1,0:T(8,128)}, f3...) custom-call(s32[1]{0:T(128)} %bitcast.me_ref, ...), custom_call_target="tpu_custom_call" | custom-call | tf_op jit(solution)/shard_map/pallas_call | solution.py:425
  78.1 1.0 copy-done.5
  79.1 0.8 copy-done.6
  79.9 1.5 collective-permute-start.16
  81.4 1.2 collective-permute-start.22
  83.0 19.8 %shard_map.290 = (f32[1024,512]{1,0:T(8,128)}, bf16[16,64,128]{2,1,0:T(8,128)(2,1)S(1)}, bf16[16,64,128]{2,1,0:T(8,128)(2,1)S(1)}, f32[8,512]{1,0:T(8,128)S(1)}) custom-call(s32[1]{0:T(128)} %bitcast.me_ref, bf16[1024,512]{1,0:T(8,128)(2,1)S(1)} %copy-done.1, bf16[1024,512]{1,0:T(8,128)(2,1)S(1)} %copy-done.2, bf16[1024,512]{1,0:T(8,128)(2,1)S(1)} %copy-done.4, ...), custom_call_target="tpu_custom_call" | custom-call | tf_op jit(solution)/shard_map/pallas_call | solution.py:425
  103.5 1.0 add_convert_fusion.2
  104.5 1.6 %collective-permute-start.23 = (bf16[8,64,128]{2,1,0:T(8,128)(2,1)S(1)}, bf16[8,64,128]{2,1,0:T(8,128)(2,1)S(1)}, u32[]{:S(2)}, u32[]{:S(2)}) collective-permute-start(bf16[8,64,128]{2,1,0:T(8,128)(2,1)S(1)} %slice.340), channel_id=1, source_target_pairs={{0,2},{1,3},{2,0},{3,1},{4,6},{5,7},{6,4},{7,5},{8,10},{9,11},{10,... | collective-permute-start | bytes 393224 | tf_op jit(solution)/shard_map/ppermute | solution.py:30
  106.1 1.0 slice.310
  108.5 1.6 %collective-permute-done.23 = bf16[8,64,128]{2,1,0:T(8,128)(2,1)S(1)} collective-permute-done((bf16[8,64,128]{2,1,0:T(8,128)(2,1)S(1)}, bf16[8,64,128]{2,1,0:T(8,128)(2,1)S(1)}, u32[]{:S(2)}, u32[]{:S(2)}) %collective-permute-start.23) | collective-permute-done | bytes 131104 | tf_op jit(solution)/shard_map/ppermute | solution.py:30
  110.2 1.4 collective-permute-start.24
  111.6 2.0 %collective-permute-done.18 = bf16[576,128]{1,0:T(8,128)(2,1)S(1)} collective-permute-done((bf16[576,128]{1,0:T(8,128)(2,1)S(1)}, bf16[576,128]{1,0:T(8,128)(2,1)S(1)}, u32[]{:S(2)}, u32[]{:S(2)}) %collective-permute-start.18) | collective-permute-done | bytes 147488 | tf_op jit(solution)/shard_map/ppermute | solution.py:30
  113.7 0.9 collective-permute-done.24
  114.6 1.7 %collective-permute-start.25 = (bf16[2,64,128]{2,1,0:T(8,128)(2,1)S(1)}, bf16[2,64,128]{2,1,0:T(8,128)(2,1)S(1)}, u32[]{:S(2)}, u32[]{:S(2)}) collective-permute-start(bf16[2,64,128]{2,1,0:T(8,128)(2,1)S(1)} %slice.344), channel_id=1, source_target_pairs={{0,8},{1,9},{2,10},{3,11},{4,12},{5,13},{6,14},{7,15},{8,0},{9,1},... | collective-permute-start | bytes 98312 | tf_op jit(solution)/shard_map/ppermute | solution.py:30
  116.3 2.2 %collective-permute-done.25 = bf16[2,64,128]{2,1,0:T(8,128)(2,1)S(1)} collective-permute-done((bf16[2,64,128]{2,1,0:T(8,128)(2,1)S(1)}, bf16[2,64,128]{2,1,0:T(8,128)(2,1)S(1)}, u32[]{:S(2)}, u32[]{:S(2)}) %collective-permute-start.25) | collective-permute-done | bytes 32800 | tf_op jit(solution)/shard_map/ppermute | solution.py:30
  119.0 1.4 collective-permute-start.19
  120.4 2.9 %collective-permute-done.26 = bf16[1,64,128]{2,1,0:T(8,128)(2,1)S(1)} collective-permute-done((bf16[1,64,128]{2,1,0:T(8,128)(2,1)S(1)}, bf16[1,64,128]{2,1,0:T(8,128)(2,1)S(1)}, u32[]{:S(2)}, u32[]{:S(2)}) %collective-permute-start.26) | collective-permute-done | bytes 16416 | tf_op jit(solution)/shard_map/ppermute | solution.py:30
  123.5 1.8 %collective-permute-start.20 = (bf16[192,128]{1,0:T(8,128)(2,1)S(1)}, bf16[192,128]{1,0:T(8,128)(2,1)S(1)}, u32[]{:S(2)}, u32[]{:S(2)}) collective-permute-start(bf16[192,128]{1,0:T(8,128)(2,1)S(1)} %pad_maximum_fusion.11), channel_id=1, source_target_pairs={{0,8},{1,9},{2,10},{3,11},{4,12},{5,13},{6,14},{7,15},{8,0},{9,1},... | collective-permute-start | bytes 147464 | tf_op jit(solution)/shard_map/ppermute | solution.py:30
  126.0 1.7 %collective-permute-done.20 = bf16[192,128]{1,0:T(8,128)(2,1)S(1)} collective-permute-done((bf16[192,128]{1,0:T(8,128)(2,1)S(1)}, bf16[192,128]{1,0:T(8,128)(2,1)S(1)}, u32[]{:S(2)}, u32[]{:S(2)}) %collective-permute-start.20) | collective-permute-done | bytes 49184 | tf_op jit(solution)/shard_map/ppermute | solution.py:30
  127.7 2.7 %collective-permute-start.21 = (bf16[128,128]{1,0:T(8,128)(2,1)S(1)}, bf16[128,128]{1,0:T(8,128)(2,1)S(1)}, u32[]{:S(2)}, u32[]{:S(2)}) collective-permute-start(bf16[128,128]{1,0:T(8,128)(2,1)S(1)} %pad_maximum_fusion.15), channel_id=1, source_target_pairs={{0,16},{1,17},{2,18},{3,19},{4,20},{5,21},{6,22},{7,23},{8,24},{9,... | collective-permute-start | bytes 98312 | tf_op jit(solution)/shard_map/ppermute | solution.py:30
  130.6 2.2 %collective-permute-start.28 = (bf16[8,64,256]{2,1,0:T(8,128)(2,1)S(1)}, bf16[8,64,256]{2,1,0:T(8,128)(2,1)S(1)}, u32[]{:S(2)}, u32[]{:S(2)}) collective-permute-start(bf16[8,64,256]{2,1,0:T(8,128)(2,1)S(1)} %slice.354), channel_id=1, source_target_pairs={{0,2},{1,3},{2,0},{3,1},{4,6},{5,7},{6,4},{7,5},{8,10},{9,11},{10,... | collective-permute-start | bytes 786440 | tf_op jit(solution)/shard_map/ppermute | solution.py:30
  133.5 3.6 %collective-permute-done.28 = bf16[8,64,256]{2,1,0:T(8,128)(2,1)S(1)} collective-permute-done((bf16[8,64,256]{2,1,0:T(8,128)(2,1)S(1)}, bf16[8,64,256]{2,1,0:T(8,128)(2,1)S(1)}, u32[]{:S(2)}, u32[]{:S(2)}) %collective-permute-start.28) | collective-permute-done | bytes 262176 | tf_op jit(solution)/shard_map/ppermute | solution.py:30
  137.2 1.4 collective-permute-start.29
  138.6 3.6 %collective-permute-done.29 = bf16[4,64,256]{2,1,0:T(8,128)(2,1)S(1)} collective-permute-done((bf16[4,64,256]{2,1,0:T(8,128)(2,1)S(1)}, bf16[4,64,256]{2,1,0:T(8,128)(2,1)S(1)}, u32[]{:S(2)}, u32[]{:S(2)}) %collective-permute-start.29) | collective-permute-done | bytes 131104 | tf_op jit(solution)/shard_map/ppermute | solution.py:30
  142.3 1.7 %collective-permute-start.30 = (bf16[2,64,256]{2,1,0:T(8,128)(2,1)S(1)}, bf16[2,64,256]{2,1,0:T(8,128)(2,1)S(1)}, u32[]{:S(2)}, u32[]{:S(2)}) collective-permute-start(bf16[2,64,256]{2,1,0:T(8,128)(2,1)S(1)} %slice.358), channel_id=1, source_target_pairs={{0,8},{1,9},{2,10},{3,11},{4,12},{5,13},{6,14},{7,15},{8,0},{9,1},... | collective-permute-start | bytes 196616 | tf_op jit(solution)/shard_map/ppermute | solution.py:30
  144.0 2.6 %collective-permute-done.30 = bf16[2,64,256]{2,1,0:T(8,128)(2,1)S(1)} collective-permute-done((bf16[2,64,256]{2,1,0:T(8,128)(2,1)S(1)}, bf16[2,64,256]{2,1,0:T(8,128)(2,1)S(1)}, u32[]{:S(2)}, u32[]{:S(2)}) %collective-permute-start.30) | collective-permute-done | bytes 65568 | tf_op jit(solution)/shard_map/ppermute | solution.py:30
  (168 shorter events, 23.0 us)
Async XLA Ops:
  7.6 15.3 %collective-permute-start = (bf16[96,128]{1,0:T(8,128)(2,1)S(1)}, bf16[96,128]{1,0:T(8,128)(2,1)S(1)}, u32[]{:S(2)}, u32[]{:S(2)}) collective-permute-start(bf16[96,128]{1,0:T(8,128)(2,1)S(1)} %pad_maximum_fusion.16), channel_id=1, source_target_pairs={{0,16},{1,17},{2,18},{3,19},{4,20},{5,21},{6,22},{7,23},{8,24},{9,... | collective-permute-start | bytes 73736 | tf_op jit(solution)/shard_map/ppermute | solution.py:30
  12.5 8.7 %collective-permute-start.6 = (bf16[1,64,128]{2,1,0:T(8,128)(2,1)S(1)}, bf16[1,64,128]{2,1,0:T(8,128)(2,1)S(1)}, u32[]{:S(2)}, u32[]{:S(2)}) collective-permute-start(bf16[1,64,128]{2,1,0:T(8,128)(2,1)S(1)} %get-tuple-element.67), channel_id=1, source_target_pairs={{0,16},{1,17},{2,18},{3,19},{4,20},{5,21},{6,22},{7,23},{8,24},{9,... | collective-permute-start | bytes 49160 | tf_op jit(solution)/shard_map/ppermute | solution.py:30
  13.3 10.2 %collective-permute-start.11 = (bf16[1,64,256]{2,1,0:T(8,128)(2,1)S(1)}, bf16[1,64,256]{2,1,0:T(8,128)(2,1)S(1)}, u32[]{:S(2)}, u32[]{:S(2)}) collective-permute-start(bf16[1,64,256]{2,1,0:T(8,128)(2,1)S(1)} %maximum_bitcast_fusion), channel_id=1, source_target_pairs={{0,16},{1,17},{2,18},{3,19},{4,20},{5,21},{6,22},{7,23},{8,24},{9,... | collective-permute-start | bytes 98312 | tf_op jit(solution)/shard_map/ppermute | solution.py:30
  21.3 4.3 %collective-permute-start.7 = (bf16[2,64,128]{2,1,0:T(8,128)(2,1)S(1)}, bf16[2,64,128]{2,1,0:T(8,128)(2,1)S(1)}, u32[]{:S(2)}, u32[]{:S(2)}) collective-permute-start(bf16[2,64,128]{2,1,0:T(8,128)(2,1)S(1)} %pad_maximum_fusion.14), channel_id=1, source_target_pairs={{0,8},{1,9},{2,10},{3,11},{4,12},{5,13},{6,14},{7,15},{8,0},{9,1},... | collective-permute-start | bytes 98312 | tf_op jit(solution)/shard_map/ppermute | solution.py:30
  22.9 4.2 %collective-permute-start.1 = (bf16[160,128]{1,0:T(8,128)(2,1)S(1)}, bf16[160,128]{1,0:T(8,128)(2,1)S(1)}, u32[]{:S(2)}, u32[]{:S(2)}) collective-permute-start(bf16[160,128]{1,0:T(8,128)(2,1)S(1)} %pad_maximum_fusion.12), channel_id=1, source_target_pairs={{0,8},{1,9},{2,10},{3,11},{4,12},{5,13},{6,14},{7,15},{8,0},{9,1},... | collective-permute-start | bytes 122888 | tf_op jit(solution)/shard_map/ppermute | solution.py:30
  23.5 5.2 %collective-permute-start.12 = (bf16[2,64,256]{2,1,0:T(8,128)(2,1)S(1)}, bf16[2,64,256]{2,1,0:T(8,128)(2,1)S(1)}, u32[]{:S(2)}, u32[]{:S(2)}) collective-permute-start(bf16[2,64,256]{2,1,0:T(8,128)(2,1)S(1)} %pad_maximum_fusion.10), channel_id=1, source_target_pairs={{0,8},{1,9},{2,10},{3,11},{4,12},{5,13},{6,14},{7,15},{8,0},{9,1},... | collective-permute-start | bytes 196616 | tf_op jit(solution)/shard_map/ppermute | solution.py:30
  25.5 5.0 %collective-permute-start.8 = (bf16[4,64,128]{2,1,0:T(8,128)(2,1)S(1)}, bf16[4,64,128]{2,1,0:T(8,128)(2,1)S(1)}, u32[]{:S(2)}, u32[]{:S(2)}) collective-permute-start(bf16[4,64,128]{2,1,0:T(8,128)(2,1)S(1)} %pad_maximum_fusion.9), channel_id=1, source_target_pairs={{0,4},{1,5},{2,6},{3,7},{4,0},{5,1},{6,2},{7,3},{8,12},{9,13},{10,... | collective-permute-start | bytes 196616 | tf_op jit(solution)/shard_map/ppermute | solution.py:30
  27.2 4.9 %collective-permute-start.2 = (bf16[288,128]{1,0:T(8,128)(2,1)S(1)}, bf16[288,128]{1,0:T(8,128)(2,1)S(1)}, u32[]{:S(2)}, u32[]{:S(2)}) collective-permute-start(bf16[288,128]{1,0:T(8,128)(2,1)S(1)} %pad_maximum_fusion.7), channel_id=1, source_target_pairs={{0,4},{1,5},{2,6},{3,7},{4,0},{5,1},{6,2},{7,3},{8,12},{9,13},{10,... | collective-permute-start | bytes 221192 | tf_op jit(solution)/shard_map/ppermute | solution.py:30
  28.7 16.5 %copy-start = (bf16[1024,512]{1,0:T(8,128)(2,1)S(1)}, bf16[1024,512]{1,0:T(8,128)(2,1)}, u32[]{:S(2)}) copy-start(bf16[1024,512]{1,0:T(8,128)(2,1)} %x_ref.5) | copy-start | bytes 3145732
  28.7 5.0 %collective-permute-start.13 = (bf16[4,64,256]{2,1,0:T(8,128)(2,1)S(1)}, bf16[4,64,256]{2,1,0:T(8,128)(2,1)S(1)}, u32[]{:S(2)}, u32[]{:S(2)}) collective-permute-start(bf16[4,64,256]{2,1,0:T(8,128)(2,1)S(1)} %pad_maximum_fusion.5), channel_id=1, source_target_pairs={{0,4},{1,5},{2,6},{3,7},{4,0},{5,1},{6,2},{7,3},{8,12},{9,13},{10,... | collective-permute-start | bytes 393224 | tf_op jit(solution)/shard_map/ppermute | solution.py:30
  30.5 12.7 %collective-permute-start.9 = (bf16[8,64,128]{2,1,0:T(8,128)(2,1)S(1)}, bf16[8,64,128]{2,1,0:T(8,128)(2,1)S(1)}, u32[]{:S(2)}, u32[]{:S(2)}) collective-permute-start(bf16[8,64,128]{2,1,0:T(8,128)(2,1)S(1)} %pad_maximum_fusion.4), channel_id=1, source_target_pairs={{0,2},{1,3},{2,0},{3,1},{4,6},{5,7},{6,4},{7,5},{8,10},{9,11},{10,... | collective-permute-start | bytes 393224 | tf_op jit(solution)/shard_map/ppermute | solution.py:30
  33.8 8.0 %collective-permute-start.14 = (bf16[8,64,256]{2,1,0:T(8,128)(2,1)S(1)}, bf16[8,64,256]{2,1,0:T(8,128)(2,1)S(1)}, u32[]{:S(2)}, u32[]{:S(2)}) collective-permute-start(bf16[8,64,256]{2,1,0:T(8,128)(2,1)S(1)} %pad_maximum_fusion.1), channel_id=1, source_target_pairs={{0,2},{1,3},{2,0},{3,1},{4,6},{5,7},{6,4},{7,5},{8,10},{9,11},{10,... | collective-permute-start | bytes 786440 | tf_op jit(solution)/shard_map/ppermute | solution.py:30
  35.3 7.8 %collective-permute-start.3 = (bf16[8,64,128]{2,1,0:T(8,128)(2,1)S(1)}, bf16[8,64,128]{2,1,0:T(8,128)(2,1)S(1)}, u32[]{:S(2)}, u32[]{:S(2)}) collective-permute-start(bf16[8,64,128]{2,1,0:T(8,128)(2,1)S(1)} %pad_maximum_fusion.3), channel_id=1, source_target_pairs={{0,2},{1,3},{2,0},{3,1},{4,6},{5,7},{6,4},{7,5},{8,10},{9,11},{10,... | collective-permute-start | bytes 393224 | tf_op jit(solution)/shard_map/ppermute | solution.py:30
  41.7 13.2 %collective-permute-start.15 = (bf16[16,64,256]{2,1,0:T(8,128)(2,1)S(1)}, bf16[16,64,256]{2,1,0:T(8,128)(2,1)S(1)}, u32[]{:S(2)}, u32[]{:S(2)}) collective-permute-start(bf16[16,64,256]{2,1,0:T(8,128)(2,1)S(1)} %constant_dynamic-update-slice_fusion.10.w0_ref), channel_id=1, source_target_pairs={{0,1},{1,0},{2,3},{3,2},{4,5},{5,4},{6,7},{7,6},{8,9},{9,8},{10,11... | collective-permute-start | bytes 1572872 | tf_op jit(solution)/shard_map/ppermute | solution.py:30
  43.1 1.6 %collective-permute-start.4 = (bf16[16,64,128]{2,1,0:T(8,128)(2,1)S(1)}, bf16[16,64,128]{2,1,0:T(8,128)(2,1)S(1)}, u32[]{:S(2)}, u32[]{:S(2)}) collective-permute-start(bf16[16,64,128]{2,1,0:T(8,128)(2,1)S(1)} %constant_dynamic-update-slice_fusion.b0_ref), channel_id=1, source_target_pairs={{0,1},{1,0},{2,3},{3,2},{4,5},{5,4},{6,7},{7,6},{8,9},{9,8},{10,11... | collective-permute-start | bytes 786440 | tf_op jit(solution)/shard_map/ppermute | solution.py:30
  43.3 11.0 %collective-permute-start.10 = (bf16[16,64,128]{2,1,0:T(8,128)(2,1)S(1)}, bf16[16,64,128]{2,1,0:T(8,128)(2,1)S(1)}, u32[]{:S(2)}, u32[]{:S(2)}) collective-permute-start(bf16[16,64,128]{2,1,0:T(8,128)(2,1)S(1)} %constant_dynamic-update-slice_fusion.5.c0_ref), channel_id=1, source_target_pairs={{0,1},{1,0},{2,3},{3,2},{4,5},{5,4},{6,7},{7,6},{8,9},{9,8},{10,11... | collective-permute-start | bytes 786440 | tf_op jit(solution)/shard_map/ppermute | solution.py:30
  51.1 1.0 copy-start.3
  52.1 2.9 %collective-permute-start.5 = (f32[8,512]{1,0:T(8,128)S(1)}, f32[8,512]{1,0:T(8,128)S(1)}, u32[]{:S(2)}, u32[]{:S(2)}) collective-permute-start(f32[8,512]{1,0:T(8,128)S(1)} %get-tuple-element.36), channel_id=1, source_target_pairs={{0,1},{2,3},{4,5},{6,7},{8,9},{10,11},{12,13},{14,15},{16,17},{18,... | collective-permute-start | bytes 49160 | tf_op jit(solution)/shard_map/ppermute | solution.py:562
  55.2 27.8 %copy-start.1 = (bf16[1024,512]{1,0:T(8,128)(2,1)S(1)}, bf16[1024,512]{1,0:T(8,128)(2,1)}, u32[]{:S(2)}) copy-start(bf16[1024,512]{1,0:T(8,128)(2,1)} %x_ref.5) | copy-start | bytes 3145732
  55.2 27.8 %copy-start.2 = (bf16[1024,512]{1,0:T(8,128)(2,1)S(1)}, bf16[1024,512]{1,0:T(8,128)(2,1)}, u32[]{:S(2)}) copy-start(bf16[1024,512]{1,0:T(8,128)(2,1)} %grad_ref.3) | copy-start | bytes 3145732
  55.2 27.8 %copy-start.4 = (bf16[1024,512]{1,0:T(8,128)(2,1)S(1)}, bf16[1024,512]{1,0:T(8,128)(2,1)}, u32[]{:S(2)}) copy-start(bf16[1024,512]{1,0:T(8,128)(2,1)} %copy-done.3) | copy-start | bytes 3145732
  78.1 1.0 copy-start.5
  79.1 0.8 copy-start.6
  79.9 3.1 %collective-permute-start.16 = (f32[8,512]{1,0:T(8,128)S(1)}, f32[8,512]{1,0:T(8,128)S(1)}, u32[]{:S(2)}, u32[]{:S(2)}) collective-permute-start(f32[8,512]{1,0:T(8,128)S(1)} %get-tuple-element.38), channel_id=1, source_target_pairs={{1,0},{3,2},{5,4},{7,6},{9,8},{11,10},{13,12},{15,14},{17,16},{19,... | collective-permute-start | bytes 49160 | tf_op jit(solution)/shard_map/ppermute | solution.py:562
  81.4 22.1 %collective-permute-start.22 = (bf16[16,64,128]{2,1,0:T(8,128)(2,1)S(1)}, bf16[16,64,128]{2,1,0:T(8,128)(2,1)}, u32[]{:S(2)}, u32[]{:S(2)}) collective-permute-start(bf16[16,64,128]{2,1,0:T(8,128)(2,1)S(1)} %get-tuple-element.49), channel_id=1, source_target_pairs={{0,1},{1,0},{2,3},{3,2},{4,5},{5,4},{6,7},{7,6},{8,9},{9,8},{10,11... | collective-permute-start | bytes 786440 | tf_op jit(solution)/shard_map/ppermute | solution.py:30
  83.0 20.1 %copy-start.7 = (bf16[16,64,256]{2,1,0:T(8,128)(2,1)S(1)}, bf16[16,64,256]{2,1,0:T(8,128)(2,1)}, u32[]{:S(2)}) copy-start(bf16[16,64,256]{2,1,0:T(8,128)(2,1)} %copy-done.6) | copy-start | bytes 1572868
  102.9 3.2 %collective-permute-start.17 = (bf16[1088,128]{1,0:T(8,128)(2,1)S(1)}, bf16[1088,128]{1,0:T(8,128)(2,1)}, u32[]{:S(2)}, u32[]{:S(2)}) collective-permute-start(bf16[1088,128]{1,0:T(8,128)(2,1)S(1)} %pad_maximum_fusion), channel_id=1, source_target_pairs={{0,1},{1,0},{2,3},{3,2},{4,5},{5,4},{6,7},{7,6},{8,9},{9,8},{10,11... | collective-permute-start | bytes 835592 | tf_op jit(solution)/shard_map/ppermute | solution.py:30
  103.1 27.3 %collective-permute-start.27 = (bf16[16,64,256]{2,1,0:T(8,128)(2,1)S(1)}, bf16[16,64,256]{2,1,0:T(8,128)(2,1)S(1)}, u32[]{:S(2)}, u32[]{:S(2)}) collective-permute-start(bf16[16,64,256]{2,1,0:T(8,128)(2,1)S(1)} %copy-done.7), channel_id=1, source_target_pairs={{0,1},{1,0},{2,3},{3,2},{4,5},{5,4},{6,7},{7,6},{8,9},{9,8},{10,11... | collective-permute-start | bytes 1572872 | tf_op jit(solution)/shard_map/ppermute | solution.py:30
  104.5 5.6 %collective-permute-start.23 = (bf16[8,64,128]{2,1,0:T(8,128)(2,1)S(1)}, bf16[8,64,128]{2,1,0:T(8,128)(2,1)S(1)}, u32[]{:S(2)}, u32[]{:S(2)}) collective-permute-start(bf16[8,64,128]{2,1,0:T(8,128)(2,1)S(1)} %slice.340), channel_id=1, source_target_pairs={{0,2},{1,3},{2,0},{3,1},{4,6},{5,7},{6,4},{7,5},{8,10},{9,11},{10,... | collective-permute-start | bytes 393224 | tf_op jit(solution)/shard_map/ppermute | solution.py:30
  107.9 5.7 %collective-permute-start.18 = (bf16[576,128]{1,0:T(8,128)(2,1)S(1)}, bf16[576,128]{1,0:T(8,128)(2,1)S(1)}, u32[]{:S(2)}, u32[]{:S(2)}) collective-permute-start(bf16[576,128]{1,0:T(8,128)(2,1)S(1)} %pad_maximum_fusion.2), channel_id=1, source_target_pairs={{0,2},{1,3},{2,0},{3,1},{4,6},{5,7},{6,4},{7,5},{8,10},{9,11},{10,... | collective-permute-start | bytes 442376 | tf_op jit(solution)/shard_map/ppermute | solution.py:30
  110.2 4.3 %collective-permute-start.24 = (bf16[4,64,128]{2,1,0:T(8,128)(2,1)S(1)}, bf16[4,64,128]{2,1,0:T(8,128)(2,1)S(1)}, u32[]{:S(2)}, u32[]{:S(2)}) collective-permute-start(bf16[4,64,128]{2,1,0:T(8,128)(2,1)S(1)} %slice.342), channel_id=1, source_target_pairs={{0,4},{1,5},{2,6},{3,7},{4,0},{5,1},{6,2},{7,3},{8,12},{9,13},{10,... | collective-permute-start | bytes 196616 | tf_op jit(solution)/shard_map/ppermute | solution.py:30
  114.6 4.0 %collective-permute-start.25 = (bf16[2,64,128]{2,1,0:T(8,128)(2,1)S(1)}, bf16[2,64,128]{2,1,0:T(8,128)(2,1)S(1)}, u32[]{:S(2)}, u32[]{:S(2)}) collective-permute-start(bf16[2,64,128]{2,1,0:T(8,128)(2,1)S(1)} %slice.344), channel_id=1, source_target_pairs={{0,8},{1,9},{2,10},{3,11},{4,12},{5,13},{6,14},{7,15},{8,0},{9,1},... | collective-permute-start | bytes 98312 | tf_op jit(solution)/shard_map/ppermute | solution.py:30
  118.6 4.7 %collective-permute-start.26 = (bf16[1,64,128]{2,1,0:T(8,128)(2,1)S(1)}, bf16[1,64,128]{2,1,0:T(8,128)(2,1)S(1)}, u32[]{:S(2)}, u32[]{:S(2)}) collective-permute-start(bf16[1,64,128]{2,1,0:T(8,128)(2,1)S(1)} %slice.346), channel_id=1, source_target_pairs={{0,16},{1,17},{2,18},{3,19},{4,20},{5,21},{6,22},{7,23},{8,24},{9,... | collective-permute-start | bytes 49160 | tf_op jit(solution)/shard_map/ppermute | solution.py:30
  119.0 4.4 %collective-permute-start.19 = (bf16[320,128]{1,0:T(8,128)(2,1)S(1)}, bf16[320,128]{1,0:T(8,128)(2,1)S(1)}, u32[]{:S(2)}, u32[]{:S(2)}) collective-permute-start(bf16[320,128]{1,0:T(8,128)(2,1)S(1)} %pad_maximum_fusion.6), channel_id=1, source_target_pairs={{0,4},{1,5},{2,6},{3,7},{4,0},{5,1},{6,2},{7,3},{8,12},{9,13},{10,... | collective-permute-start | bytes 245768 | tf_op jit(solution)/shard_map/ppermute | solution.py:30
  123.5 4.2 %collective-permute-start.20 = (bf16[192,128]{1,0:T(8,128)(2,1)S(1)}, bf16[192,128]{1,0:T(8,128)(2,1)S(1)}, u32[]{:S(2)}, u32[]{:S(2)}) collective-permute-start(bf16[192,128]{1,0:T(8,128)(2,1)S(1)} %pad_maximum_fusion.11), channel_id=1, source_target_pairs={{0,8},{1,9},{2,10},{3,11},{4,12},{5,13},{6,14},{7,15},{8,0},{9,1},... | collective-permute-start | bytes 147464 | tf_op jit(solution)/shard_map/ppermute | solution.py:30
  127.7 5.0 %collective-permute-start.21 = (bf16[128,128]{1,0:T(8,128)(2,1)S(1)}, bf16[128,128]{1,0:T(8,128)(2,1)S(1)}, u32[]{:S(2)}, u32[]{:S(2)}) collective-permute-start(bf16[128,128]{1,0:T(8,128)(2,1)S(1)} %pad_maximum_fusion.15), channel_id=1, source_target_pairs={{0,16},{1,17},{2,18},{3,19},{4,20},{5,21},{6,22},{7,23},{8,24},{9,... | collective-permute-start | bytes 98312 | tf_op jit(solution)/shard_map/ppermute | solution.py:30
  130.6 6.5 %collective-permute-start.28 = (bf16[8,64,256]{2,1,0:T(8,128)(2,1)S(1)}, bf16[8,64,256]{2,1,0:T(8,128)(2,1)S(1)}, u32[]{:S(2)}, u32[]{:S(2)}) collective-permute-start(bf16[8,64,256]{2,1,0:T(8,128)(2,1)S(1)} %slice.354), channel_id=1, source_target_pairs={{0,2},{1,3},{2,0},{3,1},{4,6},{5,7},{6,4},{7,5},{8,10},{9,11},{10,... | collective-permute-start | bytes 786440 | tf_op jit(solution)/shard_map/ppermute | solution.py:30
  137.2 5.0 %collective-permute-start.29 = (bf16[4,64,256]{2,1,0:T(8,128)(2,1)S(1)}, bf16[4,64,256]{2,1,0:T(8,128)(2,1)S(1)}, u32[]{:S(2)}, u32[]{:S(2)}) collective-permute-start(bf16[4,64,256]{2,1,0:T(8,128)(2,1)S(1)} %slice.356), channel_id=1, source_target_pairs={{0,4},{1,5},{2,6},{3,7},{4,0},{5,1},{6,2},{7,3},{8,12},{9,13},{10,... | collective-permute-start | bytes 393224 | tf_op jit(solution)/shard_map/ppermute | solution.py:30
  142.3 4.3 %collective-permute-start.30 = (bf16[2,64,256]{2,1,0:T(8,128)(2,1)S(1)}, bf16[2,64,256]{2,1,0:T(8,128)(2,1)S(1)}, u32[]{:S(2)}, u32[]{:S(2)}) collective-permute-start(bf16[2,64,256]{2,1,0:T(8,128)(2,1)S(1)} %slice.358), channel_id=1, source_target_pairs={{0,8},{1,9},{2,10},{3,11},{4,12},{5,13},{6,14},{7,15},{8,0},{9,1},... | collective-permute-start | bytes 196616 | tf_op jit(solution)/shard_map/ppermute | solution.py:30
  146.6 5.1 %collective-permute-start.31 = (bf16[1,64,256]{2,1,0:T(8,128)(2,1)S(1)}, bf16[1,64,256]{2,1,0:T(8,128)(2,1)S(1)}, u32[]{:S(2)}, u32[]{:S(2)}) collective-permute-start(bf16[1,64,256]{2,1,0:T(8,128)(2,1)S(1)} %slice.360), channel_id=1, source_target_pairs={{0,16},{1,17},{2,18},{3,19},{4,20},{5,21},{6,22},{7,23},{8,24},{9,... | collective-permute-start | bytes 98312 | tf_op jit(solution)/shard_map/ppermute | solution.py:30

commit v2 on v1

v2 whole, which is shorter than its diff:
```python
import functools
import math

import jax
import jax.numpy as jnp
from jax import lax
from jax.experimental import pallas as pl
from jax.experimental.pallas import tpu as pltpu
from jax.sharding import PartitionSpec as P

SEQ_LEN = 2048
LANES = 128
TILE = 256
SIDE = 16
AXES = ("fsdp", "tensor")
norm_epsilon = 1e-05
GELU_SCALE = math.sqrt(2.0 / math.pi)
GELU_CUBE = 0.044715
F32 = jnp.float32
BF16 = jnp.bfloat16
MIB = 1024 * 1024


def log2(value):
    return value.bit_length() - 1


def flip(value, bit, count):
    return lax.ppermute(value, AXES, [(i, i ^ (1 << bit)) for i in range(count)])


def dot(left, right, left_dim=1, right_dim=0):
    return lax.dot_general(
        left, right, (((left_dim,), (right_dim,)), ((), ())), preferred_element_type=F32
    )


def fold_rows(value):
    rows, width = value.shape
    return jnp.sum(value.reshape(rows // 8, 8, width), axis=0)


def wide(mask, width):
    return jnp.concatenate([mask] * (width // LANES), axis=1)


def grid_index(dims, axis):
    return lax.broadcasted_iota(jnp.int32, dims, axis)


def regroup_matrix(states, shards):
    own = log2(states // shards)
    width = 2 * states
    source = grid_index((width, width), 0)
    target = grid_index((width, width), 1)
    part = (source >> own) & 1
    place = part * states + ((source >> (own + 1)) << own) + (source & ((1 << own) - 1))
    return jnp.where(place == target, 1.0, 0.0).astype(BF16)


def turn_matrix():
    source = grid_index((TILE, TILE), 0)
    target = grid_index((TILE, TILE), 1)
    bits = log2(SIDE)
    place = ((source & (SIDE - 1)) << bits) + (source >> bits)
    return jnp.where(place == target, 1.0, 0.0)


class Plan:
    def __init__(self, mesh, rows, group_rows, features, states, units):
        self.fsdp = mesh.shape["fsdp"]
        self.tensor = mesh.shape["tensor"]
        self.count = self.fsdp * self.tensor
        self.bits = log2(self.count)
        outer = list(range(self.bits - 1, 2, -1))
        self.outer = outer
        self.up = [*outer, 2, 1, 0]
        self.up_crossed = [*outer, 1, 2, 0]
        self.down = [0, 1, 2, *outer[::-1]]
        self.down_crossed = [0, 2, 1, *outer[::-1]]
        self.halves = 2 if features // self.fsdp >= 32 else 1
        self.rows = rows
        self.group_rows = group_rows
        self.features = features
        self.states = states
        self.units = units
        self.own_states = states // self.tensor
        self.own_rows = features // self.fsdp
        self.pieces = SEQ_LEN // rows
        self.tiles = rows // TILE
        self.chunks = self.tiles * SIDE

    def slot_owner(self, slot, me, order):
        owner = me
        for place, bit in enumerate(order):
            owner = owner ^ (((slot >> (self.bits - 1 - place)) & 1) << bit)
        shift = log2(self.tensor)
        return owner >> shift, owner & (self.tensor - 1)

    def tile_rows(self, index):
        return pl.ds(pl.multiple_of(index * TILE, TILE), TILE)


def step_rows(tile, place):
    return pl.ds(pl.multiple_of(tile * TILE + place * SIDE, SIDE), SIDE)


def scan_pass(plan, keep_ref, start, extra, reverse, visit):
    def step(index, carried):
        now, extra = carried
        place = SIDE - 1 - index if reverse else index
        after = []
        for tile in range(plan.tiles):
            at = step_rows(tile, place)
            state, extra = visit(tile, at, keep_ref[at, :], now[tile], extra)
            after.append(state)
        return after, extra

    return lax.fori_loop(0, SIDE, step, (start, extra), unroll=2)


def local_ends(plan, source_ref, keep_ref, rate, reverse):
    states = plan.states
    zero = jnp.zeros((SIDE, states), F32)
    rate_re = jnp.broadcast_to(rate[0], zero.shape)
    rate_im = jnp.broadcast_to(rate[1], zero.shape)
    one = jnp.ones((SIDE, LANES), F32)

    def visit(tile, at, keep, state, extra):
        now_re, now_im, hold = state
        held = wide(keep, states)
        pass_re, pass_im = held * rate_re, held * rate_im
        source = source_ref[at, :]
        next_re = (source[:, :states] + pass_re * now_re) - pass_im * now_im
        next_im = (source[:, states:] + pass_re * now_im) + pass_im * now_re
        return (next_re, next_im, hold * keep), extra

    ends, _ = scan_pass(plan, keep_ref, [(zero, zero, one)] * plan.tiles, 0, reverse, visit)
    return tuple(jnp.concatenate([end[part] for end in ends], axis=0) for part in range(3))


def shifted(value, distance, reverse):
    count = value.shape[0]
    row = grid_index(value.shape, 0)
    if reverse:
        moved = pltpu.roll(value, count - distance, 0)
        return jnp.where(row < count - distance, moved, 0.0)
    moved = pltpu.roll(value, distance, 0)
    return jnp.where(row >= distance, moved, 0.0)


def chunk_entries(plan, ends_re, ends_im, hold, rate, start, reverse):
    states, count = plan.states, plan.chunks
    power_re, power_im = rate
    for _ in range(log2(SIDE)):
        power_re, power_im = power_re * power_re - power_im * power_im, 2.0 * power_re * power_im
    first = count - 1 if reverse else 0
    if start is not None:
        at_first = grid_index((count, states), 0) == first
        held = jnp.where(at_first, wide(hold, states), 0.0)
        pass_re, pass_im = held * power_re, held * power_im
        ends_re = ends_re + (pass_re * start[0] - pass_im * start[1])
        ends_im = ends_im + (pass_re * start[1] + pass_im * start[0])
    distance = 1
    while distance < count:
        earlier_re = shifted(ends_re, distance, reverse)
        earlier_im = shifted(ends_im, distance, reverse)
        held = wide(hold, states)
        pass_re, pass_im = held * power_re, held * power_im
        ends_re = ends_re + (pass_re * earlier_re - pass_im * earlier_im)
        ends_im = ends_im + (pass_re * earlier_im + pass_im * earlier_re)
        hold = hold * shifted(hold, distance, reverse)
        power_re, power_im = power_re * power_re - power_im * power_im, 2.0 * power_re * power_im
        distance *= 2
    last = slice(0, 1) if reverse else slice(count - 1, count)
    leaving = jnp.concatenate([ends_re[last], ends_im[last]], axis=1)
    if start is None:
        return None, leaving
    entry_re = shifted(ends_re, 1, reverse) + jnp.where(at_first, start[0], 0.0)
    entry_im = shifted(ends_im, 1, reverse) + jnp.where(at_first, start[1], 0.0)
    entries = []
    for tile in range(plan.tiles):
        at = slice(tile * SIDE, (tile + 1) * SIDE)
        entries.append((entry_re[at], entry_im[at]))
    return entries, leaving


def block_places(plan, me, order, refs, base, rows, start):
    slot = 0
    for ref in refs:
        for place in range(plan.count // 2):
            band, shard = plan.slot_owner(slot, me, order)
            slot += 1
            first = pl.multiple_of(band * plan.own_rows + start, rows)
            yield ref, base + place * rows, pl.ds(first, rows), shard


def collect(plan, me, order, refs, base, rows, start, targets):
    for ref, row, at, shard in block_places(plan, me, order, refs, base, rows, start):
        for first, width, out_ref, lanes in targets:
            column = pl.multiple_of(lanes + shard * width, LANES)
            out_ref[at, pl.ds(column, width)] = ref[row : row + rows, first : first + width].astype(
                out_ref.dtype
            )


def distribute(plan, me, order, refs, base, rows, start, targets):
    for ref, row, at, shard in block_places(plan, me, order, refs, base, rows, start):
        for first, width, full_ref, lanes in targets:
            column = pl.multiple_of(lanes + shard * width, LANES)
            ref[row : row + rows, first : first + width] = full_ref[at, pl.ds(column, width)].astype(
                ref.dtype
            )


def half_blocks(plan, straight, crossed):
    rows = plan.own_rows // plan.halves
    for half in range(plan.halves):
        yield (straight, crossed)[half], half * plan.count // 2 * rows, rows, half * rows


def start_copies(pairs, sems):
    copies = [
        pltpu.make_async_copy(source, target, sems.at[place])
        for place, (source, target) in enumerate(pairs)
    ]
    for copy in copies:
        copy.start()
    return copies


def pack_kernel(plan, me_ref, *refs):
    sources, outs, held, sems = refs[:14], refs[14:16], refs[16:30], refs[30]
    copies = start_copies(list(zip(sources, held)), sems)
    first_ref, second_ref = outs
    band = me_ref[0] >> log2(plan.tensor)
    rows, features = plan.own_rows, plan.features
    for copy in copies:
        copy.wait()
    first_ref[:rows, :] = jnp.concatenate([held[0][...], held[1][...]], axis=1)
    second_ref[...] = jnp.concatenate([ref[...] for ref in held[2:6]], axis=1)
    placed = []
    lane = grid_index((1, features), 1)
    for ref in held[6:]:
        length = ref.shape[1]
        value = ref[...].astype(F32)
        value = jnp.concatenate([value] * (features // length), axis=1)
        placed.append(jnp.where((lane >> log2(length)) == band, value, 0.0))
    placed = jnp.concatenate(placed, axis=0).astype(BF16)
    for part in range(features // LANES):
        first_ref[rows + 8 * part : rows + 8 * part + 8, :] = placed[
            :, part * LANES : (part + 1) * LANES
        ]


def token_kernel(plan, me_ref, x_ref, segments_ref, stats_ref, masks_ref, flags_ref):
    shard = me_ref[0] & (plan.tensor - 1)
    ids = segments_ref[...]
    count = ids.shape[0]
    lane = grid_index(ids.shape, 1)
    position = (grid_index(ids.shape, 0) * LANES + lane) & (SEQ_LEN - 1)
    turned = pltpu.roll(ids, 1, 1)
    before = jnp.where(lane == 0, pltpu.roll(turned, 1, 0), turned)
    turned = pltpu.roll(ids, LANES - 1, 1)
    after = jnp.where(lane == LANES - 1, pltpu.roll(turned, count - 1, 0), turned)
    flags_ref[0] = jnp.where((position > 0) & (ids == before), 1.0, 0.0)
    flags_ref[1] = jnp.where((position < SEQ_LEN - 1) & (ids == after), 1.0, 0.0)
    flags_ref[2] = jnp.where(ids > 0, 1.0, 0.0)
    turn = turn_matrix()
    plain = jnp.where(grid_index((TILE, TILE), 0) == grid_index((TILE, TILE), 1), 1.0, 0.0)
    ones = jnp.ones((TILE, LANES), BF16)
    per_tile = TILE // LANES
    own = plan.rows // LANES
    flags = [flags_ref[kind, pl.ds(pl.multiple_of(shard * own, own), own), :] for kind in range(3)]
    for tile in range(plan.tiles):
        at = slice(tile * TILE, (tile + 1) * TILE)
        for kind in range(4):
            rows = flags[min(kind, 2)][tile * per_tile : (tile + 1) * per_tile, :]
            line = jnp.concatenate([rows[part : part + 1, :] for part in range(per_tile)], axis=1)
            spread = (plain if kind == 3 else turn) * line
            masks_ref[kind, at, :] = dot(spread.astype(BF16), ones)

    def rows_step(index, _):
        at = plan.tile_rows(index)
        values = x_ref[at, :].astype(F32)
        mean = jnp.mean(values, axis=1, keepdims=True)
        centred = values - mean
        inverse = lax.rsqrt(jnp.mean(centred * centred, axis=1, keepdims=True) + norm_epsilon)
        stats_ref[0, at, :] = jnp.broadcast_to(mean, (TILE, LANES))
        stats_ref[1, at, :] = jnp.broadcast_to(inverse, (TILE, LANES))
        return 0

    lax.fori_loop(0, plan.tiles, rows_step, 0)


def standard_rows(plan, x_ref, stats_ref, at):
    mean = wide(stats_ref[0, at, :], plan.features)
    inverse = wide(stats_ref[1, at, :], plan.features)
    return (x_ref[at, :].astype(F32) - mean) * inverse, inverse


def read_vectors(vec_ref):
    count = vec_ref.shape[0] // 8
    parts = [vec_ref[8 * part : 8 * part + 8, :].astype(F32) for part in range(count)]
    return jnp.concatenate(parts, axis=1)


def enter_kernel(
    plan, me_ref, x_ref, stats_ref, b0_ref, b1_ref, vec_ref, masks_ref,
    normed_ref, source_ref, ends_ref, hold_ref, carry_ref, input_map_ref, params_ref,
    pack_ref,
):
    states = plan.states
    collect(
        plan, me_ref[0], plan.up[::-1], (b0_ref, b1_ref), 0, plan.own_rows, 0,
        [(0, 2 * plan.own_states, pack_ref, 0)],
    )
    input_map_ref[...] = dot(
        pack_ref[...].astype(BF16), regroup_matrix(states, plan.tensor)
    ).astype(BF16)
    vectors = read_vectors(vec_ref)
    gain, shift = vectors[0:1], vectors[1:2]
    speed = jnp.exp(vectors[5:6, :states])
    modulus = jnp.exp(-speed)
    rotation = jnp.exp(vectors[6:7, :states])
    rate = (modulus * jnp.cos(rotation), modulus * jnp.sin(rotation))
    rest = 1.0 - modulus * modulus
    gamma = jnp.exp(vectors[7:8, :states]) * jnp.sqrt(rest)
    params_ref[...] = jnp.concatenate(
        [
            jnp.concatenate(rate, axis=1),
            jnp.concatenate([gamma, speed], axis=1),
            jnp.concatenate([modulus, rest], axis=1),
            jnp.concatenate([rotation, rotation], axis=1),
            jnp.zeros((4, 2 * states), F32),
        ],
        axis=0,
    )
    gamma_pair = jnp.concatenate([gamma, gamma], axis=1)
    turn = turn_matrix().astype(BF16)

    def rows_step(index, _):
        at = plan.tile_rows(index)
        standard, _ = standard_rows(plan, x_ref, stats_ref, at)
        normed = (standard * gain + shift).astype(BF16)
        normed_ref[at, :] = normed
        turned = dot(turn, normed).astype(BF16)
        drive = dot(turned, input_map_ref[...])
        source_ref[at, :] = drive * gamma_pair * wide(masks_ref[2, at, :], 2 * states)
        return 0

    lax.fori_loop(0, plan.tiles, rows_step, 0)
    ends_re, ends_im, hold = local_ends(plan, source_ref, masks_ref.at[0], rate, False)
    ends_ref[...] = jnp.concatenate([ends_re, ends_im], axis=1)
    hold_ref[...] = hold
    _, leaving = chunk_entries(plan, ends_re, ends_im, hold, rate, None, False)
    carry_ref[...] = jnp.broadcast_to(leaving, carry_ref.shape)


def middle_kernel(
    plan, me_ref, x_ref, grad_ref, normed_ref, source_ref, ends_ref, hold_ref, carry_ref,
    g0_ref, g1_ref, vec_ref, params_ref, masks_ref,
    mixed_ref, hidden_ref, lru_grad_ref, state_grad_ref, act_ref, unit_grad_ref, low_ref, sums_ref,
    pack_ref, wpack_ref, out_map_ref,
):
    states, features, units = plan.states, plan.features, plan.units
    pair = 2 * plan.own_states
    targets = [
        (0, pair, pack_ref, 0),
        (pair, units, wpack_ref, 0),
        (pair + units, units, wpack_ref, features),
    ]
    for order, base, rows, first in half_blocks(plan, plan.up[::-1], plan.up_crossed[::-1]):
        collect(plan, me_ref[0], order, (g0_ref, g1_ref), base, rows, first, targets)
    sign = jnp.where(grid_index((1, 2 * states), 1) < states, 1.0, -1.0)
    regroup = regroup_matrix(states, plan.tensor)
    out_map_ref[...] = (dot(pack_ref[...].astype(BF16), regroup) * sign).astype(BF16)
    rate = (params_ref[0:1, :states], params_ref[0:1, states:])
    start = (carry_ref[0:1, :states], carry_ref[0:1, states:])
    entries, _ = chunk_entries(
        plan, ends_ref[:, :states], ends_ref[:, states:], hold_ref[...], rate, start, False
    )
    rate_re = jnp.broadcast_to(rate[0], (SIDE, states))
    rate_im = jnp.broadcast_to(rate[1], (SIDE, states))

    def visit(tile, at, keep, state, extra):
        now_re, now_im = state
        held = wide(keep, states)
        pass_re, pass_im = held * rate_re, held * rate_im
        source = source_ref[at, :]
        next_re = (source[:, :states] + pass_re * now_re) - pass_im * now_im
        next_im = (source[:, states:] + pass_re * now_im) + pass_im * now_re
        hidden_ref[at, :states] = next_re
        hidden_ref[at, states:] = next_im
        return (next_re, next_im), extra

    scan_pass(plan, masks_ref.at[0], entries, 0, False, visit)
    vectors = read_vectors(vec_ref)
    skip = vectors[2:3]
    biases = jnp.concatenate([vectors[3:4], vectors[4:5]], axis=1)
    sums_ref[...] = jnp.zeros_like(sums_ref)
    turn = turn_matrix().astype(BF16)

    def rows_step(index, _):
        at = plan.tile_rows(index)
        low = dot(turn, hidden_ref[at, :].astype(BF16)).astype(BF16)
        low_ref[at, :] = low
        normed = normed_ref[at, :].astype(F32)
        lru = dot(low, out_map_ref[...], 1, 1) + skip * normed
        square = lru * lru
        bent = jnp.tanh(lru * (GELU_SCALE + (GELU_SCALE * GELU_CUBE) * square))
        half = 0.5 + 0.5 * bent
        act = (lru * half).astype(BF16)
        slope = half + lru * (1.0 - bent * bent) * (
            0.5 * GELU_SCALE + (1.5 * GELU_SCALE * GELU_CUBE) * square
        )
        act_ref[at, :] = act
        mapped = dot(act, wpack_ref[...].astype(BF16)) + biases
        value = mapped[:, :features]
        opening = 0.5 + 0.5 * jnp.tanh(0.5 * mapped[:, features:])
        live = wide(masks_ref[3, at, :], features)
        gated = value * opening
        mixed_ref[at, :] = (
            x_ref[at, :].astype(F32) + live * gated.astype(BF16).astype(F32)
        ).astype(BF16)
        value_grad = live * grad_ref[at, :].astype(F32) * opening
        gate_grad = value_grad * (value - gated)
        sums_ref[8:16, :] += fold_rows(value_grad)
        sums_ref[16:24, :] += fold_rows(gate_grad)
        unit_grad = jnp.concatenate([value_grad, gate_grad], axis=1).astype(BF16)
        unit_grad_ref[at, :] = unit_grad
        act_grad = dot(unit_grad, wpack_ref[...].astype(BF16), 1, 1)
        lru_grad = act_grad * slope
        sums_ref[0:8, :] += fold_rows(lru_grad * normed)
        lru_grad = lru_grad.astype(BF16)
        lru_grad_ref[at, :] = lru_grad
        turned = dot(turn, lru_grad).astype(BF16)
        state_grad_ref[at, :] = dot(turned, out_map_ref[...])
        return 0

    lax.fori_loop(0, plan.tiles, rows_step, 0)


def back_kernel(
    plan, me_ref, state_grad_ref, params_ref, masks_ref, back_ends_ref, back_hold_ref, back_ref
):
    states = plan.states
    back_rate = (params_ref[0:1, :states], -params_ref[0:1, states:])
    ends_re, ends_im, hold = local_ends(plan, state_grad_ref, masks_ref.at[1], back_rate, True)
    back_ends_ref[...] = jnp.concatenate([ends_re, ends_im], axis=1)
    back_hold_ref[...] = hold
    _, leaving = chunk_entries(plan, ends_re, ends_im, hold, back_rate, None, True)
    back_ref[...] = jnp.broadcast_to(leaving, back_ref.shape)


def weight_kernel(
    plan, me_ref, act_ref, unit_grad_ref, lru_grad_ref, low_ref, keep_ref, send_ref, full_ref, out_ref
):
    states, features, units = plan.states, plan.features, plan.units
    pair = 2 * plan.own_states
    sign = jnp.where(grid_index((1, 2 * states), 1) < states, 1.0, -1.0)
    full_ref[...] = dot(act_ref[...], unit_grad_ref[...], 0, 0)
    out_grad = dot(lru_grad_ref[...], low_ref[...], 0, 0) * sign
    out_ref[...] = dot(out_grad.astype(BF16), regroup_matrix(states, plan.tensor), 1, 1)
    targets = [
        (0, pair, out_ref, 0),
        (pair, units, full_ref, 0),
        (pair + units, units, full_ref, features),
    ]
    for order, base, rows, first in half_blocks(plan, plan.down_crossed, plan.down):
        distribute(plan, me_ref[0], order, (keep_ref, send_ref), base, rows, first, targets)


def leave_kernel(
    plan, me_ref, x_ref, stats_ref, normed_ref, source_ref, ends_ref, hold_ref, carry_ref, hidden_ref,
    state_grad_ref, lru_grad_ref, input_map_ref, vec_ref, params_ref, masks_ref, sums_ref,
    keep_ref, send_ref, normed_grad_ref, out_sums_ref,
    drive_grad_ref, low_ref, full_ref,
):
    states, features = plan.states, plan.features
    params = params_ref[...]
    rate = (params[0:1, :states], params[0:1, states:])
    gamma, speed = params[1:2, :states], params[1:2, states:]
    modulus, rest = params[2:3, :states], params[2:3, states:]
    rotation = params[3:4, :states]
    back_rate = (rate[0], -rate[1])
    start = (carry_ref[0:1, :states], carry_ref[0:1, states:])
    entries, _ = chunk_entries(
        plan, ends_ref[:, :states], ends_ref[:, states:], hold_ref[...], back_rate, start, True
    )
    zero = jnp.zeros((SIDE, states), F32)
    rate_re = jnp.broadcast_to(back_rate[0], zero.shape)
    rate_im = jnp.broadcast_to(back_rate[1], zero.shape)
    gamma_wide = jnp.broadcast_to(gamma, zero.shape)

    def visit(tile, at, keep, state, sums):
        now_re, now_im = state
        held = wide(keep, states)
        next_re, next_im = held * now_re, held * now_im
        hidden_re, hidden_im = hidden_ref[at, :states], hidden_ref[at, states:]
        now_re = (state_grad_ref[at, :states] + rate_re * next_re) - rate_im * next_im
        now_im = (state_grad_ref[at, states:] + rate_re * next_im) + rate_im * next_re
        sums = (
            sums[0] + (hidden_re * next_re + hidden_im * next_im),
            sums[1] + (hidden_re * next_im - hidden_im * next_re),
            sums[2] + (source_ref[at, :states] * now_re + source_ref[at, states:] * now_im),
        )
        scale = gamma_wide * wide(masks_ref[2, at, :], states)
        drive_grad_ref[at, :states] = scale * now_re
        drive_grad_ref[at, states:] = scale * now_im
        return (now_re, now_im), sums

    _, sums = scan_pass(plan, masks_ref.at[1], entries, (zero, zero, zero), True, visit)
    rate_sum_re, rate_sum_im, gamma_sum = (jnp.sum(part, axis=0, keepdims=True) for part in sums)
    nu_grad = speed * (
        gamma_sum * modulus * modulus / rest - (rate_sum_re * rate[0] + rate_sum_im * rate[1])
    )
    theta_grad = rotation * (rate_sum_im * rate[0] - rate_sum_re * rate[1])
    vectors = read_vectors(vec_ref)
    skip = vectors[2:3]
    gain_sum = jnp.zeros((8, features), F32)
    turn = turn_matrix().astype(BF16)

    def rows_step(index, sums):
        gain_sum, shift_sum = sums
        at = plan.tile_rows(index)
        low = dot(turn, drive_grad_ref[at, :].astype(BF16)).astype(BF16)
        low_ref[at, :] = low
        normed_grad = dot(low, input_map_ref[...], 1, 1) + skip * lru_grad_ref[at, :].astype(F32)
        normed_grad_ref[at, :] = normed_grad
        standard, _ = standard_rows(plan, x_ref, stats_ref, at)
        return gain_sum + fold_rows(normed_grad * standard), shift_sum + fold_rows(normed_grad)

    gain_sum, shift_sum = lax.fori_loop(0, plan.tiles, rows_step, (gain_sum, gain_sum))
    into = dot(normed_ref[...], low_ref[...], 0, 0)
    full_ref[...] = dot(into.astype(BF16), regroup_matrix(states, plan.tensor), 1, 1)
    distribute(
        plan, me_ref[0], plan.down, (keep_ref, send_ref), 0, plan.own_rows, 0,
        [(0, 2 * plan.own_states, full_ref, 0)],
    )
    empty = jnp.zeros((1, features - states), F32)
    vector_sums = jnp.concatenate(
        [jnp.sum(part, axis=0, keepdims=True) for part in (gain_sum, shift_sum)]
        + [
            jnp.sum(sums_ref[8 * place : 8 * place + 8, :], axis=0, keepdims=True)
            for place in range(3)
        ]
        + [jnp.concatenate([part, empty], axis=1) for part in (nu_grad, theta_grad, gamma_sum)],
        axis=0,
    )
    base = plan.own_rows * plan.count // 2
    parts = features // LANES
    for part in range(parts):
        piece = vector_sums[:, part * LANES : (part + 1) * LANES]
        out_sums_ref[8 * part : 8 * part + 8, :] = piece
        high = piece.astype(BF16)
        low = (piece - high.astype(F32)).astype(BF16)
        send_ref[base + 8 * part : base + 8 * part + 8, :] = high
        send_ref[base + 8 * (parts + part) : base + 8 * (parts + part) + 8, :] = low


def last_kernel(plan, me_ref, *refs):
    b_keep, b_other, w_keep, w_other, summed_ref, tail_ref = refs[:6]
    outs, held, sems = refs[6:20], refs[20:34], refs[34]
    own, units = plan.own_states, plan.units
    b_mine = b_keep[...].astype(F32) + b_other[...].astype(F32)
    w_mine = w_keep[...].astype(F32) + w_other[...].astype(F32)
    half = summed_ref.shape[0]
    tail = tail_ref[...].astype(F32)
    vectors = summed_ref[...] + (tail[:half] + tail[half:])
    count = half // 8
    vectors = jnp.concatenate([vectors[8 * part : 8 * part + 8] for part in range(count)], axis=1)
    band = me_ref[0] >> log2(plan.tensor)
    at = grid_index((plan.features, LANES), 0)
    lane = grid_index((plan.features, LANES), 1)

    def pick(length):
        chosen = jnp.where(at == band * length + lane, 1.0, 0.0)
        return lax.dot_general(
            vectors,
            chosen,
            (((1,), (0,)), ((), ())),
            precision=lax.Precision.HIGHEST,
            preferred_element_type=F32,
        )

    long, short = plan.own_rows, plan.states // plan.fsdp
    long_part, short_part = pick(long), pick(short)
    held[0][...] = b_mine[:, :own]
    held[1][...] = b_mine[:, own:]
    held[2][...] = w_mine[:, :own]
    held[3][...] = w_mine[:, own : 2 * own]
    held[4][...] = w_mine[:, 2 * own : 2 * own + units]
    held[5][...] = w_mine[:, 2 * own + units :]
    for place in range(8):
        part, length = (long_part, long) if place < 5 else (short_part, short)
        held[6 + place][...] = part[place : place + 1, :length]
    for copy in start_copies(list(zip(held, outs)), sems):
        copy.wait()


def input_kernel(plan, me_ref, x_ref, stats_ref, grad_ref, normed_grad_ref, vec_ref, input_grad_ref):
    gain = read_vectors(vec_ref)[0:1]

    def rows_step(index, _):
        at = plan.tile_rows(index)
        standard, inverse = standard_rows(plan, x_ref, stats_ref, at)
        scaled = normed_grad_ref[at, :] * gain
        input_grad_ref[at, :] = grad_ref[at, :].astype(F32) + inverse * (
            scaled
            - jnp.mean(scaled, axis=1, keepdims=True)
            - standard * jnp.mean(scaled * standard, axis=1, keepdims=True)
        )
        return 0

    lax.fori_loop(0, plan.tiles, rows_step, 0)


def call(kernel, plan, outs, scratch, limit, time, *args, far_in=0, far_out=False):
    whole = pl.BlockSpec(memory_space=pltpu.VMEM)
    far = pl.BlockSpec(memory_space=pltpu.HBM)
    return pl.pallas_call(
        functools.partial(kernel, plan),
        out_shape=outs,
        in_specs=[pl.BlockSpec(memory_space=pltpu.SMEM)]
        + [far] * far_in
        + [whole] * (len(args) - 1 - far_in),
        out_specs=[far if far_out else whole] * len(outs),
        scratch_shapes=scratch,
        compiler_params=pltpu.CompilerParams(vmem_limit_bytes=limit * MIB),
        cost_estimate=pl.CostEstimate(
            flops=int(time * 1e9), bytes_accessed=int(time * 3.5e6), transcendentals=0
        ),
    )(*args)


def shape(dims, dtype=F32):
    return jax.ShapeDtypeStruct(dims, dtype)


def after(value, *others):
    return lax.optimization_barrier((value, *others))[0]


def joined(*parts):
    return jnp.concatenate(parts, axis=0)


def gather_blocks(plan, first, summed, second, cover):
    count = plan.count
    other = None
    for bit in plan.outer:
        second = joined(second, flip(second if other is None else after(second, other), bit, count))
        rows = first.shape[0]
        got = flip(joined(first, summed), bit, count)
        if other is None:
            got = after(got, cover)
        other = got
        summed = summed + other[rows:]
        first = joined(first, other[:rows])
    blocks = second.reshape(-1, plan.own_rows, second.shape[1])
    size = plan.own_rows // plan.halves
    halves = [
        after(blocks[:, half * size : half * size + size].reshape(-1, second.shape[1]), other)
        for half in range(plan.halves)
    ]
    halves = [joined(part, flip(part, bit, count)) for part, bit in zip(halves, (2, 1))]
    if plan.tensor <= 4:
        rows = first.shape[0]
        other = flip(joined(first, summed), 2, count)
        summed = summed + other[rows:]
        other = other[:rows]
    else:
        other = flip(first, 2, count)
    first = joined(first, other)
    other = flip(first, 1, count)
    halves = [
        (part, flip(after(part, other), bit, count)) for part, bit in zip(halves, (1, 2))
    ]
    first = joined(first, other)
    return first, flip(first, 0, count), summed, halves


def split_high_low(value):
    high = value.astype(BF16)
    return jnp.concatenate([high, (value - high.astype(F32)).astype(BF16)], axis=0)


def cut(value):
    count = value.shape[0] // 2
    return value[:count].astype(BF16), value[count:].astype(BF16)


def added(keep, other):
    return keep.astype(F32) + other.astype(F32)


def scatter_summed(plan, keep, send, summed, bit):
    other = flip(send, bit, plan.count)
    count, rows = keep.shape[0], summed.shape[0]
    tail = other[count:].astype(F32)
    summed = summed + (tail[:rows] + tail[rows:])
    keep, send = cut(added(keep, other[:count]))
    return keep, joined(send, split_high_low(summed)), summed, other


def scatter_halves(plan, keeps, sends, bits):
    others = [flip(send, bit, plan.count) for send, bit in zip(sends, bits)]
    pairs = [cut(added(keep, other)) for keep, other in zip(keeps, others)]
    return [pair[0] for pair in pairs], [pair[1] for pair in pairs], others


def shards(
    mesh,
    block_input,
    segments,
    ln_gain,
    ln_bias,
    b_real,
    b_imag,
    c_real,
    c_imag,
    nu_log,
    theta_log,
    gamma_log,
    d_skip,
    w_value,
    w_gate,
    b_value,
    b_gate,
    out_grad,
):
    band = lax.axis_index("fsdp")
    shard = lax.axis_index("tensor")
    rows, features = block_input.shape
    own = b_real.shape[1]
    plan = Plan(
        mesh, rows, segments.shape[0], features, own * mesh.shape["tensor"], w_value.shape[1]
    )
    states, units, chunks = plan.states, plan.units, plan.chunks
    me = (band * plan.tensor + shard).astype(jnp.int32).reshape(1)
    long, short = plan.own_rows, states // plan.fsdp
    vector_rows = 8 * features // LANES
    matrices = (b_real, b_imag, c_real, c_imag, w_value, w_gate)
    lines = [
        v.reshape(1, -1)
        for v in (ln_gain, ln_bias, d_skip, b_value, b_gate, nu_log, theta_log, gamma_log)
    ]
    block = 2 * own + 2 * units
    first, second = call(
        pack_kernel,
        plan,
        [shape((long + vector_rows, 2 * own), BF16), shape((long, block), BF16)],
        [pltpu.VMEM(v.shape, BF16) for v in (*matrices, *lines)] + [pltpu.SemaphoreType.DMA((14,))],
        60,
        1.5,
        me, *matrices, *lines,
        far_in=14,
    )
    stats, masks = call(
        token_kernel,
        plan,
        [shape((2, rows, LANES)), shape((4, rows, LANES))],
        [pltpu.VMEM((3, plan.group_rows // LANES, LANES), F32)],
        8,
        2,
        me, block_input, segments.reshape(-1, LANES),
    )
    b0, b1, vectors, halves = gather_blocks(plan, first[:long], first[long:], second, masks)

    pack_type = BF16 if long % 16 == 0 else F32
    full = (rows, 2 * states)
    normed, source, ends, hold, carry, input_map, params = call(
        enter_kernel,
        plan,
        [
            shape((rows, features), BF16),
            shape(full),
            shape((chunks, 2 * states)),
            shape((chunks, LANES)),
            shape((8, 2 * states)),
            shape((features, 2 * states), BF16),
            shape((8, 2 * states)),
        ],
        [pltpu.VMEM((features, 2 * states), pack_type)],
        8,
        3,
        me, block_input, stats, b0, b1, vectors, masks,
    )

    def pass_on(value, forward):
        pairs = []
        for one in range(0, plan.tensor, 2):
            pairs.append((one, one + 1) if forward else (one + 1, one))
        return lax.ppermute(value, "tensor", pairs)

    g0 = joined(*(joined(part, after(got, carry)) for part, got in halves))
    g1 = flip(g0, 0, plan.count)
    carry = pass_on(carry, True) if plan.pieces == 2 else jnp.zeros_like(carry)
    (
        mixed, hidden, lru_grad, state_grad, act, unit_grad, low, sums,
    ) = call(
        middle_kernel,
        plan,
        [
            shape((rows, features), BF16),
            shape(full),
            shape((rows, features), BF16),
            shape(full),
            shape((rows, features), BF16),
            shape((rows, 2 * features), BF16),
            shape(full, BF16),
            shape((24, features)),
        ],
        [
            pltpu.VMEM((features, 2 * states), pack_type),
            pltpu.VMEM((features, 2 * features), pack_type),
            pltpu.VMEM((features, 2 * states), BF16),
        ],
        14,
        10,
        me, block_input, out_grad, normed, source, ends, hold, carry, g0, g1, vectors, params, masks,
    )
    half_rows = plan.count // 2 * long
    w_keep, w_send = call(
        weight_kernel,
        plan,
        [shape((half_rows, block), BF16)] * 2,
        [
            pltpu.VMEM((features, 2 * features), F32),
            pltpu.VMEM((features, 2 * states), F32),
        ],
        10,
        2.5,
        me, act, unit_grad, lru_grad, low,
    )
    w_other = flip(w_send, 0, plan.count)
    back_ends, back_hold, back = call(
        back_kernel,
        plan,
        [shape((chunks, 2 * states)), shape((chunks, LANES)), shape((8, 2 * states))],
        [],
        8,
        1.5,
        me, after(state_grad, w_send), params, masks,
    )
    back = pass_on(back, False) if plan.pieces == 2 else jnp.zeros_like(back)
    pieces = plan.halves
    w_other = after(w_other, back_ends)
    w_total = added(w_keep, w_other)
    size = w_total.shape[0] // pieces
    halves = [cut(w_total[half * size : half * size + size]) for half in range(pieces)]
    w_keeps = [half[0] for half in halves]
    w_others = [flip(half[1], bit, plan.count) for half, bit in zip(halves, (2, 1))]
    back_ends = after(back_ends, w_other)
    b_keep, b_send, normed_grad, summed = call(
        leave_kernel,
        plan,
        [
            shape((half_rows, 2 * own), BF16),
            shape((half_rows + 2 * vector_rows, 2 * own), BF16),
            shape((rows, features)),
            shape((vector_rows, LANES)),
        ],
        [
            pltpu.VMEM(full, F32),
            pltpu.VMEM(full, BF16),
            pltpu.VMEM((features, 2 * states), F32),
        ],
        14,
        4.5,
        me, block_input, stats, normed, source, back_ends, back_hold, back, hidden,
        state_grad, lru_grad, input_map, vectors, params, masks, sums,
    )
    b_send = after(b_send, *w_others)
    w_others = [after(other, summed) for other in w_others]
    halves = [cut(added(keep, other)) for keep, other in zip(w_keeps, w_others)]
    w_keeps, w_sends = [half[0] for half in halves], [half[1] for half in halves]
    b_keep, b_send, summed, b_other = scatter_summed(plan, b_keep, b_send, summed, 0)
    w_keeps, w_sends, w_others = scatter_halves(plan, w_keeps, w_sends, (1, 2))
    b_keep, b_send, summed, b_next = scatter_summed(plan, b_keep, b_send, summed, 1)
    waited = w_others
    width = block
    w_keep, w_send = joined(*w_keeps), joined(*w_sends)
    for place, bit in enumerate([2, *plan.outer[::-1]]):
        last = bit == plan.bits - 1
        if not last:
            w_send = after(w_send, b_other)
            b_other = b_next
            w_next = flip(w_send, bit + 1, plan.count)
            if bit + 1 < plan.bits - 1:
                total = added(w_keep, w_next).reshape(pieces, -1, width)
                size = total.shape[1] // 2
                w_keep = total[:, :size].reshape(-1, width).astype(BF16)
                w_send = total[:, size:].reshape(-1, width).astype(BF16)
            else:
                w_other = w_next
        b_send = after(b_send, *waited)
        if last:
            got = flip(b_send, bit, plan.count)
            b_other, tail = got[: b_keep.shape[0]], got[b_keep.shape[0] :]
        else:
            b_keep, b_send, summed, b_next = scatter_summed(plan, b_keep, b_send, summed, bit)
        waited = [w_next]
    (input_grad,) = call(
        input_kernel,
        plan,
        [shape((rows, features))],
        [],
        8,
        2.5,
        me, block_input, stats, out_grad, normed_grad, vectors,
    )
    small = (
        [(long, own)] * 4 + [(long, units)] * 2 + [(1, long)] * 5 + [(1, short)] * 3
    )
    (
        b_real_grad, b_imag_grad, c_real_grad, c_imag_grad, value_grad, gate_grad, *lines
    ) = call(
        last_kernel,
        plan,
        [shape(dims) for dims in small],
        [pltpu.VMEM(dims, F32) for dims in small] + [pltpu.SemaphoreType.DMA((14,))],
        4,
        2,
        me, b_keep, b_other, w_keep, w_other, summed, tail,
        far_out=True,
    )
    gain_grad, bias_grad, skip_grad, value_line, gate_line, nu_grad, theta_grad, gamma_grad = (
        line.reshape(-1) for line in lines
    )
    return (
        mixed,
        input_grad,
        gain_grad,
        bias_grad,
        b_real_grad,
        b_imag_grad,
        c_real_grad,
        c_imag_grad,
        nu_grad,
        theta_grad,
        gamma_grad,
        skip_grad,
        value_grad,
        gate_grad,
        value_line,
        gate_line,
    )


def solution(mesh):
    in_specs = (
        P(("fsdp", "tensor"), None),
        P("fsdp"),
        P("fsdp"),
        P("fsdp"),
        P("fsdp", "tensor"),
        P("fsdp", "tensor"),
        P("fsdp", "tensor"),
        P("fsdp", "tensor"),
        P("fsdp"),
        P("fsdp"),
        P("fsdp"),
        P("fsdp"),
        P("fsdp", "tensor"),
        P("fsdp", "tensor"),
        P("fsdp"),
        P("fsdp"),
        P(("fsdp", "tensor"), None),
    )
    out_specs = (
        P(("fsdp", "tensor"), None),
        P(("fsdp", "tensor"), None),
        P("fsdp"),
        P("fsdp"),
        P("fsdp", "tensor"),
        P("fsdp", "tensor"),
        P("fsdp", "tensor"),
        P("fsdp", "tensor"),
        P("fsdp"),
        P("fsdp"),
        P("fsdp"),
        P("fsdp"),
        P("fsdp", "tensor"),
        P("fsdp", "tensor"),
        P("fsdp"),
        P("fsdp"),
    )
    return jax.shard_map(
        functools.partial(shards, mesh),
        mesh=mesh,
        in_specs=in_specs,
        out_specs=out_specs,
        check_vma=False,
    )
```

time: 154 us -> 90.4 us (0.59)
  Pallas kernels: 48.7 us -> 27 us
  local copies, waits for them, and re-layouts: 18.6 us -> 1.12 us
  starting transfers between devices: 41.5 us -> 29.8 us
  other arithmetic: 8.79 us -> 1.46 us
  waiting for transfers between devices: 33.5 us -> 29.3 us
    pallas_call x3 -> x9, Pallas kernels: 48.7 us -> 27 us  [call(): pl.pallas_call(functools.partial(kernel, plan), out_shape=outs, in_specs=...]
    ppermute x30 -> x24, starting transfers between devices: 38 us -> 26 us  [flip(): return lax.ppermute(value, AXES, [(i, i ^ 1 << bit) for i in range(count)])]
    another operation x20 -> x0, local copies, waits for them, and re-layouts: 6.01 us -> none  [the longest x16 5.95 us: placed(): spread = jnp.tile(vector, plan.fsdp)]
    ppermute x30 -> x24, waiting for transfers between devices: 32.3 us -> 27.5 us  [flip(): return lax.ppermute(value, AXES, [(i, i ^ 1 << bit) for i in range(count)])]
    dynamic_slice x9 -> x0, local copies, waits for them, and re-layouts: 4.66 us -> none  [the longest x8 4.66 us: vector(): return lax.dynamic_slice(vector_sums[place], (band * length,), (length,))]
    slice x22 -> x16, local copies, waits for them, and re-layouts: 4.37 us -> 0.95 us  [the longest x1 0.76 us: shards(): first[:long]]
    unnamed x25 -> x13, local copies, waits for them, and re-layouts: 2.89 us -> 0.12 us
    unnamed x3 -> x0, other arithmetic: 2.37 us -> none
  transfers between devices with their start and end apart: 32 -> 26, of which waited for: 18 -> 17; matrix products, arithmetic and copies ran while one was open for 11% -> 2% of each run, Pallas kernels for 17% -> 14%
where the time goes in v2:
time: 90.4 us; the launch traced here: 90 us
  starting transfers between devices  29.8 us (33%)
  waiting for transfers between devices  29.3 us (32%)
  Pallas kernels  27 us (30%)
  other arithmetic  1.46 us (2%)
  between operations  1.31 us (1%)
  local copies, waits for them, and re-layouts  1.12 us (1%)
    ppermute x24, waiting for transfers between devices, flip(): return lax.ppermute(value, AXES, [(i, i ^ 1 << bit) for i in range(count)])  27.5 us
    pallas_call x9, Pallas kernels, call(): pl.pallas_call(functools.partial(kernel, plan), out_shape=outs, in_specs=...  27 us
    ppermute x24, starting transfers between devices, flip(): return lax.ppermute(value, AXES, [(i, i ^ 1 << bit) for i in range(count)])  26 us
    ppermute x2, starting transfers between devices, pass_on(): return lax.ppermute(value, 'tensor', pairs)  3.86 us
  transfers between devices with their start and end apart: 26, of which 17 were waited for; matrix products, arithmetic and copies ran while one was open for 2% of the time, Pallas kernels for 14%

profile of v2, /device:TPU:0, one launch (start us, length us, event | category | flops | bytes accessed | tf_op | source)
XLA Modules:
  0.0 90.0 jit_solution(10592859970387426035)
XLA Ops:
  0.7 1.7 %shard_map.289 = (bf16[96,128]{1,0:T(8,128)(2,1)}, bf16[64,384]{1,0:T(8,128)(2,1)}) custom-call(s32[1]{0:T(128)} %bitcast.me_ref, bf16[64,64]{1,0:T(8,128)(2,1)} %refs_0_.1, bf16[64,64]{1,0:T(8,128)(2,1)} %refs_1_.1, bf16[64,64]{1,0:T(8,128)(2,1)} %refs_2_.1, bf16[64,64]{1,0:T(8,128)(2,1)} %refs_3_.1, bf16[64,128]{1,0:T(8,128)(2,1)} %refs_4_.1, ...), custom_call_target="tpu_custom_call" | custom-call | flops 1500000000 | bytes 5250000 | tf_op jit(solution)/shard_map/pallas_call | solution.py:622
  2.4 4.1 %collective-permute-start = (bf16[96,128]{1,0:T(8,128)(2,1)}, bf16[96,128]{1,0:T(8,128)(2,1)S(1)}, u32[]{:S(2)}, u32[]{:S(2)}) collective-permute-start(bf16[96,128]{1,0:T(8,128)(2,1)} %get-tuple-element.78), channel_id=1, source_target_pairs={{0,16},{1,17},{2,18},{3,19},{4,20},{5,21},{6,22},{7,23},{8,24},{9,... | collective-permute-start | bytes 73736 | tf_op jit(solution)/shard_map/ppermute | solution.py:29
  6.5 0.8 fusion.17
  7.3 1.7 %shard_map.288 = (f32[2,1024,128]{2,1,0:T(8,128)S(1)}, f32[4,1024,128]{2,1,0:T(8,128)S(1)}) custom-call(s32[1]{0:T(128)} %bitcast.me_ref, bf16[1024,512]{1,0:T(8,128)(2,1)S(1)} %copy-done, s32[32,128]{1,0:T(8,128)S(1)} %bitcast.25), custom_call_target="tpu_custom_call" | custom-call | flops 2000000000 | bytes 7000000 | tf_op jit(solution)/shard_map/pallas_call | solution.py:622
  9.0 0.7 slice_add_fusion.6
  9.8 1.6 %collective-permute-start.1 = (bf16[160,128]{1,0:T(8,128)(2,1)S(1)}, bf16[160,128]{1,0:T(8,128)(2,1)S(1)}, u32[]{:S(2)}, u32[]{:S(2)}) collective-permute-start(bf16[160,128]{1,0:T(8,128)(2,1)S(1)} %pad_maximum_fusion.10), channel_id=1, source_target_pairs={{0,8},{1,9},{2,10},{3,11},{4,12},{5,13},{6,14},{7,15},{8,0},{9,1},... | collective-permute-start | bytes 122888 | tf_op jit(solution)/shard_map/ppermute | solution.py:29
  11.4 2.6 %collective-permute-start.6 = (bf16[64,384]{1,0:T(8,128)(2,1)S(1)}, bf16[64,384]{1,0:T(8,128)(2,1)S(1)}, u32[]{:S(2)}, u32[]{:S(2)}) collective-permute-start(bf16[64,384]{1,0:T(8,128)(2,1)S(1)} %copy-done.3), channel_id=1, source_target_pairs={{0,16},{1,17},{2,18},{3,19},{4,20},{5,21},{6,22},{7,23},{8,24},{9,... | collective-permute-start | bytes 147464 | tf_op jit(solution)/shard_map/ppermute | solution.py:29
  14.0 1.6 %collective-permute-start.2 = (bf16[288,128]{1,0:T(8,128)(2,1)S(1)}, bf16[288,128]{1,0:T(8,128)(2,1)S(1)}, u32[]{:S(2)}, u32[]{:S(2)}) collective-permute-start(bf16[288,128]{1,0:T(8,128)(2,1)S(1)} %pad_maximum_fusion.8), channel_id=1, source_target_pairs={{0,4},{1,5},{2,6},{3,7},{4,0},{5,1},{6,2},{7,3},{8,12},{9,13},{10,... | collective-permute-start | bytes 221192 | tf_op jit(solution)/shard_map/ppermute | solution.py:29
  15.6 1.2 %collective-permute-done.6 = bf16[64,384]{1,0:T(8,128)(2,1)S(1)} collective-permute-done((bf16[64,384]{1,0:T(8,128)(2,1)S(1)}, bf16[64,384]{1,0:T(8,128)(2,1)S(1)}, u32[]{:S(2)}, u32[]{:S(2)}) %collective-permute-start.6) | collective-permute-done | bytes 49184 | tf_op jit(solution)/shard_map/ppermute | solution.py:29
  16.8 0.7 collective-permute-start.7
  17.5 0.9 %collective-permute-done.2 = bf16[288,128]{1,0:T(8,128)(2,1)S(1)} collective-permute-done((bf16[288,128]{1,0:T(8,128)(2,1)S(1)}, bf16[288,128]{1,0:T(8,128)(2,1)S(1)}, u32[]{:S(2)}, u32[]{:S(2)}) %collective-permute-start.2) | collective-permute-done | bytes 73760 | tf_op jit(solution)/shard_map/ppermute | solution.py:29
  18.5 1.6 %collective-permute-start.3 = (bf16[512,128]{1,0:T(8,128)(2,1)S(1)}, bf16[512,128]{1,0:T(8,128)(2,1)S(1)}, u32[]{:S(2)}, u32[]{:S(2)}) collective-permute-start(bf16[512,128]{1,0:T(8,128)(2,1)S(1)} %pad_maximum_fusion.4), channel_id=1, source_target_pairs={{0,2},{1,3},{2,0},{3,1},{4,6},{5,7},{6,4},{7,5},{8,10},{9,11},{10,... | collective-permute-start | bytes 393224 | tf_op jit(solution)/shard_map/ppermute | solution.py:29
  20.0 1.5 %collective-permute-done.7 = bf16[128,384]{1,0:T(8,128)(2,1)S(1)} collective-permute-done((bf16[128,384]{1,0:T(8,128)(2,1)S(1)}, bf16[128,384]{1,0:T(8,128)(2,1)S(1)}, u32[]{:S(2)}, u32[]{:S(2)}) %collective-permute-start.7) | collective-permute-done | bytes 98336 | tf_op jit(solution)/shard_map/ppermute | solution.py:29
  21.6 1.6 %collective-permute-start.10 = (bf16[128,384]{1,0:T(8,128)(2,1)S(1)}, bf16[128,384]{1,0:T(8,128)(2,1)S(1)}, u32[]{:S(2)}, u32[]{:S(2)}) collective-permute-start(bf16[128,384]{1,0:T(8,128)(2,1)S(1)} %bitcast.26), channel_id=1, source_target_pairs={{0,2},{1,3},{2,0},{3,1},{4,6},{5,7},{6,4},{7,5},{8,10},{9,11},{10,... | collective-permute-start | bytes 294920 | tf_op jit(solution)/shard_map/ppermute | solution.py:29
  23.1 1.5 %collective-permute-start.8 = (bf16[128,384]{1,0:T(8,128)(2,1)S(1)}, bf16[128,384]{1,0:T(8,128)(2,1)S(1)}, u32[]{:S(2)}, u32[]{:S(2)}) collective-permute-start(bf16[128,384]{1,0:T(8,128)(2,1)S(1)} %bitcast.29), channel_id=1, source_target_pairs={{0,4},{1,5},{2,6},{3,7},{4,0},{5,1},{6,2},{7,3},{8,12},{9,13},{10,... | collective-permute-start | bytes 294920 | tf_op jit(solution)/shard_map/ppermute | solution.py:29
  24.8 3.0 %collective-permute-done.8 = bf16[128,384]{1,0:T(8,128)(2,1)S(1)} collective-permute-done((bf16[128,384]{1,0:T(8,128)(2,1)S(1)}, bf16[128,384]{1,0:T(8,128)(2,1)S(1)}, u32[]{:S(2)}, u32[]{:S(2)}) %collective-permute-start.8) | collective-permute-done | bytes 98336 | tf_op jit(solution)/shard_map/ppermute | solution.py:29
  27.8 2.3 %collective-permute-start.11 = (bf16[256,384]{1,0:T(8,128)(2,1)S(1)}, bf16[256,384]{1,0:T(8,128)(2,1)S(1)}, u32[]{:S(2)}, u32[]{:S(2)}) collective-permute-start(bf16[256,384]{1,0:T(8,128)(2,1)S(1)} %pad_maximum_fusion.2), channel_id=1, source_target_pairs={{0,4},{1,5},{2,6},{3,7},{4,0},{5,1},{6,2},{7,3},{8,12},{9,13},{10,... | collective-permute-start | bytes 589832 | tf_op jit(solution)/shard_map/ppermute | solution.py:29
  30.1 3.0 %shard_map.290 = (bf16[1024,512]{1,0:T(8,128)(2,1)S(1)}, f32[1024,512]{1,0:T(8,128)S(1)}, f32[64,512]{1,0:T(8,128)S(1)}, f32[64,128]{1,0:T(8,128)S(1)}, f32[8,51...) custom-call(s32[1]{0:T(128)} %bitcast.me_ref, bf16[1024,512]{1,0:T(8,128)(2,1)S(1)} %copy-done, ...), custom_call_target="tpu_custom_call" | custom-call | flops 3000000000 | bytes 10500000 | tf_op jit(solution)/shard_map/pallas_call | solution.py:622
  33.2 0.6 collective-permute-done.11
  33.8 2.0 %collective-permute-done.9 = bf16[256,384]{1,0:T(8,128)(2,1)S(1)} collective-permute-done((bf16[256,384]{1,0:T(8,128)(2,1)S(1)}, bf16[256,384]{1,0:T(8,128)(2,1)S(1)}, u32[]{:S(2)}, u32[]{:S(2)}) %collective-permute-start.9) | collective-permute-done | bytes 196640 | tf_op jit(solution)/shard_map/ppermute | solution.py:29
  36.0 2.4 %collective-permute-start.5 = (f32[8,512]{1,0:T(8,128)S(1)}, f32[8,512]{1,0:T(8,128)S(1)}, u32[]{:S(2)}, u32[]{:S(2)}) collective-permute-start(f32[8,512]{1,0:T(8,128)S(1)} %get-tuple-element.85), channel_id=1, source_target_pairs={{0,1},{2,3},{4,5},{6,7},{8,9},{10,11},{12,13},{14,15},{16,17},{18,... | collective-permute-start | bytes 49160 | tf_op jit(solution)/shard_map/ppermute | solution.py:795
  38.4 0.8 collective-permute-done.5.carry_ref
  39.2 9.5 %shard_map.291 = (bf16[1024,512]{1,0:T(8,128)(2,1)}, f32[1024,512]{1,0:T(8,128)S(1)}, bf16[1024,512]{1,0:T(8,128)(2,1)S(1)}, f32[1024,512]{1,0:T(8,128)S(1)}, bf...) custom-call(s32[1]{0:T(128)} %bitcast.me_ref, ...), custom_call_target="tpu_custom_call" | custom-call | flops 10000000000 | bytes 35000000 | tf_op jit(solution)/shard_map/pallas_call | solution.py:622
  48.8 2.5 %shard_map.292 = (bf16[1024,384]{1,0:T(8,128)(2,1)S(1)}, bf16[1024,384]{1,0:T(8,128)(2,1)S(1)}) custom-call(s32[1]{0:T(128)} %bitcast.me_ref, bf16[1024,512]{1,0:T(8,128)(2,1)S(1)} %get-tuple-element.97.act_ref, bf16[1024,1024]{1,0:T(8,128)(2,1)S(1)} %get-tuple-element.98.unit_grad_ref, bf16[1024,512]{1,0:T(8,128)(2,1)S(1)} %get-tuple-element.99.lru_grad_ref, ...), custom_call_target="tpu_custom_call" | custom-call | flops 2500000000 | bytes 8750000 | tf_op jit(solution)/shard_map/pallas_call | solution.py:622
  51.3 0.4 collective-permute-start.13
  51.7 0.6 shard_map.293
  52.3 1.5 %collective-permute-start.14 = (f32[8,512]{1,0:T(8,128)S(1)}, f32[8,512]{1,0:T(8,128)S(1)}, u32[]{:S(2)}, u32[]{:S(2)}) collective-permute-start(f32[8,512]{1,0:T(8,128)S(1)} %get-tuple-element.107), channel_id=1, source_target_pairs={{1,0},{3,2},{5,4},{7,6},{9,8},{11,10},{13,12},{15,14},{17,16},{19,... | collective-permute-start | bytes 49160 | tf_op jit(solution)/shard_map/ppermute | solution.py:795
  53.8 0.2 add_convert_fusion
  54.2 0.3 collective-permute-start.15
  54.5 0.9 %collective-permute-done.14.carry_ref = f32[8,512]{1,0:T(8,128)S(1)} collective-permute-done((f32[8,512]{1,0:T(8,128)S(1)}, f32[8,512]{1,0:T(8,128)S(1)}, u32[]{:S(2)}, u32[]{:S(2)}) %collective-permute-start.14) | collective-permute-done | bytes 16416 | tf_op jit(solution)/shard_map/ppermute | solution.py:795
  55.4 4.4 %shard_map.294 = (bf16[1024,128]{1,0:T(8,128)(2,1)S(1)}, bf16[1088,128]{1,0:T(8,128)(2,1)S(1)}, f32[1024,512]{1,0:T(8,128)S(1)}, f32[32,128]{1,0:T(8,128)S(1)}) custom-call(s32[1]{0:T(128)} %bitcast.me_ref, bf16[1024,512]{1,0:T(8,128)(2,1)S(1)} %copy-done, f32[2,1024,128]{2,1,0:T(8,128)S(1)} %get-tuple-element.77.stats_ref, ...), custom_call_target="tpu_custom_call" | custom-call | flops 4499999744 | bytes 15750000 | tf_op jit(solution)/shard_map/pallas_call | solution.py:622
  59.8 2.0 %collective-permute-done.16 = bf16[256,384]{1,0:T(8,128)(2,1)S(1)} collective-permute-done((bf16[256,384]{1,0:T(8,128)(2,1)S(1)}, bf16[256,384]{1,0:T(8,128)(2,1)S(1)}, u32[]{:S(2)}, u32[]{:S(2)}) %collective-permute-start.16) | collective-permute-done | bytes 196640 | tf_op jit(solution)/shard_map/ppermute | solution.py:29
  62.0 2.0 %collective-permute-start.19 = (bf16[128,384]{1,0:T(8,128)(2,1)S(1)}, bf16[128,384]{1,0:T(8,128)(2,1)S(1)}, u32[]{:S(2)}, u32[]{:S(2)}) collective-permute-start(bf16[128,384]{1,0:T(8,128)(2,1)S(1)} %slice.250), channel_id=1, source_target_pairs={{0,2},{1,3},{2,0},{3,1},{4,6},{5,7},{6,4},{7,5},{8,10},{9,11},{10,... | collective-permute-start | bytes 294920 | tf_op jit(solution)/shard_map/ppermute | solution.py:29
  64.0 0.2 collective-permute-start.20
  64.2 2.7 %collective-permute-done.19 = bf16[128,384]{1,0:T(8,128)(2,1)S(1)} collective-permute-done((bf16[128,384]{1,0:T(8,128)(2,1)S(1)}, bf16[128,384]{1,0:T(8,128)(2,1)S(1)}, u32[]{:S(2)}, u32[]{:S(2)}) %collective-permute-start.19) | collective-permute-done | bytes 98336 | tf_op jit(solution)/shard_map/ppermute | solution.py:29
  67.0 1.7 %collective-permute-done.20 = bf16[128,384]{1,0:T(8,128)(2,1)S(1)} collective-permute-done((bf16[128,384]{1,0:T(8,128)(2,1)S(1)}, bf16[128,384]{1,0:T(8,128)(2,1)S(1)}, u32[]{:S(2)}, u32[]{:S(2)}) %collective-permute-start.20) | collective-permute-done | bytes 98336 | tf_op jit(solution)/shard_map/ppermute | solution.py:29
  68.9 0.2 collective-permute-start.18
  69.1 0.1 collective-permute-start.22
  69.2 4.9 %collective-permute-done.18 = bf16[576,128]{1,0:T(8,128)(2,1)S(1)} collective-permute-done((bf16[576,128]{1,0:T(8,128)(2,1)S(1)}, bf16[576,128]{1,0:T(8,128)(2,1)S(1)}, u32[]{:S(2)}, u32[]{:S(2)}) %collective-permute-start.18) | collective-permute-done | bytes 147488 | tf_op jit(solution)/shard_map/ppermute | solution.py:29
  74.2 0.2 collective-permute-start.21
  74.4 4.3 %collective-permute-done.21 = bf16[320,128]{1,0:T(8,128)(2,1)S(1)} collective-permute-done((bf16[320,128]{1,0:T(8,128)(2,1)S(1)}, bf16[320,128]{1,0:T(8,128)(2,1)S(1)}, u32[]{:S(2)}, u32[]{:S(2)}) %collective-permute-start.21) | collective-permute-done | bytes 81952 | tf_op jit(solution)/shard_map/ppermute | solution.py:29
  78.9 2.4 %collective-permute-start.24 = (bf16[64,384]{1,0:T(8,128)(2,1)S(1)}, bf16[64,384]{1,0:T(8,128)(2,1)S(1)}, u32[]{:S(2)}, u32[]{:S(2)}) collective-permute-start(bf16[64,384]{1,0:T(8,128)(2,1)S(1)} %bitcast.34), channel_id=1, source_target_pairs={{0,16},{1,17},{2,18},{3,19},{4,20},{5,21},{6,22},{7,23},{8,24},{9,... | collective-permute-start | bytes 147464 | tf_op jit(solution)/shard_map/ppermute | solution.py:29
  81.3 2.0 %collective-permute-done.23 = bf16[192,128]{1,0:T(8,128)(2,1)S(1)} collective-permute-done((bf16[192,128]{1,0:T(8,128)(2,1)S(1)}, bf16[192,128]{1,0:T(8,128)(2,1)S(1)}, u32[]{:S(2)}, u32[]{:S(2)}) %collective-permute-start.23) | collective-permute-done | bytes 49184 | tf_op jit(solution)/shard_map/ppermute | solution.py:29
  83.4 0.6 collective-permute-done.24.refs_3_
  84.0 2.3 %collective-permute-start.25 = (bf16[128,128]{1,0:T(8,128)(2,1)S(1)}, bf16[128,128]{1,0:T(8,128)(2,1)S(1)}, u32[]{:S(2)}, u32[]{:S(2)}) collective-permute-start(bf16[128,128]{1,0:T(8,128)(2,1)S(1)} %pad_maximum_fusion.11), channel_id=1, source_target_pairs={{0,16},{1,17},{2,18},{3,19},{4,20},{5,21},{6,22},{7,23},{8,24},{9,... | collective-permute-start | bytes 98312 | tf_op jit(solution)/shard_map/ppermute | solution.py:29
  86.3 2.4 %shard_map.295 = f32[1024,512]{1,0:T(8,128)} custom-call(s32[1]{0:T(128)} %bitcast.me_ref, bf16[1024,512]{1,0:T(8,128)(2,1)S(1)} %copy-done, f32[2,1024,128]{2,1,0:T(8,128)S(1)} %get-tuple-element.77.stats_ref, bf16[1024,512]{1,0:T(8,128)(2,1)S(1)} %copy-done.1, f32[1024,512]{1,0:T(8,128)S(1)} %get-tuple-element.111.normed_grad_ref, ...), custom_call_target="tpu_custom_call" | custom-call | flops 2500000000 | bytes 8750000 | tf_op jit(solution)/shard_map/pallas_call | solution.py:622
  88.7 0.1 collective-permute-done.25
  88.8 1.1 %shard_map.296 = (f32[64,64]{1,0:T(8,128)}, f32[64,64]{1,0:T(8,128)}, f32[64,64]{1,0:T(8,128)}, f32[64,64]{1,0:T(8,128)}, f32[64,128]{1,0:T(8,128)}, /*index=5*/...) custom-call(s32[1]{0:T(128)} %bitcast.me_ref, ...), custom_call_target="tpu_custom_call" | custom-call | flops 2000000000 | bytes 7000000 | tf_op jit(solution)/shard_map/pallas_call | solution.py:622
  (76 shorter events, 1.3 us)
Async XLA Ops:
  0.7 6.6 %copy-start = (bf16[1024,512]{1,0:T(8,128)(2,1)S(1)}, bf16[1024,512]{1,0:T(8,128)(2,1)}, u32[]{:S(2)}) copy-start(bf16[1024,512]{1,0:T(8,128)(2,1)} %x_ref.9) | copy-start | bytes 3145732
  0.7 6.6 %copy-start.2 = (s32[4096]{0:T(1024)S(1)}, s32[4096]{0:T(1024)}, u32[]{:S(2)}) copy-start(s32[4096]{0:T(1024)} %param.18) | copy-start | bytes 49156
  2.4 6.6 %collective-permute-start = (bf16[96,128]{1,0:T(8,128)(2,1)}, bf16[96,128]{1,0:T(8,128)(2,1)S(1)}, u32[]{:S(2)}, u32[]{:S(2)}) collective-permute-start(bf16[96,128]{1,0:T(8,128)(2,1)} %get-tuple-element.78), channel_id=1, source_target_pairs={{0,16},{1,17},{2,18},{3,19},{4,20},{5,21},{6,22},{7,23},{8,24},{9,... | collective-permute-start | bytes 73736 | tf_op jit(solution)/shard_map/ppermute | solution.py:29
  7.3 4.1 %copy-start.3 = (bf16[64,384]{1,0:T(8,128)(2,1)S(1)}, bf16[64,384]{1,0:T(8,128)(2,1)}, u32[]{:S(2)}) copy-start(bf16[64,384]{1,0:T(8,128)(2,1)} %get-tuple-element.86) | copy-start | bytes 147460
  9.8 4.2 %collective-permute-start.1 = (bf16[160,128]{1,0:T(8,128)(2,1)S(1)}, bf16[160,128]{1,0:T(8,128)(2,1)S(1)}, u32[]{:S(2)}, u32[]{:S(2)}) collective-permute-start(bf16[160,128]{1,0:T(8,128)(2,1)S(1)} %pad_maximum_fusion.10), channel_id=1, source_target_pairs={{0,8},{1,9},{2,10},{3,11},{4,12},{5,13},{6,14},{7,15},{8,0},{9,1},... | collective-permute-start | bytes 122888 | tf_op jit(solution)/shard_map/ppermute | solution.py:29
  11.4 5.4 %collective-permute-start.6 = (bf16[64,384]{1,0:T(8,128)(2,1)S(1)}, bf16[64,384]{1,0:T(8,128)(2,1)S(1)}, u32[]{:S(2)}, u32[]{:S(2)}) collective-permute-start(bf16[64,384]{1,0:T(8,128)(2,1)S(1)} %copy-done.3), channel_id=1, source_target_pairs={{0,16},{1,17},{2,18},{3,19},{4,20},{5,21},{6,22},{7,23},{8,24},{9,... | collective-permute-start | bytes 147464 | tf_op jit(solution)/shard_map/ppermute | solution.py:29
  14.0 4.4 %collective-permute-start.2 = (bf16[288,128]{1,0:T(8,128)(2,1)S(1)}, bf16[288,128]{1,0:T(8,128)(2,1)S(1)}, u32[]{:S(2)}, u32[]{:S(2)}) collective-permute-start(bf16[288,128]{1,0:T(8,128)(2,1)S(1)} %pad_maximum_fusion.8), channel_id=1, source_target_pairs={{0,4},{1,5},{2,6},{3,7},{4,0},{5,1},{6,2},{7,3},{8,12},{9,13},{10,... | collective-permute-start | bytes 221192 | tf_op jit(solution)/shard_map/ppermute | solution.py:29
  16.8 4.7 %collective-permute-start.7 = (bf16[128,384]{1,0:T(8,128)(2,1)S(1)}, bf16[128,384]{1,0:T(8,128)(2,1)S(1)}, u32[]{:S(2)}, u32[]{:S(2)}) collective-permute-start(bf16[128,384]{1,0:T(8,128)(2,1)S(1)} %pad_maximum_fusion.5), channel_id=1, source_target_pairs={{0,8},{1,9},{2,10},{3,11},{4,12},{5,13},{6,14},{7,15},{8,0},{9,1},... | collective-permute-start | bytes 294920 | tf_op jit(solution)/shard_map/ppermute | solution.py:29
  18.5 6.2 %collective-permute-start.3 = (bf16[512,128]{1,0:T(8,128)(2,1)S(1)}, bf16[512,128]{1,0:T(8,128)(2,1)S(1)}, u32[]{:S(2)}, u32[]{:S(2)}) collective-permute-start(bf16[512,128]{1,0:T(8,128)(2,1)S(1)} %pad_maximum_fusion.4), channel_id=1, source_target_pairs={{0,2},{1,3},{2,0},{3,1},{4,6},{5,7},{6,4},{7,5},{8,10},{9,11},{10,... | collective-permute-start | bytes 393224 | tf_op jit(solution)/shard_map/ppermute | solution.py:29
  21.6 6.2 %collective-permute-start.10 = (bf16[128,384]{1,0:T(8,128)(2,1)S(1)}, bf16[128,384]{1,0:T(8,128)(2,1)S(1)}, u32[]{:S(2)}, u32[]{:S(2)}) collective-permute-start(bf16[128,384]{1,0:T(8,128)(2,1)S(1)} %bitcast.26), channel_id=1, source_target_pairs={{0,2},{1,3},{2,0},{3,1},{4,6},{5,7},{6,4},{7,5},{8,10},{9,11},{10,... | collective-permute-start | bytes 294920 | tf_op jit(solution)/shard_map/ppermute | solution.py:29
  23.1 4.6 %collective-permute-start.8 = (bf16[128,384]{1,0:T(8,128)(2,1)S(1)}, bf16[128,384]{1,0:T(8,128)(2,1)S(1)}, u32[]{:S(2)}, u32[]{:S(2)}) collective-permute-start(bf16[128,384]{1,0:T(8,128)(2,1)S(1)} %bitcast.29), channel_id=1, source_target_pairs={{0,4},{1,5},{2,6},{3,7},{4,0},{5,1},{6,2},{7,3},{8,12},{9,13},{10,... | collective-permute-start | bytes 294920 | tf_op jit(solution)/shard_map/ppermute | solution.py:29
  24.7 5.5 %collective-permute-start.4 = (bf16[1024,128]{1,0:T(8,128)(2,1)S(1)}, bf16[1024,128]{1,0:T(8,128)(2,1)S(1)}, u32[]{:S(2)}, u32[]{:S(2)}) collective-permute-start(bf16[1024,128]{1,0:T(8,128)(2,1)S(1)} %constant_dynamic-update-slice_fusion.b0_ref), channel_id=1, source_target_pairs={{0,1},{1,0},{2,3},{3,2},{4,5},{5,4},{6,7},{7,6},{8,9},{9,8},{10,11... | collective-permute-start | bytes 786440 | tf_op jit(solution)/shard_map/ppermute | solution.py:29
  27.8 6.0 %collective-permute-start.11 = (bf16[256,384]{1,0:T(8,128)(2,1)S(1)}, bf16[256,384]{1,0:T(8,128)(2,1)S(1)}, u32[]{:S(2)}, u32[]{:S(2)}) collective-permute-start(bf16[256,384]{1,0:T(8,128)(2,1)S(1)} %pad_maximum_fusion.2), channel_id=1, source_target_pairs={{0,4},{1,5},{2,6},{3,7},{4,0},{5,1},{6,2},{7,3},{8,12},{9,13},{10,... | collective-permute-start | bytes 589832 | tf_op jit(solution)/shard_map/ppermute | solution.py:29
  30.1 5.7 %collective-permute-start.9 = (bf16[256,384]{1,0:T(8,128)(2,1)S(1)}, bf16[256,384]{1,0:T(8,128)(2,1)S(1)}, u32[]{:S(2)}, u32[]{:S(2)}) collective-permute-start(bf16[256,384]{1,0:T(8,128)(2,1)S(1)} %pad_maximum_fusion.1), channel_id=1, source_target_pairs={{0,2},{1,3},{2,0},{3,1},{4,6},{5,7},{6,4},{7,5},{8,10},{9,11},{10,... | collective-permute-start | bytes 589832 | tf_op jit(solution)/shard_map/ppermute | solution.py:29
  30.1 9.1 %copy-start.1 = (bf16[1024,512]{1,0:T(8,128)(2,1)S(1)}, bf16[1024,512]{1,0:T(8,128)(2,1)}, u32[]{:S(2)}) copy-start(bf16[1024,512]{1,0:T(8,128)(2,1)} %grad_ref.3) | copy-start | bytes 3145732
  35.9 3.3 %collective-permute-start.12 = (bf16[1024,384]{1,0:T(8,128)(2,1)S(1)}, bf16[1024,384]{1,0:T(8,128)(2,1)S(1)}, u32[]{:S(2)}, u32[]{:S(2)}) collective-permute-start(bf16[1024,384]{1,0:T(8,128)(2,1)S(1)} %constant_dynamic-update-slice_fusion.5.g0_ref), channel_id=1, source_target_pairs={{0,1},{1,0},{2,3},{3,2},{4,5},{5,4},{6,7},{7,6},{8,9},{9,8},{10,11... | collective-permute-start | bytes 2359304 | tf_op jit(solution)/shard_map/ppermute | solution.py:29
  36.0 3.2 %collective-permute-start.5 = (f32[8,512]{1,0:T(8,128)S(1)}, f32[8,512]{1,0:T(8,128)S(1)}, u32[]{:S(2)}, u32[]{:S(2)}) collective-permute-start(f32[8,512]{1,0:T(8,128)S(1)} %get-tuple-element.85), channel_id=1, source_target_pairs={{0,1},{2,3},{4,5},{6,7},{8,9},{10,11},{12,13},{14,15},{16,17},{18,... | collective-permute-start | bytes 49160 | tf_op jit(solution)/shard_map/ppermute | solution.py:795
  51.3 2.5 %collective-permute-start.13 = (bf16[1024,384]{1,0:T(8,128)(2,1)S(1)}, bf16[1024,384]{1,0:T(8,128)(2,1)S(1)}, u32[]{:S(2)}, u32[]{:S(2)}) collective-permute-start(bf16[1024,384]{1,0:T(8,128)(2,1)S(1)} %get-tuple-element.101), channel_id=1, source_target_pairs={{0,1},{1,0},{2,3},{3,2},{4,5},{5,4},{6,7},{7,6},{8,9},{9,8},{10,11... | collective-permute-start | bytes 2359304 | tf_op jit(solution)/shard_map/ppermute | solution.py:29
  52.3 3.1 %collective-permute-start.14 = (f32[8,512]{1,0:T(8,128)S(1)}, f32[8,512]{1,0:T(8,128)S(1)}, u32[]{:S(2)}, u32[]{:S(2)}) collective-permute-start(f32[8,512]{1,0:T(8,128)S(1)} %get-tuple-element.107), channel_id=1, source_target_pairs={{1,0},{3,2},{5,4},{7,6},{9,8},{11,10},{13,12},{15,14},{17,16},{19,... | collective-permute-start | bytes 49160 | tf_op jit(solution)/shard_map/ppermute | solution.py:795
  54.1 7.7 %collective-permute-start.16 = (bf16[256,384]{1,0:T(8,128)(2,1)S(1)}, bf16[256,384]{1,0:T(8,128)(2,1)S(1)}, u32[]{:S(2)}, u32[]{:S(2)}) collective-permute-start(bf16[256,384]{1,0:T(8,128)(2,1)S(1)} %get-tuple-element.152), channel_id=1, source_target_pairs={{0,2},{1,3},{2,0},{3,1},{4,6},{5,7},{6,4},{7,5},{8,10},{9,11},{10,... | collective-permute-start | bytes 589832 | tf_op jit(solution)/shard_map/ppermute | solution.py:29
  54.2 7.7 %collective-permute-start.15 = (bf16[256,384]{1,0:T(8,128)(2,1)S(1)}, bf16[256,384]{1,0:T(8,128)(2,1)S(1)}, u32[]{:S(2)}, u32[]{:S(2)}) collective-permute-start(bf16[256,384]{1,0:T(8,128)(2,1)S(1)} %get-tuple-element.153), channel_id=1, source_target_pairs={{0,4},{1,5},{2,6},{3,7},{4,0},{5,1},{6,2},{7,3},{8,12},{9,13},{10,... | collective-permute-start | bytes 589832 | tf_op jit(solution)/shard_map/ppermute | solution.py:29
  62.0 5.0 %collective-permute-start.19 = (bf16[128,384]{1,0:T(8,128)(2,1)S(1)}, bf16[128,384]{1,0:T(8,128)(2,1)S(1)}, u32[]{:S(2)}, u32[]{:S(2)}) collective-permute-start(bf16[128,384]{1,0:T(8,128)(2,1)S(1)} %slice.250), channel_id=1, source_target_pairs={{0,2},{1,3},{2,0},{3,1},{4,6},{5,7},{6,4},{7,5},{8,10},{9,11},{10,... | collective-permute-start | bytes 294920 | tf_op jit(solution)/shard_map/ppermute | solution.py:29
  64.0 4.7 %collective-permute-start.20 = (bf16[128,384]{1,0:T(8,128)(2,1)S(1)}, bf16[128,384]{1,0:T(8,128)(2,1)S(1)}, u32[]{:S(2)}, u32[]{:S(2)}) collective-permute-start(bf16[128,384]{1,0:T(8,128)(2,1)S(1)} %slice.252), channel_id=1, source_target_pairs={{0,4},{1,5},{2,6},{3,7},{4,0},{5,1},{6,2},{7,3},{8,12},{9,13},{10,... | collective-permute-start | bytes 294920 | tf_op jit(solution)/shard_map/ppermute | solution.py:29
  64.2 4.5 %collective-permute-start.17 = (bf16[1088,128]{1,0:T(8,128)(2,1)S(1)}, bf16[1088,128]{1,0:T(8,128)(2,1)S(1)}, u32[]{:S(2)}, u32[]{:S(2)}) collective-permute-start(bf16[1088,128]{1,0:T(8,128)(2,1)S(1)} %get-tuple-element.115), channel_id=1, source_target_pairs={{0,1},{1,0},{2,3},{3,2},{4,5},{5,4},{6,7},{7,6},{8,9},{9,8},{10,11... | collective-permute-start | bytes 835592 | tf_op jit(solution)/shard_map/ppermute | solution.py:29
  68.9 5.2 %collective-permute-start.18 = (bf16[576,128]{1,0:T(8,128)(2,1)S(1)}, bf16[576,128]{1,0:T(8,128)(2,1)S(1)}, u32[]{:S(2)}, u32[]{:S(2)}) collective-permute-start(bf16[576,128]{1,0:T(8,128)(2,1)S(1)} %pad_maximum_fusion.3), channel_id=1, source_target_pairs={{0,2},{1,3},{2,0},{3,1},{4,6},{5,7},{6,4},{7,5},{8,10},{9,11},{10,... | collective-permute-start | bytes 442376 | tf_op jit(solution)/shard_map/ppermute | solution.py:29
  69.1 5.3 %collective-permute-start.22 = (bf16[128,384]{1,0:T(8,128)(2,1)S(1)}, bf16[128,384]{1,0:T(8,128)(2,1)S(1)}, u32[]{:S(2)}, u32[]{:S(2)}) collective-permute-start(bf16[128,384]{1,0:T(8,128)(2,1)S(1)} %pad_maximum_fusion.6), channel_id=1, source_target_pairs={{0,8},{1,9},{2,10},{3,11},{4,12},{5,13},{6,14},{7,15},{8,0},{9,1},... | collective-permute-start | bytes 294920 | tf_op jit(solution)/shard_map/ppermute | solution.py:29
  74.2 4.5 %collective-permute-start.21 = (bf16[320,128]{1,0:T(8,128)(2,1)S(1)}, bf16[320,128]{1,0:T(8,128)(2,1)S(1)}, u32[]{:S(2)}, u32[]{:S(2)}) collective-permute-start(bf16[320,128]{1,0:T(8,128)(2,1)S(1)} %pad_maximum_fusion.7), channel_id=1, source_target_pairs={{0,4},{1,5},{2,6},{3,7},{4,0},{5,1},{6,2},{7,3},{8,12},{9,13},{10,... | collective-permute-start | bytes 245768 | tf_op jit(solution)/shard_map/ppermute | solution.py:29
  78.8 4.5 %collective-permute-start.23 = (bf16[192,128]{1,0:T(8,128)(2,1)S(1)}, bf16[192,128]{1,0:T(8,128)(2,1)S(1)}, u32[]{:S(2)}, u32[]{:S(2)}) collective-permute-start(bf16[192,128]{1,0:T(8,128)(2,1)S(1)} %pad_maximum_fusion.9), channel_id=1, source_target_pairs={{0,8},{1,9},{2,10},{3,11},{4,12},{5,13},{6,14},{7,15},{8,0},{9,1},... | collective-permute-start | bytes 147464 | tf_op jit(solution)/shard_map/ppermute | solution.py:29
  78.9 5.1 %collective-permute-start.24 = (bf16[64,384]{1,0:T(8,128)(2,1)S(1)}, bf16[64,384]{1,0:T(8,128)(2,1)S(1)}, u32[]{:S(2)}, u32[]{:S(2)}) collective-permute-start(bf16[64,384]{1,0:T(8,128)(2,1)S(1)} %bitcast.34), channel_id=1, source_target_pairs={{0,16},{1,17},{2,18},{3,19},{4,20},{5,21},{6,22},{7,23},{8,24},{9,... | collective-permute-start | bytes 147464 | tf_op jit(solution)/shard_map/ppermute | solution.py:29
  84.0 4.8 %collective-permute-start.25 = (bf16[128,128]{1,0:T(8,128)(2,1)S(1)}, bf16[128,128]{1,0:T(8,128)(2,1)S(1)}, u32[]{:S(2)}, u32[]{:S(2)}) collective-permute-start(bf16[128,128]{1,0:T(8,128)(2,1)S(1)} %pad_maximum_fusion.11), channel_id=1, source_target_pairs={{0,16},{1,17},{2,18},{3,19},{4,20},{5,21},{6,22},{7,23},{8,24},{9,... | collective-permute-start | bytes 98312 | tf_op jit(solution)/shard_map/ppermute | solution.py:29

commit v3 on v2

--- a/solution.py
+++ b/solution.py
@@ -12,6 +12,7 @@
 LANES = 128
 TILE = 256
 SIDE = 16
+BLOCK = 1024
 AXES = ("fsdp", "tensor")
 norm_epsilon = 1e-05
 GELU_SCALE = math.sqrt(2.0 / math.pi)
@@ -66,18 +67,23 @@
     return jnp.where(place == target, 1.0, 0.0)
 
 
+def turn_rows(turn, value):
+    parts = [dot(turn, value[at : at + TILE]) for at in range(0, value.shape[0], TILE)]
+    return jnp.concatenate(parts, axis=0).astype(BF16)
+
+
 class Plan:
     def __init__(self, mesh, rows, group_rows, features, states, units):
         self.fsdp = mesh.shape["fsdp"]
         self.tensor = mesh.shape["tensor"]
         self.count = self.fsdp * self.tensor
         self.bits = log2(self.count)
-        outer = list(range(self.bits - 1, 2, -1))
-        self.outer = outer
-        self.up = [*outer, 2, 1, 0]
-        self.up_crossed = [*outer, 1, 2, 0]
-        self.down = [0, 1, 2, *outer[::-1]]
-        self.down_crossed = [0, 2, 1, *outer[::-1]]
+        far = list(range(self.bits - 1, 3, -1))
+        self.far = far
+        self.up = [*far, 3, 2, 1, 0]
+        self.up_crossed = ([*far, 1, 3, 2, 0], [*far, 1, 2, 3, 0])
+        self.down = [0, 1, 2, 3, *far[::-1]]
+        self.down_crossed = ([0, 2, 3, 1, *far[::-1]], [0, 3, 2, 1, *far[::-1]])
         self.halves = 2 if features // self.fsdp >= 32 else 1
         self.rows = rows
         self.group_rows = group_rows
@@ -89,6 +95,8 @@
         self.pieces = SEQ_LEN // rows
         self.tiles = rows // TILE
         self.chunks = self.tiles * SIDE
+        self.block = BLOCK if rows % BLOCK == 0 else TILE
+        self.blocks = rows // self.block
 
     def slot_owner(self, slot, me, order):
         owner = me
@@ -97,8 +105,8 @@
         shift = log2(self.tensor)
         return owner >> shift, owner & (self.tensor - 1)
 
-    def tile_rows(self, index):
-        return pl.ds(pl.multiple_of(index * TILE, TILE), TILE)
+    def block_rows(self, index):
+        return pl.ds(pl.multiple_of(index * self.block, self.block), self.block)
 
 
 def step_rows(tile, place):
@@ -213,10 +221,10 @@
             )
 
 
-def half_blocks(plan, straight, crossed):
+def half_blocks(plan, orders):
     rows = plan.own_rows // plan.halves
     for half in range(plan.halves):
-        yield (straight, crossed)[half], half * plan.count // 2 * rows, rows, half * rows
+        yield orders[half], half * plan.count // 2 * rows, rows, half * rows
 
 
 def start_copies(pairs, sems):
@@ -281,16 +289,16 @@
             masks_ref[kind, at, :] = dot(spread.astype(BF16), ones)
 
     def rows_step(index, _):
-        at = plan.tile_rows(index)
+        at = plan.block_rows(index)
         values = x_ref[at, :].astype(F32)
         mean = jnp.mean(values, axis=1, keepdims=True)
         centred = values - mean
         inverse = lax.rsqrt(jnp.mean(centred * centred, axis=1, keepdims=True) + norm_epsilon)
-        stats_ref[0, at, :] = jnp.broadcast_to(mean, (TILE, LANES))
-        stats_ref[1, at, :] = jnp.broadcast_to(inverse, (TILE, LANES))
+        stats_ref[0, at, :] = jnp.broadcast_to(mean, (plan.block, LANES))
+        stats_ref[1, at, :] = jnp.broadcast_to(inverse, (plan.block, LANES))
         return 0
 
-    lax.fori_loop(0, plan.tiles, rows_step, 0)
+    lax.fori_loop(0, plan.blocks, rows_step, 0)
 
 
 def standard_rows(plan, x_ref, stats_ref, at):
@@ -340,16 +348,16 @@
     turn = turn_matrix().astype(BF16)
 
     def rows_step(index, _):
-        at = plan.tile_rows(index)
+        at = plan.block_rows(index)
         standard, _ = standard_rows(plan, x_ref, stats_ref, at)
         normed = (standard * gain + shift).astype(BF16)
         normed_ref[at, :] = normed
-        turned = dot(turn, normed).astype(BF16)
+        turned = turn_rows(turn, normed)
         drive = dot(turned, input_map_ref[...])
         source_ref[at, :] = drive * gamma_pair * wide(masks_ref[2, at, :], 2 * states)
         return 0
 
-    lax.fori_loop(0, plan.tiles, rows_step, 0)
+    lax.fori_loop(0, plan.blocks, rows_step, 0)
     ends_re, ends_im, hold = local_ends(plan, source_ref, masks_ref.at[0], rate, False)
     ends_ref[...] = jnp.concatenate([ends_re, ends_im], axis=1)
     hold_ref[...] = hold
@@ -370,8 +378,8 @@
         (pair, units, wpack_ref, 0),
         (pair + units, units, wpack_ref, features),
     ]
-    for order, base, rows, first in half_blocks(plan, plan.up[::-1], plan.up_crossed[::-1]):
-        collect(plan, me_ref[0], order, (g0_ref, g1_ref), base, rows, first, targets)
+    for order, base, rows, first in half_blocks(plan, plan.up_crossed):
+        collect(plan, me_ref[0], order[::-1], (g0_ref, g1_ref), base, rows, first, targets)
     sign = jnp.where(grid_index((1, 2 * states), 1) < states, 1.0, -1.0)
     regroup = regroup_matrix(states, plan.tensor)
     out_map_ref[...] = (dot(pack_ref[...].astype(BF16), regroup) * sign).astype(BF16)
@@ -402,28 +410,27 @@
     turn = turn_matrix().astype(BF16)
 
     def rows_step(index, _):
-        at = plan.tile_rows(index)
-        low = dot(turn, hidden_ref[at, :].astype(BF16)).astype(BF16)
+        at = plan.block_rows(index)
+        low = turn_rows(turn, hidden_ref[at, :].astype(BF16))
         low_ref[at, :] = low
         normed = normed_ref[at, :].astype(F32)
         lru = dot(low, out_map_ref[...], 1, 1) + skip * normed
         square = lru * lru
         bent = jnp.tanh(lru * (GELU_SCALE + (GELU_SCALE * GELU_CUBE) * square))
         half = 0.5 + 0.5 * bent
-        act = (lru * half).astype(BF16)
-        slope = half + lru * (1.0 - bent * bent) * (
-            0.5 * GELU_SCALE + (1.5 * GELU_SCALE * GELU_CUBE) * square
+        act_wide = lru * half
+        slope = half + act_wide * (1.0 - half) * (
+            2.0 * GELU_SCALE + (6.0 * GELU_SCALE * GELU_CUBE) * square
         )
+        act = act_wide.astype(BF16)
         act_ref[at, :] = act
         mapped = dot(act, wpack_ref[...].astype(BF16)) + biases
         value = mapped[:, :features]
-        opening = 0.5 + 0.5 * jnp.tanh(0.5 * mapped[:, features:])
-        live = wide(masks_ref[3, at, :], features)
+        live_half = wide(0.5 * masks_ref[3, at, :], features)
+        opening = live_half + live_half * jnp.tanh(0.5 * mapped[:, features:])
         gated = value * opening
-        mixed_ref[at, :] = (
-            x_ref[at, :].astype(F32) + live * gated.astype(BF16).astype(F32)
-        ).astype(BF16)
-        value_grad = live * grad_ref[at, :].astype(F32) * opening
+        mixed_ref[at, :] = (x_ref[at, :].astype(F32) + gated).astype(BF16)
+        value_grad = grad_ref[at, :].astype(F32) * opening
         gate_grad = value_grad * (value - gated)
         sums_ref[8:16, :] += fold_rows(value_grad)
         sums_ref[16:24, :] += fold_rows(gate_grad)
@@ -434,11 +441,11 @@
         sums_ref[0:8, :] += fold_rows(lru_grad * normed)
         lru_grad = lru_grad.astype(BF16)
         lru_grad_ref[at, :] = lru_grad
-        turned = dot(turn, lru_grad).astype(BF16)
+        turned = turn_rows(turn, lru_grad)
         state_grad_ref[at, :] = dot(turned, out_map_ref[...])
         return 0
 
-    lax.fori_loop(0, plan.tiles, rows_step, 0)
+    lax.fori_loop(0, plan.blocks, rows_step, 0)
 
 
 def back_kernel(
@@ -467,14 +474,14 @@
         (pair, units, full_ref, 0),
         (pair + units, units, full_ref, features),
     ]
-    for order, base, rows, first in half_blocks(plan, plan.down_crossed, plan.down):
+    for order, base, rows, first in half_blocks(plan, plan.down_crossed):
         distribute(plan, me_ref[0], order, (keep_ref, send_ref), base, rows, first, targets)
 
 
 def leave_kernel(
     plan, me_ref, x_ref, stats_ref, normed_ref, source_ref, ends_ref, hold_ref, carry_ref, hidden_ref,
     state_grad_ref, lru_grad_ref, input_map_ref, vec_ref, params_ref, masks_ref, sums_ref,
-    keep_ref, send_ref, normed_grad_ref, out_sums_ref,
+    keep_ref, send_ref, normed_grad_ref,
     drive_grad_ref, low_ref, full_ref,
 ):
     states, features = plan.states, plan.features
@@ -523,15 +530,15 @@
 
     def rows_step(index, sums):
         gain_sum, shift_sum = sums
-        at = plan.tile_rows(index)
-        low = dot(turn, drive_grad_ref[at, :].astype(BF16)).astype(BF16)
+        at = plan.block_rows(index)
+        low = turn_rows(turn, drive_grad_ref[at, :].astype(BF16))
         low_ref[at, :] = low
         normed_grad = dot(low, input_map_ref[...], 1, 1) + skip * lru_grad_ref[at, :].astype(F32)
         normed_grad_ref[at, :] = normed_grad
         standard, _ = standard_rows(plan, x_ref, stats_ref, at)
         return gain_sum + fold_rows(normed_grad * standard), shift_sum + fold_rows(normed_grad)
 
-    gain_sum, shift_sum = lax.fori_loop(0, plan.tiles, rows_step, (gain_sum, gain_sum))
+    gain_sum, shift_sum = lax.fori_loop(0, plan.blocks, rows_step, (gain_sum, gain_sum))
     into = dot(normed_ref[...], low_ref[...], 0, 0)
     full_ref[...] = dot(into.astype(BF16), regroup_matrix(states, plan.tensor), 1, 1)
     distribute(
@@ -552,7 +559,6 @@
     parts = features // LANES
     for part in range(parts):
         piece = vector_sums[:, part * LANES : (part + 1) * LANES]
-        out_sums_ref[8 * part : 8 * part + 8, :] = piece
         high = piece.astype(BF16)
         low = (piece - high.astype(F32)).astype(BF16)
         send_ref[base + 8 * part : base + 8 * part + 8, :] = high
@@ -560,14 +566,14 @@
 
 
 def last_kernel(plan, me_ref, *refs):
-    b_keep, b_other, w_keep, w_other, summed_ref, tail_ref = refs[:6]
-    outs, held, sems = refs[6:20], refs[20:34], refs[34]
+    b_keep, b_other, w_keep, w_other, tail_ref = refs[:5]
+    outs, held, sems = refs[5:19], refs[19:33], refs[33]
     own, units = plan.own_states, plan.units
     b_mine = b_keep[...].astype(F32) + b_other[...].astype(F32)
     w_mine = w_keep[...].astype(F32) + w_other[...].astype(F32)
-    half = summed_ref.shape[0]
-    tail = tail_ref[...].astype(F32)
-    vectors = summed_ref[...] + (tail[:half] + tail[half:])
+    half = tail_ref.shape[0] // 4
+    tail = [tail_ref[part * half : part * half + half, :].astype(F32) for part in range(4)]
+    vectors = (tail[0] + tail[1]) + (tail[2] + tail[3])
     count = half // 8
     vectors = jnp.concatenate([vectors[8 * part : 8 * part + 8] for part in range(count)], axis=1)
     band = me_ref[0] >> log2(plan.tensor)
@@ -603,7 +609,7 @@
     gain = read_vectors(vec_ref)[0:1]
 
     def rows_step(index, _):
-        at = plan.tile_rows(index)
+        at = plan.block_rows(index)
         standard, inverse = standard_rows(plan, x_ref, stats_ref, at)
         scaled = normed_grad_ref[at, :] * gain
         input_grad_ref[at, :] = grad_ref[at, :].astype(F32) + inverse * (
@@ -613,10 +619,11 @@
         )
         return 0
 
-    lax.fori_loop(0, plan.tiles, rows_step, 0)
+    lax.fori_loop(0, plan.blocks, rows_step, 0)
 
 
 def call(kernel, plan, outs, scratch, limit, time, *args, far_in=0, far_out=False):
+    args = [*args[:1], *(pltpu.with_memory_space_constraint(a, pltpu.HBM) for a in args[1 : 1 + far_in]), *args[1 + far_in :]]
     whole = pl.BlockSpec(memory_space=pltpu.VMEM)
     far = pl.BlockSpec(memory_space=pltpu.HBM)
     return pl.pallas_call(
@@ -647,43 +654,42 @@
 
 
 def gather_blocks(plan, first, summed, second, cover):
-    count = plan.count
+    count, width = plan.count, second.shape[1]
+    tensor_bits = log2(plan.tensor)
     other = None
-    for bit in plan.outer:
-        second = joined(second, flip(second if other is None else after(second, other), bit, count))
+
+    def first_step(bit):
         rows = first.shape[0]
+        if bit < tensor_bits:
+            got = flip(first, bit, count)
+            return got, joined(first, got), summed
         got = flip(joined(first, summed), bit, count)
         if other is None:
-            got = after(got, cover)
-        other = got
-        summed = summed + other[rows:]
-        first = joined(first, other[:rows])
-    blocks = second.reshape(-1, plan.own_rows, second.shape[1])
+            got = after(got, cover, second_other)
+        return got, joined(first, got[:rows]), summed + got[rows:]
+
+    for bit in plan.far:
+        second_other = flip(second if other is None else after(second, other), bit, count)
+        other, first, summed = first_step(bit)
+        second = joined(second, second_other)
+    second = joined(second, flip(after(second, other), 1, count))
+    other, first, summed = first_step(3)
+    blocks = second.reshape(-1, plan.own_rows, width)
     size = plan.own_rows // plan.halves
     halves = [
-        after(blocks[:, half * size : half * size + size].reshape(-1, second.shape[1]), other)
+        after(blocks[:, half * size : half * size + size].reshape(-1, width), other)
         for half in range(plan.halves)
     ]
-    halves = [joined(part, flip(part, bit, count)) for part, bit in zip(halves, (2, 1))]
-    if plan.tensor <= 4:
-        rows = first.shape[0]
-        other = flip(joined(first, summed), 2, count)
-        summed = summed + other[rows:]
-        other = other[:rows]
-    else:
-        other = flip(first, 2, count)
-    first = joined(first, other)
-    other = flip(first, 1, count)
-    halves = [
-        (part, flip(after(part, other), bit, count)) for part, bit in zip(halves, (1, 2))
-    ]
-    first = joined(first, other)
+    halves = [joined(part, flip(part, bit, count)) for part, bit in zip(halves, (3, 2))]
+    other, first, summed = first_step(2)
+    halves = [(part, flip(part, bit, count)) for part, bit in zip(halves, (2, 3))]
+    other, first, summed = first_step(1)
     return first, flip(first, 0, count), summed, halves
 
 
 def split_high_low(value):
-    high = value.astype(BF16)
-    return jnp.concatenate([high, (value - high.astype(F32)).astype(BF16)], axis=0)
+    high = lax.reduce_precision(value, 8, 7)
+    return jnp.concatenate([high, value - high], axis=0).astype(BF16)
 
 
 def cut(value):
@@ -695,19 +701,17 @@
     return keep.astype(F32) + other.astype(F32)
 
 
-def scatter_summed(plan, keep, send, summed, bit):
-    other = flip(send, bit, plan.count)
-    count, rows = keep.shape[0], summed.shape[0]
-    tail = other[count:].astype(F32)
-    summed = summed + (tail[:rows] + tail[rows:])
+def summed_step(keep, send, other):
+    count = keep.shape[0]
+    rows = (send.shape[0] - count) // 2
+    pairs = [part[count:].astype(F32) for part in (send, other)]
+    summed = sum(pair[:rows] + pair[rows:] for pair in pairs)
     keep, send = cut(added(keep, other[:count]))
-    return keep, joined(send, split_high_low(summed)), summed, other
-
-
-def scatter_halves(plan, keeps, sends, bits):
-    others = [flip(send, bit, plan.count) for send, bit in zip(sends, bits)]
-    pairs = [cut(added(keep, other)) for keep, other in zip(keeps, others)]
-    return [pair[0] for pair in pairs], [pair[1] for pair in pairs], others
+    return keep, joined(send, split_high_low(summed))
+
+
+def together(*values):
+    return lax.optimization_barrier(values)
 
 
 def shards(
@@ -752,7 +756,7 @@
         plan,
         [shape((long + vector_rows, 2 * own), BF16), shape((long, block), BF16)],
         [pltpu.VMEM(v.shape, BF16) for v in (*matrices, *lines)] + [pltpu.SemaphoreType.DMA((14,))],
-        60,
+        4,
         1.5,
         me, *matrices, *lines,
         far_in=14,
@@ -794,9 +798,10 @@
             pairs.append((one, one + 1) if forward else (one + 1, one))
         return lax.ppermute(value, "tensor", pairs)
 
-    g0 = joined(*(joined(part, after(got, carry)) for part, got in halves))
-    g1 = flip(g0, 0, plan.count)
+    left = carry
     carry = pass_on(carry, True) if plan.pieces == 2 else jnp.zeros_like(carry)
+    g0 = joined(*(joined(part, after(got, left)) for part, got in halves))
+    g1 = flip(after(g0, carry), 0, plan.count)
     (
         mixed, hidden, lru_grad, state_grad, act, unit_grad, low, sums,
     ) = call(
@@ -817,7 +822,7 @@
             pltpu.VMEM((features, 2 * features), pack_type),
             pltpu.VMEM((features, 2 * states), BF16),
         ],
-        14,
+        24,
         10,
         me, block_input, out_grad, normed, source, ends, hold, carry, g0, g1, vectors, params, masks,
     )
@@ -851,16 +856,15 @@
     size = w_total.shape[0] // pieces
     halves = [cut(w_total[half * size : half * size + size]) for half in range(pieces)]
     w_keeps = [half[0] for half in halves]
-    w_others = [flip(half[1], bit, plan.count) for half, bit in zip(halves, (2, 1))]
+    w_others = [flip(half[1], bit, plan.count) for half, bit in zip(halves, (2, 3))]
     back_ends = after(back_ends, w_other)
-    b_keep, b_send, normed_grad, summed = call(
+    b_keep, b_send, normed_grad = call(
         leave_kernel,
         plan,
         [
             shape((half_rows, 2 * own), BF16),
             shape((half_rows + 2 * vector_rows, 2 * own), BF16),
             shape((rows, features)),
-            shape((vector_rows, LANES)),
         ],
         [
             pltpu.VMEM(full, F32),
@@ -872,36 +876,6 @@
         me, block_input, stats, normed, source, back_ends, back_hold, back, hidden,
         state_grad, lru_grad, input_map, vectors, params, masks, sums,
     )
-    b_send = after(b_send, *w_others)
-    w_others = [after(other, summed) for other in w_others]
-    halves = [cut(added(keep, other)) for keep, other in zip(w_keeps, w_others)]
-    w_keeps, w_sends = [half[0] for half in halves], [half[1] for half in halves]
-    b_keep, b_send, summed, b_other = scatter_summed(plan, b_keep, b_send, summed, 0)
-    w_keeps, w_sends, w_others = scatter_halves(plan, w_keeps, w_sends, (1, 2))
-    b_keep, b_send, summed, b_next = scatter_summed(plan, b_keep, b_send, summed, 1)
-    waited = w_others
-    width = block
-    w_keep, w_send = joined(*w_keeps), joined(*w_sends)
-    for place, bit in enumerate([2, *plan.outer[::-1]]):
-        last = bit == plan.bits - 1
-        if not last:
-            w_send = after(w_send, b_other)
-            b_other = b_next
-            w_next = flip(w_send, bit + 1, plan.count)
-            if bit + 1 < plan.bits - 1:
-                total = added(w_keep, w_next).reshape(pieces, -1, width)
-                size = total.shape[1] // 2
-                w_keep = total[:, :size].reshape(-1, width).astype(BF16)
-                w_send = total[:, size:].reshape(-1, width).astype(BF16)
-            else:
-                w_other = w_next
-        b_send = after(b_send, *waited)
-        if last:
-            got = flip(b_send, bit, plan.count)
-            b_other, tail = got[: b_keep.shape[0]], got[b_keep.shape[0] :]
-        else:
-            b_keep, b_send, summed, b_next = scatter_summed(plan, b_keep, b_send, summed, bit)
-        waited = [w_next]
     (input_grad,) = call(
         input_kernel,
         plan,
@@ -911,6 +885,31 @@
         2.5,
         me, block_input, stats, out_grad, normed_grad, vectors,
     )
+    b_keep, b_send, input_grad, w_others = together(b_keep, b_send, input_grad, w_others)
+    parts = [cut(added(keep, other)) for keep, other in zip(w_keeps, w_others)]
+    w_others = [flip(part[1], bit, plan.count) for part, bit in zip(parts, (3, 2))]
+    b_other = flip(b_send, 0, plan.count)
+    b_keep, b_send = summed_step(b_keep, b_send, b_other)
+    b_other = flip(b_send, 1, plan.count)
+    b_other, w_others = together(b_other, w_others)
+    b_keep, b_send = summed_step(b_keep, b_send, b_other)
+    halves = [cut(added(part[0], other)) for part, other in zip(parts, w_others)]
+    w_keep = joined(*(half[0] for half in halves))
+    w_send = joined(*(half[1] for half in halves))
+    for bit, w_bit in zip(plan.down[2:-1], [1, *plan.down[4:]]):
+        b_send, w_send = together(b_send, w_send)
+        b_other = flip(b_send, bit, plan.count)
+        w_other = flip(w_send, w_bit, plan.count)
+        if bit < plan.bits - 2:
+            b_other, w_other = together(b_other, w_other)
+        b_keep, b_send = summed_step(b_keep, b_send, b_other)
+        if w_bit < plan.bits - 1:
+            total = added(w_keep, w_other).reshape(pieces, -1, block)
+            size = total.shape[1] // 2
+            w_keep = total[:, :size].reshape(-1, block).astype(BF16)
+            w_send = total[:, size:].reshape(-1, block).astype(BF16)
+    b_other = flip(b_send, plan.bits - 1, plan.count)
+    b_other, tail = b_other[:long], joined(b_send[long:], b_other[long:])
     small = (
         [(long, own)] * 4 + [(long, units)] * 2 + [(1, long)] * 5 + [(1, short)] * 3
     )
@@ -923,7 +922,7 @@
         [pltpu.VMEM(dims, F32) for dims in small] + [pltpu.SemaphoreType.DMA((14,))],
         4,
         2,
-        me, b_keep, b_other, w_keep, w_other, summed, tail,
+        me, b_keep, b_other, w_keep, w_other, tail,
         far_out=True,
     )
     gain_grad, bias_grad, skip_grad, value_line, gate_line, nu_grad, theta_grad, gamma_grad = (

time: 90.4 us -> 84.6 us (0.936)
  Pallas kernels: 27 us -> 21.6 us
  starting transfers between devices: 29.8 us -> 32.3 us
  waiting for transfers between devices: 29.3 us -> 28 us
    pallas_call x9, Pallas kernels: 27 us -> 21.6 us  [call(): pl.pallas_call(functools.partial(kernel, plan), out_shape=outs, in_specs=...]
    ppermute x24, starting transfers between devices: 26 us -> 28.8 us  [flip(): return lax.ppermute(value, AXES, [(i, i ^ 1 << bit) for i in range(count)])]
    ppermute x2, waiting for transfers between devices: 1.76 us -> 0.01 us  [pass_on(): return lax.ppermute(value, 'tensor', pairs)]
  transfers between devices with their start and end apart: 26 -> 26, of which waited for: 17 -> 17; matrix products, arithmetic and copies ran while one was open for 2% -> 1% of each run, Pallas kernels for 14% -> 12%
where the time goes in v3:
time: 84.6 us; the launch traced here: 84.3 us
  starting transfers between devices  32.3 us (38%)
  waiting for transfers between devices  28 us (33%)
  Pallas kernels  21.6 us (26%)
  between operations  1.31 us (2%)
    ppermute x24, starting transfers between devices, flip(): return lax.ppermute(value, AXES, [(i, i ^ 1 << bit) for i in range(count)])  28.8 us
    ppermute x24, waiting for transfers between devices, flip(): return lax.ppermute(value, AXES, [(i, i ^ 1 << bit) for i in range(count)])  28 us
    pallas_call x9, Pallas kernels, call(): pl.pallas_call(functools.partial(kernel, plan), out_shape=outs, in_specs=...  21.6 us
    ppermute x2, starting transfers between devices, pass_on(): return lax.ppermute(value, 'tensor', pairs)  3.52 us
  transfers between devices with their start and end apart: 26, of which 17 were waited for; matrix products, arithmetic and copies ran while one was open for 1% of the time, Pallas kernels for 12%

profile of v3, /device:TPU:0, one launch (start us, length us, event | category | flops | bytes accessed | tf_op | source)
XLA Modules:
  0.0 84.3 jit_solution(6425560142675893989)
XLA Ops:
  0.7 1.1 %shard_map.289 = (bf16[96,128]{1,0:T(8,128)(2,1)S(1)}, bf16[64,384]{1,0:T(8,128)(2,1)S(1)}) custom-call(s32[1]{0:T(128)} %bitcast.me_ref, bf16[64,64]{1,0:T(8,128)(2,1)} %refs_0_.1, bf16[64,64]{1,0:T(8,128)(2,1)} %refs_1_.1, bf16[64,64]{1,0:T(8,128)(2,1)} %refs_2_.1, bf16[64,64]{1,0:T(8,128)(2,1)} %refs_3_.1, bf16[64,128]{1,0:T(8,128)(2,1)} %refs_4_.1, ...), custom_call_target="tpu_custom_call" | custom-call | flops 1500000000 | bytes 5250000 | tf_op jit(solution)/shard_map/pallas_call | solution.py:629
  1.8 4.1 %collective-permute-start = (bf16[96,128]{1,0:T(8,128)(2,1)S(1)}, bf16[96,128]{1,0:T(8,128)(2,1)S(1)}, u32[]{:S(2)}, u32[]{:S(2)}) collective-permute-start(bf16[96,128]{1,0:T(8,128)(2,1)S(1)} %get-tuple-element.82), channel_id=1, source_target_pairs={{0,16},{1,17},{2,18},{3,19},{4,20},{5,21},{6,22},{7,23},{8,24},{9,... | collective-permute-start | bytes 73736 | tf_op jit(solution)/shard_map/ppermute | solution.py:30
  6.0 1.1 %shard_map.288 = (f32[2,1024,128]{2,1,0:T(8,128)S(1)}, f32[4,1024,128]{2,1,0:T(8,128)S(1)}) custom-call(s32[1]{0:T(128)} %bitcast.me_ref, bf16[1024,512]{1,0:T(8,128)(2,1)S(1)} %copy-done, s32[32,128]{1,0:T(8,128)S(1)} %bitcast.25), custom_call_target="tpu_custom_call" | custom-call | flops 2000000000 | bytes 7000000 | tf_op jit(solution)/shard_map/pallas_call | solution.py:629
  7.1 0.7 collective-permute-done
  7.7 3.3 %collective-permute-done.1 = bf16[64,384]{1,0:T(8,128)(2,1)S(1)} collective-permute-done((bf16[64,384]{1,0:T(8,128)(2,1)S(1)}, bf16[64,384]{1,0:T(8,128)(2,1)S(1)}, u32[]{:S(2)}, u32[]{:S(2)}) %collective-permute-start.1) | collective-permute-done | bytes 49184 | tf_op jit(solution)/shard_map/ppermute | solution.py:30
  11.0 1.5 %collective-permute-start.2 = (bf16[160,128]{1,0:T(8,128)(2,1)S(1)}, bf16[160,128]{1,0:T(8,128)(2,1)S(1)}, u32[]{:S(2)}, u32[]{:S(2)}) collective-permute-start(bf16[160,128]{1,0:T(8,128)(2,1)S(1)} %pad_maximum_fusion.10), channel_id=1, source_target_pairs={{0,8},{1,9},{2,10},{3,11},{4,12},{5,13},{6,14},{7,15},{8,0},{9,1},... | collective-permute-start | bytes 122888 | tf_op jit(solution)/shard_map/ppermute | solution.py:30
  12.6 1.6 %collective-permute-start.7 = (bf16[128,384]{1,0:T(8,128)(2,1)S(1)}, bf16[128,384]{1,0:T(8,128)(2,1)S(1)}, u32[]{:S(2)}, u32[]{:S(2)}) collective-permute-start(bf16[128,384]{1,0:T(8,128)(2,1)S(1)} %pad_maximum_fusion.5), channel_id=1, source_target_pairs={{0,2},{1,3},{2,0},{3,1},{4,6},{5,7},{6,4},{7,5},{8,10},{9,11},{10,... | collective-permute-start | bytes 294920 | tf_op jit(solution)/shard_map/ppermute | solution.py:30
  14.1 1.0 %collective-permute-done.2 = bf16[160,128]{1,0:T(8,128)(2,1)S(1)} collective-permute-done((bf16[160,128]{1,0:T(8,128)(2,1)S(1)}, bf16[160,128]{1,0:T(8,128)(2,1)S(1)}, u32[]{:S(2)}, u32[]{:S(2)}) %collective-permute-start.2) | collective-permute-done | bytes 40992 | tf_op jit(solution)/shard_map/ppermute | solution.py:30
  15.1 1.6 %collective-permute-start.3 = (bf16[288,128]{1,0:T(8,128)(2,1)S(1)}, bf16[288,128]{1,0:T(8,128)(2,1)S(1)}, u32[]{:S(2)}, u32[]{:S(2)}) collective-permute-start(bf16[288,128]{1,0:T(8,128)(2,1)S(1)} %pad_maximum_fusion.8), channel_id=1, source_target_pairs={{0,4},{1,5},{2,6},{3,7},{4,0},{5,1},{6,2},{7,3},{8,12},{9,13},{10,... | collective-permute-start | bytes 221192 | tf_op jit(solution)/shard_map/ppermute | solution.py:30
  16.7 0.5 collective-permute-done.7
  17.3 1.6 %collective-permute-start.10 = (bf16[128,384]{1,0:T(8,128)(2,1)S(1)}, bf16[128,384]{1,0:T(8,128)(2,1)S(1)}, u32[]{:S(2)}, u32[]{:S(2)}) collective-permute-start(bf16[128,384]{1,0:T(8,128)(2,1)S(1)} %bitcast.26), channel_id=1, source_target_pairs={{0,4},{1,5},{2,6},{3,7},{4,0},{5,1},{6,2},{7,3},{8,12},{9,13},{10,... | collective-permute-start | bytes 294920 | tf_op jit(solution)/shard_map/ppermute | solution.py:30
  18.9 0.6 collective-permute-start.8
  19.6 1.6 %collective-permute-start.4 = (bf16[512,128]{1,0:T(8,128)(2,1)S(1)}, bf16[512,128]{1,0:T(8,128)(2,1)S(1)}, u32[]{:S(2)}, u32[]{:S(2)}) collective-permute-start(bf16[512,128]{1,0:T(8,128)(2,1)S(1)} %pad_maximum_fusion.4), channel_id=1, source_target_pairs={{0,2},{1,3},{2,0},{3,1},{4,6},{5,7},{6,4},{7,5},{8,10},{9,11},{10,... | collective-permute-start | bytes 393224 | tf_op jit(solution)/shard_map/ppermute | solution.py:30
  21.2 3.5 %collective-permute-done.4 = bf16[512,128]{1,0:T(8,128)(2,1)S(1)} collective-permute-done((bf16[512,128]{1,0:T(8,128)(2,1)S(1)}, bf16[512,128]{1,0:T(8,128)(2,1)S(1)}, u32[]{:S(2)}, u32[]{:S(2)}) %collective-permute-start.4) | collective-permute-done | bytes 131104 | tf_op jit(solution)/shard_map/ppermute | solution.py:30
  24.8 1.5 %collective-permute-start.11 = (bf16[256,384]{1,0:T(8,128)(2,1)S(1)}, bf16[256,384]{1,0:T(8,128)(2,1)S(1)}, u32[]{:S(2)}, u32[]{:S(2)}) collective-permute-start(bf16[256,384]{1,0:T(8,128)(2,1)S(1)} %pad_maximum_fusion.2), channel_id=1, source_target_pairs={{0,8},{1,9},{2,10},{3,11},{4,12},{5,13},{6,14},{7,15},{8,0},{9,1},... | collective-permute-start | bytes 589832 | tf_op jit(solution)/shard_map/ppermute | solution.py:30
  26.3 1.6 %collective-permute-start.9 = (bf16[256,384]{1,0:T(8,128)(2,1)S(1)}, bf16[256,384]{1,0:T(8,128)(2,1)S(1)}, u32[]{:S(2)}, u32[]{:S(2)}) collective-permute-start(bf16[256,384]{1,0:T(8,128)(2,1)S(1)} %pad_maximum_fusion.1), channel_id=1, source_target_pairs={{0,4},{1,5},{2,6},{3,7},{4,0},{5,1},{6,2},{7,3},{8,12},{9,13},{10,... | collective-permute-start | bytes 589832 | tf_op jit(solution)/shard_map/ppermute | solution.py:30
  28.0 2.2 %shard_map.290 = (bf16[1024,512]{1,0:T(8,128)(2,1)S(1)}, f32[1024,512]{1,0:T(8,128)S(1)}, f32[64,512]{1,0:T(8,128)S(1)}, f32[64,128]{1,0:T(8,128)S(1)}, f32[8,51...) custom-call(s32[1]{0:T(128)} %bitcast.me_ref, bf16[1024,512]{1,0:T(8,128)(2,1)S(1)} %copy-done, ...), custom_call_target="tpu_custom_call" | custom-call | flops 3000000000 | bytes 10500000 | tf_op jit(solution)/shard_map/pallas_call | solution.py:629
  30.2 2.0 %collective-permute-start.6 = (f32[8,512]{1,0:T(8,128)S(1)}, f32[8,512]{1,0:T(8,128)S(1)}, u32[]{:S(2)}, u32[]{:S(2)}) collective-permute-start(f32[8,512]{1,0:T(8,128)S(1)} %get-tuple-element.90), channel_id=1, source_target_pairs={{0,1},{2,3},{4,5},{6,7},{8,9},{10,11},{12,13},{14,15},{16,17},{18,... | collective-permute-start | bytes 49160 | tf_op jit(solution)/shard_map/ppermute | solution.py:799
  32.2 1.2 %collective-permute-done.9 = bf16[256,384]{1,0:T(8,128)(2,1)S(1)} collective-permute-done((bf16[256,384]{1,0:T(8,128)(2,1)S(1)}, bf16[256,384]{1,0:T(8,128)(2,1)S(1)}, u32[]{:S(2)}, u32[]{:S(2)}) %collective-permute-start.9) | collective-permute-done | bytes 196640 | tf_op jit(solution)/shard_map/ppermute | solution.py:30
  33.6 2.3 %collective-permute-done.12.g1_ref = bf16[1024,384]{1,0:T(8,128)(2,1)S(1)} collective-permute-done((bf16[1024,384]{1,0:T(8,128)(2,1)S(1)}, bf16[1024,384]{1,0:T(8,128)(2,1)S(1)}, u32[]{:S(2)}, u32[]{:S(2)}) %collective-permute-start.12) | collective-permute-done | bytes 786464 | tf_op jit(solution)/shard_map/ppermute | solution.py:30
  35.9 6.9 %shard_map.291 = (bf16[1024,512]{1,0:T(8,128)(2,1)}, f32[1024,512]{1,0:T(8,128)S(1)}, bf16[1024,512]{1,0:T(8,128)(2,1)S(1)}, f32[1024,512]{1,0:T(8,128)S(1)}, bf...) custom-call(s32[1]{0:T(128)} %bitcast.me_ref, ...), custom_call_target="tpu_custom_call" | custom-call | flops 10000000000 | bytes 35000000 | tf_op jit(solution)/shard_map/pallas_call | solution.py:629
  42.8 2.5 %shard_map.292 = (bf16[1024,384]{1,0:T(8,128)(2,1)S(1)}, bf16[1024,384]{1,0:T(8,128)(2,1)S(1)}) custom-call(s32[1]{0:T(128)} %bitcast.me_ref, bf16[1024,512]{1,0:T(8,128)(2,1)S(1)} %get-tuple-element.100.act_ref, bf16[1024,1024]{1,0:T(8,128)(2,1)S(1)} %get-tuple-element.101.unit_grad_ref, bf16[1024,512]{1,0:T(8,128)(2,1)S(1)} %get-tuple-element.102.lru_grad_ref, ...), custom_call_target="tpu_custom_call" | custom-call | flops 2500000000 | bytes 8750000 | tf_op jit(solution)/shard_map/pallas_call | solution.py:629
  45.3 0.2 collective-permute-start.13
  45.5 0.6 shard_map.293
  46.2 1.5 %collective-permute-start.14 = (f32[8,512]{1,0:T(8,128)S(1)}, f32[8,512]{1,0:T(8,128)S(1)}, u32[]{:S(2)}, u32[]{:S(2)}) collective-permute-start(f32[8,512]{1,0:T(8,128)S(1)} %get-tuple-element.110), channel_id=1, source_target_pairs={{1,0},{3,2},{5,4},{7,6},{9,8},{11,10},{13,12},{15,14},{17,16},{19,... | collective-permute-start | bytes 49160 | tf_op jit(solution)/shard_map/ppermute | solution.py:799
  47.7 0.2 add_convert_fusion
  48.0 0.6 collective-permute-start.16
  48.6 1.5 %collective-permute-start.15 = (bf16[256,384]{1,0:T(8,128)(2,1)S(1)}, bf16[256,384]{1,0:T(8,128)(2,1)S(1)}, u32[]{:S(2)}, u32[]{:S(2)}) collective-permute-start(bf16[256,384]{1,0:T(8,128)(2,1)S(1)} %get-tuple-element.157), channel_id=1, source_target_pairs={{0,4},{1,5},{2,6},{3,7},{4,0},{5,1},{6,2},{7,3},{8,12},{9,13},{10,... | collective-permute-start | bytes 589832 | tf_op jit(solution)/shard_map/ppermute | solution.py:30
  50.1 3.6 %shard_map.294 = (bf16[1024,128]{1,0:T(8,128)(2,1)S(1)}, bf16[1088,128]{1,0:T(8,128)(2,1)S(1)}, f32[1024,512]{1,0:T(8,128)S(1)}) custom-call(s32[1]{0:T(128)} %bitcast.me_ref, bf16[1024,512]{1,0:T(8,128)(2,1)S(1)} %copy-done, f32[2,1024,128]{2,1,0:T(8,128)S(1)} %get-tuple-element.81.stats_ref, bf16[1024,512]{1,0:T(8,128)(2,1)S(1)} %get-tuple-element.86.normed_ref, ...), custom_call_target="tpu_custom_call" | custom-call | flops 4499999744 | bytes 15750000 | tf_op jit(solution)/shard_map/pallas_call | solution.py:629
  53.8 2.4 %shard_map.295 = f32[1024,512]{1,0:T(8,128)} custom-call(s32[1]{0:T(128)} %bitcast.me_ref, bf16[1024,512]{1,0:T(8,128)(2,1)S(1)} %copy-done, f32[2,1024,128]{2,1,0:T(8,128)S(1)} %get-tuple-element.81.stats_ref, bf16[1024,512]{1,0:T(8,128)(2,1)S(1)} %copy-done.1, f32[1024,512]{1,0:T(8,128)S(1)} %get-tuple-element.116.normed_grad_ref, ...), custom_call_target="tpu_custom_call" | custom-call | flops 2500000000 | bytes 8750000 | tf_op jit(solution)/shard_map/pallas_call | solution.py:629
  56.2 0.4 collective-permute-start.17
  56.7 1.2 %collective-permute-done.17 = bf16[1088,128]{1,0:T(8,128)(2,1)S(1)} collective-permute-done((bf16[1088,128]{1,0:T(8,128)(2,1)S(1)}, bf16[1088,128]{1,0:T(8,128)(2,1)S(1)}, u32[]{:S(2)}, u32[]{:S(2)}) %collective-permute-start.17) | collective-permute-done | bytes 278560 | tf_op jit(solution)/shard_map/ppermute | solution.py:30
  58.0 1.6 %collective-permute-start.18 = (bf16[576,128]{1,0:T(8,128)(2,1)S(1)}, bf16[576,128]{1,0:T(8,128)(2,1)S(1)}, u32[]{:S(2)}, u32[]{:S(2)}) collective-permute-start(bf16[576,128]{1,0:T(8,128)(2,1)S(1)} %pad_maximum_fusion.3), channel_id=1, source_target_pairs={{0,2},{1,3},{2,0},{3,1},{4,6},{5,7},{6,4},{7,5},{8,10},{9,11},{10,... | collective-permute-start | bytes 442376 | tf_op jit(solution)/shard_map/ppermute | solution.py:30
  59.7 1.5 %collective-permute-start.19 = (bf16[128,384]{1,0:T(8,128)(2,1)S(1)}, bf16[128,384]{1,0:T(8,128)(2,1)S(1)}, u32[]{:S(2)}, u32[]{:S(2)}) collective-permute-start(bf16[128,384]{1,0:T(8,128)(2,1)S(1)} %slice.290), channel_id=1, source_target_pairs={{0,8},{1,9},{2,10},{3,11},{4,12},{5,13},{6,14},{7,15},{8,0},{9,1},... | collective-permute-start | bytes 294920 | tf_op jit(solution)/shard_map/ppermute | solution.py:30
  61.3 1.4 %collective-permute-start.20 = (bf16[128,384]{1,0:T(8,128)(2,1)S(1)}, bf16[128,384]{1,0:T(8,128)(2,1)S(1)}, u32[]{:S(2)}, u32[]{:S(2)}) collective-permute-start(bf16[128,384]{1,0:T(8,128)(2,1)S(1)} %slice.292), channel_id=1, source_target_pairs={{0,4},{1,5},{2,6},{3,7},{4,0},{5,1},{6,2},{7,3},{8,12},{9,13},{10,... | collective-permute-start | bytes 294920 | tf_op jit(solution)/shard_map/ppermute | solution.py:30
  62.7 1.9 %collective-permute-done.19 = bf16[128,384]{1,0:T(8,128)(2,1)S(1)} collective-permute-done((bf16[128,384]{1,0:T(8,128)(2,1)S(1)}, bf16[128,384]{1,0:T(8,128)(2,1)S(1)}, u32[]{:S(2)}, u32[]{:S(2)}) %collective-permute-start.19) | collective-permute-done | bytes 98336 | tf_op jit(solution)/shard_map/ppermute | solution.py:30
  64.6 1.3 %collective-permute-done.20 = bf16[128,384]{1,0:T(8,128)(2,1)S(1)} collective-permute-done((bf16[128,384]{1,0:T(8,128)(2,1)S(1)}, bf16[128,384]{1,0:T(8,128)(2,1)S(1)}, u32[]{:S(2)}, u32[]{:S(2)}) %collective-permute-start.20) | collective-permute-done | bytes 98336 | tf_op jit(solution)/shard_map/ppermute | solution.py:30
  66.1 1.5 %collective-permute-start.21 = (bf16[320,128]{1,0:T(8,128)(2,1)S(1)}, bf16[320,128]{1,0:T(8,128)(2,1)S(1)}, u32[]{:S(2)}, u32[]{:S(2)}) collective-permute-start(bf16[320,128]{1,0:T(8,128)(2,1)S(1)} %pad_maximum_fusion.7), channel_id=1, source_target_pairs={{0,4},{1,5},{2,6},{3,7},{4,0},{5,1},{6,2},{7,3},{8,12},{9,13},{10,... | collective-permute-start | bytes 245768 | tf_op jit(solution)/shard_map/ppermute | solution.py:30
  67.6 0.5 collective-permute-start.22
  68.2 2.5 %collective-permute-done.21 = bf16[320,128]{1,0:T(8,128)(2,1)S(1)} collective-permute-done((bf16[320,128]{1,0:T(8,128)(2,1)S(1)}, bf16[320,128]{1,0:T(8,128)(2,1)S(1)}, u32[]{:S(2)}, u32[]{:S(2)}) %collective-permute-start.21) | collective-permute-done | bytes 81952 | tf_op jit(solution)/shard_map/ppermute | solution.py:30
  70.6 1.6 %collective-permute-done.22 = bf16[128,384]{1,0:T(8,128)(2,1)S(1)} collective-permute-done((bf16[128,384]{1,0:T(8,128)(2,1)S(1)}, bf16[128,384]{1,0:T(8,128)(2,1)S(1)}, u32[]{:S(2)}, u32[]{:S(2)}) %collective-permute-start.22) | collective-permute-done | bytes 98336 | tf_op jit(solution)/shard_map/ppermute | solution.py:30
  72.4 0.6 collective-permute-start.23
  73.0 3.7 %collective-permute-done.23 = bf16[192,128]{1,0:T(8,128)(2,1)S(1)} collective-permute-done((bf16[192,128]{1,0:T(8,128)(2,1)S(1)}, bf16[192,128]{1,0:T(8,128)(2,1)S(1)}, u32[]{:S(2)}, u32[]{:S(2)}) %collective-permute-start.23) | collective-permute-done | bytes 49184 | tf_op jit(solution)/shard_map/ppermute | solution.py:30
  76.8 1.3 %collective-permute-start.24 = (bf16[128,128]{1,0:T(8,128)(2,1)S(1)}, bf16[128,128]{1,0:T(8,128)(2,1)S(1)}, u32[]{:S(2)}, u32[]{:S(2)}) collective-permute-start(bf16[128,128]{1,0:T(8,128)(2,1)S(1)} %pad_maximum_fusion.11), channel_id=1, source_target_pairs={{0,16},{1,17},{2,18},{3,19},{4,20},{5,21},{6,22},{7,23},{8,24},{9,... | collective-permute-start | bytes 98312 | tf_op jit(solution)/shard_map/ppermute | solution.py:30
  78.1 1.7 %collective-permute-start.25 = (bf16[64,384]{1,0:T(8,128)(2,1)S(1)}, bf16[64,384]{1,0:T(8,128)(2,1)S(1)}, u32[]{:S(2)}, u32[]{:S(2)}) collective-permute-start(bf16[64,384]{1,0:T(8,128)(2,1)S(1)} %bitcast.34), channel_id=1, source_target_pairs={{0,16},{1,17},{2,18},{3,19},{4,20},{5,21},{6,22},{7,23},{8,24},{9,... | collective-permute-start | bytes 147464 | tf_op jit(solution)/shard_map/ppermute | solution.py:30
  79.8 2.2 %collective-permute-done.24 = bf16[128,128]{1,0:T(8,128)(2,1)S(1)} collective-permute-done((bf16[128,128]{1,0:T(8,128)(2,1)S(1)}, bf16[128,128]{1,0:T(8,128)(2,1)S(1)}, u32[]{:S(2)}, u32[]{:S(2)}) %collective-permute-start.24) | collective-permute-done | bytes 32800 | tf_op jit(solution)/shard_map/ppermute | solution.py:30
  82.0 1.0 %collective-permute-done.25.refs_3_ = bf16[64,384]{1,0:T(8,128)(2,1)S(1)} collective-permute-done((bf16[64,384]{1,0:T(8,128)(2,1)S(1)}, bf16[64,384]{1,0:T(8,128)(2,1)S(1)}, u32[]{:S(2)}, u32[]{:S(2)}) %collective-permute-start.25) | collective-permute-done | bytes 49184 | tf_op jit(solution)/shard_map/ppermute | solution.py:30
  83.1 1.1 %shard_map.296 = (f32[64,64]{1,0:T(8,128)}, f32[64,64]{1,0:T(8,128)}, f32[64,64]{1,0:T(8,128)}, f32[64,64]{1,0:T(8,128)}, f32[64,128]{1,0:T(8,128)}, /*index=5*/...) custom-call(s32[1]{0:T(128)} %bitcast.me_ref, ...), custom_call_target="tpu_custom_call" | custom-call | flops 2000000000 | bytes 7000000 | tf_op jit(solution)/shard_map/pallas_call | solution.py:629
  (82 shorter events, 1.4 us)
Async XLA Ops:
  0.7 5.3 %copy-start = (bf16[1024,512]{1,0:T(8,128)(2,1)S(1)}, bf16[1024,512]{1,0:T(8,128)(2,1)}, u32[]{:S(2)}) copy-start(bf16[1024,512]{1,0:T(8,128)(2,1)} %x_ref.9) | copy-start | bytes 3145732
  0.7 5.3 %copy-start.2 = (s32[4096]{0:T(1024)S(1)}, s32[4096]{0:T(1024)}, u32[]{:S(2)}) copy-start(s32[4096]{0:T(1024)} %param.18) | copy-start | bytes 49156
  1.8 5.9 %collective-permute-start = (bf16[96,128]{1,0:T(8,128)(2,1)S(1)}, bf16[96,128]{1,0:T(8,128)(2,1)S(1)}, u32[]{:S(2)}, u32[]{:S(2)}) collective-permute-start(bf16[96,128]{1,0:T(8,128)(2,1)S(1)} %get-tuple-element.82), channel_id=1, source_target_pairs={{0,16},{1,17},{2,18},{3,19},{4,20},{5,21},{6,22},{7,23},{8,24},{9,... | collective-permute-start | bytes 73736 | tf_op jit(solution)/shard_map/ppermute | solution.py:30
  5.9 5.1 %collective-permute-start.1 = (bf16[64,384]{1,0:T(8,128)(2,1)S(1)}, bf16[64,384]{1,0:T(8,128)(2,1)S(1)}, u32[]{:S(2)}, u32[]{:S(2)}) collective-permute-start(bf16[64,384]{1,0:T(8,128)(2,1)S(1)} %get-tuple-element.84), channel_id=1, source_target_pairs={{0,16},{1,17},{2,18},{3,19},{4,20},{5,21},{6,22},{7,23},{8,24},{9,... | collective-permute-start | bytes 147464 | tf_op jit(solution)/shard_map/ppermute | solution.py:30
  11.0 4.1 %collective-permute-start.2 = (bf16[160,128]{1,0:T(8,128)(2,1)S(1)}, bf16[160,128]{1,0:T(8,128)(2,1)S(1)}, u32[]{:S(2)}, u32[]{:S(2)}) collective-permute-start(bf16[160,128]{1,0:T(8,128)(2,1)S(1)} %pad_maximum_fusion.10), channel_id=1, source_target_pairs={{0,8},{1,9},{2,10},{3,11},{4,12},{5,13},{6,14},{7,15},{8,0},{9,1},... | collective-permute-start | bytes 122888 | tf_op jit(solution)/shard_map/ppermute | solution.py:30
  12.6 4.7 %collective-permute-start.7 = (bf16[128,384]{1,0:T(8,128)(2,1)S(1)}, bf16[128,384]{1,0:T(8,128)(2,1)S(1)}, u32[]{:S(2)}, u32[]{:S(2)}) collective-permute-start(bf16[128,384]{1,0:T(8,128)(2,1)S(1)} %pad_maximum_fusion.5), channel_id=1, source_target_pairs={{0,2},{1,3},{2,0},{3,1},{4,6},{5,7},{6,4},{7,5},{8,10},{9,11},{10,... | collective-permute-start | bytes 294920 | tf_op jit(solution)/shard_map/ppermute | solution.py:30
  15.1 4.4 %collective-permute-start.3 = (bf16[288,128]{1,0:T(8,128)(2,1)S(1)}, bf16[288,128]{1,0:T(8,128)(2,1)S(1)}, u32[]{:S(2)}, u32[]{:S(2)}) collective-permute-start(bf16[288,128]{1,0:T(8,128)(2,1)S(1)} %pad_maximum_fusion.8), channel_id=1, source_target_pairs={{0,4},{1,5},{2,6},{3,7},{4,0},{5,1},{6,2},{7,3},{8,12},{9,13},{10,... | collective-permute-start | bytes 221192 | tf_op jit(solution)/shard_map/ppermute | solution.py:30
  17.3 7.4 %collective-permute-start.10 = (bf16[128,384]{1,0:T(8,128)(2,1)S(1)}, bf16[128,384]{1,0:T(8,128)(2,1)S(1)}, u32[]{:S(2)}, u32[]{:S(2)}) collective-permute-start(bf16[128,384]{1,0:T(8,128)(2,1)S(1)} %bitcast.26), channel_id=1, source_target_pairs={{0,4},{1,5},{2,6},{3,7},{4,0},{5,1},{6,2},{7,3},{8,12},{9,13},{10,... | collective-permute-start | bytes 294920 | tf_op jit(solution)/shard_map/ppermute | solution.py:30
  18.9 7.4 %collective-permute-start.8 = (bf16[128,384]{1,0:T(8,128)(2,1)S(1)}, bf16[128,384]{1,0:T(8,128)(2,1)S(1)}, u32[]{:S(2)}, u32[]{:S(2)}) collective-permute-start(bf16[128,384]{1,0:T(8,128)(2,1)S(1)} %bitcast.29), channel_id=1, source_target_pairs={{0,8},{1,9},{2,10},{3,11},{4,12},{5,13},{6,14},{7,15},{8,0},{9,1},... | collective-permute-start | bytes 294920 | tf_op jit(solution)/shard_map/ppermute | solution.py:30
  19.6 5.0 %collective-permute-start.4 = (bf16[512,128]{1,0:T(8,128)(2,1)S(1)}, bf16[512,128]{1,0:T(8,128)(2,1)S(1)}, u32[]{:S(2)}, u32[]{:S(2)}) collective-permute-start(bf16[512,128]{1,0:T(8,128)(2,1)S(1)} %pad_maximum_fusion.4), channel_id=1, source_target_pairs={{0,2},{1,3},{2,0},{3,1},{4,6},{5,7},{6,4},{7,5},{8,10},{9,11},{10,... | collective-permute-start | bytes 393224 | tf_op jit(solution)/shard_map/ppermute | solution.py:30
  24.7 3.3 %collective-permute-start.5 = (bf16[1024,128]{1,0:T(8,128)(2,1)S(1)}, bf16[1024,128]{1,0:T(8,128)(2,1)S(1)}, u32[]{:S(2)}, u32[]{:S(2)}) collective-permute-start(bf16[1024,128]{1,0:T(8,128)(2,1)S(1)} %constant_dynamic-update-slice_fusion.b0_ref), channel_id=1, source_target_pairs={{0,1},{1,0},{2,3},{3,2},{4,5},{5,4},{6,7},{7,6},{8,9},{9,8},{10,11... | collective-permute-start | bytes 786440 | tf_op jit(solution)/shard_map/ppermute | solution.py:30
  24.8 7.4 %collective-permute-start.11 = (bf16[256,384]{1,0:T(8,128)(2,1)S(1)}, bf16[256,384]{1,0:T(8,128)(2,1)S(1)}, u32[]{:S(2)}, u32[]{:S(2)}) collective-permute-start(bf16[256,384]{1,0:T(8,128)(2,1)S(1)} %pad_maximum_fusion.2), channel_id=1, source_target_pairs={{0,8},{1,9},{2,10},{3,11},{4,12},{5,13},{6,14},{7,15},{8,0},{9,1},... | collective-permute-start | bytes 589832 | tf_op jit(solution)/shard_map/ppermute | solution.py:30
  26.3 7.1 %collective-permute-start.9 = (bf16[256,384]{1,0:T(8,128)(2,1)S(1)}, bf16[256,384]{1,0:T(8,128)(2,1)S(1)}, u32[]{:S(2)}, u32[]{:S(2)}) collective-permute-start(bf16[256,384]{1,0:T(8,128)(2,1)S(1)} %pad_maximum_fusion.1), channel_id=1, source_target_pairs={{0,4},{1,5},{2,6},{3,7},{4,0},{5,1},{6,2},{7,3},{8,12},{9,13},{10,... | collective-permute-start | bytes 589832 | tf_op jit(solution)/shard_map/ppermute | solution.py:30
  27.9 8.0 %copy-start.1 = (bf16[1024,512]{1,0:T(8,128)(2,1)S(1)}, bf16[1024,512]{1,0:T(8,128)(2,1)}, u32[]{:S(2)}) copy-start(bf16[1024,512]{1,0:T(8,128)(2,1)} %grad_ref.3) | copy-start | bytes 3145732
  30.2 3.3 %collective-permute-start.6 = (f32[8,512]{1,0:T(8,128)S(1)}, f32[8,512]{1,0:T(8,128)S(1)}, u32[]{:S(2)}, u32[]{:S(2)}) collective-permute-start(f32[8,512]{1,0:T(8,128)S(1)} %get-tuple-element.90), channel_id=1, source_target_pairs={{0,1},{2,3},{4,5},{6,7},{8,9},{10,11},{12,13},{14,15},{16,17},{18,... | collective-permute-start | bytes 49160 | tf_op jit(solution)/shard_map/ppermute | solution.py:799
  33.5 2.4 %collective-permute-start.12 = (bf16[1024,384]{1,0:T(8,128)(2,1)S(1)}, bf16[1024,384]{1,0:T(8,128)(2,1)S(1)}, u32[]{:S(2)}, u32[]{:S(2)}) collective-permute-start(bf16[1024,384]{1,0:T(8,128)(2,1)S(1)} %constant_dynamic-update-slice_fusion.5.g0_ref), channel_id=1, source_target_pairs={{0,1},{1,0},{2,3},{3,2},{4,5},{5,4},{6,7},{7,6},{8,9},{9,8},{10,11... | collective-permute-start | bytes 2359304 | tf_op jit(solution)/shard_map/ppermute | solution.py:30
  45.3 2.4 %collective-permute-start.13 = (bf16[1024,384]{1,0:T(8,128)(2,1)S(1)}, bf16[1024,384]{1,0:T(8,128)(2,1)S(1)}, u32[]{:S(2)}, u32[]{:S(2)}) collective-permute-start(bf16[1024,384]{1,0:T(8,128)(2,1)S(1)} %get-tuple-element.104), channel_id=1, source_target_pairs={{0,1},{1,0},{2,3},{3,2},{4,5},{5,4},{6,7},{7,6},{8,9},{9,8},{10,11... | collective-permute-start | bytes 2359304 | tf_op jit(solution)/shard_map/ppermute | solution.py:30
  46.2 4.0 %collective-permute-start.14 = (f32[8,512]{1,0:T(8,128)S(1)}, f32[8,512]{1,0:T(8,128)S(1)}, u32[]{:S(2)}, u32[]{:S(2)}) collective-permute-start(f32[8,512]{1,0:T(8,128)S(1)} %get-tuple-element.110), channel_id=1, source_target_pairs={{1,0},{3,2},{5,4},{7,6},{9,8},{11,10},{13,12},{15,14},{17,16},{19,... | collective-permute-start | bytes 49160 | tf_op jit(solution)/shard_map/ppermute | solution.py:799
  48.0 8.2 %collective-permute-start.16 = (bf16[256,384]{1,0:T(8,128)(2,1)S(1)}, bf16[256,384]{1,0:T(8,128)(2,1)S(1)}, u32[]{:S(2)}, u32[]{:S(2)}) collective-permute-start(bf16[256,384]{1,0:T(8,128)(2,1)S(1)} %get-tuple-element.156), channel_id=1, source_target_pairs={{0,8},{1,9},{2,10},{3,11},{4,12},{5,13},{6,14},{7,15},{8,0},{9,1},... | collective-permute-start | bytes 589832 | tf_op jit(solution)/shard_map/ppermute | solution.py:30
  48.6 7.6 %collective-permute-start.15 = (bf16[256,384]{1,0:T(8,128)(2,1)S(1)}, bf16[256,384]{1,0:T(8,128)(2,1)S(1)}, u32[]{:S(2)}, u32[]{:S(2)}) collective-permute-start(bf16[256,384]{1,0:T(8,128)(2,1)S(1)} %get-tuple-element.157), channel_id=1, source_target_pairs={{0,4},{1,5},{2,6},{3,7},{4,0},{5,1},{6,2},{7,3},{8,12},{9,13},{10,... | collective-permute-start | bytes 589832 | tf_op jit(solution)/shard_map/ppermute | solution.py:30
  56.2 1.6 %collective-permute-start.17 = (bf16[1088,128]{1,0:T(8,128)(2,1)S(1)}, bf16[1088,128]{1,0:T(8,128)(2,1)S(1)}, u32[]{:S(2)}, u32[]{:S(2)}) collective-permute-start(bf16[1088,128]{1,0:T(8,128)(2,1)S(1)} %get-tuple-element.120), channel_id=1, source_target_pairs={{0,1},{1,0},{2,3},{3,2},{4,5},{5,4},{6,7},{7,6},{8,9},{9,8},{10,11... | collective-permute-start | bytes 835592 | tf_op jit(solution)/shard_map/ppermute | solution.py:30
  58.0 7.9 %collective-permute-start.18 = (bf16[576,128]{1,0:T(8,128)(2,1)S(1)}, bf16[576,128]{1,0:T(8,128)(2,1)S(1)}, u32[]{:S(2)}, u32[]{:S(2)}) collective-permute-start(bf16[576,128]{1,0:T(8,128)(2,1)S(1)} %pad_maximum_fusion.3), channel_id=1, source_target_pairs={{0,2},{1,3},{2,0},{3,1},{4,6},{5,7},{6,4},{7,5},{8,10},{9,11},{10,... | collective-permute-start | bytes 442376 | tf_op jit(solution)/shard_map/ppermute | solution.py:30
  59.7 4.8 %collective-permute-start.19 = (bf16[128,384]{1,0:T(8,128)(2,1)S(1)}, bf16[128,384]{1,0:T(8,128)(2,1)S(1)}, u32[]{:S(2)}, u32[]{:S(2)}) collective-permute-start(bf16[128,384]{1,0:T(8,128)(2,1)S(1)} %slice.290), channel_id=1, source_target_pairs={{0,8},{1,9},{2,10},{3,11},{4,12},{5,13},{6,14},{7,15},{8,0},{9,1},... | collective-permute-start | bytes 294920 | tf_op jit(solution)/shard_map/ppermute | solution.py:30
  61.3 4.6 %collective-permute-start.20 = (bf16[128,384]{1,0:T(8,128)(2,1)S(1)}, bf16[128,384]{1,0:T(8,128)(2,1)S(1)}, u32[]{:S(2)}, u32[]{:S(2)}) collective-permute-start(bf16[128,384]{1,0:T(8,128)(2,1)S(1)} %slice.292), channel_id=1, source_target_pairs={{0,4},{1,5},{2,6},{3,7},{4,0},{5,1},{6,2},{7,3},{8,12},{9,13},{10,... | collective-permute-start | bytes 294920 | tf_op jit(solution)/shard_map/ppermute | solution.py:30
  66.1 4.5 %collective-permute-start.21 = (bf16[320,128]{1,0:T(8,128)(2,1)S(1)}, bf16[320,128]{1,0:T(8,128)(2,1)S(1)}, u32[]{:S(2)}, u32[]{:S(2)}) collective-permute-start(bf16[320,128]{1,0:T(8,128)(2,1)S(1)} %pad_maximum_fusion.7), channel_id=1, source_target_pairs={{0,4},{1,5},{2,6},{3,7},{4,0},{5,1},{6,2},{7,3},{8,12},{9,13},{10,... | collective-permute-start | bytes 245768 | tf_op jit(solution)/shard_map/ppermute | solution.py:30
  67.6 4.6 %collective-permute-start.22 = (bf16[128,384]{1,0:T(8,128)(2,1)S(1)}, bf16[128,384]{1,0:T(8,128)(2,1)S(1)}, u32[]{:S(2)}, u32[]{:S(2)}) collective-permute-start(bf16[128,384]{1,0:T(8,128)(2,1)S(1)} %pad_maximum_fusion.6), channel_id=1, source_target_pairs={{0,2},{1,3},{2,0},{3,1},{4,6},{5,7},{6,4},{7,5},{8,10},{9,11},{10,... | collective-permute-start | bytes 294920 | tf_op jit(solution)/shard_map/ppermute | solution.py:30
  72.4 4.3 %collective-permute-start.23 = (bf16[192,128]{1,0:T(8,128)(2,1)S(1)}, bf16[192,128]{1,0:T(8,128)(2,1)S(1)}, u32[]{:S(2)}, u32[]{:S(2)}) collective-permute-start(bf16[192,128]{1,0:T(8,128)(2,1)S(1)} %pad_maximum_fusion.9), channel_id=1, source_target_pairs={{0,8},{1,9},{2,10},{3,11},{4,12},{5,13},{6,14},{7,15},{8,0},{9,1},... | collective-permute-start | bytes 147464 | tf_op jit(solution)/shard_map/ppermute | solution.py:30
  76.8 5.2 %collective-permute-start.24 = (bf16[128,128]{1,0:T(8,128)(2,1)S(1)}, bf16[128,128]{1,0:T(8,128)(2,1)S(1)}, u32[]{:S(2)}, u32[]{:S(2)}) collective-permute-start(bf16[128,128]{1,0:T(8,128)(2,1)S(1)} %pad_maximum_fusion.11), channel_id=1, source_target_pairs={{0,16},{1,17},{2,18},{3,19},{4,20},{5,21},{6,22},{7,23},{8,24},{9,... | collective-permute-start | bytes 98312 | tf_op jit(solution)/shard_map/ppermute | solution.py:30
  78.1 5.0 %collective-permute-start.25 = (bf16[64,384]{1,0:T(8,128)(2,1)S(1)}, bf16[64,384]{1,0:T(8,128)(2,1)S(1)}, u32[]{:S(2)}, u32[]{:S(2)}) collective-permute-start(bf16[64,384]{1,0:T(8,128)(2,1)S(1)} %bitcast.34), channel_id=1, source_target_pairs={{0,16},{1,17},{2,18},{3,19},{4,20},{5,21},{6,22},{7,23},{8,24},{9,... | collective-permute-start | bytes 147464 | tf_op jit(solution)/shard_map/ppermute | solution.py:30

commit v4 on v3

--- a/solution.py
+++ b/solution.py
@@ -566,11 +566,11 @@
 
 
 def last_kernel(plan, me_ref, *refs):
-    b_keep, b_other, w_keep, w_other, tail_ref = refs[:5]
-    outs, held, sems = refs[5:19], refs[19:33], refs[33]
+    b_keep, b_other, w_mine_ref, tail_ref = refs[:4]
+    outs, held, sems = refs[4:18], refs[18:32], refs[32]
     own, units = plan.own_states, plan.units
     b_mine = b_keep[...].astype(F32) + b_other[...].astype(F32)
-    w_mine = w_keep[...].astype(F32) + w_other[...].astype(F32)
+    w_mine = w_mine_ref[...]
     half = tail_ref.shape[0] // 4
     tail = [tail_ref[part * half : part * half + half, :].astype(F32) for part in range(4)]
     vectors = (tail[0] + tail[1]) + (tail[2] + tail[3])
@@ -788,7 +788,7 @@
         ],
         [pltpu.VMEM((features, 2 * states), pack_type)],
         8,
-        3,
+        0.3,
         me, block_input, stats, b0, b1, vectors, masks,
     )
 
@@ -846,18 +846,16 @@
         [shape((chunks, 2 * states)), shape((chunks, LANES)), shape((8, 2 * states))],
         [],
         8,
-        1.5,
+        1,
         me, after(state_grad, w_send), params, masks,
     )
     back = pass_on(back, False) if plan.pieces == 2 else jnp.zeros_like(back)
     pieces = plan.halves
-    w_other = after(w_other, back_ends)
-    w_total = added(w_keep, w_other)
+    w_total = added(w_keep, after(w_other, back_ends))
     size = w_total.shape[0] // pieces
     halves = [cut(w_total[half * size : half * size + size]) for half in range(pieces)]
-    w_keeps = [half[0] for half in halves]
     w_others = [flip(half[1], bit, plan.count) for half, bit in zip(halves, (2, 3))]
-    back_ends = after(back_ends, w_other)
+    back_ends = after(back_ends, *(half[1] for half in halves))
     b_keep, b_send, normed_grad = call(
         leave_kernel,
         plan,
@@ -876,6 +874,12 @@
         me, block_input, stats, normed, source, back_ends, back_hold, back, hidden,
         state_grad, lru_grad, input_map, vectors, params, masks, sums,
     )
+    w_others = [after(other, b_keep) for other in w_others]
+    halves = [cut(added(half[0], other)) for half, other in zip(halves, w_others)]
+    b_other = after(flip(b_send, 0, plan.count), *(half[1] for half in halves))
+    b_keep, b_send = summed_step(b_keep, b_send, b_other)
+    b_other = flip(b_send, 1, plan.count)
+    w_others = [flip(half[1], bit, plan.count) for half, bit in zip(halves, (3, 2))]
     (input_grad,) = call(
         input_kernel,
         plan,
@@ -883,32 +887,26 @@
         [],
         8,
         2.5,
-        me, block_input, stats, out_grad, normed_grad, vectors,
-    )
-    b_keep, b_send, input_grad, w_others = together(b_keep, b_send, input_grad, w_others)
-    parts = [cut(added(keep, other)) for keep, other in zip(w_keeps, w_others)]
-    w_others = [flip(part[1], bit, plan.count) for part, bit in zip(parts, (3, 2))]
-    b_other = flip(b_send, 0, plan.count)
+        me, block_input, stats, out_grad, after(normed_grad, b_send), vectors,
+    )
+    b_other = after(b_other, input_grad)
     b_keep, b_send = summed_step(b_keep, b_send, b_other)
-    b_other = flip(b_send, 1, plan.count)
-    b_other, w_others = together(b_other, w_others)
-    b_keep, b_send = summed_step(b_keep, b_send, b_other)
-    halves = [cut(added(part[0], other)) for part, other in zip(parts, w_others)]
+    halves = [cut(added(half[0], after(other, b_send))) for half, other in zip(halves, w_others)]
     w_keep = joined(*(half[0] for half in halves))
     w_send = joined(*(half[1] for half in halves))
-    for bit, w_bit in zip(plan.down[2:-1], [1, *plan.down[4:]]):
-        b_send, w_send = together(b_send, w_send)
+    for bit in range(2, plan.bits - 1):
+        w_bit = 1 if bit == 2 else bit + 1
         b_other = flip(b_send, bit, plan.count)
         w_other = flip(w_send, w_bit, plan.count)
-        if bit < plan.bits - 2:
-            b_other, w_other = together(b_other, w_other)
         b_keep, b_send = summed_step(b_keep, b_send, b_other)
         if w_bit < plan.bits - 1:
+            w_other = after(w_other, b_send)
             total = added(w_keep, w_other).reshape(pieces, -1, block)
             size = total.shape[1] // 2
             w_keep = total[:, :size].reshape(-1, block).astype(BF16)
             w_send = total[:, size:].reshape(-1, block).astype(BF16)
-    b_other = flip(b_send, plan.bits - 1, plan.count)
+    w_mine = added(w_keep, w_other)
+    b_other = after(flip(b_send, plan.bits - 1, plan.count), w_mine)
     b_other, tail = b_other[:long], joined(b_send[long:], b_other[long:])
     small = (
         [(long, own)] * 4 + [(long, units)] * 2 + [(1, long)] * 5 + [(1, short)] * 3
@@ -922,7 +920,7 @@
         [pltpu.VMEM(dims, F32) for dims in small] + [pltpu.SemaphoreType.DMA((14,))],
         4,
         2,
-        me, b_keep, b_other, w_keep, w_other, tail,
+        me, b_keep, b_other, w_mine, tail,
         far_out=True,
     )
     gain_grad, bias_grad, skip_grad, value_line, gate_line, nu_grad, theta_grad, gamma_grad = (

time: 84.6 us -> 78.1 us (0.923)
  waiting for transfers between devices: 28 us -> 19.5 us
  starting transfers between devices: 32.3 us -> 34.5 us
    ppermute x24, waiting for transfers between devices: 28 us -> 19 us  [flip(): return lax.ppermute(value, AXES, [(i, i ^ 1 << bit) for i in range(count)])]
    ppermute x24, starting transfers between devices: 28.8 us -> 30.7 us  [flip(): return lax.ppermute(value, AXES, [(i, i ^ 1 << bit) for i in range(count)])]
  transfers between devices with their start and end apart: 26 -> 26, of which waited for: 17 -> 16; matrix products, arithmetic and copies ran while one was open for 1% -> 1% of each run, Pallas kernels for 12% -> 13%
where the time goes in v4:
time: 78.1 us; the launch traced here: 77.9 us
  starting transfers between devices  34.5 us (44%)
  Pallas kernels  21.5 us (28%)
  waiting for transfers between devices  19.5 us (25%)
  between operations  1.3 us (2%)
  other arithmetic  0.83 us (1%)
    ppermute x24, starting transfers between devices, flip(): return lax.ppermute(value, AXES, [(i, i ^ 1 << bit) for i in range(count)])  30.7 us
    pallas_call x9, Pallas kernels, call(): pl.pallas_call(functools.partial(kernel, plan), out_shape=outs, in_specs=...  21.5 us
    ppermute x24, waiting for transfers between devices, flip(): return lax.ppermute(value, AXES, [(i, i ^ 1 << bit) for i in range(count)])  19 us
    ppermute x2, starting transfers between devices, pass_on(): return lax.ppermute(value, 'tensor', pairs)  3.73 us
  transfers between devices with their start and end apart: 26, of which 16 were waited for; matrix products, arithmetic and copies ran while one was open for 1% of the time, Pallas kernels for 13%

profile of v4, /device:TPU:0, one launch (start us, length us, event | category | flops | bytes accessed | tf_op | source)
XLA Modules:
  0.0 77.9 jit_solution(7597267372496213946)
XLA Ops:
  0.7 1.1 %shard_map.289 = (bf16[96,128]{1,0:T(8,128)(2,1)S(1)}, bf16[64,384]{1,0:T(8,128)(2,1)S(1)}) custom-call(s32[1]{0:T(128)} %bitcast.me_ref, bf16[64,64]{1,0:T(8,128)(2,1)} %refs_0_.1, bf16[64,64]{1,0:T(8,128)(2,1)} %refs_1_.1, bf16[64,64]{1,0:T(8,128)(2,1)} %refs_2_.1, bf16[64,64]{1,0:T(8,128)(2,1)} %refs_3_.1, bf16[64,128]{1,0:T(8,128)(2,1)} %refs_4_.1, ...), custom_call_target="tpu_custom_call" | custom-call | flops 1500000000 | bytes 5250000 | tf_op jit(solution)/shard_map/pallas_call | solution.py:629
  1.8 4.1 %collective-permute-start = (bf16[96,128]{1,0:T(8,128)(2,1)S(1)}, bf16[96,128]{1,0:T(8,128)(2,1)S(1)}, u32[]{:S(2)}, u32[]{:S(2)}) collective-permute-start(bf16[96,128]{1,0:T(8,128)(2,1)S(1)} %get-tuple-element.77), channel_id=1, source_target_pairs={{0,16},{1,17},{2,18},{3,19},{4,20},{5,21},{6,22},{7,23},{8,24},{9,... | collective-permute-start | bytes 73736 | tf_op jit(solution)/shard_map/ppermute | solution.py:30
  6.0 1.1 %shard_map.288 = (f32[2,1024,128]{2,1,0:T(8,128)S(1)}, f32[4,1024,128]{2,1,0:T(8,128)S(1)}) custom-call(s32[1]{0:T(128)} %bitcast.me_ref, bf16[1024,512]{1,0:T(8,128)(2,1)S(1)} %copy-done, s32[32,128]{1,0:T(8,128)S(1)} %bitcast.26), custom_call_target="tpu_custom_call" | custom-call | flops 2000000000 | bytes 7000000 | tf_op jit(solution)/shard_map/pallas_call | solution.py:629
  7.1 0.7 collective-permute-done
  7.7 3.3 %collective-permute-done.1 = bf16[64,384]{1,0:T(8,128)(2,1)S(1)} collective-permute-done((bf16[64,384]{1,0:T(8,128)(2,1)S(1)}, bf16[64,384]{1,0:T(8,128)(2,1)S(1)}, u32[]{:S(2)}, u32[]{:S(2)}) %collective-permute-start.1) | collective-permute-done | bytes 49184 | tf_op jit(solution)/shard_map/ppermute | solution.py:30
  11.0 1.5 %collective-permute-start.2 = (bf16[160,128]{1,0:T(8,128)(2,1)S(1)}, bf16[160,128]{1,0:T(8,128)(2,1)S(1)}, u32[]{:S(2)}, u32[]{:S(2)}) collective-permute-start(bf16[160,128]{1,0:T(8,128)(2,1)S(1)} %pad_maximum_fusion.10), channel_id=1, source_target_pairs={{0,8},{1,9},{2,10},{3,11},{4,12},{5,13},{6,14},{7,15},{8,0},{9,1},... | collective-permute-start | bytes 122888 | tf_op jit(solution)/shard_map/ppermute | solution.py:30
  12.6 1.6 %collective-permute-start.7 = (bf16[128,384]{1,0:T(8,128)(2,1)S(1)}, bf16[128,384]{1,0:T(8,128)(2,1)S(1)}, u32[]{:S(2)}, u32[]{:S(2)}) collective-permute-start(bf16[128,384]{1,0:T(8,128)(2,1)S(1)} %pad_maximum_fusion.5), channel_id=1, source_target_pairs={{0,2},{1,3},{2,0},{3,1},{4,6},{5,7},{6,4},{7,5},{8,10},{9,11},{10,... | collective-permute-start | bytes 294920 | tf_op jit(solution)/shard_map/ppermute | solution.py:30
  14.1 1.0 %collective-permute-done.2 = bf16[160,128]{1,0:T(8,128)(2,1)S(1)} collective-permute-done((bf16[160,128]{1,0:T(8,128)(2,1)S(1)}, bf16[160,128]{1,0:T(8,128)(2,1)S(1)}, u32[]{:S(2)}, u32[]{:S(2)}) %collective-permute-start.2) | collective-permute-done | bytes 40992 | tf_op jit(solution)/shard_map/ppermute | solution.py:30
  15.1 1.6 %collective-permute-start.3 = (bf16[288,128]{1,0:T(8,128)(2,1)S(1)}, bf16[288,128]{1,0:T(8,128)(2,1)S(1)}, u32[]{:S(2)}, u32[]{:S(2)}) collective-permute-start(bf16[288,128]{1,0:T(8,128)(2,1)S(1)} %pad_maximum_fusion.8), channel_id=1, source_target_pairs={{0,4},{1,5},{2,6},{3,7},{4,0},{5,1},{6,2},{7,3},{8,12},{9,13},{10,... | collective-permute-start | bytes 221192 | tf_op jit(solution)/shard_map/ppermute | solution.py:30
  16.7 0.5 collective-permute-done.7
  17.3 1.6 %collective-permute-start.10 = (bf16[128,384]{1,0:T(8,128)(2,1)S(1)}, bf16[128,384]{1,0:T(8,128)(2,1)S(1)}, u32[]{:S(2)}, u32[]{:S(2)}) collective-permute-start(bf16[128,384]{1,0:T(8,128)(2,1)S(1)} %bitcast.27), channel_id=1, source_target_pairs={{0,4},{1,5},{2,6},{3,7},{4,0},{5,1},{6,2},{7,3},{8,12},{9,13},{10,... | collective-permute-start | bytes 294920 | tf_op jit(solution)/shard_map/ppermute | solution.py:30
  18.9 0.6 collective-permute-start.8
  19.6 1.6 %collective-permute-start.4 = (bf16[512,128]{1,0:T(8,128)(2,1)S(1)}, bf16[512,128]{1,0:T(8,128)(2,1)S(1)}, u32[]{:S(2)}, u32[]{:S(2)}) collective-permute-start(bf16[512,128]{1,0:T(8,128)(2,1)S(1)} %pad_maximum_fusion.4), channel_id=1, source_target_pairs={{0,2},{1,3},{2,0},{3,1},{4,6},{5,7},{6,4},{7,5},{8,10},{9,11},{10,... | collective-permute-start | bytes 393224 | tf_op jit(solution)/shard_map/ppermute | solution.py:30
  21.2 0.8 %collective-permute-done.10 = bf16[128,384]{1,0:T(8,128)(2,1)S(1)} collective-permute-done((bf16[128,384]{1,0:T(8,128)(2,1)S(1)}, bf16[128,384]{1,0:T(8,128)(2,1)S(1)}, u32[]{:S(2)}, u32[]{:S(2)}) %collective-permute-start.10) | collective-permute-done | bytes 98336 | tf_op jit(solution)/shard_map/ppermute | solution.py:30
  22.0 1.6 %collective-permute-start.11 = (bf16[256,384]{1,0:T(8,128)(2,1)S(1)}, bf16[256,384]{1,0:T(8,128)(2,1)S(1)}, u32[]{:S(2)}, u32[]{:S(2)}) collective-permute-start(bf16[256,384]{1,0:T(8,128)(2,1)S(1)} %pad_maximum_fusion.2), channel_id=1, source_target_pairs={{0,8},{1,9},{2,10},{3,11},{4,12},{5,13},{6,14},{7,15},{8,0},{9,1},... | collective-permute-start | bytes 589832 | tf_op jit(solution)/shard_map/ppermute | solution.py:30
  23.7 1.5 %collective-permute-start.9 = (bf16[256,384]{1,0:T(8,128)(2,1)S(1)}, bf16[256,384]{1,0:T(8,128)(2,1)S(1)}, u32[]{:S(2)}, u32[]{:S(2)}) collective-permute-start(bf16[256,384]{1,0:T(8,128)(2,1)S(1)} %pad_maximum_fusion.1), channel_id=1, source_target_pairs={{0,4},{1,5},{2,6},{3,7},{4,0},{5,1},{6,2},{7,3},{8,12},{9,13},{10,... | collective-permute-start | bytes 589832 | tf_op jit(solution)/shard_map/ppermute | solution.py:30
  25.3 1.5 %collective-permute-done.5.b1_ref = bf16[1024,128]{1,0:T(8,128)(2,1)S(1)} collective-permute-done((bf16[1024,128]{1,0:T(8,128)(2,1)S(1)}, bf16[1024,128]{1,0:T(8,128)(2,1)S(1)}, u32[]{:S(2)}, u32[]{:S(2)}) %collective-permute-start.5) | collective-permute-done | bytes 262176 | tf_op jit(solution)/shard_map/ppermute | solution.py:30
  26.8 2.2 %shard_map.290 = (bf16[1024,512]{1,0:T(8,128)(2,1)S(1)}, f32[1024,512]{1,0:T(8,128)S(1)}, f32[64,512]{1,0:T(8,128)S(1)}, f32[64,128]{1,0:T(8,128)S(1)}, f32[8,51...) custom-call(s32[1]{0:T(128)} %bitcast.me_ref, bf16[1024,512]{1,0:T(8,128)(2,1)S(1)} %copy-done, ...), custom_call_target="tpu_custom_call" | custom-call | flops 300000000 | bytes 1050000 | tf_op jit(solution)/shard_map/pallas_call | solution.py:629
  29.0 2.2 %collective-permute-start.6 = (f32[8,512]{1,0:T(8,128)S(1)}, f32[8,512]{1,0:T(8,128)S(1)}, u32[]{:S(2)}, u32[]{:S(2)}) collective-permute-start(f32[8,512]{1,0:T(8,128)S(1)} %get-tuple-element.85), channel_id=1, source_target_pairs={{0,1},{2,3},{4,5},{6,7},{8,9},{10,11},{12,13},{14,15},{16,17},{18,... | collective-permute-start | bytes 49160 | tf_op jit(solution)/shard_map/ppermute | solution.py:799
  31.4 0.5 collective-permute-done.6.carry_ref
  31.9 0.3 collective-permute-start.12
  32.2 1.9 %collective-permute-done.12.g1_ref = bf16[1024,384]{1,0:T(8,128)(2,1)S(1)} collective-permute-done((bf16[1024,384]{1,0:T(8,128)(2,1)S(1)}, bf16[1024,384]{1,0:T(8,128)(2,1)S(1)}, u32[]{:S(2)}, u32[]{:S(2)}) %collective-permute-start.12) | collective-permute-done | bytes 786464 | tf_op jit(solution)/shard_map/ppermute | solution.py:30
  34.2 6.9 %shard_map.291 = (bf16[1024,512]{1,0:T(8,128)(2,1)}, f32[1024,512]{1,0:T(8,128)S(1)}, bf16[1024,512]{1,0:T(8,128)(2,1)S(1)}, f32[1024,512]{1,0:T(8,128)S(1)}, bf...) custom-call(s32[1]{0:T(128)} %bitcast.me_ref, ...), custom_call_target="tpu_custom_call" | custom-call | flops 10000000000 | bytes 35000000 | tf_op jit(solution)/shard_map/pallas_call | solution.py:629
  41.1 2.5 %shard_map.292 = (bf16[1024,384]{1,0:T(8,128)(2,1)S(1)}, bf16[1024,384]{1,0:T(8,128)(2,1)S(1)}) custom-call(s32[1]{0:T(128)} %bitcast.me_ref, bf16[1024,512]{1,0:T(8,128)(2,1)S(1)} %get-tuple-element.95.act_ref, bf16[1024,1024]{1,0:T(8,128)(2,1)S(1)} %get-tuple-element.96.unit_grad_ref, bf16[1024,512]{1,0:T(8,128)(2,1)S(1)} %get-tuple-element.97.lru_grad_ref, ...), custom_call_target="tpu_custom_call" | custom-call | flops 2500000000 | bytes 8750000 | tf_op jit(solution)/shard_map/pallas_call | solution.py:629
  43.6 0.4 collective-permute-start.13
  44.0 0.6 shard_map.293
  44.6 1.5 %collective-permute-start.14 = (f32[8,512]{1,0:T(8,128)S(1)}, f32[8,512]{1,0:T(8,128)S(1)}, u32[]{:S(2)}, u32[]{:S(2)}) collective-permute-start(f32[8,512]{1,0:T(8,128)S(1)} %get-tuple-element.106), channel_id=1, source_target_pairs={{1,0},{3,2},{5,4},{7,6},{9,8},{11,10},{13,12},{15,14},{17,16},{19,... | collective-permute-start | bytes 49160 | tf_op jit(solution)/shard_map/ppermute | solution.py:799
  46.2 0.2 add_convert_fusion
  46.5 1.4 %collective-permute-start.17 = (bf16[256,384]{1,0:T(8,128)(2,1)S(1)}, bf16[256,384]{1,0:T(8,128)(2,1)S(1)}, u32[]{:S(2)}, u32[]{:S(2)}) collective-permute-start(bf16[256,384]{1,0:T(8,128)(2,1)S(1)} %get-tuple-element.146), channel_id=1, source_target_pairs={{0,8},{1,9},{2,10},{3,11},{4,12},{5,13},{6,14},{7,15},{8,0},{9,1},... | collective-permute-start | bytes 589832 | tf_op jit(solution)/shard_map/ppermute | solution.py:30
  47.8 1.1 %collective-permute-start.16 = (bf16[256,384]{1,0:T(8,128)(2,1)S(1)}, bf16[256,384]{1,0:T(8,128)(2,1)S(1)}, u32[]{:S(2)}, u32[]{:S(2)}) collective-permute-start(bf16[256,384]{1,0:T(8,128)(2,1)S(1)} %get-tuple-element.147), channel_id=1, source_target_pairs={{0,4},{1,5},{2,6},{3,7},{4,0},{5,1},{6,2},{7,3},{8,12},{9,13},{10,... | collective-permute-start | bytes 589832 | tf_op jit(solution)/shard_map/ppermute | solution.py:30
  49.0 3.6 %shard_map.294 = (bf16[1024,128]{1,0:T(8,128)(2,1)S(1)}, bf16[1088,128]{1,0:T(8,128)(2,1)S(1)}, f32[1024,512]{1,0:T(8,128)S(1)}) custom-call(s32[1]{0:T(128)} %bitcast.me_ref, bf16[1024,512]{1,0:T(8,128)(2,1)S(1)} %copy-done, f32[2,1024,128]{2,1,0:T(8,128)S(1)} %get-tuple-element.76.stats_ref, bf16[1024,512]{1,0:T(8,128)(2,1)S(1)} %get-tuple-element.81.normed_ref, ...), custom_call_target="tpu_custom_call" | custom-call | flops 4499999744 | bytes 15750000 | tf_op jit(solution)/shard_map/pallas_call | solution.py:629
  52.5 0.6 collective-permute-start.15
  53.2 1.0 %collective-permute-done.17 = bf16[256,384]{1,0:T(8,128)(2,1)S(1)} collective-permute-done((bf16[256,384]{1,0:T(8,128)(2,1)S(1)}, bf16[256,384]{1,0:T(8,128)(2,1)S(1)}, u32[]{:S(2)}, u32[]{:S(2)}) %collective-permute-start.17) | collective-permute-done | bytes 196640 | tf_op jit(solution)/shard_map/ppermute | solution.py:30
  54.1 1.4 %collective-permute-done.16 = bf16[256,384]{1,0:T(8,128)(2,1)S(1)} collective-permute-done((bf16[256,384]{1,0:T(8,128)(2,1)S(1)}, bf16[256,384]{1,0:T(8,128)(2,1)S(1)}, u32[]{:S(2)}, u32[]{:S(2)}) %collective-permute-start.16) | collective-permute-done | bytes 196640 | tf_op jit(solution)/shard_map/ppermute | solution.py:30
  55.6 0.8 collective-permute-start.22
  56.4 1.0 %collective-permute-start.23 = (bf16[128,384]{1,0:T(8,128)(2,1)S(1)}, bf16[128,384]{1,0:T(8,128)(2,1)S(1)}, u32[]{:S(2)}, u32[]{:S(2)}) collective-permute-start(bf16[128,384]{1,0:T(8,128)(2,1)S(1)} %slice.276), channel_id=1, source_target_pairs={{0,4},{1,5},{2,6},{3,7},{4,0},{5,1},{6,2},{7,3},{8,12},{9,13},{10,... | collective-permute-start | bytes 294920 | tf_op jit(solution)/shard_map/ppermute | solution.py:30
  57.6 1.6 %collective-permute-start.18 = (bf16[576,128]{1,0:T(8,128)(2,1)S(1)}, bf16[576,128]{1,0:T(8,128)(2,1)S(1)}, u32[]{:S(2)}, u32[]{:S(2)}) collective-permute-start(bf16[576,128]{1,0:T(8,128)(2,1)S(1)} %pad_maximum_fusion.3), channel_id=1, source_target_pairs={{0,2},{1,3},{2,0},{3,1},{4,6},{5,7},{6,4},{7,5},{8,10},{9,11},{10,... | collective-permute-start | bytes 442376 | tf_op jit(solution)/shard_map/ppermute | solution.py:30
  59.1 2.4 %shard_map.295 = f32[1024,512]{1,0:T(8,128)} custom-call(s32[1]{0:T(128)} %bitcast.me_ref, bf16[1024,512]{1,0:T(8,128)(2,1)S(1)} %copy-done, f32[2,1024,128]{2,1,0:T(8,128)S(1)} %get-tuple-element.76.stats_ref, bf16[1024,512]{1,0:T(8,128)(2,1)S(1)} %copy-done.1, f32[1024,512]{1,0:T(8,128)S(1)} %get-tuple-element.116.normed_grad_ref, ...), custom_call_target="tpu_custom_call" | custom-call | flops 2500000000 | bytes 8750000 | tf_op jit(solution)/shard_map/pallas_call | solution.py:629
  61.5 1.3 %collective-permute-done.18 = bf16[576,128]{1,0:T(8,128)(2,1)S(1)} collective-permute-done((bf16[576,128]{1,0:T(8,128)(2,1)S(1)}, bf16[576,128]{1,0:T(8,128)(2,1)S(1)}, u32[]{:S(2)}, u32[]{:S(2)}) %collective-permute-start.18) | collective-permute-done | bytes 147488 | tf_op jit(solution)/shard_map/ppermute | solution.py:30
  62.9 1.1 %collective-permute-start.19 = (bf16[320,128]{1,0:T(8,128)(2,1)S(1)}, bf16[320,128]{1,0:T(8,128)(2,1)S(1)}, u32[]{:S(2)}, u32[]{:S(2)}) collective-permute-start(bf16[320,128]{1,0:T(8,128)(2,1)S(1)} %pad_maximum_fusion.7), channel_id=1, source_target_pairs={{0,4},{1,5},{2,6},{3,7},{4,0},{5,1},{6,2},{7,3},{8,12},{9,13},{10,... | collective-permute-start | bytes 245768 | tf_op jit(solution)/shard_map/ppermute | solution.py:30
  64.1 1.5 %collective-permute-start.24 = (bf16[128,384]{1,0:T(8,128)(2,1)S(1)}, bf16[128,384]{1,0:T(8,128)(2,1)S(1)}, u32[]{:S(2)}, u32[]{:S(2)}) collective-permute-start(bf16[128,384]{1,0:T(8,128)(2,1)S(1)} %pad_maximum_fusion.6), channel_id=1, source_target_pairs={{0,2},{1,3},{2,0},{3,1},{4,6},{5,7},{6,4},{7,5},{8,10},{9,11},{10,... | collective-permute-start | bytes 294920 | tf_op jit(solution)/shard_map/ppermute | solution.py:30
  65.7 1.7 %collective-permute-done.19 = bf16[320,128]{1,0:T(8,128)(2,1)S(1)} collective-permute-done((bf16[320,128]{1,0:T(8,128)(2,1)S(1)}, bf16[320,128]{1,0:T(8,128)(2,1)S(1)}, u32[]{:S(2)}, u32[]{:S(2)}) %collective-permute-start.19) | collective-permute-done | bytes 81952 | tf_op jit(solution)/shard_map/ppermute | solution.py:30
  67.5 1.5 %collective-permute-start.20 = (bf16[192,128]{1,0:T(8,128)(2,1)S(1)}, bf16[192,128]{1,0:T(8,128)(2,1)S(1)}, u32[]{:S(2)}, u32[]{:S(2)}) collective-permute-start(bf16[192,128]{1,0:T(8,128)(2,1)S(1)} %pad_maximum_fusion.9), channel_id=1, source_target_pairs={{0,8},{1,9},{2,10},{3,11},{4,12},{5,13},{6,14},{7,15},{8,0},{9,1},... | collective-permute-start | bytes 147464 | tf_op jit(solution)/shard_map/ppermute | solution.py:30
  69.1 1.5 %collective-permute-start.25 = (bf16[64,384]{1,0:T(8,128)(2,1)S(1)}, bf16[64,384]{1,0:T(8,128)(2,1)S(1)}, u32[]{:S(2)}, u32[]{:S(2)}) collective-permute-start(bf16[64,384]{1,0:T(8,128)(2,1)S(1)} %bitcast.35), channel_id=1, source_target_pairs={{0,16},{1,17},{2,18},{3,19},{4,20},{5,21},{6,22},{7,23},{8,24},{9,... | collective-permute-start | bytes 147464 | tf_op jit(solution)/shard_map/ppermute | solution.py:30
  70.5 1.1 %collective-permute-done.20 = bf16[192,128]{1,0:T(8,128)(2,1)S(1)} collective-permute-done((bf16[192,128]{1,0:T(8,128)(2,1)S(1)}, bf16[192,128]{1,0:T(8,128)(2,1)S(1)}, u32[]{:S(2)}, u32[]{:S(2)}) %collective-permute-start.20) | collective-permute-done | bytes 49184 | tf_op jit(solution)/shard_map/ppermute | solution.py:30
  71.8 2.2 %collective-permute-start.21 = (bf16[128,128]{1,0:T(8,128)(2,1)S(1)}, bf16[128,128]{1,0:T(8,128)(2,1)S(1)}, u32[]{:S(2)}, u32[]{:S(2)}) collective-permute-start(bf16[128,128]{1,0:T(8,128)(2,1)S(1)} %pad_maximum_fusion.11), channel_id=1, source_target_pairs={{0,16},{1,17},{2,18},{3,19},{4,20},{5,21},{6,22},{7,23},{8,24},{9,... | collective-permute-start | bytes 98312 | tf_op jit(solution)/shard_map/ppermute | solution.py:30
  74.2 2.5 %collective-permute-done.21 = bf16[128,128]{1,0:T(8,128)(2,1)S(1)} collective-permute-done((bf16[128,128]{1,0:T(8,128)(2,1)S(1)}, bf16[128,128]{1,0:T(8,128)(2,1)S(1)}, u32[]{:S(2)}, u32[]{:S(2)}) %collective-permute-start.21) | collective-permute-done | bytes 32800 | tf_op jit(solution)/shard_map/ppermute | solution.py:30
  76.6 1.1 %shard_map.296 = (f32[64,64]{1,0:T(8,128)}, f32[64,64]{1,0:T(8,128)}, f32[64,64]{1,0:T(8,128)}, f32[64,64]{1,0:T(8,128)}, f32[64,128]{1,0:T(8,128)}, /*index=5*/...) custom-call(s32[1]{0:T(128)} %bitcast.me_ref, ...), custom_call_target="tpu_custom_call" | custom-call | flops 2000000000 | bytes 7000000 | tf_op jit(solution)/shard_map/pallas_call | solution.py:629
  (83 shorter events, 1.4 us)
Async XLA Ops:
  0.7 5.3 %copy-start = (bf16[1024,512]{1,0:T(8,128)(2,1)S(1)}, bf16[1024,512]{1,0:T(8,128)(2,1)}, u32[]{:S(2)}) copy-start(bf16[1024,512]{1,0:T(8,128)(2,1)} %x_ref.9) | copy-start | bytes 3145732
  0.7 5.3 %copy-start.2 = (s32[4096]{0:T(1024)S(1)}, s32[4096]{0:T(1024)}, u32[]{:S(2)}) copy-start(s32[4096]{0:T(1024)} %param.18) | copy-start | bytes 49156
  1.8 5.9 %collective-permute-start = (bf16[96,128]{1,0:T(8,128)(2,1)S(1)}, bf16[96,128]{1,0:T(8,128)(2,1)S(1)}, u32[]{:S(2)}, u32[]{:S(2)}) collective-permute-start(bf16[96,128]{1,0:T(8,128)(2,1)S(1)} %get-tuple-element.77), channel_id=1, source_target_pairs={{0,16},{1,17},{2,18},{3,19},{4,20},{5,21},{6,22},{7,23},{8,24},{9,... | collective-permute-start | bytes 73736 | tf_op jit(solution)/shard_map/ppermute | solution.py:30
  5.9 5.1 %collective-permute-start.1 = (bf16[64,384]{1,0:T(8,128)(2,1)S(1)}, bf16[64,384]{1,0:T(8,128)(2,1)S(1)}, u32[]{:S(2)}, u32[]{:S(2)}) collective-permute-start(bf16[64,384]{1,0:T(8,128)(2,1)S(1)} %get-tuple-element.79), channel_id=1, source_target_pairs={{0,16},{1,17},{2,18},{3,19},{4,20},{5,21},{6,22},{7,23},{8,24},{9,... | collective-permute-start | bytes 147464 | tf_op jit(solution)/shard_map/ppermute | solution.py:30
  11.0 4.1 %collective-permute-start.2 = (bf16[160,128]{1,0:T(8,128)(2,1)S(1)}, bf16[160,128]{1,0:T(8,128)(2,1)S(1)}, u32[]{:S(2)}, u32[]{:S(2)}) collective-permute-start(bf16[160,128]{1,0:T(8,128)(2,1)S(1)} %pad_maximum_fusion.10), channel_id=1, source_target_pairs={{0,8},{1,9},{2,10},{3,11},{4,12},{5,13},{6,14},{7,15},{8,0},{9,1},... | collective-permute-start | bytes 122888 | tf_op jit(solution)/shard_map/ppermute | solution.py:30
  12.6 4.7 %collective-permute-start.7 = (bf16[128,384]{1,0:T(8,128)(2,1)S(1)}, bf16[128,384]{1,0:T(8,128)(2,1)S(1)}, u32[]{:S(2)}, u32[]{:S(2)}) collective-permute-start(bf16[128,384]{1,0:T(8,128)(2,1)S(1)} %pad_maximum_fusion.5), channel_id=1, source_target_pairs={{0,2},{1,3},{2,0},{3,1},{4,6},{5,7},{6,4},{7,5},{8,10},{9,11},{10,... | collective-permute-start | bytes 294920 | tf_op jit(solution)/shard_map/ppermute | solution.py:30
  15.1 4.4 %collective-permute-start.3 = (bf16[288,128]{1,0:T(8,128)(2,1)S(1)}, bf16[288,128]{1,0:T(8,128)(2,1)S(1)}, u32[]{:S(2)}, u32[]{:S(2)}) collective-permute-start(bf16[288,128]{1,0:T(8,128)(2,1)S(1)} %pad_maximum_fusion.8), channel_id=1, source_target_pairs={{0,4},{1,5},{2,6},{3,7},{4,0},{5,1},{6,2},{7,3},{8,12},{9,13},{10,... | collective-permute-start | bytes 221192 | tf_op jit(solution)/shard_map/ppermute | solution.py:30
  17.3 4.7 %collective-permute-start.10 = (bf16[128,384]{1,0:T(8,128)(2,1)S(1)}, bf16[128,384]{1,0:T(8,128)(2,1)S(1)}, u32[]{:S(2)}, u32[]{:S(2)}) collective-permute-start(bf16[128,384]{1,0:T(8,128)(2,1)S(1)} %bitcast.27), channel_id=1, source_target_pairs={{0,4},{1,5},{2,6},{3,7},{4,0},{5,1},{6,2},{7,3},{8,12},{9,13},{10,... | collective-permute-start | bytes 294920 | tf_op jit(solution)/shard_map/ppermute | solution.py:30
  18.9 4.8 %collective-permute-start.8 = (bf16[128,384]{1,0:T(8,128)(2,1)S(1)}, bf16[128,384]{1,0:T(8,128)(2,1)S(1)}, u32[]{:S(2)}, u32[]{:S(2)}) collective-permute-start(bf16[128,384]{1,0:T(8,128)(2,1)S(1)} %bitcast.30), channel_id=1, source_target_pairs={{0,8},{1,9},{2,10},{3,11},{4,12},{5,13},{6,14},{7,15},{8,0},{9,1},... | collective-permute-start | bytes 294920 | tf_op jit(solution)/shard_map/ppermute | solution.py:30
  19.6 5.6 %collective-permute-start.4 = (bf16[512,128]{1,0:T(8,128)(2,1)S(1)}, bf16[512,128]{1,0:T(8,128)(2,1)S(1)}, u32[]{:S(2)}, u32[]{:S(2)}) collective-permute-start(bf16[512,128]{1,0:T(8,128)(2,1)S(1)} %pad_maximum_fusion.4), channel_id=1, source_target_pairs={{0,2},{1,3},{2,0},{3,1},{4,6},{5,7},{6,4},{7,5},{8,10},{9,11},{10,... | collective-permute-start | bytes 393224 | tf_op jit(solution)/shard_map/ppermute | solution.py:30
  22.0 9.2 %collective-permute-start.11 = (bf16[256,384]{1,0:T(8,128)(2,1)S(1)}, bf16[256,384]{1,0:T(8,128)(2,1)S(1)}, u32[]{:S(2)}, u32[]{:S(2)}) collective-permute-start(bf16[256,384]{1,0:T(8,128)(2,1)S(1)} %pad_maximum_fusion.2), channel_id=1, source_target_pairs={{0,8},{1,9},{2,10},{3,11},{4,12},{5,13},{6,14},{7,15},{8,0},{9,1},... | collective-permute-start | bytes 589832 | tf_op jit(solution)/shard_map/ppermute | solution.py:30
  23.7 7.6 %collective-permute-start.9 = (bf16[256,384]{1,0:T(8,128)(2,1)S(1)}, bf16[256,384]{1,0:T(8,128)(2,1)S(1)}, u32[]{:S(2)}, u32[]{:S(2)}) collective-permute-start(bf16[256,384]{1,0:T(8,128)(2,1)S(1)} %pad_maximum_fusion.1), channel_id=1, source_target_pairs={{0,4},{1,5},{2,6},{3,7},{4,0},{5,1},{6,2},{7,3},{8,12},{9,13},{10,... | collective-permute-start | bytes 589832 | tf_op jit(solution)/shard_map/ppermute | solution.py:30
  25.2 1.6 %collective-permute-start.5 = (bf16[1024,128]{1,0:T(8,128)(2,1)S(1)}, bf16[1024,128]{1,0:T(8,128)(2,1)S(1)}, u32[]{:S(2)}, u32[]{:S(2)}) collective-permute-start(bf16[1024,128]{1,0:T(8,128)(2,1)S(1)} %constant_dynamic-update-slice_fusion.b0_ref), channel_id=1, source_target_pairs={{0,1},{1,0},{2,3},{3,2},{4,5},{5,4},{6,7},{7,6},{8,9},{9,8},{10,11... | collective-permute-start | bytes 786440 | tf_op jit(solution)/shard_map/ppermute | solution.py:30
  26.8 7.4 %copy-start.1 = (bf16[1024,512]{1,0:T(8,128)(2,1)S(1)}, bf16[1024,512]{1,0:T(8,128)(2,1)}, u32[]{:S(2)}) copy-start(bf16[1024,512]{1,0:T(8,128)(2,1)} %grad_ref.3) | copy-start | bytes 3145732
  29.0 2.9 %collective-permute-start.6 = (f32[8,512]{1,0:T(8,128)S(1)}, f32[8,512]{1,0:T(8,128)S(1)}, u32[]{:S(2)}, u32[]{:S(2)}) collective-permute-start(f32[8,512]{1,0:T(8,128)S(1)} %get-tuple-element.85), channel_id=1, source_target_pairs={{0,1},{2,3},{4,5},{6,7},{8,9},{10,11},{12,13},{14,15},{16,17},{18,... | collective-permute-start | bytes 49160 | tf_op jit(solution)/shard_map/ppermute | solution.py:799
  31.9 2.3 %collective-permute-start.12 = (bf16[1024,384]{1,0:T(8,128)(2,1)S(1)}, bf16[1024,384]{1,0:T(8,128)(2,1)S(1)}, u32[]{:S(2)}, u32[]{:S(2)}) collective-permute-start(bf16[1024,384]{1,0:T(8,128)(2,1)S(1)} %constant_dynamic-update-slice_fusion.5.g0_ref), channel_id=1, source_target_pairs={{0,1},{1,0},{2,3},{3,2},{4,5},{5,4},{6,7},{7,6},{8,9},{9,8},{10,11... | collective-permute-start | bytes 2359304 | tf_op jit(solution)/shard_map/ppermute | solution.py:30
  43.6 2.6 %collective-permute-start.13 = (bf16[1024,384]{1,0:T(8,128)(2,1)S(1)}, bf16[1024,384]{1,0:T(8,128)(2,1)S(1)}, u32[]{:S(2)}, u32[]{:S(2)}) collective-permute-start(bf16[1024,384]{1,0:T(8,128)(2,1)S(1)} %get-tuple-element.99), channel_id=1, source_target_pairs={{0,1},{1,0},{2,3},{3,2},{4,5},{5,4},{6,7},{7,6},{8,9},{9,8},{10,11... | collective-permute-start | bytes 2359304 | tf_op jit(solution)/shard_map/ppermute | solution.py:30
  44.6 4.3 %collective-permute-start.14 = (f32[8,512]{1,0:T(8,128)S(1)}, f32[8,512]{1,0:T(8,128)S(1)}, u32[]{:S(2)}, u32[]{:S(2)}) collective-permute-start(f32[8,512]{1,0:T(8,128)S(1)} %get-tuple-element.106), channel_id=1, source_target_pairs={{1,0},{3,2},{5,4},{7,6},{9,8},{11,10},{13,12},{15,14},{17,16},{19,... | collective-permute-start | bytes 49160 | tf_op jit(solution)/shard_map/ppermute | solution.py:799
  46.5 7.7 %collective-permute-start.17 = (bf16[256,384]{1,0:T(8,128)(2,1)S(1)}, bf16[256,384]{1,0:T(8,128)(2,1)S(1)}, u32[]{:S(2)}, u32[]{:S(2)}) collective-permute-start(bf16[256,384]{1,0:T(8,128)(2,1)S(1)} %get-tuple-element.146), channel_id=1, source_target_pairs={{0,8},{1,9},{2,10},{3,11},{4,12},{5,13},{6,14},{7,15},{8,0},{9,1},... | collective-permute-start | bytes 589832 | tf_op jit(solution)/shard_map/ppermute | solution.py:30
  47.8 7.6 %collective-permute-start.16 = (bf16[256,384]{1,0:T(8,128)(2,1)S(1)}, bf16[256,384]{1,0:T(8,128)(2,1)S(1)}, u32[]{:S(2)}, u32[]{:S(2)}) collective-permute-start(bf16[256,384]{1,0:T(8,128)(2,1)S(1)} %get-tuple-element.147), channel_id=1, source_target_pairs={{0,4},{1,5},{2,6},{3,7},{4,0},{5,1},{6,2},{7,3},{8,12},{9,13},{10,... | collective-permute-start | bytes 589832 | tf_op jit(solution)/shard_map/ppermute | solution.py:30
  52.5 4.9 %collective-permute-start.15 = (bf16[1088,128]{1,0:T(8,128)(2,1)S(1)}, bf16[1088,128]{1,0:T(8,128)(2,1)S(1)}, u32[]{:S(2)}, u32[]{:S(2)}) collective-permute-start(bf16[1088,128]{1,0:T(8,128)(2,1)S(1)} %get-tuple-element.112), channel_id=1, source_target_pairs={{0,1},{1,0},{2,3},{3,2},{4,5},{5,4},{6,7},{7,6},{8,9},{9,8},{10,11... | collective-permute-start | bytes 835592 | tf_op jit(solution)/shard_map/ppermute | solution.py:30
  55.6 8.4 %collective-permute-start.22 = (bf16[128,384]{1,0:T(8,128)(2,1)S(1)}, bf16[128,384]{1,0:T(8,128)(2,1)S(1)}, u32[]{:S(2)}, u32[]{:S(2)}) collective-permute-start(bf16[128,384]{1,0:T(8,128)(2,1)S(1)} %slice.274), channel_id=1, source_target_pairs={{0,8},{1,9},{2,10},{3,11},{4,12},{5,13},{6,14},{7,15},{8,0},{9,1},... | collective-permute-start | bytes 294920 | tf_op jit(solution)/shard_map/ppermute | solution.py:30
  56.4 7.6 %collective-permute-start.23 = (bf16[128,384]{1,0:T(8,128)(2,1)S(1)}, bf16[128,384]{1,0:T(8,128)(2,1)S(1)}, u32[]{:S(2)}, u32[]{:S(2)}) collective-permute-start(bf16[128,384]{1,0:T(8,128)(2,1)S(1)} %slice.276), channel_id=1, source_target_pairs={{0,4},{1,5},{2,6},{3,7},{4,0},{5,1},{6,2},{7,3},{8,12},{9,13},{10,... | collective-permute-start | bytes 294920 | tf_op jit(solution)/shard_map/ppermute | solution.py:30
  57.6 5.2 %collective-permute-start.18 = (bf16[576,128]{1,0:T(8,128)(2,1)S(1)}, bf16[576,128]{1,0:T(8,128)(2,1)S(1)}, u32[]{:S(2)}, u32[]{:S(2)}) collective-permute-start(bf16[576,128]{1,0:T(8,128)(2,1)S(1)} %pad_maximum_fusion.3), channel_id=1, source_target_pairs={{0,2},{1,3},{2,0},{3,1},{4,6},{5,7},{6,4},{7,5},{8,10},{9,11},{10,... | collective-permute-start | bytes 442376 | tf_op jit(solution)/shard_map/ppermute | solution.py:30
  62.9 4.5 %collective-permute-start.19 = (bf16[320,128]{1,0:T(8,128)(2,1)S(1)}, bf16[320,128]{1,0:T(8,128)(2,1)S(1)}, u32[]{:S(2)}, u32[]{:S(2)}) collective-permute-start(bf16[320,128]{1,0:T(8,128)(2,1)S(1)} %pad_maximum_fusion.7), channel_id=1, source_target_pairs={{0,4},{1,5},{2,6},{3,7},{4,0},{5,1},{6,2},{7,3},{8,12},{9,13},{10,... | collective-permute-start | bytes 245768 | tf_op jit(solution)/shard_map/ppermute | solution.py:30
  64.1 4.9 %collective-permute-start.24 = (bf16[128,384]{1,0:T(8,128)(2,1)S(1)}, bf16[128,384]{1,0:T(8,128)(2,1)S(1)}, u32[]{:S(2)}, u32[]{:S(2)}) collective-permute-start(bf16[128,384]{1,0:T(8,128)(2,1)S(1)} %pad_maximum_fusion.6), channel_id=1, source_target_pairs={{0,2},{1,3},{2,0},{3,1},{4,6},{5,7},{6,4},{7,5},{8,10},{9,11},{10,... | collective-permute-start | bytes 294920 | tf_op jit(solution)/shard_map/ppermute | solution.py:30
  67.5 4.2 %collective-permute-start.20 = (bf16[192,128]{1,0:T(8,128)(2,1)S(1)}, bf16[192,128]{1,0:T(8,128)(2,1)S(1)}, u32[]{:S(2)}, u32[]{:S(2)}) collective-permute-start(bf16[192,128]{1,0:T(8,128)(2,1)S(1)} %pad_maximum_fusion.9), channel_id=1, source_target_pairs={{0,8},{1,9},{2,10},{3,11},{4,12},{5,13},{6,14},{7,15},{8,0},{9,1},... | collective-permute-start | bytes 147464 | tf_op jit(solution)/shard_map/ppermute | solution.py:30
  69.1 5.1 %collective-permute-start.25 = (bf16[64,384]{1,0:T(8,128)(2,1)S(1)}, bf16[64,384]{1,0:T(8,128)(2,1)S(1)}, u32[]{:S(2)}, u32[]{:S(2)}) collective-permute-start(bf16[64,384]{1,0:T(8,128)(2,1)S(1)} %bitcast.35), channel_id=1, source_target_pairs={{0,16},{1,17},{2,18},{3,19},{4,20},{5,21},{6,22},{7,23},{8,24},{9,... | collective-permute-start | bytes 147464 | tf_op jit(solution)/shard_map/ppermute | solution.py:30
  71.8 4.9 %collective-permute-start.21 = (bf16[128,128]{1,0:T(8,128)(2,1)S(1)}, bf16[128,128]{1,0:T(8,128)(2,1)S(1)}, u32[]{:S(2)}, u32[]{:S(2)}) collective-permute-start(bf16[128,128]{1,0:T(8,128)(2,1)S(1)} %pad_maximum_fusion.11), channel_id=1, source_target_pairs={{0,16},{1,17},{2,18},{3,19},{4,20},{5,21},{6,22},{7,23},{8,24},{9,... | collective-permute-start | bytes 98312 | tf_op jit(solution)/shard_map/ppermute | solution.py:30

commit v5 on v4

--- a/solution.py
+++ b/solution.py
@@ -313,6 +313,11 @@
     return jnp.concatenate(parts, axis=1)
 
 
+def received(carry_ref, wanted, states):
+    value = jnp.where(wanted, carry_ref[0:1, :], 0.0)
+    return value[:, :states], value[:, states:]
+
+
 def enter_kernel(
     plan, me_ref, x_ref, stats_ref, b0_ref, b1_ref, vec_ref, masks_ref,
     normed_ref, source_ref, ends_ref, hold_ref, carry_ref, input_map_ref, params_ref,
@@ -384,7 +389,7 @@
     regroup = regroup_matrix(states, plan.tensor)
     out_map_ref[...] = (dot(pack_ref[...].astype(BF16), regroup) * sign).astype(BF16)
     rate = (params_ref[0:1, :states], params_ref[0:1, states:])
-    start = (carry_ref[0:1, :states], carry_ref[0:1, states:])
+    start = received(carry_ref, me_ref[0] & 1 == 1, states)
     entries, _ = chunk_entries(
         plan, ends_ref[:, :states], ends_ref[:, states:], hold_ref[...], rate, start, False
     )
@@ -491,7 +496,7 @@
     modulus, rest = params[2:3, :states], params[2:3, states:]
     rotation = params[3:4, :states]
     back_rate = (rate[0], -rate[1])
-    start = (carry_ref[0:1, :states], carry_ref[0:1, states:])
+    start = received(carry_ref, me_ref[0] & 1 == 0, states)
     entries, _ = chunk_entries(
         plan, ends_ref[:, :states], ends_ref[:, states:], hold_ref[...], back_rate, start, True
     )
@@ -792,16 +797,10 @@
         me, block_input, stats, b0, b1, vectors, masks,
     )
 
-    def pass_on(value, forward):
-        pairs = []
-        for one in range(0, plan.tensor, 2):
-            pairs.append((one, one + 1) if forward else (one + 1, one))
-        return lax.ppermute(value, "tensor", pairs)
-
     left = carry
-    carry = pass_on(carry, True) if plan.pieces == 2 else jnp.zeros_like(carry)
+    carry = flip(carry, 0, plan.count) if plan.pieces == 2 else jnp.zeros_like(carry)
     g0 = joined(*(joined(part, after(got, left)) for part, got in halves))
-    g1 = flip(after(g0, carry), 0, plan.count)
+    g1 = flip(g0, 0, plan.count)
     (
         mixed, hidden, lru_grad, state_grad, act, unit_grad, low, sums,
     ) = call(
@@ -849,7 +848,7 @@
         1,
         me, after(state_grad, w_send), params, masks,
     )
-    back = pass_on(back, False) if plan.pieces == 2 else jnp.zeros_like(back)
+    back = flip(back, 0, plan.count) if plan.pieces == 2 else jnp.zeros_like(back)
     pieces = plan.halves
     w_total = added(w_keep, after(w_other, back_ends))
     size = w_total.shape[0] // pieces

time: 78.1 us -> 75.1 us (0.962)
  starting transfers between devices: 34.5 us -> 30.6 us
    ppermute x2 -> x0, starting transfers between devices: 3.73 us -> none  [pass_on(): return lax.ppermute(value, 'tensor', pairs)]
    ppermute x24 -> x26, waiting for transfers between devices: 19 us -> 20 us  [flip(): return lax.ppermute(value, AXES, [(i, i ^ 1 << bit) for i in range(count)])]
    ppermute x24 -> x26, starting transfers between devices: 30.7 us -> 30.6 us  [flip(): return lax.ppermute(value, AXES, [(i, i ^ 1 << bit) for i in range(count)])]
  transfers between devices with their start and end apart: 26 -> 26, of which waited for: 16 -> 17; matrix products, arithmetic and copies ran while one was open for 1% -> 1% of each run, Pallas kernels for 13% -> 14%
where the time goes in v5:
time: 75.1 us; the launch traced here: 74.9 us
  starting transfers between devices  30.6 us (41%)
  Pallas kernels  21.9 us (29%)
  waiting for transfers between devices  20 us (27%)
  between operations  1.29 us (2%)
  other arithmetic  0.83 us (1%)
    ppermute x26, starting transfers between devices, flip(): return lax.ppermute(value, AXES, [(i, i ^ 1 << bit) for i in range(count)])  30.6 us
    pallas_call x9, Pallas kernels, call(): pl.pallas_call(functools.partial(kernel, plan), out_shape=outs, in_specs=...  21.9 us
    ppermute x26, waiting for transfers between devices, flip(): return lax.ppermute(value, AXES, [(i, i ^ 1 << bit) for i in range(count)])  20 us
  transfers between devices with their start and end apart: 26, of which 17 were waited for; matrix products, arithmetic and copies ran while one was open for 1% of the time, Pallas kernels for 14%

profile of v5, /device:TPU:0, one launch (start us, length us, event | category | flops | bytes accessed | tf_op | source)
XLA Modules:
  0.0 74.9 jit_solution(15908730518463409115)
XLA Ops:
  0.7 1.1 %shard_map.289 = (bf16[96,128]{1,0:T(8,128)(2,1)S(1)}, bf16[64,384]{1,0:T(8,128)(2,1)S(1)}) custom-call(s32[1]{0:T(128)} %bitcast.me_ref, bf16[64,64]{1,0:T(8,128)(2,1)} %refs_0_.1, bf16[64,64]{1,0:T(8,128)(2,1)} %refs_1_.1, bf16[64,64]{1,0:T(8,128)(2,1)} %refs_2_.1, bf16[64,64]{1,0:T(8,128)(2,1)} %refs_3_.1, bf16[64,128]{1,0:T(8,128)(2,1)} %refs_4_.1, ...), custom_call_target="tpu_custom_call" | custom-call | flops 1500000000 | bytes 5250000 | tf_op jit(solution)/shard_map/pallas_call | solution.py:634
  1.8 4.1 %collective-permute-start = (bf16[96,128]{1,0:T(8,128)(2,1)S(1)}, bf16[96,128]{1,0:T(8,128)(2,1)S(1)}, u32[]{:S(2)}, u32[]{:S(2)}) collective-permute-start(bf16[96,128]{1,0:T(8,128)(2,1)S(1)} %get-tuple-element.76), channel_id=1, source_target_pairs={{0,16},{1,17},{2,18},{3,19},{4,20},{5,21},{6,22},{7,23},{8,24},{9,... | collective-permute-start | bytes 73736 | tf_op jit(solution)/shard_map/ppermute | solution.py:30
  6.0 1.1 %shard_map.288 = (f32[2,1024,128]{2,1,0:T(8,128)S(1)}, f32[4,1024,128]{2,1,0:T(8,128)S(1)}) custom-call(s32[1]{0:T(128)} %bitcast.me_ref, bf16[1024,512]{1,0:T(8,128)(2,1)S(1)} %copy-done, s32[32,128]{1,0:T(8,128)S(1)} %bitcast.26), custom_call_target="tpu_custom_call" | custom-call | flops 2000000000 | bytes 7000000 | tf_op jit(solution)/shard_map/pallas_call | solution.py:634
  7.1 0.7 collective-permute-done
  7.7 3.3 %collective-permute-done.1 = bf16[64,384]{1,0:T(8,128)(2,1)S(1)} collective-permute-done((bf16[64,384]{1,0:T(8,128)(2,1)S(1)}, bf16[64,384]{1,0:T(8,128)(2,1)S(1)}, u32[]{:S(2)}, u32[]{:S(2)}) %collective-permute-start.1) | collective-permute-done | bytes 49184 | tf_op jit(solution)/shard_map/ppermute | solution.py:30
  11.0 1.5 %collective-permute-start.2 = (bf16[160,128]{1,0:T(8,128)(2,1)S(1)}, bf16[160,128]{1,0:T(8,128)(2,1)S(1)}, u32[]{:S(2)}, u32[]{:S(2)}) collective-permute-start(bf16[160,128]{1,0:T(8,128)(2,1)S(1)} %pad_maximum_fusion.10), channel_id=1, source_target_pairs={{0,8},{1,9},{2,10},{3,11},{4,12},{5,13},{6,14},{7,15},{8,0},{9,1},... | collective-permute-start | bytes 122888 | tf_op jit(solution)/shard_map/ppermute | solution.py:30
  12.6 1.6 %collective-permute-start.7 = (bf16[128,384]{1,0:T(8,128)(2,1)S(1)}, bf16[128,384]{1,0:T(8,128)(2,1)S(1)}, u32[]{:S(2)}, u32[]{:S(2)}) collective-permute-start(bf16[128,384]{1,0:T(8,128)(2,1)S(1)} %pad_maximum_fusion.5), channel_id=1, source_target_pairs={{0,2},{1,3},{2,0},{3,1},{4,6},{5,7},{6,4},{7,5},{8,10},{9,11},{10,... | collective-permute-start | bytes 294920 | tf_op jit(solution)/shard_map/ppermute | solution.py:30
  14.1 1.0 %collective-permute-done.2 = bf16[160,128]{1,0:T(8,128)(2,1)S(1)} collective-permute-done((bf16[160,128]{1,0:T(8,128)(2,1)S(1)}, bf16[160,128]{1,0:T(8,128)(2,1)S(1)}, u32[]{:S(2)}, u32[]{:S(2)}) %collective-permute-start.2) | collective-permute-done | bytes 40992 | tf_op jit(solution)/shard_map/ppermute | solution.py:30
  15.1 1.6 %collective-permute-start.3 = (bf16[288,128]{1,0:T(8,128)(2,1)S(1)}, bf16[288,128]{1,0:T(8,128)(2,1)S(1)}, u32[]{:S(2)}, u32[]{:S(2)}) collective-permute-start(bf16[288,128]{1,0:T(8,128)(2,1)S(1)} %pad_maximum_fusion.8), channel_id=1, source_target_pairs={{0,4},{1,5},{2,6},{3,7},{4,0},{5,1},{6,2},{7,3},{8,12},{9,13},{10,... | collective-permute-start | bytes 221192 | tf_op jit(solution)/shard_map/ppermute | solution.py:30
  16.7 0.5 collective-permute-done.7
  17.3 1.6 %collective-permute-start.10 = (bf16[128,384]{1,0:T(8,128)(2,1)S(1)}, bf16[128,384]{1,0:T(8,128)(2,1)S(1)}, u32[]{:S(2)}, u32[]{:S(2)}) collective-permute-start(bf16[128,384]{1,0:T(8,128)(2,1)S(1)} %bitcast.27), channel_id=1, source_target_pairs={{0,4},{1,5},{2,6},{3,7},{4,0},{5,1},{6,2},{7,3},{8,12},{9,13},{10,... | collective-permute-start | bytes 294920 | tf_op jit(solution)/shard_map/ppermute | solution.py:30
  18.9 0.6 collective-permute-start.8
  19.6 1.6 %collective-permute-start.4 = (bf16[512,128]{1,0:T(8,128)(2,1)S(1)}, bf16[512,128]{1,0:T(8,128)(2,1)S(1)}, u32[]{:S(2)}, u32[]{:S(2)}) collective-permute-start(bf16[512,128]{1,0:T(8,128)(2,1)S(1)} %pad_maximum_fusion.4), channel_id=1, source_target_pairs={{0,2},{1,3},{2,0},{3,1},{4,6},{5,7},{6,4},{7,5},{8,10},{9,11},{10,... | collective-permute-start | bytes 393224 | tf_op jit(solution)/shard_map/ppermute | solution.py:30
  21.2 0.8 %collective-permute-done.10 = bf16[128,384]{1,0:T(8,128)(2,1)S(1)} collective-permute-done((bf16[128,384]{1,0:T(8,128)(2,1)S(1)}, bf16[128,384]{1,0:T(8,128)(2,1)S(1)}, u32[]{:S(2)}, u32[]{:S(2)}) %collective-permute-start.10) | collective-permute-done | bytes 98336 | tf_op jit(solution)/shard_map/ppermute | solution.py:30
  22.0 1.6 %collective-permute-start.11 = (bf16[256,384]{1,0:T(8,128)(2,1)S(1)}, bf16[256,384]{1,0:T(8,128)(2,1)S(1)}, u32[]{:S(2)}, u32[]{:S(2)}) collective-permute-start(bf16[256,384]{1,0:T(8,128)(2,1)S(1)} %pad_maximum_fusion.2), channel_id=1, source_target_pairs={{0,8},{1,9},{2,10},{3,11},{4,12},{5,13},{6,14},{7,15},{8,0},{9,1},... | collective-permute-start | bytes 589832 | tf_op jit(solution)/shard_map/ppermute | solution.py:30
  23.7 1.5 %collective-permute-start.9 = (bf16[256,384]{1,0:T(8,128)(2,1)S(1)}, bf16[256,384]{1,0:T(8,128)(2,1)S(1)}, u32[]{:S(2)}, u32[]{:S(2)}) collective-permute-start(bf16[256,384]{1,0:T(8,128)(2,1)S(1)} %pad_maximum_fusion.1), channel_id=1, source_target_pairs={{0,4},{1,5},{2,6},{3,7},{4,0},{5,1},{6,2},{7,3},{8,12},{9,13},{10,... | collective-permute-start | bytes 589832 | tf_op jit(solution)/shard_map/ppermute | solution.py:30
  25.3 1.5 %collective-permute-done.5.b1_ref = bf16[1024,128]{1,0:T(8,128)(2,1)S(1)} collective-permute-done((bf16[1024,128]{1,0:T(8,128)(2,1)S(1)}, bf16[1024,128]{1,0:T(8,128)(2,1)S(1)}, u32[]{:S(2)}, u32[]{:S(2)}) %collective-permute-start.5) | collective-permute-done | bytes 262176 | tf_op jit(solution)/shard_map/ppermute | solution.py:30
  26.8 2.4 %shard_map.290 = (bf16[1024,512]{1,0:T(8,128)(2,1)S(1)}, f32[1024,512]{1,0:T(8,128)S(1)}, f32[64,512]{1,0:T(8,128)S(1)}, f32[64,128]{1,0:T(8,128)S(1)}, f32[8,51...) custom-call(s32[1]{0:T(128)} %bitcast.me_ref, bf16[1024,512]{1,0:T(8,128)(2,1)S(1)} %copy-done, ...), custom_call_target="tpu_custom_call" | custom-call | flops 300000000 | bytes 1050000 | tf_op jit(solution)/shard_map/pallas_call | solution.py:634
  29.2 0.2 collective-permute-done.9
  29.6 0.5 collective-permute-start.6
  30.1 1.8 %collective-permute-done.6.carry_ref = f32[8,512]{1,0:T(8,128)S(1)} collective-permute-done((f32[8,512]{1,0:T(8,128)S(1)}, f32[8,512]{1,0:T(8,128)S(1)}, u32[]{:S(2)}, u32[]{:S(2)}) %collective-permute-start.6) | collective-permute-done | bytes 16416 | tf_op jit(solution)/shard_map/ppermute | solution.py:30
  31.9 6.9 %shard_map.291 = (bf16[1024,512]{1,0:T(8,128)(2,1)}, f32[1024,512]{1,0:T(8,128)S(1)}, bf16[1024,512]{1,0:T(8,128)(2,1)S(1)}, f32[1024,512]{1,0:T(8,128)S(1)}, bf...) custom-call(s32[1]{0:T(128)} %bitcast.me_ref, ...), custom_call_target="tpu_custom_call" | custom-call | flops 10000000000 | bytes 35000000 | tf_op jit(solution)/shard_map/pallas_call | solution.py:634
  38.9 2.5 %shard_map.292 = (bf16[1024,384]{1,0:T(8,128)(2,1)S(1)}, bf16[1024,384]{1,0:T(8,128)(2,1)S(1)}) custom-call(s32[1]{0:T(128)} %bitcast.me_ref, bf16[1024,512]{1,0:T(8,128)(2,1)S(1)} %get-tuple-element.93.act_ref, bf16[1024,1024]{1,0:T(8,128)(2,1)S(1)} %get-tuple-element.94.unit_grad_ref, bf16[1024,512]{1,0:T(8,128)(2,1)S(1)} %get-tuple-element.95.lru_grad_ref, ...), custom_call_target="tpu_custom_call" | custom-call | flops 2500000000 | bytes 8750000 | tf_op jit(solution)/shard_map/pallas_call | solution.py:634
  41.4 0.2 collective-permute-start.13
  41.6 0.6 shard_map.293
  42.2 0.4 collective-permute-start.14
  42.6 1.1 %collective-permute-done.13 = bf16[1024,384]{1,0:T(8,128)(2,1)S(1)} collective-permute-done((bf16[1024,384]{1,0:T(8,128)(2,1)S(1)}, bf16[1024,384]{1,0:T(8,128)(2,1)S(1)}, u32[]{:S(2)}, u32[]{:S(2)}) %collective-permute-start.13) | collective-permute-done | bytes 786464 | tf_op jit(solution)/shard_map/ppermute | solution.py:30
  43.7 0.2 add_convert_fusion
  44.0 1.2 %collective-permute-start.17 = (bf16[256,384]{1,0:T(8,128)(2,1)S(1)}, bf16[256,384]{1,0:T(8,128)(2,1)S(1)}, u32[]{:S(2)}, u32[]{:S(2)}) collective-permute-start(bf16[256,384]{1,0:T(8,128)(2,1)S(1)} %get-tuple-element.144), channel_id=1, source_target_pairs={{0,8},{1,9},{2,10},{3,11},{4,12},{5,13},{6,14},{7,15},{8,0},{9,1},... | collective-permute-start | bytes 589832 | tf_op jit(solution)/shard_map/ppermute | solution.py:30
  45.2 1.6 %collective-permute-start.16 = (bf16[256,384]{1,0:T(8,128)(2,1)S(1)}, bf16[256,384]{1,0:T(8,128)(2,1)S(1)}, u32[]{:S(2)}, u32[]{:S(2)}) collective-permute-start(bf16[256,384]{1,0:T(8,128)(2,1)S(1)} %get-tuple-element.145), channel_id=1, source_target_pairs={{0,4},{1,5},{2,6},{3,7},{4,0},{5,1},{6,2},{7,3},{8,12},{9,13},{10,... | collective-permute-start | bytes 589832 | tf_op jit(solution)/shard_map/ppermute | solution.py:30
  46.8 3.8 %shard_map.294 = (bf16[1024,128]{1,0:T(8,128)(2,1)S(1)}, bf16[1088,128]{1,0:T(8,128)(2,1)S(1)}, f32[1024,512]{1,0:T(8,128)S(1)}) custom-call(s32[1]{0:T(128)} %bitcast.me_ref, bf16[1024,512]{1,0:T(8,128)(2,1)S(1)} %copy-done, f32[2,1024,128]{2,1,0:T(8,128)S(1)} %get-tuple-element.75.stats_ref, bf16[1024,512]{1,0:T(8,128)(2,1)S(1)} %get-tuple-element.80.normed_ref, ...), custom_call_target="tpu_custom_call" | custom-call | flops 4499999744 | bytes 15750000 | tf_op jit(solution)/shard_map/pallas_call | solution.py:634
  50.7 0.3 collective-permute-done.17
  51.0 0.8 %collective-permute-done.16 = bf16[256,384]{1,0:T(8,128)(2,1)S(1)} collective-permute-done((bf16[256,384]{1,0:T(8,128)(2,1)S(1)}, bf16[256,384]{1,0:T(8,128)(2,1)S(1)}, u32[]{:S(2)}, u32[]{:S(2)}) %collective-permute-start.16) | collective-permute-done | bytes 196640 | tf_op jit(solution)/shard_map/ppermute | solution.py:30
  52.0 1.0 %collective-permute-start.22 = (bf16[128,384]{1,0:T(8,128)(2,1)S(1)}, bf16[128,384]{1,0:T(8,128)(2,1)S(1)}, u32[]{:S(2)}, u32[]{:S(2)}) collective-permute-start(bf16[128,384]{1,0:T(8,128)(2,1)S(1)} %slice.274), channel_id=1, source_target_pairs={{0,8},{1,9},{2,10},{3,11},{4,12},{5,13},{6,14},{7,15},{8,0},{9,1},... | collective-permute-start | bytes 294920 | tf_op jit(solution)/shard_map/ppermute | solution.py:30
  53.0 1.4 %collective-permute-start.23 = (bf16[128,384]{1,0:T(8,128)(2,1)S(1)}, bf16[128,384]{1,0:T(8,128)(2,1)S(1)}, u32[]{:S(2)}, u32[]{:S(2)}) collective-permute-start(bf16[128,384]{1,0:T(8,128)(2,1)S(1)} %slice.276), channel_id=1, source_target_pairs={{0,4},{1,5},{2,6},{3,7},{4,0},{5,1},{6,2},{7,3},{8,12},{9,13},{10,... | collective-permute-start | bytes 294920 | tf_op jit(solution)/shard_map/ppermute | solution.py:30
  54.5 1.6 %collective-permute-start.18 = (bf16[576,128]{1,0:T(8,128)(2,1)S(1)}, bf16[576,128]{1,0:T(8,128)(2,1)S(1)}, u32[]{:S(2)}, u32[]{:S(2)}) collective-permute-start(bf16[576,128]{1,0:T(8,128)(2,1)S(1)} %pad_maximum_fusion.3), channel_id=1, source_target_pairs={{0,2},{1,3},{2,0},{3,1},{4,6},{5,7},{6,4},{7,5},{8,10},{9,11},{10,... | collective-permute-start | bytes 442376 | tf_op jit(solution)/shard_map/ppermute | solution.py:30
  56.1 2.4 %shard_map.295 = f32[1024,512]{1,0:T(8,128)} custom-call(s32[1]{0:T(128)} %bitcast.me_ref, bf16[1024,512]{1,0:T(8,128)(2,1)S(1)} %copy-done, f32[2,1024,128]{2,1,0:T(8,128)S(1)} %get-tuple-element.75.stats_ref, bf16[1024,512]{1,0:T(8,128)(2,1)S(1)} %copy-done.1, f32[1024,512]{1,0:T(8,128)S(1)} %get-tuple-element.114.normed_grad_ref, ...), custom_call_target="tpu_custom_call" | custom-call | flops 2500000000 | bytes 8750000 | tf_op jit(solution)/shard_map/pallas_call | solution.py:634
  58.5 1.3 %collective-permute-done.18 = bf16[576,128]{1,0:T(8,128)(2,1)S(1)} collective-permute-done((bf16[576,128]{1,0:T(8,128)(2,1)S(1)}, bf16[576,128]{1,0:T(8,128)(2,1)S(1)}, u32[]{:S(2)}, u32[]{:S(2)}) %collective-permute-start.18) | collective-permute-done | bytes 147488 | tf_op jit(solution)/shard_map/ppermute | solution.py:30
  59.9 0.7 collective-permute-start.19
  60.7 1.6 %collective-permute-start.24 = (bf16[128,384]{1,0:T(8,128)(2,1)S(1)}, bf16[128,384]{1,0:T(8,128)(2,1)S(1)}, u32[]{:S(2)}, u32[]{:S(2)}) collective-permute-start(bf16[128,384]{1,0:T(8,128)(2,1)S(1)} %pad_maximum_fusion.6), channel_id=1, source_target_pairs={{0,2},{1,3},{2,0},{3,1},{4,6},{5,7},{6,4},{7,5},{8,10},{9,11},{10,... | collective-permute-start | bytes 294920 | tf_op jit(solution)/shard_map/ppermute | solution.py:30
  62.3 2.1 %collective-permute-done.19 = bf16[320,128]{1,0:T(8,128)(2,1)S(1)} collective-permute-done((bf16[320,128]{1,0:T(8,128)(2,1)S(1)}, bf16[320,128]{1,0:T(8,128)(2,1)S(1)}, u32[]{:S(2)}, u32[]{:S(2)}) %collective-permute-start.19) | collective-permute-done | bytes 81952 | tf_op jit(solution)/shard_map/ppermute | solution.py:30
  64.4 1.4 %collective-permute-start.20 = (bf16[192,128]{1,0:T(8,128)(2,1)S(1)}, bf16[192,128]{1,0:T(8,128)(2,1)S(1)}, u32[]{:S(2)}, u32[]{:S(2)}) collective-permute-start(bf16[192,128]{1,0:T(8,128)(2,1)S(1)} %pad_maximum_fusion.9), channel_id=1, source_target_pairs={{0,8},{1,9},{2,10},{3,11},{4,12},{5,13},{6,14},{7,15},{8,0},{9,1},... | collective-permute-start | bytes 147464 | tf_op jit(solution)/shard_map/ppermute | solution.py:30
  65.9 1.8 %collective-permute-start.25 = (bf16[64,384]{1,0:T(8,128)(2,1)S(1)}, bf16[64,384]{1,0:T(8,128)(2,1)S(1)}, u32[]{:S(2)}, u32[]{:S(2)}) collective-permute-start(bf16[64,384]{1,0:T(8,128)(2,1)S(1)} %bitcast.35), channel_id=1, source_target_pairs={{0,16},{1,17},{2,18},{3,19},{4,20},{5,21},{6,22},{7,23},{8,24},{9,... | collective-permute-start | bytes 147464 | tf_op jit(solution)/shard_map/ppermute | solution.py:30
  67.7 1.0 %collective-permute-done.20 = bf16[192,128]{1,0:T(8,128)(2,1)S(1)} collective-permute-done((bf16[192,128]{1,0:T(8,128)(2,1)S(1)}, bf16[192,128]{1,0:T(8,128)(2,1)S(1)}, u32[]{:S(2)}, u32[]{:S(2)}) %collective-permute-start.20) | collective-permute-done | bytes 49184 | tf_op jit(solution)/shard_map/ppermute | solution.py:30
  68.8 1.4 %collective-permute-start.21 = (bf16[128,128]{1,0:T(8,128)(2,1)S(1)}, bf16[128,128]{1,0:T(8,128)(2,1)S(1)}, u32[]{:S(2)}, u32[]{:S(2)}) collective-permute-start(bf16[128,128]{1,0:T(8,128)(2,1)S(1)} %pad_maximum_fusion.11), channel_id=1, source_target_pairs={{0,16},{1,17},{2,18},{3,19},{4,20},{5,21},{6,22},{7,23},{8,24},{9,... | collective-permute-start | bytes 98312 | tf_op jit(solution)/shard_map/ppermute | solution.py:30
  70.2 1.3 %collective-permute-done.25 = bf16[64,384]{1,0:T(8,128)(2,1)S(1)} collective-permute-done((bf16[64,384]{1,0:T(8,128)(2,1)S(1)}, bf16[64,384]{1,0:T(8,128)(2,1)S(1)}, u32[]{:S(2)}, u32[]{:S(2)}) %collective-permute-start.25) | collective-permute-done | bytes 49184 | tf_op jit(solution)/shard_map/ppermute | solution.py:30
  71.5 2.1 %collective-permute-done.21 = bf16[128,128]{1,0:T(8,128)(2,1)S(1)} collective-permute-done((bf16[128,128]{1,0:T(8,128)(2,1)S(1)}, bf16[128,128]{1,0:T(8,128)(2,1)S(1)}, u32[]{:S(2)}, u32[]{:S(2)}) %collective-permute-start.21) | collective-permute-done | bytes 32800 | tf_op jit(solution)/shard_map/ppermute | solution.py:30
  73.7 1.1 %shard_map.296 = (f32[64,64]{1,0:T(8,128)}, f32[64,64]{1,0:T(8,128)}, f32[64,64]{1,0:T(8,128)}, f32[64,64]{1,0:T(8,128)}, f32[64,128]{1,0:T(8,128)}, /*index=5*/...) custom-call(s32[1]{0:T(128)} %bitcast.me_ref, ...), custom_call_target="tpu_custom_call" | custom-call | flops 2000000000 | bytes 7000000 | tf_op jit(solution)/shard_map/pallas_call | solution.py:634
  (83 shorter events, 1.4 us)
Async XLA Ops:
  0.7 5.3 %copy-start = (bf16[1024,512]{1,0:T(8,128)(2,1)S(1)}, bf16[1024,512]{1,0:T(8,128)(2,1)}, u32[]{:S(2)}) copy-start(bf16[1024,512]{1,0:T(8,128)(2,1)} %x_ref.9) | copy-start | bytes 3145732
  0.7 5.3 %copy-start.2 = (s32[4096]{0:T(1024)S(1)}, s32[4096]{0:T(1024)}, u32[]{:S(2)}) copy-start(s32[4096]{0:T(1024)} %param.18) | copy-start | bytes 49156
  1.8 5.9 %collective-permute-start = (bf16[96,128]{1,0:T(8,128)(2,1)S(1)}, bf16[96,128]{1,0:T(8,128)(2,1)S(1)}, u32[]{:S(2)}, u32[]{:S(2)}) collective-permute-start(bf16[96,128]{1,0:T(8,128)(2,1)S(1)} %get-tuple-element.76), channel_id=1, source_target_pairs={{0,16},{1,17},{2,18},{3,19},{4,20},{5,21},{6,22},{7,23},{8,24},{9,... | collective-permute-start | bytes 73736 | tf_op jit(solution)/shard_map/ppermute | solution.py:30
  5.9 5.1 %collective-permute-start.1 = (bf16[64,384]{1,0:T(8,128)(2,1)S(1)}, bf16[64,384]{1,0:T(8,128)(2,1)S(1)}, u32[]{:S(2)}, u32[]{:S(2)}) collective-permute-start(bf16[64,384]{1,0:T(8,128)(2,1)S(1)} %get-tuple-element.78), channel_id=1, source_target_pairs={{0,16},{1,17},{2,18},{3,19},{4,20},{5,21},{6,22},{7,23},{8,24},{9,... | collective-permute-start | bytes 147464 | tf_op jit(solution)/shard_map/ppermute | solution.py:30
  11.0 4.1 %collective-permute-start.2 = (bf16[160,128]{1,0:T(8,128)(2,1)S(1)}, bf16[160,128]{1,0:T(8,128)(2,1)S(1)}, u32[]{:S(2)}, u32[]{:S(2)}) collective-permute-start(bf16[160,128]{1,0:T(8,128)(2,1)S(1)} %pad_maximum_fusion.10), channel_id=1, source_target_pairs={{0,8},{1,9},{2,10},{3,11},{4,12},{5,13},{6,14},{7,15},{8,0},{9,1},... | collective-permute-start | bytes 122888 | tf_op jit(solution)/shard_map/ppermute | solution.py:30
  12.6 4.7 %collective-permute-start.7 = (bf16[128,384]{1,0:T(8,128)(2,1)S(1)}, bf16[128,384]{1,0:T(8,128)(2,1)S(1)}, u32[]{:S(2)}, u32[]{:S(2)}) collective-permute-start(bf16[128,384]{1,0:T(8,128)(2,1)S(1)} %pad_maximum_fusion.5), channel_id=1, source_target_pairs={{0,2},{1,3},{2,0},{3,1},{4,6},{5,7},{6,4},{7,5},{8,10},{9,11},{10,... | collective-permute-start | bytes 294920 | tf_op jit(solution)/shard_map/ppermute | solution.py:30
  15.1 4.4 %collective-permute-start.3 = (bf16[288,128]{1,0:T(8,128)(2,1)S(1)}, bf16[288,128]{1,0:T(8,128)(2,1)S(1)}, u32[]{:S(2)}, u32[]{:S(2)}) collective-permute-start(bf16[288,128]{1,0:T(8,128)(2,1)S(1)} %pad_maximum_fusion.8), channel_id=1, source_target_pairs={{0,4},{1,5},{2,6},{3,7},{4,0},{5,1},{6,2},{7,3},{8,12},{9,13},{10,... | collective-permute-start | bytes 221192 | tf_op jit(solution)/shard_map/ppermute | solution.py:30
  17.3 4.7 %collective-permute-start.10 = (bf16[128,384]{1,0:T(8,128)(2,1)S(1)}, bf16[128,384]{1,0:T(8,128)(2,1)S(1)}, u32[]{:S(2)}, u32[]{:S(2)}) collective-permute-start(bf16[128,384]{1,0:T(8,128)(2,1)S(1)} %bitcast.27), channel_id=1, source_target_pairs={{0,4},{1,5},{2,6},{3,7},{4,0},{5,1},{6,2},{7,3},{8,12},{9,13},{10,... | collective-permute-start | bytes 294920 | tf_op jit(solution)/shard_map/ppermute | solution.py:30
  18.9 4.8 %collective-permute-start.8 = (bf16[128,384]{1,0:T(8,128)(2,1)S(1)}, bf16[128,384]{1,0:T(8,128)(2,1)S(1)}, u32[]{:S(2)}, u32[]{:S(2)}) collective-permute-start(bf16[128,384]{1,0:T(8,128)(2,1)S(1)} %bitcast.30), channel_id=1, source_target_pairs={{0,8},{1,9},{2,10},{3,11},{4,12},{5,13},{6,14},{7,15},{8,0},{9,1},... | collective-permute-start | bytes 294920 | tf_op jit(solution)/shard_map/ppermute | solution.py:30
  19.6 5.6 %collective-permute-start.4 = (bf16[512,128]{1,0:T(8,128)(2,1)S(1)}, bf16[512,128]{1,0:T(8,128)(2,1)S(1)}, u32[]{:S(2)}, u32[]{:S(2)}) collective-permute-start(bf16[512,128]{1,0:T(8,128)(2,1)S(1)} %pad_maximum_fusion.4), channel_id=1, source_target_pairs={{0,2},{1,3},{2,0},{3,1},{4,6},{5,7},{6,4},{7,5},{8,10},{9,11},{10,... | collective-permute-start | bytes 393224 | tf_op jit(solution)/shard_map/ppermute | solution.py:30
  22.0 7.2 %collective-permute-start.11 = (bf16[256,384]{1,0:T(8,128)(2,1)S(1)}, bf16[256,384]{1,0:T(8,128)(2,1)S(1)}, u32[]{:S(2)}, u32[]{:S(2)}) collective-permute-start(bf16[256,384]{1,0:T(8,128)(2,1)S(1)} %pad_maximum_fusion.2), channel_id=1, source_target_pairs={{0,8},{1,9},{2,10},{3,11},{4,12},{5,13},{6,14},{7,15},{8,0},{9,1},... | collective-permute-start | bytes 589832 | tf_op jit(solution)/shard_map/ppermute | solution.py:30
  23.7 5.7 %collective-permute-start.9 = (bf16[256,384]{1,0:T(8,128)(2,1)S(1)}, bf16[256,384]{1,0:T(8,128)(2,1)S(1)}, u32[]{:S(2)}, u32[]{:S(2)}) collective-permute-start(bf16[256,384]{1,0:T(8,128)(2,1)S(1)} %pad_maximum_fusion.1), channel_id=1, source_target_pairs={{0,4},{1,5},{2,6},{3,7},{4,0},{5,1},{6,2},{7,3},{8,12},{9,13},{10,... | collective-permute-start | bytes 589832 | tf_op jit(solution)/shard_map/ppermute | solution.py:30
  25.2 1.6 %collective-permute-start.5 = (bf16[1024,128]{1,0:T(8,128)(2,1)S(1)}, bf16[1024,128]{1,0:T(8,128)(2,1)S(1)}, u32[]{:S(2)}, u32[]{:S(2)}) collective-permute-start(bf16[1024,128]{1,0:T(8,128)(2,1)S(1)} %constant_dynamic-update-slice_fusion.b0_ref), channel_id=1, source_target_pairs={{0,1},{1,0},{2,3},{3,2},{4,5},{5,4},{6,7},{7,6},{8,9},{9,8},{10,11... | collective-permute-start | bytes 786440 | tf_op jit(solution)/shard_map/ppermute | solution.py:30
  26.8 5.2 %copy-start.1 = (bf16[1024,512]{1,0:T(8,128)(2,1)S(1)}, bf16[1024,512]{1,0:T(8,128)(2,1)}, u32[]{:S(2)}) copy-start(bf16[1024,512]{1,0:T(8,128)(2,1)} %grad_ref.3) | copy-start | bytes 3145732
  29.6 2.4 %collective-permute-start.12 = (bf16[1024,384]{1,0:T(8,128)(2,1)S(1)}, bf16[1024,384]{1,0:T(8,128)(2,1)S(1)}, u32[]{:S(2)}, u32[]{:S(2)}) collective-permute-start(bf16[1024,384]{1,0:T(8,128)(2,1)S(1)} %constant_dynamic-update-slice_fusion.5.g0_ref), channel_id=1, source_target_pairs={{0,1},{1,0},{2,3},{3,2},{4,5},{5,4},{6,7},{7,6},{8,9},{9,8},{10,11... | collective-permute-start | bytes 2359304 | tf_op jit(solution)/shard_map/ppermute | solution.py:30
  29.6 2.3 %collective-permute-start.6 = (f32[8,512]{1,0:T(8,128)S(1)}, f32[8,512]{1,0:T(8,128)S(1)}, u32[]{:S(2)}, u32[]{:S(2)}) collective-permute-start(f32[8,512]{1,0:T(8,128)S(1)} %get-tuple-element.84), channel_id=1, source_target_pairs={{0,1},{1,0},{2,3},{3,2},{4,5},{5,4},{6,7},{7,6},{8,9},{9,8},{10,11... | collective-permute-start | bytes 49160 | tf_op jit(solution)/shard_map/ppermute | solution.py:30
  41.4 2.4 %collective-permute-start.13 = (bf16[1024,384]{1,0:T(8,128)(2,1)S(1)}, bf16[1024,384]{1,0:T(8,128)(2,1)S(1)}, u32[]{:S(2)}, u32[]{:S(2)}) collective-permute-start(bf16[1024,384]{1,0:T(8,128)(2,1)S(1)} %get-tuple-element.97), channel_id=1, source_target_pairs={{0,1},{1,0},{2,3},{3,2},{4,5},{5,4},{6,7},{7,6},{8,9},{9,8},{10,11... | collective-permute-start | bytes 2359304 | tf_op jit(solution)/shard_map/ppermute | solution.py:30
  42.2 4.6 %collective-permute-start.14 = (f32[8,512]{1,0:T(8,128)S(1)}, f32[8,512]{1,0:T(8,128)S(1)}, u32[]{:S(2)}, u32[]{:S(2)}) collective-permute-start(f32[8,512]{1,0:T(8,128)S(1)} %get-tuple-element.104), channel_id=1, source_target_pairs={{0,1},{1,0},{2,3},{3,2},{4,5},{5,4},{6,7},{7,6},{8,9},{9,8},{10,11... | collective-permute-start | bytes 49160 | tf_op jit(solution)/shard_map/ppermute | solution.py:30
  44.0 7.0 %collective-permute-start.17 = (bf16[256,384]{1,0:T(8,128)(2,1)S(1)}, bf16[256,384]{1,0:T(8,128)(2,1)S(1)}, u32[]{:S(2)}, u32[]{:S(2)}) collective-permute-start(bf16[256,384]{1,0:T(8,128)(2,1)S(1)} %get-tuple-element.144), channel_id=1, source_target_pairs={{0,8},{1,9},{2,10},{3,11},{4,12},{5,13},{6,14},{7,15},{8,0},{9,1},... | collective-permute-start | bytes 589832 | tf_op jit(solution)/shard_map/ppermute | solution.py:30
  45.2 6.7 %collective-permute-start.16 = (bf16[256,384]{1,0:T(8,128)(2,1)S(1)}, bf16[256,384]{1,0:T(8,128)(2,1)S(1)}, u32[]{:S(2)}, u32[]{:S(2)}) collective-permute-start(bf16[256,384]{1,0:T(8,128)(2,1)S(1)} %get-tuple-element.145), channel_id=1, source_target_pairs={{0,4},{1,5},{2,6},{3,7},{4,0},{5,1},{6,2},{7,3},{8,12},{9,13},{10,... | collective-permute-start | bytes 589832 | tf_op jit(solution)/shard_map/ppermute | solution.py:30
  50.6 3.8 %collective-permute-start.15 = (bf16[1088,128]{1,0:T(8,128)(2,1)S(1)}, bf16[1088,128]{1,0:T(8,128)(2,1)S(1)}, u32[]{:S(2)}, u32[]{:S(2)}) collective-permute-start(bf16[1088,128]{1,0:T(8,128)(2,1)S(1)} %get-tuple-element.110), channel_id=1, source_target_pairs={{0,1},{1,0},{2,3},{3,2},{4,5},{5,4},{6,7},{7,6},{8,9},{9,8},{10,11... | collective-permute-start | bytes 835592 | tf_op jit(solution)/shard_map/ppermute | solution.py:30
  52.0 8.6 %collective-permute-start.22 = (bf16[128,384]{1,0:T(8,128)(2,1)S(1)}, bf16[128,384]{1,0:T(8,128)(2,1)S(1)}, u32[]{:S(2)}, u32[]{:S(2)}) collective-permute-start(bf16[128,384]{1,0:T(8,128)(2,1)S(1)} %slice.274), channel_id=1, source_target_pairs={{0,8},{1,9},{2,10},{3,11},{4,12},{5,13},{6,14},{7,15},{8,0},{9,1},... | collective-permute-start | bytes 294920 | tf_op jit(solution)/shard_map/ppermute | solution.py:30
  53.0 7.6 %collective-permute-start.23 = (bf16[128,384]{1,0:T(8,128)(2,1)S(1)}, bf16[128,384]{1,0:T(8,128)(2,1)S(1)}, u32[]{:S(2)}, u32[]{:S(2)}) collective-permute-start(bf16[128,384]{1,0:T(8,128)(2,1)S(1)} %slice.276), channel_id=1, source_target_pairs={{0,4},{1,5},{2,6},{3,7},{4,0},{5,1},{6,2},{7,3},{8,12},{9,13},{10,... | collective-permute-start | bytes 294920 | tf_op jit(solution)/shard_map/ppermute | solution.py:30
  54.5 5.2 %collective-permute-start.18 = (bf16[576,128]{1,0:T(8,128)(2,1)S(1)}, bf16[576,128]{1,0:T(8,128)(2,1)S(1)}, u32[]{:S(2)}, u32[]{:S(2)}) collective-permute-start(bf16[576,128]{1,0:T(8,128)(2,1)S(1)} %pad_maximum_fusion.3), channel_id=1, source_target_pairs={{0,2},{1,3},{2,0},{3,1},{4,6},{5,7},{6,4},{7,5},{8,10},{9,11},{10,... | collective-permute-start | bytes 442376 | tf_op jit(solution)/shard_map/ppermute | solution.py:30
  59.9 4.5 %collective-permute-start.19 = (bf16[320,128]{1,0:T(8,128)(2,1)S(1)}, bf16[320,128]{1,0:T(8,128)(2,1)S(1)}, u32[]{:S(2)}, u32[]{:S(2)}) collective-permute-start(bf16[320,128]{1,0:T(8,128)(2,1)S(1)} %pad_maximum_fusion.7), channel_id=1, source_target_pairs={{0,4},{1,5},{2,6},{3,7},{4,0},{5,1},{6,2},{7,3},{8,12},{9,13},{10,... | collective-permute-start | bytes 245768 | tf_op jit(solution)/shard_map/ppermute | solution.py:30
  60.7 5.2 %collective-permute-start.24 = (bf16[128,384]{1,0:T(8,128)(2,1)S(1)}, bf16[128,384]{1,0:T(8,128)(2,1)S(1)}, u32[]{:S(2)}, u32[]{:S(2)}) collective-permute-start(bf16[128,384]{1,0:T(8,128)(2,1)S(1)} %pad_maximum_fusion.6), channel_id=1, source_target_pairs={{0,2},{1,3},{2,0},{3,1},{4,6},{5,7},{6,4},{7,5},{8,10},{9,11},{10,... | collective-permute-start | bytes 294920 | tf_op jit(solution)/shard_map/ppermute | solution.py:30
  64.4 4.2 %collective-permute-start.20 = (bf16[192,128]{1,0:T(8,128)(2,1)S(1)}, bf16[192,128]{1,0:T(8,128)(2,1)S(1)}, u32[]{:S(2)}, u32[]{:S(2)}) collective-permute-start(bf16[192,128]{1,0:T(8,128)(2,1)S(1)} %pad_maximum_fusion.9), channel_id=1, source_target_pairs={{0,8},{1,9},{2,10},{3,11},{4,12},{5,13},{6,14},{7,15},{8,0},{9,1},... | collective-permute-start | bytes 147464 | tf_op jit(solution)/shard_map/ppermute | solution.py:30
  65.9 5.6 %collective-permute-start.25 = (bf16[64,384]{1,0:T(8,128)(2,1)S(1)}, bf16[64,384]{1,0:T(8,128)(2,1)S(1)}, u32[]{:S(2)}, u32[]{:S(2)}) collective-permute-start(bf16[64,384]{1,0:T(8,128)(2,1)S(1)} %bitcast.35), channel_id=1, source_target_pairs={{0,16},{1,17},{2,18},{3,19},{4,20},{5,21},{6,22},{7,23},{8,24},{9,... | collective-permute-start | bytes 147464 | tf_op jit(solution)/shard_map/ppermute | solution.py:30
  68.8 4.9 %collective-permute-start.21 = (bf16[128,128]{1,0:T(8,128)(2,1)S(1)}, bf16[128,128]{1,0:T(8,128)(2,1)S(1)}, u32[]{:S(2)}, u32[]{:S(2)}) collective-permute-start(bf16[128,128]{1,0:T(8,128)(2,1)S(1)} %pad_maximum_fusion.11), channel_id=1, source_target_pairs={{0,16},{1,17},{2,18},{3,19},{4,20},{5,21},{6,22},{7,23},{8,24},{9,... | collective-permute-start | bytes 98312 | tf_op jit(solution)/shard_map/ppermute | solution.py:30

commit v6 on v5

--- a/solution.py
+++ b/solution.py
@@ -124,7 +124,7 @@
             after.append(state)
         return after, extra
 
-    return lax.fori_loop(0, SIDE, step, (start, extra), unroll=2)
+    return lax.fori_loop(0, SIDE, step, (start, extra), unroll=True)
 
 
 def local_ends(plan, source_ref, keep_ref, rate, reverse):
@@ -561,13 +561,9 @@
         axis=0,
     )
     base = plan.own_rows * plan.count // 2
-    parts = features // LANES
-    for part in range(parts):
+    for part in range(features // LANES):
         piece = vector_sums[:, part * LANES : (part + 1) * LANES]
-        high = piece.astype(BF16)
-        low = (piece - high.astype(F32)).astype(BF16)
-        send_ref[base + 8 * part : base + 8 * part + 8, :] = high
-        send_ref[base + 8 * (parts + part) : base + 8 * (parts + part) + 8, :] = low
+        send_ref[base + 8 * part : base + 8 * part + 8, :] = piece.astype(BF16)
 
 
 def last_kernel(plan, me_ref, *refs):
@@ -576,9 +572,8 @@
     own, units = plan.own_states, plan.units
     b_mine = b_keep[...].astype(F32) + b_other[...].astype(F32)
     w_mine = w_mine_ref[...]
-    half = tail_ref.shape[0] // 4
-    tail = [tail_ref[part * half : part * half + half, :].astype(F32) for part in range(4)]
-    vectors = (tail[0] + tail[1]) + (tail[2] + tail[3])
+    half = tail_ref.shape[0] // 2
+    vectors = tail_ref[:half, :].astype(F32) + tail_ref[half:, :].astype(F32)
     count = half // 8
     vectors = jnp.concatenate([vectors[8 * part : 8 * part + 8] for part in range(count)], axis=1)
     band = me_ref[0] >> log2(plan.tensor)
@@ -692,11 +687,6 @@
     return first, flip(first, 0, count), summed, halves
 
 
-def split_high_low(value):
-    high = lax.reduce_precision(value, 8, 7)
-    return jnp.concatenate([high, value - high], axis=0).astype(BF16)
-
-
 def cut(value):
     count = value.shape[0] // 2
     return value[:count].astype(BF16), value[count:].astype(BF16)
@@ -708,11 +698,9 @@
 
 def summed_step(keep, send, other):
     count = keep.shape[0]
-    rows = (send.shape[0] - count) // 2
-    pairs = [part[count:].astype(F32) for part in (send, other)]
-    summed = sum(pair[:rows] + pair[rows:] for pair in pairs)
+    summed = added(send[count:], other[count:]).astype(BF16)
     keep, send = cut(added(keep, other[:count]))
-    return keep, joined(send, split_high_low(summed))
+    return keep, joined(send, summed)
 
 
 def together(*values):
@@ -860,7 +848,7 @@
         plan,
         [
             shape((half_rows, 2 * own), BF16),
-            shape((half_rows + 2 * vector_rows, 2 * own), BF16),
+            shape((half_rows + vector_rows, 2 * own), BF16),
             shape((rows, features)),
         ],
         [
@@ -879,16 +867,6 @@
     b_keep, b_send = summed_step(b_keep, b_send, b_other)
     b_other = flip(b_send, 1, plan.count)
     w_others = [flip(half[1], bit, plan.count) for half, bit in zip(halves, (3, 2))]
-    (input_grad,) = call(
-        input_kernel,
-        plan,
-        [shape((rows, features))],
-        [],
-        8,
-        2.5,
-        me, block_input, stats, out_grad, after(normed_grad, b_send), vectors,
-    )
-    b_other = after(b_other, input_grad)
     b_keep, b_send = summed_step(b_keep, b_send, b_other)
     halves = [cut(added(half[0], after(other, b_send))) for half, other in zip(halves, w_others)]
     w_keep = joined(*(half[0] for half in halves))
@@ -904,8 +882,17 @@
             size = total.shape[1] // 2
             w_keep = total[:, :size].reshape(-1, block).astype(BF16)
             w_send = total[:, size:].reshape(-1, block).astype(BF16)
+    (input_grad,) = call(
+        input_kernel,
+        plan,
+        [shape((rows, features))],
+        [],
+        8,
+        2.5,
+        me, block_input, stats, out_grad, after(normed_grad, b_send), vectors,
+    )
     w_mine = added(w_keep, w_other)
-    b_other = after(flip(b_send, plan.bits - 1, plan.count), w_mine)
+    b_other = after(flip(b_send, plan.bits - 1, plan.count), w_mine, input_grad)
     b_other, tail = b_other[:long], joined(b_send[long:], b_other[long:])
     small = (
         [(long, own)] * 4 + [(long, units)] * 2 + [(1, long)] * 5 + [(1, short)] * 3

time: 75.1 us -> 72.5 us (0.965)
  waiting for transfers between devices: 20 us -> 18.4 us
  Pallas kernels: 21.9 us -> 20.8 us
    ppermute x26, waiting for transfers between devices: 20 us -> 18.4 us  [flip(): return lax.ppermute(value, AXES, [(i, i ^ 1 << bit) for i in range(count)])]
    pallas_call x9, Pallas kernels: 21.9 us -> 20.8 us  [call(): pl.pallas_call(functools.partial(kernel, plan), out_shape=outs, in_specs=...]
  transfers between devices with their start and end apart: 26 -> 26, of which waited for: 17 -> 18; matrix products, arithmetic and copies ran while one was open for 1% -> 1% of each run, Pallas kernels for 14% -> 13%
where the time goes in v6:
time: 72.5 us; the launch traced here: 72.3 us
  starting transfers between devices  30.8 us (42%)
  Pallas kernels  20.8 us (29%)
  waiting for transfers between devices  18.4 us (25%)
  between operations  1.22 us (2%)
  other arithmetic  0.75 us (1%)
    ppermute x26, starting transfers between devices, flip(): return lax.ppermute(value, AXES, [(i, i ^ 1 << bit) for i in range(count)])  30.8 us
    pallas_call x9, Pallas kernels, call(): pl.pallas_call(functools.partial(kernel, plan), out_shape=outs, in_specs=...  20.8 us
    ppermute x26, waiting for transfers between devices, flip(): return lax.ppermute(value, AXES, [(i, i ^ 1 << bit) for i in range(count)])  18.4 us
  transfers between devices with their start and end apart: 26, of which 18 were waited for; matrix products, arithmetic and copies ran while one was open for 1% of the time, Pallas kernels for 13%

profile of v6, /device:TPU:0, one launch (start us, length us, event | category | flops | bytes accessed | tf_op | source)
XLA Modules:
  0.0 72.3 jit_solution(10073853191207870274)
XLA Ops:
  0.7 1.1 %shard_map.289 = (bf16[96,128]{1,0:T(8,128)(2,1)S(1)}, bf16[64,384]{1,0:T(8,128)(2,1)S(1)}) custom-call(s32[1]{0:T(128)} %bitcast.me_ref, bf16[64,64]{1,0:T(8,128)(2,1)} %refs_0_.1, bf16[64,64]{1,0:T(8,128)(2,1)} %refs_1_.1, bf16[64,64]{1,0:T(8,128)(2,1)} %refs_2_.1, bf16[64,64]{1,0:T(8,128)(2,1)} %refs_3_.1, bf16[64,128]{1,0:T(8,128)(2,1)} %refs_4_.1, ...), custom_call_target="tpu_custom_call" | custom-call | flops 1500000000 | bytes 5250000 | tf_op jit(solution)/shard_map/pallas_call | solution.py:629
  1.8 4.1 %collective-permute-start = (bf16[96,128]{1,0:T(8,128)(2,1)S(1)}, bf16[96,128]{1,0:T(8,128)(2,1)S(1)}, u32[]{:S(2)}, u32[]{:S(2)}) collective-permute-start(bf16[96,128]{1,0:T(8,128)(2,1)S(1)} %get-tuple-element.75), channel_id=1, source_target_pairs={{0,16},{1,17},{2,18},{3,19},{4,20},{5,21},{6,22},{7,23},{8,24},{9,... | collective-permute-start | bytes 73736 | tf_op jit(solution)/shard_map/ppermute | solution.py:30
  6.0 1.1 %shard_map.288 = (f32[2,1024,128]{2,1,0:T(8,128)S(1)}, f32[4,1024,128]{2,1,0:T(8,128)S(1)}) custom-call(s32[1]{0:T(128)} %bitcast.me_ref, bf16[1024,512]{1,0:T(8,128)(2,1)S(1)} %copy-done, s32[32,128]{1,0:T(8,128)S(1)} %bitcast.26), custom_call_target="tpu_custom_call" | custom-call | flops 2000000000 | bytes 7000000 | tf_op jit(solution)/shard_map/pallas_call | solution.py:629
  7.1 0.7 collective-permute-done
  7.7 3.3 %collective-permute-done.1 = bf16[64,384]{1,0:T(8,128)(2,1)S(1)} collective-permute-done((bf16[64,384]{1,0:T(8,128)(2,1)S(1)}, bf16[64,384]{1,0:T(8,128)(2,1)S(1)}, u32[]{:S(2)}, u32[]{:S(2)}) %collective-permute-start.1) | collective-permute-done | bytes 49184 | tf_op jit(solution)/shard_map/ppermute | solution.py:30
  11.0 1.5 %collective-permute-start.2 = (bf16[160,128]{1,0:T(8,128)(2,1)S(1)}, bf16[160,128]{1,0:T(8,128)(2,1)S(1)}, u32[]{:S(2)}, u32[]{:S(2)}) collective-permute-start(bf16[160,128]{1,0:T(8,128)(2,1)S(1)} %pad_maximum_fusion.9), channel_id=1, source_target_pairs={{0,8},{1,9},{2,10},{3,11},{4,12},{5,13},{6,14},{7,15},{8,0},{9,1},... | collective-permute-start | bytes 122888 | tf_op jit(solution)/shard_map/ppermute | solution.py:30
  12.6 1.6 %collective-permute-start.7 = (bf16[128,384]{1,0:T(8,128)(2,1)S(1)}, bf16[128,384]{1,0:T(8,128)(2,1)S(1)}, u32[]{:S(2)}, u32[]{:S(2)}) collective-permute-start(bf16[128,384]{1,0:T(8,128)(2,1)S(1)} %pad_maximum_fusion.5), channel_id=1, source_target_pairs={{0,2},{1,3},{2,0},{3,1},{4,6},{5,7},{6,4},{7,5},{8,10},{9,11},{10,... | collective-permute-start | bytes 294920 | tf_op jit(solution)/shard_map/ppermute | solution.py:30
  14.1 1.0 %collective-permute-done.2 = bf16[160,128]{1,0:T(8,128)(2,1)S(1)} collective-permute-done((bf16[160,128]{1,0:T(8,128)(2,1)S(1)}, bf16[160,128]{1,0:T(8,128)(2,1)S(1)}, u32[]{:S(2)}, u32[]{:S(2)}) %collective-permute-start.2) | collective-permute-done | bytes 40992 | tf_op jit(solution)/shard_map/ppermute | solution.py:30
  15.1 1.6 %collective-permute-start.3 = (bf16[288,128]{1,0:T(8,128)(2,1)S(1)}, bf16[288,128]{1,0:T(8,128)(2,1)S(1)}, u32[]{:S(2)}, u32[]{:S(2)}) collective-permute-start(bf16[288,128]{1,0:T(8,128)(2,1)S(1)} %pad_maximum_fusion.7), channel_id=1, source_target_pairs={{0,4},{1,5},{2,6},{3,7},{4,0},{5,1},{6,2},{7,3},{8,12},{9,13},{10,... | collective-permute-start | bytes 221192 | tf_op jit(solution)/shard_map/ppermute | solution.py:30
  16.7 0.5 collective-permute-done.7
  17.3 1.6 %collective-permute-start.10 = (bf16[128,384]{1,0:T(8,128)(2,1)S(1)}, bf16[128,384]{1,0:T(8,128)(2,1)S(1)}, u32[]{:S(2)}, u32[]{:S(2)}) collective-permute-start(bf16[128,384]{1,0:T(8,128)(2,1)S(1)} %bitcast.27), channel_id=1, source_target_pairs={{0,4},{1,5},{2,6},{3,7},{4,0},{5,1},{6,2},{7,3},{8,12},{9,13},{10,... | collective-permute-start | bytes 294920 | tf_op jit(solution)/shard_map/ppermute | solution.py:30
  18.9 0.6 collective-permute-start.8
  19.6 1.6 %collective-permute-start.4 = (bf16[512,128]{1,0:T(8,128)(2,1)S(1)}, bf16[512,128]{1,0:T(8,128)(2,1)S(1)}, u32[]{:S(2)}, u32[]{:S(2)}) collective-permute-start(bf16[512,128]{1,0:T(8,128)(2,1)S(1)} %pad_maximum_fusion.4), channel_id=1, source_target_pairs={{0,2},{1,3},{2,0},{3,1},{4,6},{5,7},{6,4},{7,5},{8,10},{9,11},{10,... | collective-permute-start | bytes 393224 | tf_op jit(solution)/shard_map/ppermute | solution.py:30
  21.2 0.8 %collective-permute-done.10 = bf16[128,384]{1,0:T(8,128)(2,1)S(1)} collective-permute-done((bf16[128,384]{1,0:T(8,128)(2,1)S(1)}, bf16[128,384]{1,0:T(8,128)(2,1)S(1)}, u32[]{:S(2)}, u32[]{:S(2)}) %collective-permute-start.10) | collective-permute-done | bytes 98336 | tf_op jit(solution)/shard_map/ppermute | solution.py:30
  22.0 1.6 %collective-permute-start.11 = (bf16[256,384]{1,0:T(8,128)(2,1)S(1)}, bf16[256,384]{1,0:T(8,128)(2,1)S(1)}, u32[]{:S(2)}, u32[]{:S(2)}) collective-permute-start(bf16[256,384]{1,0:T(8,128)(2,1)S(1)} %pad_maximum_fusion.2), channel_id=1, source_target_pairs={{0,8},{1,9},{2,10},{3,11},{4,12},{5,13},{6,14},{7,15},{8,0},{9,1},... | collective-permute-start | bytes 589832 | tf_op jit(solution)/shard_map/ppermute | solution.py:30
  23.7 1.5 %collective-permute-start.9 = (bf16[256,384]{1,0:T(8,128)(2,1)S(1)}, bf16[256,384]{1,0:T(8,128)(2,1)S(1)}, u32[]{:S(2)}, u32[]{:S(2)}) collective-permute-start(bf16[256,384]{1,0:T(8,128)(2,1)S(1)} %pad_maximum_fusion.1), channel_id=1, source_target_pairs={{0,4},{1,5},{2,6},{3,7},{4,0},{5,1},{6,2},{7,3},{8,12},{9,13},{10,... | collective-permute-start | bytes 589832 | tf_op jit(solution)/shard_map/ppermute | solution.py:30
  25.3 1.5 %collective-permute-done.5.b1_ref = bf16[1024,128]{1,0:T(8,128)(2,1)S(1)} collective-permute-done((bf16[1024,128]{1,0:T(8,128)(2,1)S(1)}, bf16[1024,128]{1,0:T(8,128)(2,1)S(1)}, u32[]{:S(2)}, u32[]{:S(2)}) %collective-permute-start.5) | collective-permute-done | bytes 262176 | tf_op jit(solution)/shard_map/ppermute | solution.py:30
  26.8 2.0 %shard_map.290 = (bf16[1024,512]{1,0:T(8,128)(2,1)S(1)}, f32[1024,512]{1,0:T(8,128)S(1)}, f32[64,512]{1,0:T(8,128)S(1)}, f32[64,128]{1,0:T(8,128)S(1)}, f32[8,51...) custom-call(s32[1]{0:T(128)} %bitcast.me_ref, bf16[1024,512]{1,0:T(8,128)(2,1)S(1)} %copy-done, ...), custom_call_target="tpu_custom_call" | custom-call | flops 300000000 | bytes 1050000 | tf_op jit(solution)/shard_map/pallas_call | solution.py:629
  28.8 0.6 collective-permute-done.9
  29.6 0.5 collective-permute-start.6
  30.1 1.8 %collective-permute-done.6.carry_ref = f32[8,512]{1,0:T(8,128)S(1)} collective-permute-done((f32[8,512]{1,0:T(8,128)S(1)}, f32[8,512]{1,0:T(8,128)S(1)}, u32[]{:S(2)}, u32[]{:S(2)}) %collective-permute-start.6) | collective-permute-done | bytes 16416 | tf_op jit(solution)/shard_map/ppermute | solution.py:30
  31.9 6.6 %shard_map.291 = (bf16[1024,512]{1,0:T(8,128)(2,1)}, f32[1024,512]{1,0:T(8,128)S(1)}, bf16[1024,512]{1,0:T(8,128)(2,1)S(1)}, f32[1024,512]{1,0:T(8,128)S(1)}, bf...) custom-call(s32[1]{0:T(128)} %bitcast.me_ref, ...), custom_call_target="tpu_custom_call" | custom-call | flops 10000000000 | bytes 35000000 | tf_op jit(solution)/shard_map/pallas_call | solution.py:629
  38.5 2.6 %shard_map.292 = (bf16[1024,384]{1,0:T(8,128)(2,1)S(1)}, bf16[1024,384]{1,0:T(8,128)(2,1)S(1)}) custom-call(s32[1]{0:T(128)} %bitcast.me_ref, bf16[1024,512]{1,0:T(8,128)(2,1)S(1)} %get-tuple-element.92.act_ref, bf16[1024,1024]{1,0:T(8,128)(2,1)S(1)} %get-tuple-element.93.unit_grad_ref, bf16[1024,512]{1,0:T(8,128)(2,1)S(1)} %get-tuple-element.94.lru_grad_ref, ...), custom_call_target="tpu_custom_call" | custom-call | flops 2500000000 | bytes 8750000 | tf_op jit(solution)/shard_map/pallas_call | solution.py:629
  41.2 0.2 collective-permute-start.13
  41.4 0.5 shard_map.293
  41.9 0.4 collective-permute-start.14
  42.3 1.2 %collective-permute-done.13 = bf16[1024,384]{1,0:T(8,128)(2,1)S(1)} collective-permute-done((bf16[1024,384]{1,0:T(8,128)(2,1)S(1)}, bf16[1024,384]{1,0:T(8,128)(2,1)S(1)}, u32[]{:S(2)}, u32[]{:S(2)}) %collective-permute-start.13) | collective-permute-done | bytes 786464 | tf_op jit(solution)/shard_map/ppermute | solution.py:30
  43.5 0.2 add_convert_fusion
  43.8 1.0 %collective-permute-start.17 = (bf16[256,384]{1,0:T(8,128)(2,1)S(1)}, bf16[256,384]{1,0:T(8,128)(2,1)S(1)}, u32[]{:S(2)}, u32[]{:S(2)}) collective-permute-start(bf16[256,384]{1,0:T(8,128)(2,1)S(1)} %get-tuple-element.134), channel_id=1, source_target_pairs={{0,8},{1,9},{2,10},{3,11},{4,12},{5,13},{6,14},{7,15},{8,0},{9,1},... | collective-permute-start | bytes 589832 | tf_op jit(solution)/shard_map/ppermute | solution.py:30
  44.8 1.8 %collective-permute-start.16 = (bf16[256,384]{1,0:T(8,128)(2,1)S(1)}, bf16[256,384]{1,0:T(8,128)(2,1)S(1)}, u32[]{:S(2)}, u32[]{:S(2)}) collective-permute-start(bf16[256,384]{1,0:T(8,128)(2,1)S(1)} %get-tuple-element.135), channel_id=1, source_target_pairs={{0,4},{1,5},{2,6},{3,7},{4,0},{5,1},{6,2},{7,3},{8,12},{9,13},{10,... | collective-permute-start | bytes 589832 | tf_op jit(solution)/shard_map/ppermute | solution.py:30
  46.6 3.4 %shard_map.294 = (bf16[1024,128]{1,0:T(8,128)(2,1)S(1)}, bf16[1056,128]{1,0:T(8,128)(2,1)S(1)}, f32[1024,512]{1,0:T(8,128)S(1)}) custom-call(s32[1]{0:T(128)} %bitcast.me_ref, bf16[1024,512]{1,0:T(8,128)(2,1)S(1)} %copy-done, f32[2,1024,128]{2,1,0:T(8,128)S(1)} %get-tuple-element.74.stats_ref, bf16[1024,512]{1,0:T(8,128)(2,1)S(1)} %get-tuple-element.79.normed_ref, ...), custom_call_target="tpu_custom_call" | custom-call | flops 4499999744 | bytes 15750000 | tf_op jit(solution)/shard_map/pallas_call | solution.py:629
  50.1 0.7 %collective-permute-done.17 = bf16[256,384]{1,0:T(8,128)(2,1)S(1)} collective-permute-done((bf16[256,384]{1,0:T(8,128)(2,1)S(1)}, bf16[256,384]{1,0:T(8,128)(2,1)S(1)}, u32[]{:S(2)}, u32[]{:S(2)}) %collective-permute-start.17) | collective-permute-done | bytes 196640 | tf_op jit(solution)/shard_map/ppermute | solution.py:30
  50.8 0.7 collective-permute-done.16
  51.8 1.9 %collective-permute-start.18 = (bf16[544,128]{1,0:T(8,128)(2,1)S(1)}, bf16[544,128]{1,0:T(8,128)(2,1)S(1)}, u32[]{:S(2)}, u32[]{:S(2)}) collective-permute-start(bf16[544,128]{1,0:T(8,128)(2,1)S(1)} %pad_maximum_fusion.3), channel_id=1, source_target_pairs={{0,2},{1,3},{2,0},{3,1},{4,6},{5,7},{6,4},{7,5},{8,10},{9,11},{10,... | collective-permute-start | bytes 417800 | tf_op jit(solution)/shard_map/ppermute | solution.py:30
  53.7 0.8 %collective-permute-start.22 = (bf16[128,384]{1,0:T(8,128)(2,1)S(1)}, bf16[128,384]{1,0:T(8,128)(2,1)S(1)}, u32[]{:S(2)}, u32[]{:S(2)}) collective-permute-start(bf16[128,384]{1,0:T(8,128)(2,1)S(1)} %slice.210), channel_id=1, source_target_pairs={{0,8},{1,9},{2,10},{3,11},{4,12},{5,13},{6,14},{7,15},{8,0},{9,1},... | collective-permute-start | bytes 294920 | tf_op jit(solution)/shard_map/ppermute | solution.py:30
  54.4 1.4 %collective-permute-start.23 = (bf16[128,384]{1,0:T(8,128)(2,1)S(1)}, bf16[128,384]{1,0:T(8,128)(2,1)S(1)}, u32[]{:S(2)}, u32[]{:S(2)}) collective-permute-start(bf16[128,384]{1,0:T(8,128)(2,1)S(1)} %slice.212), channel_id=1, source_target_pairs={{0,4},{1,5},{2,6},{3,7},{4,0},{5,1},{6,2},{7,3},{8,12},{9,13},{10,... | collective-permute-start | bytes 294920 | tf_op jit(solution)/shard_map/ppermute | solution.py:30
  55.8 1.8 %collective-permute-done.18 = bf16[544,128]{1,0:T(8,128)(2,1)S(1)} collective-permute-done((bf16[544,128]{1,0:T(8,128)(2,1)S(1)}, bf16[544,128]{1,0:T(8,128)(2,1)S(1)}, u32[]{:S(2)}, u32[]{:S(2)}) %collective-permute-start.18) | collective-permute-done | bytes 139296 | tf_op jit(solution)/shard_map/ppermute | solution.py:30
  57.7 1.1 %collective-permute-start.19 = (bf16[288,128]{1,0:T(8,128)(2,1)S(1)}, bf16[288,128]{1,0:T(8,128)(2,1)S(1)}, u32[]{:S(2)}, u32[]{:S(2)}) collective-permute-start(bf16[288,128]{1,0:T(8,128)(2,1)S(1)} %pad_maximum_fusion.8), channel_id=1, source_target_pairs={{0,4},{1,5},{2,6},{3,7},{4,0},{5,1},{6,2},{7,3},{8,12},{9,13},{10,... | collective-permute-start | bytes 221192 | tf_op jit(solution)/shard_map/ppermute | solution.py:30
  58.8 0.2 collective-permute-done.23
  59.2 1.6 %collective-permute-start.24 = (bf16[128,384]{1,0:T(8,128)(2,1)S(1)}, bf16[128,384]{1,0:T(8,128)(2,1)S(1)}, u32[]{:S(2)}, u32[]{:S(2)}) collective-permute-start(bf16[128,384]{1,0:T(8,128)(2,1)S(1)} %pad_maximum_fusion.6), channel_id=1, source_target_pairs={{0,2},{1,3},{2,0},{3,1},{4,6},{5,7},{6,4},{7,5},{8,10},{9,11},{10,... | collective-permute-start | bytes 294920 | tf_op jit(solution)/shard_map/ppermute | solution.py:30
  60.8 1.3 %collective-permute-done.19 = bf16[288,128]{1,0:T(8,128)(2,1)S(1)} collective-permute-done((bf16[288,128]{1,0:T(8,128)(2,1)S(1)}, bf16[288,128]{1,0:T(8,128)(2,1)S(1)}, u32[]{:S(2)}, u32[]{:S(2)}) %collective-permute-start.19) | collective-permute-done | bytes 73760 | tf_op jit(solution)/shard_map/ppermute | solution.py:30
  62.1 0.7 collective-permute-start.20
  62.9 1.0 %collective-permute-done.24 = bf16[128,384]{1,0:T(8,128)(2,1)S(1)} collective-permute-done((bf16[128,384]{1,0:T(8,128)(2,1)S(1)}, bf16[128,384]{1,0:T(8,128)(2,1)S(1)}, u32[]{:S(2)}, u32[]{:S(2)}) %collective-permute-start.24) | collective-permute-done | bytes 98336 | tf_op jit(solution)/shard_map/ppermute | solution.py:30
  63.9 2.3 %collective-permute-start.25 = (bf16[64,384]{1,0:T(8,128)(2,1)S(1)}, bf16[64,384]{1,0:T(8,128)(2,1)S(1)}, u32[]{:S(2)}, u32[]{:S(2)}) collective-permute-start(bf16[64,384]{1,0:T(8,128)(2,1)S(1)} %bitcast.35), channel_id=1, source_target_pairs={{0,16},{1,17},{2,18},{3,19},{4,20},{5,21},{6,22},{7,23},{8,24},{9,... | collective-permute-start | bytes 147464 | tf_op jit(solution)/shard_map/ppermute | solution.py:30
  66.3 1.3 %collective-permute-start.21 = (bf16[96,128]{1,0:T(8,128)(2,1)S(1)}, bf16[96,128]{1,0:T(8,128)(2,1)S(1)}, u32[]{:S(2)}, u32[]{:S(2)}) collective-permute-start(bf16[96,128]{1,0:T(8,128)(2,1)S(1)} %pad_maximum_fusion.11), channel_id=1, source_target_pairs={{0,16},{1,17},{2,18},{3,19},{4,20},{5,21},{6,22},{7,23},{8,24},{9,... | collective-permute-start | bytes 73736 | tf_op jit(solution)/shard_map/ppermute | solution.py:30
  67.5 2.4 %shard_map.295 = f32[1024,512]{1,0:T(8,128)} custom-call(s32[1]{0:T(128)} %bitcast.me_ref, bf16[1024,512]{1,0:T(8,128)(2,1)S(1)} %copy-done, f32[2,1024,128]{2,1,0:T(8,128)S(1)} %get-tuple-element.74.stats_ref, bf16[1024,512]{1,0:T(8,128)(2,1)S(1)} %copy-done.1, f32[1024,512]{1,0:T(8,128)S(1)} %get-tuple-element.113.normed_grad_ref, ...), custom_call_target="tpu_custom_call" | custom-call | flops 2500000000 | bytes 8750000 | tf_op jit(solution)/shard_map/pallas_call | solution.py:629
  69.9 1.1 %collective-permute-done.21 = bf16[96,128]{1,0:T(8,128)(2,1)S(1)} collective-permute-done((bf16[96,128]{1,0:T(8,128)(2,1)S(1)}, bf16[96,128]{1,0:T(8,128)(2,1)S(1)}, u32[]{:S(2)}, u32[]{:S(2)}) %collective-permute-start.21) | collective-permute-done | bytes 24608 | tf_op jit(solution)/shard_map/ppermute | solution.py:30
  71.1 1.1 %shard_map.296 = (f32[64,64]{1,0:T(8,128)}, f32[64,64]{1,0:T(8,128)}, f32[64,64]{1,0:T(8,128)}, f32[64,64]{1,0:T(8,128)}, f32[64,128]{1,0:T(8,128)}, /*index=5*/...) custom-call(s32[1]{0:T(128)} %bitcast.me_ref, ...), custom_call_target="tpu_custom_call" | custom-call | flops 2000000000 | bytes 7000000 | tf_op jit(solution)/shard_map/pallas_call | solution.py:629
  (72 shorter events, 1.3 us)
Async XLA Ops:
  0.7 5.3 %copy-start = (bf16[1024,512]{1,0:T(8,128)(2,1)S(1)}, bf16[1024,512]{1,0:T(8,128)(2,1)}, u32[]{:S(2)}) copy-start(bf16[1024,512]{1,0:T(8,128)(2,1)} %x_ref.9) | copy-start | bytes 3145732
  0.7 5.3 %copy-start.2 = (s32[4096]{0:T(1024)S(1)}, s32[4096]{0:T(1024)}, u32[]{:S(2)}) copy-start(s32[4096]{0:T(1024)} %param.18) | copy-start | bytes 49156
  1.8 5.9 %collective-permute-start = (bf16[96,128]{1,0:T(8,128)(2,1)S(1)}, bf16[96,128]{1,0:T(8,128)(2,1)S(1)}, u32[]{:S(2)}, u32[]{:S(2)}) collective-permute-start(bf16[96,128]{1,0:T(8,128)(2,1)S(1)} %get-tuple-element.75), channel_id=1, source_target_pairs={{0,16},{1,17},{2,18},{3,19},{4,20},{5,21},{6,22},{7,23},{8,24},{9,... | collective-permute-start | bytes 73736 | tf_op jit(solution)/shard_map/ppermute | solution.py:30
  5.9 5.1 %collective-permute-start.1 = (bf16[64,384]{1,0:T(8,128)(2,1)S(1)}, bf16[64,384]{1,0:T(8,128)(2,1)S(1)}, u32[]{:S(2)}, u32[]{:S(2)}) collective-permute-start(bf16[64,384]{1,0:T(8,128)(2,1)S(1)} %get-tuple-element.77), channel_id=1, source_target_pairs={{0,16},{1,17},{2,18},{3,19},{4,20},{5,21},{6,22},{7,23},{8,24},{9,... | collective-permute-start | bytes 147464 | tf_op jit(solution)/shard_map/ppermute | solution.py:30
  11.0 4.1 %collective-permute-start.2 = (bf16[160,128]{1,0:T(8,128)(2,1)S(1)}, bf16[160,128]{1,0:T(8,128)(2,1)S(1)}, u32[]{:S(2)}, u32[]{:S(2)}) collective-permute-start(bf16[160,128]{1,0:T(8,128)(2,1)S(1)} %pad_maximum_fusion.9), channel_id=1, source_target_pairs={{0,8},{1,9},{2,10},{3,11},{4,12},{5,13},{6,14},{7,15},{8,0},{9,1},... | collective-permute-start | bytes 122888 | tf_op jit(solution)/shard_map/ppermute | solution.py:30
  12.6 4.7 %collective-permute-start.7 = (bf16[128,384]{1,0:T(8,128)(2,1)S(1)}, bf16[128,384]{1,0:T(8,128)(2,1)S(1)}, u32[]{:S(2)}, u32[]{:S(2)}) collective-permute-start(bf16[128,384]{1,0:T(8,128)(2,1)S(1)} %pad_maximum_fusion.5), channel_id=1, source_target_pairs={{0,2},{1,3},{2,0},{3,1},{4,6},{5,7},{6,4},{7,5},{8,10},{9,11},{10,... | collective-permute-start | bytes 294920 | tf_op jit(solution)/shard_map/ppermute | solution.py:30
  15.1 4.4 %collective-permute-start.3 = (bf16[288,128]{1,0:T(8,128)(2,1)S(1)}, bf16[288,128]{1,0:T(8,128)(2,1)S(1)}, u32[]{:S(2)}, u32[]{:S(2)}) collective-permute-start(bf16[288,128]{1,0:T(8,128)(2,1)S(1)} %pad_maximum_fusion.7), channel_id=1, source_target_pairs={{0,4},{1,5},{2,6},{3,7},{4,0},{5,1},{6,2},{7,3},{8,12},{9,13},{10,... | collective-permute-start | bytes 221192 | tf_op jit(solution)/shard_map/ppermute | solution.py:30
  17.3 4.7 %collective-permute-start.10 = (bf16[128,384]{1,0:T(8,128)(2,1)S(1)}, bf16[128,384]{1,0:T(8,128)(2,1)S(1)}, u32[]{:S(2)}, u32[]{:S(2)}) collective-permute-start(bf16[128,384]{1,0:T(8,128)(2,1)S(1)} %bitcast.27), channel_id=1, source_target_pairs={{0,4},{1,5},{2,6},{3,7},{4,0},{5,1},{6,2},{7,3},{8,12},{9,13},{10,... | collective-permute-start | bytes 294920 | tf_op jit(solution)/shard_map/ppermute | solution.py:30
  18.9 4.8 %collective-permute-start.8 = (bf16[128,384]{1,0:T(8,128)(2,1)S(1)}, bf16[128,384]{1,0:T(8,128)(2,1)S(1)}, u32[]{:S(2)}, u32[]{:S(2)}) collective-permute-start(bf16[128,384]{1,0:T(8,128)(2,1)S(1)} %bitcast.30), channel_id=1, source_target_pairs={{0,8},{1,9},{2,10},{3,11},{4,12},{5,13},{6,14},{7,15},{8,0},{9,1},... | collective-permute-start | bytes 294920 | tf_op jit(solution)/shard_map/ppermute | solution.py:30
  19.6 5.6 %collective-permute-start.4 = (bf16[512,128]{1,0:T(8,128)(2,1)S(1)}, bf16[512,128]{1,0:T(8,128)(2,1)S(1)}, u32[]{:S(2)}, u32[]{:S(2)}) collective-permute-start(bf16[512,128]{1,0:T(8,128)(2,1)S(1)} %pad_maximum_fusion.4), channel_id=1, source_target_pairs={{0,2},{1,3},{2,0},{3,1},{4,6},{5,7},{6,4},{7,5},{8,10},{9,11},{10,... | collective-permute-start | bytes 393224 | tf_op jit(solution)/shard_map/ppermute | solution.py:30
  22.0 6.8 %collective-permute-start.11 = (bf16[256,384]{1,0:T(8,128)(2,1)S(1)}, bf16[256,384]{1,0:T(8,128)(2,1)S(1)}, u32[]{:S(2)}, u32[]{:S(2)}) collective-permute-start(bf16[256,384]{1,0:T(8,128)(2,1)S(1)} %pad_maximum_fusion.2), channel_id=1, source_target_pairs={{0,8},{1,9},{2,10},{3,11},{4,12},{5,13},{6,14},{7,15},{8,0},{9,1},... | collective-permute-start | bytes 589832 | tf_op jit(solution)/shard_map/ppermute | solution.py:30
  23.7 5.7 %collective-permute-start.9 = (bf16[256,384]{1,0:T(8,128)(2,1)S(1)}, bf16[256,384]{1,0:T(8,128)(2,1)S(1)}, u32[]{:S(2)}, u32[]{:S(2)}) collective-permute-start(bf16[256,384]{1,0:T(8,128)(2,1)S(1)} %pad_maximum_fusion.1), channel_id=1, source_target_pairs={{0,4},{1,5},{2,6},{3,7},{4,0},{5,1},{6,2},{7,3},{8,12},{9,13},{10,... | collective-permute-start | bytes 589832 | tf_op jit(solution)/shard_map/ppermute | solution.py:30
  25.2 1.6 %collective-permute-start.5 = (bf16[1024,128]{1,0:T(8,128)(2,1)S(1)}, bf16[1024,128]{1,0:T(8,128)(2,1)S(1)}, u32[]{:S(2)}, u32[]{:S(2)}) collective-permute-start(bf16[1024,128]{1,0:T(8,128)(2,1)S(1)} %constant_dynamic-update-slice_fusion.b0_ref), channel_id=1, source_target_pairs={{0,1},{1,0},{2,3},{3,2},{4,5},{5,4},{6,7},{7,6},{8,9},{9,8},{10,11... | collective-permute-start | bytes 786440 | tf_op jit(solution)/shard_map/ppermute | solution.py:30
  26.8 5.2 %copy-start.1 = (bf16[1024,512]{1,0:T(8,128)(2,1)S(1)}, bf16[1024,512]{1,0:T(8,128)(2,1)}, u32[]{:S(2)}) copy-start(bf16[1024,512]{1,0:T(8,128)(2,1)} %grad_ref.3) | copy-start | bytes 3145732
  29.6 2.4 %collective-permute-start.12 = (bf16[1024,384]{1,0:T(8,128)(2,1)S(1)}, bf16[1024,384]{1,0:T(8,128)(2,1)S(1)}, u32[]{:S(2)}, u32[]{:S(2)}) collective-permute-start(bf16[1024,384]{1,0:T(8,128)(2,1)S(1)} %constant_dynamic-update-slice_fusion.5.g0_ref), channel_id=1, source_target_pairs={{0,1},{1,0},{2,3},{3,2},{4,5},{5,4},{6,7},{7,6},{8,9},{9,8},{10,11... | collective-permute-start | bytes 2359304 | tf_op jit(solution)/shard_map/ppermute | solution.py:30
  29.6 2.3 %collective-permute-start.6 = (f32[8,512]{1,0:T(8,128)S(1)}, f32[8,512]{1,0:T(8,128)S(1)}, u32[]{:S(2)}, u32[]{:S(2)}) collective-permute-start(f32[8,512]{1,0:T(8,128)S(1)} %get-tuple-element.83), channel_id=1, source_target_pairs={{0,1},{1,0},{2,3},{3,2},{4,5},{5,4},{6,7},{7,6},{8,9},{9,8},{10,11... | collective-permute-start | bytes 49160 | tf_op jit(solution)/shard_map/ppermute | solution.py:30
  41.2 2.4 %collective-permute-start.13 = (bf16[1024,384]{1,0:T(8,128)(2,1)S(1)}, bf16[1024,384]{1,0:T(8,128)(2,1)S(1)}, u32[]{:S(2)}, u32[]{:S(2)}) collective-permute-start(bf16[1024,384]{1,0:T(8,128)(2,1)S(1)} %get-tuple-element.96), channel_id=1, source_target_pairs={{0,1},{1,0},{2,3},{3,2},{4,5},{5,4},{6,7},{7,6},{8,9},{9,8},{10,11... | collective-permute-start | bytes 2359304 | tf_op jit(solution)/shard_map/ppermute | solution.py:30
  41.9 4.7 %collective-permute-start.14 = (f32[8,512]{1,0:T(8,128)S(1)}, f32[8,512]{1,0:T(8,128)S(1)}, u32[]{:S(2)}, u32[]{:S(2)}) collective-permute-start(f32[8,512]{1,0:T(8,128)S(1)} %get-tuple-element.103), channel_id=1, source_target_pairs={{0,1},{1,0},{2,3},{3,2},{4,5},{5,4},{6,7},{7,6},{8,9},{9,8},{10,11... | collective-permute-start | bytes 49160 | tf_op jit(solution)/shard_map/ppermute | solution.py:30
  43.8 7.0 %collective-permute-start.17 = (bf16[256,384]{1,0:T(8,128)(2,1)S(1)}, bf16[256,384]{1,0:T(8,128)(2,1)S(1)}, u32[]{:S(2)}, u32[]{:S(2)}) collective-permute-start(bf16[256,384]{1,0:T(8,128)(2,1)S(1)} %get-tuple-element.134), channel_id=1, source_target_pairs={{0,8},{1,9},{2,10},{3,11},{4,12},{5,13},{6,14},{7,15},{8,0},{9,1},... | collective-permute-start | bytes 589832 | tf_op jit(solution)/shard_map/ppermute | solution.py:30
  44.8 6.7 %collective-permute-start.16 = (bf16[256,384]{1,0:T(8,128)(2,1)S(1)}, bf16[256,384]{1,0:T(8,128)(2,1)S(1)}, u32[]{:S(2)}, u32[]{:S(2)}) collective-permute-start(bf16[256,384]{1,0:T(8,128)(2,1)S(1)} %get-tuple-element.135), channel_id=1, source_target_pairs={{0,4},{1,5},{2,6},{3,7},{4,0},{5,1},{6,2},{7,3},{8,12},{9,13},{10,... | collective-permute-start | bytes 589832 | tf_op jit(solution)/shard_map/ppermute | solution.py:30
  50.0 1.6 %collective-permute-start.15 = (bf16[1056,128]{1,0:T(8,128)(2,1)S(1)}, bf16[1056,128]{1,0:T(8,128)(2,1)S(1)}, u32[]{:S(2)}, u32[]{:S(2)}) collective-permute-start(bf16[1056,128]{1,0:T(8,128)(2,1)S(1)} %get-tuple-element.109), channel_id=1, source_target_pairs={{0,1},{1,0},{2,3},{3,2},{4,5},{5,4},{6,7},{7,6},{8,9},{9,8},{10,11... | collective-permute-start | bytes 811016 | tf_op jit(solution)/shard_map/ppermute | solution.py:30
  51.8 5.8 %collective-permute-start.18 = (bf16[544,128]{1,0:T(8,128)(2,1)S(1)}, bf16[544,128]{1,0:T(8,128)(2,1)S(1)}, u32[]{:S(2)}, u32[]{:S(2)}) collective-permute-start(bf16[544,128]{1,0:T(8,128)(2,1)S(1)} %pad_maximum_fusion.3), channel_id=1, source_target_pairs={{0,2},{1,3},{2,0},{3,1},{4,6},{5,7},{6,4},{7,5},{8,10},{9,11},{10,... | collective-permute-start | bytes 417800 | tf_op jit(solution)/shard_map/ppermute | solution.py:30
  53.7 5.4 %collective-permute-start.22 = (bf16[128,384]{1,0:T(8,128)(2,1)S(1)}, bf16[128,384]{1,0:T(8,128)(2,1)S(1)}, u32[]{:S(2)}, u32[]{:S(2)}) collective-permute-start(bf16[128,384]{1,0:T(8,128)(2,1)S(1)} %slice.210), channel_id=1, source_target_pairs={{0,8},{1,9},{2,10},{3,11},{4,12},{5,13},{6,14},{7,15},{8,0},{9,1},... | collective-permute-start | bytes 294920 | tf_op jit(solution)/shard_map/ppermute | solution.py:30
  54.4 4.6 %collective-permute-start.23 = (bf16[128,384]{1,0:T(8,128)(2,1)S(1)}, bf16[128,384]{1,0:T(8,128)(2,1)S(1)}, u32[]{:S(2)}, u32[]{:S(2)}) collective-permute-start(bf16[128,384]{1,0:T(8,128)(2,1)S(1)} %slice.212), channel_id=1, source_target_pairs={{0,4},{1,5},{2,6},{3,7},{4,0},{5,1},{6,2},{7,3},{8,12},{9,13},{10,... | collective-permute-start | bytes 294920 | tf_op jit(solution)/shard_map/ppermute | solution.py:30
  57.7 4.4 %collective-permute-start.19 = (bf16[288,128]{1,0:T(8,128)(2,1)S(1)}, bf16[288,128]{1,0:T(8,128)(2,1)S(1)}, u32[]{:S(2)}, u32[]{:S(2)}) collective-permute-start(bf16[288,128]{1,0:T(8,128)(2,1)S(1)} %pad_maximum_fusion.8), channel_id=1, source_target_pairs={{0,4},{1,5},{2,6},{3,7},{4,0},{5,1},{6,2},{7,3},{8,12},{9,13},{10,... | collective-permute-start | bytes 221192 | tf_op jit(solution)/shard_map/ppermute | solution.py:30
  59.2 4.7 %collective-permute-start.24 = (bf16[128,384]{1,0:T(8,128)(2,1)S(1)}, bf16[128,384]{1,0:T(8,128)(2,1)S(1)}, u32[]{:S(2)}, u32[]{:S(2)}) collective-permute-start(bf16[128,384]{1,0:T(8,128)(2,1)S(1)} %pad_maximum_fusion.6), channel_id=1, source_target_pairs={{0,2},{1,3},{2,0},{3,1},{4,6},{5,7},{6,4},{7,5},{8,10},{9,11},{10,... | collective-permute-start | bytes 294920 | tf_op jit(solution)/shard_map/ppermute | solution.py:30
  62.1 4.1 %collective-permute-start.20 = (bf16[160,128]{1,0:T(8,128)(2,1)S(1)}, bf16[160,128]{1,0:T(8,128)(2,1)S(1)}, u32[]{:S(2)}, u32[]{:S(2)}) collective-permute-start(bf16[160,128]{1,0:T(8,128)(2,1)S(1)} %pad_maximum_fusion.10), channel_id=1, source_target_pairs={{0,8},{1,9},{2,10},{3,11},{4,12},{5,13},{6,14},{7,15},{8,0},{9,1},... | collective-permute-start | bytes 122888 | tf_op jit(solution)/shard_map/ppermute | solution.py:30
  63.9 6.0 %collective-permute-start.25 = (bf16[64,384]{1,0:T(8,128)(2,1)S(1)}, bf16[64,384]{1,0:T(8,128)(2,1)S(1)}, u32[]{:S(2)}, u32[]{:S(2)}) collective-permute-start(bf16[64,384]{1,0:T(8,128)(2,1)S(1)} %bitcast.35), channel_id=1, source_target_pairs={{0,16},{1,17},{2,18},{3,19},{4,20},{5,21},{6,22},{7,23},{8,24},{9,... | collective-permute-start | bytes 147464 | tf_op jit(solution)/shard_map/ppermute | solution.py:30
  66.3 4.8 %collective-permute-start.21 = (bf16[96,128]{1,0:T(8,128)(2,1)S(1)}, bf16[96,128]{1,0:T(8,128)(2,1)S(1)}, u32[]{:S(2)}, u32[]{:S(2)}) collective-permute-start(bf16[96,128]{1,0:T(8,128)(2,1)S(1)} %pad_maximum_fusion.11), channel_id=1, source_target_pairs={{0,16},{1,17},{2,18},{3,19},{4,20},{5,21},{6,22},{7,23},{8,24},{9,... | collective-permute-start | bytes 73736 | tf_op jit(solution)/shard_map/ppermute | solution.py:30

commit v7 on v6

--- a/solution.py
+++ b/solution.py
@@ -196,7 +196,7 @@
 def block_places(plan, me, order, refs, base, rows, start):
     slot = 0
     for ref in refs:
-        for place in range(plan.count // 2):
+        for place in range(plan.count // len(refs)):
             band, shard = plan.slot_owner(slot, me, order)
             slot += 1
             first = pl.multiple_of(band * plan.own_rows + start, rows)
@@ -221,10 +221,10 @@
             )
 
 
-def half_blocks(plan, orders):
+def half_blocks(plan, orders, arrays):
     rows = plan.own_rows // plan.halves
     for half in range(plan.halves):
-        yield orders[half], half * plan.count // 2 * rows, rows, half * rows
+        yield orders[half], half * plan.count // arrays * rows, rows, half * rows
 
 
 def start_copies(pairs, sems):
@@ -372,7 +372,7 @@
 
 def middle_kernel(
     plan, me_ref, x_ref, grad_ref, normed_ref, source_ref, ends_ref, hold_ref, carry_ref,
-    g0_ref, g1_ref, vec_ref, params_ref, masks_ref,
+    g0_ref, g1_ref, g2_ref, g3_ref, vec_ref, params_ref, masks_ref,
     mixed_ref, hidden_ref, lru_grad_ref, state_grad_ref, act_ref, unit_grad_ref, low_ref, sums_ref,
     pack_ref, wpack_ref, out_map_ref,
 ):
@@ -383,8 +383,9 @@
         (pair, units, wpack_ref, 0),
         (pair + units, units, wpack_ref, features),
     ]
-    for order, base, rows, first in half_blocks(plan, plan.up_crossed):
-        collect(plan, me_ref[0], order[::-1], (g0_ref, g1_ref), base, rows, first, targets)
+    block_refs = (g0_ref, g1_ref, g2_ref, g3_ref)
+    for order, base, rows, first in half_blocks(plan, plan.up_crossed, len(block_refs)):
+        collect(plan, me_ref[0], order[::-1], block_refs, base, rows, first, targets)
     sign = jnp.where(grid_index((1, 2 * states), 1) < states, 1.0, -1.0)
     regroup = regroup_matrix(states, plan.tensor)
     out_map_ref[...] = (dot(pack_ref[...].astype(BF16), regroup) * sign).astype(BF16)
@@ -466,8 +467,9 @@
 
 
 def weight_kernel(
-    plan, me_ref, act_ref, unit_grad_ref, lru_grad_ref, low_ref, keep_ref, send_ref, full_ref, out_ref
+    plan, me_ref, act_ref, unit_grad_ref, lru_grad_ref, low_ref, *refs
 ):
+    outs, (full_ref, out_ref) = refs[:-2], refs[-2:]
     states, features, units = plan.states, plan.features, plan.units
     pair = 2 * plan.own_states
     sign = jnp.where(grid_index((1, 2 * states), 1) < states, 1.0, -1.0)
@@ -479,8 +481,9 @@
         (pair, units, full_ref, 0),
         (pair + units, units, full_ref, features),
     ]
-    for order, base, rows, first in half_blocks(plan, plan.down_crossed):
-        distribute(plan, me_ref[0], order, (keep_ref, send_ref), base, rows, first, targets)
+    for half, (order, _, rows, first) in enumerate(half_blocks(plan, plan.down_crossed, 2)):
+        pair_refs = outs[2 * half : 2 * half + 2]
+        distribute(plan, me_ref[0], order, pair_refs, 0, rows, first, targets)
 
 
 def leave_kernel(
@@ -787,8 +790,10 @@
 
     left = carry
     carry = flip(carry, 0, plan.count) if plan.pieces == 2 else jnp.zeros_like(carry)
-    g0 = joined(*(joined(part, after(got, left)) for part, got in halves))
-    g1 = flip(g0, 0, plan.count)
+    held = joined(*(part for part, _ in halves))
+    held_other = flip(held, 0, plan.count)
+    came = joined(*(after(got, left) for _, got in halves))
+    came_other = flip(came, 0, plan.count)
     (
         mixed, hidden, lru_grad, state_grad, act, unit_grad, low, sums,
     ) = call(
@@ -811,13 +816,15 @@
         ],
         24,
         10,
-        me, block_input, out_grad, normed, source, ends, hold, carry, g0, g1, vectors, params, masks,
+        me, block_input, out_grad, normed, source, ends, hold, carry,
+        held, came, held_other, came_other, vectors, params, masks,
     )
     half_rows = plan.count // 2 * long
-    w_keep, w_send = call(
+    pieces = plan.halves
+    outs = call(
         weight_kernel,
         plan,
-        [shape((half_rows, block), BF16)] * 2,
+        [shape((half_rows // pieces, block), BF16)] * (2 * pieces),
         [
             pltpu.VMEM((features, 2 * features), F32),
             pltpu.VMEM((features, 2 * states), F32),
@@ -826,7 +833,8 @@
         2.5,
         me, act, unit_grad, lru_grad, low,
     )
-    w_other = flip(w_send, 0, plan.count)
+    w_keeps, w_sends = outs[::2], outs[1::2]
+    w_others = [flip(send, 0, plan.count) for send in w_sends]
     back_ends, back_hold, back = call(
         back_kernel,
         plan,
@@ -834,13 +842,12 @@
         [],
         8,
         1,
-        me, after(state_grad, w_send), params, masks,
+        me, after(state_grad, *w_sends), params, masks,
     )
     back = flip(back, 0, plan.count) if plan.pieces == 2 else jnp.zeros_like(back)
-    pieces = plan.halves
-    w_total = added(w_keep, after(w_other, back_ends))
-    size = w_total.shape[0] // pieces
-    halves = [cut(w_total[half * size : half * size + size]) for half in range(pieces)]
+    halves = [
+        cut(added(keep, after(other, back_ends))) for keep, other in zip(w_keeps, w_others)
+    ]
     w_others = [flip(half[1], bit, plan.count) for half, bit in zip(halves, (2, 3))]
     back_ends = after(back_ends, *(half[1] for half in halves))
     b_keep, b_send, normed_grad = call(

time: 72.5 us -> 71.7 us (0.989)
  starting transfers between devices: 30.8 us -> 28.5 us
  waiting for transfers between devices: 18.4 us -> 19.7 us
    ppermute x26 -> x28, starting transfers between devices: 30.8 us -> 28.5 us  [flip(): return lax.ppermute(value, AXES, [(i, i ^ 1 << bit) for i in range(count)])]
    ppermute x26 -> x28, waiting for transfers between devices: 18.4 us -> 19.7 us  [flip(): return lax.ppermute(value, AXES, [(i, i ^ 1 << bit) for i in range(count)])]
  transfers between devices with their start and end apart: 26 -> 28, of which waited for: 18 -> 19; matrix products, arithmetic and copies ran while one was open for 1% -> 1% of each run, Pallas kernels for 13% -> 13%
where the time goes in v7:
time: 71.7 us; the launch traced here: 71.5 us
  starting transfers between devices  28.5 us (40%)
  Pallas kernels  21 us (29%)
  waiting for transfers between devices  19.7 us (27%)
  between operations  1.24 us (2%)
  other arithmetic  0.73 us (1%)
    ppermute x28, starting transfers between devices, flip(): return lax.ppermute(value, AXES, [(i, i ^ 1 << bit) for i in range(count)])  28.5 us
    pallas_call x9, Pallas kernels, call(): pl.pallas_call(functools.partial(kernel, plan), out_shape=outs, in_specs=...  21 us
    ppermute x28, waiting for transfers between devices, flip(): return lax.ppermute(value, AXES, [(i, i ^ 1 << bit) for i in range(count)])  19.7 us
  transfers between devices with their start and end apart: 28, of which 19 were waited for; matrix products, arithmetic and copies ran while one was open for 1% of the time, Pallas kernels for 13%

profile of v7, /device:TPU:0, one launch (start us, length us, event | category | flops | bytes accessed | tf_op | source)
XLA Modules:
  0.0 71.5 jit_solution(16775332850906956390)
XLA Ops:
  0.7 1.1 %shard_map.289 = (bf16[96,128]{1,0:T(8,128)(2,1)S(1)}, bf16[64,384]{1,0:T(8,128)(2,1)S(1)}) custom-call(s32[1]{0:T(128)} %bitcast.me_ref, bf16[64,64]{1,0:T(8,128)(2,1)} %refs_0_.1, bf16[64,64]{1,0:T(8,128)(2,1)} %refs_1_.1, bf16[64,64]{1,0:T(8,128)(2,1)} %refs_2_.1, bf16[64,64]{1,0:T(8,128)(2,1)} %refs_3_.1, bf16[64,128]{1,0:T(8,128)(2,1)} %refs_4_.1, ...), custom_call_target="tpu_custom_call" | custom-call | flops 1500000000 | bytes 5250000 | tf_op jit(solution)/shard_map/pallas_call | solution.py:632
  1.8 4.1 %collective-permute-start = (bf16[96,128]{1,0:T(8,128)(2,1)S(1)}, bf16[96,128]{1,0:T(8,128)(2,1)S(1)}, u32[]{:S(2)}, u32[]{:S(2)}) collective-permute-start(bf16[96,128]{1,0:T(8,128)(2,1)S(1)} %get-tuple-element.78), channel_id=1, source_target_pairs={{0,16},{1,17},{2,18},{3,19},{4,20},{5,21},{6,22},{7,23},{8,24},{9,... | collective-permute-start | bytes 73736 | tf_op jit(solution)/shard_map/ppermute | solution.py:30
  6.0 1.1 %shard_map.288 = (f32[2,1024,128]{2,1,0:T(8,128)S(1)}, f32[4,1024,128]{2,1,0:T(8,128)S(1)}) custom-call(s32[1]{0:T(128)} %bitcast.me_ref, bf16[1024,512]{1,0:T(8,128)(2,1)S(1)} %copy-done, s32[32,128]{1,0:T(8,128)S(1)} %bitcast.26), custom_call_target="tpu_custom_call" | custom-call | flops 2000000000 | bytes 7000000 | tf_op jit(solution)/shard_map/pallas_call | solution.py:632
  7.1 0.7 collective-permute-done
  7.7 3.3 %collective-permute-done.1 = bf16[64,384]{1,0:T(8,128)(2,1)S(1)} collective-permute-done((bf16[64,384]{1,0:T(8,128)(2,1)S(1)}, bf16[64,384]{1,0:T(8,128)(2,1)S(1)}, u32[]{:S(2)}, u32[]{:S(2)}) %collective-permute-start.1) | collective-permute-done | bytes 49184 | tf_op jit(solution)/shard_map/ppermute | solution.py:30
  11.0 1.5 %collective-permute-start.2 = (bf16[160,128]{1,0:T(8,128)(2,1)S(1)}, bf16[160,128]{1,0:T(8,128)(2,1)S(1)}, u32[]{:S(2)}, u32[]{:S(2)}) collective-permute-start(bf16[160,128]{1,0:T(8,128)(2,1)S(1)} %pad_maximum_fusion.9), channel_id=1, source_target_pairs={{0,8},{1,9},{2,10},{3,11},{4,12},{5,13},{6,14},{7,15},{8,0},{9,1},... | collective-permute-start | bytes 122888 | tf_op jit(solution)/shard_map/ppermute | solution.py:30
  12.6 1.6 %collective-permute-start.7 = (bf16[128,384]{1,0:T(8,128)(2,1)S(1)}, bf16[128,384]{1,0:T(8,128)(2,1)S(1)}, u32[]{:S(2)}, u32[]{:S(2)}) collective-permute-start(bf16[128,384]{1,0:T(8,128)(2,1)S(1)} %pad_maximum_fusion.5), channel_id=1, source_target_pairs={{0,2},{1,3},{2,0},{3,1},{4,6},{5,7},{6,4},{7,5},{8,10},{9,11},{10,... | collective-permute-start | bytes 294920 | tf_op jit(solution)/shard_map/ppermute | solution.py:30
  14.1 1.0 %collective-permute-done.2 = bf16[160,128]{1,0:T(8,128)(2,1)S(1)} collective-permute-done((bf16[160,128]{1,0:T(8,128)(2,1)S(1)}, bf16[160,128]{1,0:T(8,128)(2,1)S(1)}, u32[]{:S(2)}, u32[]{:S(2)}) %collective-permute-start.2) | collective-permute-done | bytes 40992 | tf_op jit(solution)/shard_map/ppermute | solution.py:30
  15.1 1.6 %collective-permute-start.3 = (bf16[288,128]{1,0:T(8,128)(2,1)S(1)}, bf16[288,128]{1,0:T(8,128)(2,1)S(1)}, u32[]{:S(2)}, u32[]{:S(2)}) collective-permute-start(bf16[288,128]{1,0:T(8,128)(2,1)S(1)} %pad_maximum_fusion.7), channel_id=1, source_target_pairs={{0,4},{1,5},{2,6},{3,7},{4,0},{5,1},{6,2},{7,3},{8,12},{9,13},{10,... | collective-permute-start | bytes 221192 | tf_op jit(solution)/shard_map/ppermute | solution.py:30
  16.7 0.5 collective-permute-done.7
  17.3 1.6 %collective-permute-start.9 = (bf16[128,384]{1,0:T(8,128)(2,1)S(1)}, bf16[128,384]{1,0:T(8,128)(2,1)S(1)}, u32[]{:S(2)}, u32[]{:S(2)}) collective-permute-start(bf16[128,384]{1,0:T(8,128)(2,1)S(1)} %bitcast.27), channel_id=1, source_target_pairs={{0,4},{1,5},{2,6},{3,7},{4,0},{5,1},{6,2},{7,3},{8,12},{9,13},{10,... | collective-permute-start | bytes 294920 | tf_op jit(solution)/shard_map/ppermute | solution.py:30
  18.9 0.6 collective-permute-start.8
  19.6 1.6 %collective-permute-start.4 = (bf16[512,128]{1,0:T(8,128)(2,1)S(1)}, bf16[512,128]{1,0:T(8,128)(2,1)S(1)}, u32[]{:S(2)}, u32[]{:S(2)}) collective-permute-start(bf16[512,128]{1,0:T(8,128)(2,1)S(1)} %pad_maximum_fusion.4), channel_id=1, source_target_pairs={{0,2},{1,3},{2,0},{3,1},{4,6},{5,7},{6,4},{7,5},{8,10},{9,11},{10,... | collective-permute-start | bytes 393224 | tf_op jit(solution)/shard_map/ppermute | solution.py:30
  21.2 0.8 %collective-permute-done.9 = bf16[128,384]{1,0:T(8,128)(2,1)S(1)} collective-permute-done((bf16[128,384]{1,0:T(8,128)(2,1)S(1)}, bf16[128,384]{1,0:T(8,128)(2,1)S(1)}, u32[]{:S(2)}, u32[]{:S(2)}) %collective-permute-start.9) | collective-permute-done | bytes 98336 | tf_op jit(solution)/shard_map/ppermute | solution.py:30
  22.0 1.6 %collective-permute-start.11 = (bf16[256,384]{1,0:T(8,128)(2,1)S(1)}, bf16[256,384]{1,0:T(8,128)(2,1)S(1)}, u32[]{:S(2)}, u32[]{:S(2)}) collective-permute-start(bf16[256,384]{1,0:T(8,128)(2,1)S(1)} %pad_maximum_fusion.2), channel_id=1, source_target_pairs={{0,8},{1,9},{2,10},{3,11},{4,12},{5,13},{6,14},{7,15},{8,0},{9,1},... | collective-permute-start | bytes 589832 | tf_op jit(solution)/shard_map/ppermute | solution.py:30
  23.7 1.5 %collective-permute-start.10 = (bf16[256,384]{1,0:T(8,128)(2,1)S(1)}, bf16[256,384]{1,0:T(8,128)(2,1)S(1)}, u32[]{:S(2)}, u32[]{:S(2)}) collective-permute-start(bf16[256,384]{1,0:T(8,128)(2,1)S(1)} %pad_maximum_fusion.1), channel_id=1, source_target_pairs={{0,4},{1,5},{2,6},{3,7},{4,0},{5,1},{6,2},{7,3},{8,12},{9,13},{10,... | collective-permute-start | bytes 589832 | tf_op jit(solution)/shard_map/ppermute | solution.py:30
  25.3 0.6 collective-permute-start.12
  25.9 0.9 %collective-permute-done.5.b1_ref = bf16[1024,128]{1,0:T(8,128)(2,1)S(1)} collective-permute-done((bf16[1024,128]{1,0:T(8,128)(2,1)S(1)}, bf16[1024,128]{1,0:T(8,128)(2,1)S(1)}, u32[]{:S(2)}, u32[]{:S(2)}) %collective-permute-start.5) | collective-permute-done | bytes 262176 | tf_op jit(solution)/shard_map/ppermute | solution.py:30
  26.8 2.0 %shard_map.290 = (bf16[1024,512]{1,0:T(8,128)(2,1)S(1)}, f32[1024,512]{1,0:T(8,128)S(1)}, f32[64,512]{1,0:T(8,128)S(1)}, f32[64,128]{1,0:T(8,128)S(1)}, f32[8,51...) custom-call(s32[1]{0:T(128)} %bitcast.me_ref, bf16[1024,512]{1,0:T(8,128)(2,1)S(1)} %copy-done, ...), custom_call_target="tpu_custom_call" | custom-call | flops 300000000 | bytes 1050000 | tf_op jit(solution)/shard_map/pallas_call | solution.py:632
  28.8 0.6 collective-permute-done.10
  29.6 0.5 collective-permute-start.6
  30.1 1.2 %collective-permute-done.6.carry_ref = f32[8,512]{1,0:T(8,128)S(1)} collective-permute-done((f32[8,512]{1,0:T(8,128)S(1)}, f32[8,512]{1,0:T(8,128)S(1)}, u32[]{:S(2)}, u32[]{:S(2)}) %collective-permute-start.6) | collective-permute-done | bytes 16416 | tf_op jit(solution)/shard_map/ppermute | solution.py:30
  31.3 6.6 %shard_map.291 = (bf16[1024,512]{1,0:T(8,128)(2,1)}, f32[1024,512]{1,0:T(8,128)S(1)}, bf16[1024,512]{1,0:T(8,128)(2,1)S(1)}, f32[1024,512]{1,0:T(8,128)S(1)}, bf...) custom-call(s32[1]{0:T(128)} %bitcast.me_ref, ...), custom_call_target="tpu_custom_call" | custom-call | flops 10000000000 | bytes 35000000 | tf_op jit(solution)/shard_map/pallas_call | solution.py:632
  38.0 2.7 %shard_map.292 = (bf16[512,384]{1,0:T(8,128)(2,1)S(1)}, bf16[512,384]{1,0:T(8,128)(2,1)S(1)}, bf16[512,384]{1,0:T(8,128)(2,1)S(1)}, bf16[512,384]{1,0:T(8,128)(2,1)S(1)}) custom-call(s32[1]{0:T(128)} %bitcast.me_ref, bf16[1024,512]{1,0:T(8,128)(2,1)S(1)} %get-tuple-element.95.act_ref, bf16[1024,1024]{1,0:T(8,128)(2,1)S(1)} %get-tuple-element.96.unit_grad_ref, ...), custom_call_target="tpu_custom_call" | custom-call | flops 2500000000 | bytes 8750000 | tf_op jit(solution)/shard_map/pallas_call | solution.py:632
  40.7 0.2 collective-permute-start.14
  40.8 0.4 collective-permute-start.15
  41.2 0.5 shard_map.293
  41.9 0.6 collective-permute-done.14
  42.6 1.4 %collective-permute-start.18 = (bf16[256,384]{1,0:T(8,128)(2,1)S(1)}, bf16[256,384]{1,0:T(8,128)(2,1)S(1)}, u32[]{:S(2)}, u32[]{:S(2)}) collective-permute-start(bf16[256,384]{1,0:T(8,128)(2,1)S(1)} %slice.201), channel_id=1, source_target_pairs={{0,4},{1,5},{2,6},{3,7},{4,0},{5,1},{6,2},{7,3},{8,12},{9,13},{10,... | collective-permute-start | bytes 589832 | tf_op jit(solution)/shard_map/ppermute | solution.py:30
  44.2 1.4 %collective-permute-start.19 = (bf16[256,384]{1,0:T(8,128)(2,1)S(1)}, bf16[256,384]{1,0:T(8,128)(2,1)S(1)}, u32[]{:S(2)}, u32[]{:S(2)}) collective-permute-start(bf16[256,384]{1,0:T(8,128)(2,1)S(1)} %slice.202), channel_id=1, source_target_pairs={{0,8},{1,9},{2,10},{3,11},{4,12},{5,13},{6,14},{7,15},{8,0},{9,1},... | collective-permute-start | bytes 589832 | tf_op jit(solution)/shard_map/ppermute | solution.py:30
  45.5 3.5 %shard_map.294 = (bf16[1024,128]{1,0:T(8,128)(2,1)S(1)}, bf16[1056,128]{1,0:T(8,128)(2,1)S(1)}, f32[1024,512]{1,0:T(8,128)S(1)}) custom-call(s32[1]{0:T(128)} %bitcast.me_ref, bf16[1024,512]{1,0:T(8,128)(2,1)S(1)} %copy-done, f32[2,1024,128]{2,1,0:T(8,128)S(1)} %get-tuple-element.77.stats_ref, bf16[1024,512]{1,0:T(8,128)(2,1)S(1)} %get-tuple-element.82.normed_ref, ...), custom_call_target="tpu_custom_call" | custom-call | flops 4499999744 | bytes 15750000 | tf_op jit(solution)/shard_map/pallas_call | solution.py:632
  49.1 0.5 collective-permute-done.18
  49.7 1.2 %collective-permute-done.19 = bf16[256,384]{1,0:T(8,128)(2,1)S(1)} collective-permute-done((bf16[256,384]{1,0:T(8,128)(2,1)S(1)}, bf16[256,384]{1,0:T(8,128)(2,1)S(1)}, u32[]{:S(2)}, u32[]{:S(2)}) %collective-permute-start.19) | collective-permute-done | bytes 196640 | tf_op jit(solution)/shard_map/ppermute | solution.py:30
  51.1 1.6 %collective-permute-start.20 = (bf16[544,128]{1,0:T(8,128)(2,1)S(1)}, bf16[544,128]{1,0:T(8,128)(2,1)S(1)}, u32[]{:S(2)}, u32[]{:S(2)}) collective-permute-start(bf16[544,128]{1,0:T(8,128)(2,1)S(1)} %pad_maximum_fusion.3), channel_id=1, source_target_pairs={{0,2},{1,3},{2,0},{3,1},{4,6},{5,7},{6,4},{7,5},{8,10},{9,11},{10,... | collective-permute-start | bytes 417800 | tf_op jit(solution)/shard_map/ppermute | solution.py:30
  52.7 1.6 %collective-permute-start.24 = (bf16[128,384]{1,0:T(8,128)(2,1)S(1)}, bf16[128,384]{1,0:T(8,128)(2,1)S(1)}, u32[]{:S(2)}, u32[]{:S(2)}) collective-permute-start(bf16[128,384]{1,0:T(8,128)(2,1)S(1)} %slice.204), channel_id=1, source_target_pairs={{0,8},{1,9},{2,10},{3,11},{4,12},{5,13},{6,14},{7,15},{8,0},{9,1},... | collective-permute-start | bytes 294920 | tf_op jit(solution)/shard_map/ppermute | solution.py:30
  54.3 0.6 collective-permute-start.25
  54.9 1.7 %collective-permute-done.20 = bf16[544,128]{1,0:T(8,128)(2,1)S(1)} collective-permute-done((bf16[544,128]{1,0:T(8,128)(2,1)S(1)}, bf16[544,128]{1,0:T(8,128)(2,1)S(1)}, u32[]{:S(2)}, u32[]{:S(2)}) %collective-permute-start.20) | collective-permute-done | bytes 139296 | tf_op jit(solution)/shard_map/ppermute | solution.py:30
  56.7 0.4 collective-permute-start.21
  57.1 2.4 %collective-permute-done.25 = bf16[128,384]{1,0:T(8,128)(2,1)S(1)} collective-permute-done((bf16[128,384]{1,0:T(8,128)(2,1)S(1)}, bf16[128,384]{1,0:T(8,128)(2,1)S(1)}, u32[]{:S(2)}, u32[]{:S(2)}) %collective-permute-start.25) | collective-permute-done | bytes 98336 | tf_op jit(solution)/shard_map/ppermute | solution.py:30
  59.7 1.4 %collective-permute-done.21 = bf16[288,128]{1,0:T(8,128)(2,1)S(1)} collective-permute-done((bf16[288,128]{1,0:T(8,128)(2,1)S(1)}, bf16[288,128]{1,0:T(8,128)(2,1)S(1)}, u32[]{:S(2)}, u32[]{:S(2)}) %collective-permute-start.21) | collective-permute-done | bytes 73760 | tf_op jit(solution)/shard_map/ppermute | solution.py:30
  61.2 1.0 %collective-permute-start.22 = (bf16[160,128]{1,0:T(8,128)(2,1)S(1)}, bf16[160,128]{1,0:T(8,128)(2,1)S(1)}, u32[]{:S(2)}, u32[]{:S(2)}) collective-permute-start(bf16[160,128]{1,0:T(8,128)(2,1)S(1)} %pad_maximum_fusion.10), channel_id=1, source_target_pairs={{0,8},{1,9},{2,10},{3,11},{4,12},{5,13},{6,14},{7,15},{8,0},{9,1},... | collective-permute-start | bytes 122888 | tf_op jit(solution)/shard_map/ppermute | solution.py:30
  62.2 2.2 %collective-permute-done.26 = bf16[128,384]{1,0:T(8,128)(2,1)S(1)} collective-permute-done((bf16[128,384]{1,0:T(8,128)(2,1)S(1)}, bf16[128,384]{1,0:T(8,128)(2,1)S(1)}, u32[]{:S(2)}, u32[]{:S(2)}) %collective-permute-start.26) | collective-permute-done | bytes 98336 | tf_op jit(solution)/shard_map/ppermute | solution.py:30
  64.4 0.6 collective-permute-start.27
  64.9 0.3 collective-permute-done.22
  65.3 2.2 %collective-permute-start.23 = (bf16[96,128]{1,0:T(8,128)(2,1)S(1)}, bf16[96,128]{1,0:T(8,128)(2,1)S(1)}, u32[]{:S(2)}, u32[]{:S(2)}) collective-permute-start(bf16[96,128]{1,0:T(8,128)(2,1)S(1)} %pad_maximum_fusion.11), channel_id=1, source_target_pairs={{0,16},{1,17},{2,18},{3,19},{4,20},{5,21},{6,22},{7,23},{8,24},{9,... | collective-permute-start | bytes 73736 | tf_op jit(solution)/shard_map/ppermute | solution.py:30
  67.5 2.4 %shard_map.295 = f32[1024,512]{1,0:T(8,128)} custom-call(s32[1]{0:T(128)} %bitcast.me_ref, bf16[1024,512]{1,0:T(8,128)(2,1)S(1)} %copy-done, f32[2,1024,128]{2,1,0:T(8,128)S(1)} %get-tuple-element.77.stats_ref, bf16[1024,512]{1,0:T(8,128)(2,1)S(1)} %copy-done.1, f32[1024,512]{1,0:T(8,128)S(1)} %get-tuple-element.119.normed_grad_ref, ...), custom_call_target="tpu_custom_call" | custom-call | flops 2500000000 | bytes 8750000 | tf_op jit(solution)/shard_map/pallas_call | solution.py:632
  70.0 0.2 collective-permute-done.23
  70.2 1.1 %shard_map.296 = (f32[64,64]{1,0:T(8,128)}, f32[64,64]{1,0:T(8,128)}, f32[64,64]{1,0:T(8,128)}, f32[64,64]{1,0:T(8,128)}, f32[64,128]{1,0:T(8,128)}, /*index=5*/...) custom-call(s32[1]{0:T(128)} %bitcast.me_ref, ...), custom_call_target="tpu_custom_call" | custom-call | flops 2000000000 | bytes 7000000 | tf_op jit(solution)/shard_map/pallas_call | solution.py:632
  (79 shorter events, 1.8 us)
Async XLA Ops:
  0.7 5.3 %copy-start = (bf16[1024,512]{1,0:T(8,128)(2,1)S(1)}, bf16[1024,512]{1,0:T(8,128)(2,1)}, u32[]{:S(2)}) copy-start(bf16[1024,512]{1,0:T(8,128)(2,1)} %x_ref.9) | copy-start | bytes 3145732
  0.7 5.3 %copy-start.2 = (s32[4096]{0:T(1024)S(1)}, s32[4096]{0:T(1024)}, u32[]{:S(2)}) copy-start(s32[4096]{0:T(1024)} %param.18) | copy-start | bytes 49156
  1.8 5.9 %collective-permute-start = (bf16[96,128]{1,0:T(8,128)(2,1)S(1)}, bf16[96,128]{1,0:T(8,128)(2,1)S(1)}, u32[]{:S(2)}, u32[]{:S(2)}) collective-permute-start(bf16[96,128]{1,0:T(8,128)(2,1)S(1)} %get-tuple-element.78), channel_id=1, source_target_pairs={{0,16},{1,17},{2,18},{3,19},{4,20},{5,21},{6,22},{7,23},{8,24},{9,... | collective-permute-start | bytes 73736 | tf_op jit(solution)/shard_map/ppermute | solution.py:30
  5.9 5.1 %collective-permute-start.1 = (bf16[64,384]{1,0:T(8,128)(2,1)S(1)}, bf16[64,384]{1,0:T(8,128)(2,1)S(1)}, u32[]{:S(2)}, u32[]{:S(2)}) collective-permute-start(bf16[64,384]{1,0:T(8,128)(2,1)S(1)} %get-tuple-element.80), channel_id=1, source_target_pairs={{0,16},{1,17},{2,18},{3,19},{4,20},{5,21},{6,22},{7,23},{8,24},{9,... | collective-permute-start | bytes 147464 | tf_op jit(solution)/shard_map/ppermute | solution.py:30
  11.0 4.1 %collective-permute-start.2 = (bf16[160,128]{1,0:T(8,128)(2,1)S(1)}, bf16[160,128]{1,0:T(8,128)(2,1)S(1)}, u32[]{:S(2)}, u32[]{:S(2)}) collective-permute-start(bf16[160,128]{1,0:T(8,128)(2,1)S(1)} %pad_maximum_fusion.9), channel_id=1, source_target_pairs={{0,8},{1,9},{2,10},{3,11},{4,12},{5,13},{6,14},{7,15},{8,0},{9,1},... | collective-permute-start | bytes 122888 | tf_op jit(solution)/shard_map/ppermute | solution.py:30
  12.6 4.7 %collective-permute-start.7 = (bf16[128,384]{1,0:T(8,128)(2,1)S(1)}, bf16[128,384]{1,0:T(8,128)(2,1)S(1)}, u32[]{:S(2)}, u32[]{:S(2)}) collective-permute-start(bf16[128,384]{1,0:T(8,128)(2,1)S(1)} %pad_maximum_fusion.5), channel_id=1, source_target_pairs={{0,2},{1,3},{2,0},{3,1},{4,6},{5,7},{6,4},{7,5},{8,10},{9,11},{10,... | collective-permute-start | bytes 294920 | tf_op jit(solution)/shard_map/ppermute | solution.py:30
  15.1 4.4 %collective-permute-start.3 = (bf16[288,128]{1,0:T(8,128)(2,1)S(1)}, bf16[288,128]{1,0:T(8,128)(2,1)S(1)}, u32[]{:S(2)}, u32[]{:S(2)}) collective-permute-start(bf16[288,128]{1,0:T(8,128)(2,1)S(1)} %pad_maximum_fusion.7), channel_id=1, source_target_pairs={{0,4},{1,5},{2,6},{3,7},{4,0},{5,1},{6,2},{7,3},{8,12},{9,13},{10,... | collective-permute-start | bytes 221192 | tf_op jit(solution)/shard_map/ppermute | solution.py:30
  17.3 4.7 %collective-permute-start.9 = (bf16[128,384]{1,0:T(8,128)(2,1)S(1)}, bf16[128,384]{1,0:T(8,128)(2,1)S(1)}, u32[]{:S(2)}, u32[]{:S(2)}) collective-permute-start(bf16[128,384]{1,0:T(8,128)(2,1)S(1)} %bitcast.27), channel_id=1, source_target_pairs={{0,4},{1,5},{2,6},{3,7},{4,0},{5,1},{6,2},{7,3},{8,12},{9,13},{10,... | collective-permute-start | bytes 294920 | tf_op jit(solution)/shard_map/ppermute | solution.py:30
  18.9 4.8 %collective-permute-start.8 = (bf16[128,384]{1,0:T(8,128)(2,1)S(1)}, bf16[128,384]{1,0:T(8,128)(2,1)S(1)}, u32[]{:S(2)}, u32[]{:S(2)}) collective-permute-start(bf16[128,384]{1,0:T(8,128)(2,1)S(1)} %bitcast.30), channel_id=1, source_target_pairs={{0,8},{1,9},{2,10},{3,11},{4,12},{5,13},{6,14},{7,15},{8,0},{9,1},... | collective-permute-start | bytes 294920 | tf_op jit(solution)/shard_map/ppermute | solution.py:30
  19.6 5.6 %collective-permute-start.4 = (bf16[512,128]{1,0:T(8,128)(2,1)S(1)}, bf16[512,128]{1,0:T(8,128)(2,1)S(1)}, u32[]{:S(2)}, u32[]{:S(2)}) collective-permute-start(bf16[512,128]{1,0:T(8,128)(2,1)S(1)} %pad_maximum_fusion.4), channel_id=1, source_target_pairs={{0,2},{1,3},{2,0},{3,1},{4,6},{5,7},{6,4},{7,5},{8,10},{9,11},{10,... | collective-permute-start | bytes 393224 | tf_op jit(solution)/shard_map/ppermute | solution.py:30
  22.0 6.8 %collective-permute-start.11 = (bf16[256,384]{1,0:T(8,128)(2,1)S(1)}, bf16[256,384]{1,0:T(8,128)(2,1)S(1)}, u32[]{:S(2)}, u32[]{:S(2)}) collective-permute-start(bf16[256,384]{1,0:T(8,128)(2,1)S(1)} %pad_maximum_fusion.2), channel_id=1, source_target_pairs={{0,8},{1,9},{2,10},{3,11},{4,12},{5,13},{6,14},{7,15},{8,0},{9,1},... | collective-permute-start | bytes 589832 | tf_op jit(solution)/shard_map/ppermute | solution.py:30
  23.7 5.7 %collective-permute-start.10 = (bf16[256,384]{1,0:T(8,128)(2,1)S(1)}, bf16[256,384]{1,0:T(8,128)(2,1)S(1)}, u32[]{:S(2)}, u32[]{:S(2)}) collective-permute-start(bf16[256,384]{1,0:T(8,128)(2,1)S(1)} %pad_maximum_fusion.1), channel_id=1, source_target_pairs={{0,4},{1,5},{2,6},{3,7},{4,0},{5,1},{6,2},{7,3},{8,12},{9,13},{10,... | collective-permute-start | bytes 589832 | tf_op jit(solution)/shard_map/ppermute | solution.py:30
  25.2 1.6 %collective-permute-start.5 = (bf16[1024,128]{1,0:T(8,128)(2,1)S(1)}, bf16[1024,128]{1,0:T(8,128)(2,1)S(1)}, u32[]{:S(2)}, u32[]{:S(2)}) collective-permute-start(bf16[1024,128]{1,0:T(8,128)(2,1)S(1)} %constant_dynamic-update-slice_fusion.b0_ref), channel_id=1, source_target_pairs={{0,1},{1,0},{2,3},{3,2},{4,5},{5,4},{6,7},{7,6},{8,9},{9,8},{10,11... | collective-permute-start | bytes 786440 | tf_op jit(solution)/shard_map/ppermute | solution.py:30
  25.3 6.0 %collective-permute-start.12 = (bf16[512,384]{1,0:T(8,128)(2,1)S(1)}, bf16[512,384]{1,0:T(8,128)(2,1)S(1)}, u32[]{:S(2)}, u32[]{:S(2)}) collective-permute-start(bf16[512,384]{1,0:T(8,128)(2,1)S(1)} %constant_dynamic-update-slice_fusion.5.g0_ref), channel_id=1, source_target_pairs={{0,1},{1,0},{2,3},{3,2},{4,5},{5,4},{6,7},{7,6},{8,9},{9,8},{10,11... | collective-permute-start | bytes 1179656 | tf_op jit(solution)/shard_map/ppermute | solution.py:30
  26.8 4.5 %copy-start.1 = (bf16[1024,512]{1,0:T(8,128)(2,1)S(1)}, bf16[1024,512]{1,0:T(8,128)(2,1)}, u32[]{:S(2)}) copy-start(bf16[1024,512]{1,0:T(8,128)(2,1)} %grad_ref.3) | copy-start | bytes 3145732
  29.5 1.8 %collective-permute-start.13 = (bf16[512,384]{1,0:T(8,128)(2,1)S(1)}, bf16[512,384]{1,0:T(8,128)(2,1)S(1)}, u32[]{:S(2)}, u32[]{:S(2)}) collective-permute-start(bf16[512,384]{1,0:T(8,128)(2,1)S(1)} %constant_dynamic-update-slice_fusion.9.g1_ref), channel_id=1, source_target_pairs={{0,1},{1,0},{2,3},{3,2},{4,5},{5,4},{6,7},{7,6},{8,9},{9,8},{10,11... | collective-permute-start | bytes 1179656 | tf_op jit(solution)/shard_map/ppermute | solution.py:30
  29.6 1.7 %collective-permute-start.6 = (f32[8,512]{1,0:T(8,128)S(1)}, f32[8,512]{1,0:T(8,128)S(1)}, u32[]{:S(2)}, u32[]{:S(2)}) collective-permute-start(f32[8,512]{1,0:T(8,128)S(1)} %get-tuple-element.86), channel_id=1, source_target_pairs={{0,1},{1,0},{2,3},{3,2},{4,5},{5,4},{6,7},{7,6},{8,9},{9,8},{10,11... | collective-permute-start | bytes 49160 | tf_op jit(solution)/shard_map/ppermute | solution.py:30
  40.7 1.8 %collective-permute-start.14 = (bf16[512,384]{1,0:T(8,128)(2,1)S(1)}, bf16[512,384]{1,0:T(8,128)(2,1)S(1)}, u32[]{:S(2)}, u32[]{:S(2)}) collective-permute-start(bf16[512,384]{1,0:T(8,128)(2,1)S(1)} %get-tuple-element.99), channel_id=1, source_target_pairs={{0,1},{1,0},{2,3},{3,2},{4,5},{5,4},{6,7},{7,6},{8,9},{9,8},{10,11... | collective-permute-start | bytes 1179656 | tf_op jit(solution)/shard_map/ppermute | solution.py:30
  40.8 3.2 %collective-permute-start.15 = (bf16[512,384]{1,0:T(8,128)(2,1)S(1)}, bf16[512,384]{1,0:T(8,128)(2,1)S(1)}, u32[]{:S(2)}, u32[]{:S(2)}) collective-permute-start(bf16[512,384]{1,0:T(8,128)(2,1)S(1)} %get-tuple-element.100), channel_id=1, source_target_pairs={{0,1},{1,0},{2,3},{3,2},{4,5},{5,4},{6,7},{7,6},{8,9},{9,8},{10,11... | collective-permute-start | bytes 1179656 | tf_op jit(solution)/shard_map/ppermute | solution.py:30
  41.7 3.8 %collective-permute-start.16 = (f32[8,512]{1,0:T(8,128)S(1)}, f32[8,512]{1,0:T(8,128)S(1)}, u32[]{:S(2)}, u32[]{:S(2)}) collective-permute-start(f32[8,512]{1,0:T(8,128)S(1)} %get-tuple-element.109), channel_id=1, source_target_pairs={{0,1},{1,0},{2,3},{3,2},{4,5},{5,4},{6,7},{7,6},{8,9},{9,8},{10,11... | collective-permute-start | bytes 49160 | tf_op jit(solution)/shard_map/ppermute | solution.py:30
  42.6 7.0 %collective-permute-start.18 = (bf16[256,384]{1,0:T(8,128)(2,1)S(1)}, bf16[256,384]{1,0:T(8,128)(2,1)S(1)}, u32[]{:S(2)}, u32[]{:S(2)}) collective-permute-start(bf16[256,384]{1,0:T(8,128)(2,1)S(1)} %slice.201), channel_id=1, source_target_pairs={{0,4},{1,5},{2,6},{3,7},{4,0},{5,1},{6,2},{7,3},{8,12},{9,13},{10,... | collective-permute-start | bytes 589832 | tf_op jit(solution)/shard_map/ppermute | solution.py:30
  44.2 6.7 %collective-permute-start.19 = (bf16[256,384]{1,0:T(8,128)(2,1)S(1)}, bf16[256,384]{1,0:T(8,128)(2,1)S(1)}, u32[]{:S(2)}, u32[]{:S(2)}) collective-permute-start(bf16[256,384]{1,0:T(8,128)(2,1)S(1)} %slice.202), channel_id=1, source_target_pairs={{0,8},{1,9},{2,10},{3,11},{4,12},{5,13},{6,14},{7,15},{8,0},{9,1},... | collective-permute-start | bytes 589832 | tf_op jit(solution)/shard_map/ppermute | solution.py:30
  49.0 1.9 %collective-permute-start.17 = (bf16[1056,128]{1,0:T(8,128)(2,1)S(1)}, bf16[1056,128]{1,0:T(8,128)(2,1)S(1)}, u32[]{:S(2)}, u32[]{:S(2)}) collective-permute-start(bf16[1056,128]{1,0:T(8,128)(2,1)S(1)} %get-tuple-element.115), channel_id=1, source_target_pairs={{0,1},{1,0},{2,3},{3,2},{4,5},{5,4},{6,7},{7,6},{8,9},{9,8},{10,11... | collective-permute-start | bytes 811016 | tf_op jit(solution)/shard_map/ppermute | solution.py:30
  51.1 5.5 %collective-permute-start.20 = (bf16[544,128]{1,0:T(8,128)(2,1)S(1)}, bf16[544,128]{1,0:T(8,128)(2,1)S(1)}, u32[]{:S(2)}, u32[]{:S(2)}) collective-permute-start(bf16[544,128]{1,0:T(8,128)(2,1)S(1)} %pad_maximum_fusion.3), channel_id=1, source_target_pairs={{0,2},{1,3},{2,0},{3,1},{4,6},{5,7},{6,4},{7,5},{8,10},{9,11},{10,... | collective-permute-start | bytes 417800 | tf_op jit(solution)/shard_map/ppermute | solution.py:30
  52.7 6.9 %collective-permute-start.24 = (bf16[128,384]{1,0:T(8,128)(2,1)S(1)}, bf16[128,384]{1,0:T(8,128)(2,1)S(1)}, u32[]{:S(2)}, u32[]{:S(2)}) collective-permute-start(bf16[128,384]{1,0:T(8,128)(2,1)S(1)} %slice.204), channel_id=1, source_target_pairs={{0,8},{1,9},{2,10},{3,11},{4,12},{5,13},{6,14},{7,15},{8,0},{9,1},... | collective-permute-start | bytes 294920 | tf_op jit(solution)/shard_map/ppermute | solution.py:30
  54.3 5.2 %collective-permute-start.25 = (bf16[128,384]{1,0:T(8,128)(2,1)S(1)}, bf16[128,384]{1,0:T(8,128)(2,1)S(1)}, u32[]{:S(2)}, u32[]{:S(2)}) collective-permute-start(bf16[128,384]{1,0:T(8,128)(2,1)S(1)} %slice.206), channel_id=1, source_target_pairs={{0,4},{1,5},{2,6},{3,7},{4,0},{5,1},{6,2},{7,3},{8,12},{9,13},{10,... | collective-permute-start | bytes 294920 | tf_op jit(solution)/shard_map/ppermute | solution.py:30
  56.7 4.4 %collective-permute-start.21 = (bf16[288,128]{1,0:T(8,128)(2,1)S(1)}, bf16[288,128]{1,0:T(8,128)(2,1)S(1)}, u32[]{:S(2)}, u32[]{:S(2)}) collective-permute-start(bf16[288,128]{1,0:T(8,128)(2,1)S(1)} %pad_maximum_fusion.8), channel_id=1, source_target_pairs={{0,4},{1,5},{2,6},{3,7},{4,0},{5,1},{6,2},{7,3},{8,12},{9,13},{10,... | collective-permute-start | bytes 221192 | tf_op jit(solution)/shard_map/ppermute | solution.py:30
  59.7 4.7 %collective-permute-start.26 = (bf16[128,384]{1,0:T(8,128)(2,1)S(1)}, bf16[128,384]{1,0:T(8,128)(2,1)S(1)}, u32[]{:S(2)}, u32[]{:S(2)}) collective-permute-start(bf16[128,384]{1,0:T(8,128)(2,1)S(1)} %pad_maximum_fusion.6), channel_id=1, source_target_pairs={{0,2},{1,3},{2,0},{3,1},{4,6},{5,7},{6,4},{7,5},{8,10},{9,11},{10,... | collective-permute-start | bytes 294920 | tf_op jit(solution)/shard_map/ppermute | solution.py:30
  61.2 4.1 %collective-permute-start.22 = (bf16[160,128]{1,0:T(8,128)(2,1)S(1)}, bf16[160,128]{1,0:T(8,128)(2,1)S(1)}, u32[]{:S(2)}, u32[]{:S(2)}) collective-permute-start(bf16[160,128]{1,0:T(8,128)(2,1)S(1)} %pad_maximum_fusion.10), channel_id=1, source_target_pairs={{0,8},{1,9},{2,10},{3,11},{4,12},{5,13},{6,14},{7,15},{8,0},{9,1},... | collective-permute-start | bytes 122888 | tf_op jit(solution)/shard_map/ppermute | solution.py:30
  64.4 5.6 %collective-permute-start.27 = (bf16[64,384]{1,0:T(8,128)(2,1)S(1)}, bf16[64,384]{1,0:T(8,128)(2,1)S(1)}, u32[]{:S(2)}, u32[]{:S(2)}) collective-permute-start(bf16[64,384]{1,0:T(8,128)(2,1)S(1)} %bitcast.35), channel_id=1, source_target_pairs={{0,16},{1,17},{2,18},{3,19},{4,20},{5,21},{6,22},{7,23},{8,24},{9,... | collective-permute-start | bytes 147464 | tf_op jit(solution)/shard_map/ppermute | solution.py:30
  65.3 4.9 %collective-permute-start.23 = (bf16[96,128]{1,0:T(8,128)(2,1)S(1)}, bf16[96,128]{1,0:T(8,128)(2,1)S(1)}, u32[]{:S(2)}, u32[]{:S(2)}) collective-permute-start(bf16[96,128]{1,0:T(8,128)(2,1)S(1)} %pad_maximum_fusion.11), channel_id=1, source_target_pairs={{0,16},{1,17},{2,18},{3,19},{4,20},{5,21},{6,22},{7,23},{8,24},{9,... | collective-permute-start | bytes 73736 | tf_op jit(solution)/shard_map/ppermute | solution.py:30

commit v8 on v7

--- a/solution.py
+++ b/solution.py
@@ -261,7 +261,9 @@
         ]
 
 
-def token_kernel(plan, me_ref, x_ref, segments_ref, stats_ref, masks_ref, flags_ref):
+def token_kernel(
+    plan, me_ref, x_ref, segments_ref, stats_ref, masks_ref, turn_ref, regroup_ref, flags_ref
+):
     shard = me_ref[0] & (plan.tensor - 1)
     ids = segments_ref[...]
     count = ids.shape[0]
@@ -275,6 +277,8 @@
     flags_ref[1] = jnp.where((position < SEQ_LEN - 1) & (ids == after), 1.0, 0.0)
     flags_ref[2] = jnp.where(ids > 0, 1.0, 0.0)
     turn = turn_matrix()
+    turn_ref[...] = turn.astype(BF16)
+    regroup_ref[...] = regroup_matrix(plan.states, plan.tensor)
     plain = jnp.where(grid_index((TILE, TILE), 0) == grid_index((TILE, TILE), 1), 1.0, 0.0)
     ones = jnp.ones((TILE, LANES), BF16)
     per_tile = TILE // LANES
@@ -319,7 +323,7 @@
 
 
 def enter_kernel(
-    plan, me_ref, x_ref, stats_ref, b0_ref, b1_ref, vec_ref, masks_ref,
+    plan, me_ref, x_ref, stats_ref, b0_ref, b1_ref, vec_ref, masks_ref, turn_ref, regroup_ref,
     normed_ref, source_ref, ends_ref, hold_ref, carry_ref, input_map_ref, params_ref,
     pack_ref,
 ):
@@ -329,7 +333,7 @@
         [(0, 2 * plan.own_states, pack_ref, 0)],
     )
     input_map_ref[...] = dot(
-        pack_ref[...].astype(BF16), regroup_matrix(states, plan.tensor)
+        pack_ref[...].astype(BF16), regroup_ref[...]
     ).astype(BF16)
     vectors = read_vectors(vec_ref)
     gain, shift = vectors[0:1], vectors[1:2]
@@ -350,7 +354,7 @@
         axis=0,
     )
     gamma_pair = jnp.concatenate([gamma, gamma], axis=1)
-    turn = turn_matrix().astype(BF16)
+    turn = turn_ref[...]
 
     def rows_step(index, _):
         at = plan.block_rows(index)
@@ -372,7 +376,7 @@
 
 def middle_kernel(
     plan, me_ref, x_ref, grad_ref, normed_ref, source_ref, ends_ref, hold_ref, carry_ref,
-    g0_ref, g1_ref, g2_ref, g3_ref, vec_ref, params_ref, masks_ref,
+    g0_ref, g1_ref, g2_ref, g3_ref, vec_ref, params_ref, masks_ref, turn_ref, regroup_ref,
     mixed_ref, hidden_ref, lru_grad_ref, state_grad_ref, act_ref, unit_grad_ref, low_ref, sums_ref,
     pack_ref, wpack_ref, out_map_ref,
 ):
@@ -387,7 +391,7 @@
     for order, base, rows, first in half_blocks(plan, plan.up_crossed, len(block_refs)):
         collect(plan, me_ref[0], order[::-1], block_refs, base, rows, first, targets)
     sign = jnp.where(grid_index((1, 2 * states), 1) < states, 1.0, -1.0)
-    regroup = regroup_matrix(states, plan.tensor)
+    regroup = regroup_ref[...]
     out_map_ref[...] = (dot(pack_ref[...].astype(BF16), regroup) * sign).astype(BF16)
     rate = (params_ref[0:1, :states], params_ref[0:1, states:])
     start = received(carry_ref, me_ref[0] & 1 == 1, states)
@@ -413,7 +417,7 @@
     skip = vectors[2:3]
     biases = jnp.concatenate([vectors[3:4], vectors[4:5]], axis=1)
     sums_ref[...] = jnp.zeros_like(sums_ref)
-    turn = turn_matrix().astype(BF16)
+    turn = turn_ref[...]
 
     def rows_step(index, _):
         at = plan.block_rows(index)
@@ -467,7 +471,7 @@
 
 
 def weight_kernel(
-    plan, me_ref, act_ref, unit_grad_ref, lru_grad_ref, low_ref, *refs
+    plan, me_ref, act_ref, unit_grad_ref, lru_grad_ref, low_ref, regroup_ref, *refs
 ):
     outs, (full_ref, out_ref) = refs[:-2], refs[-2:]
     states, features, units = plan.states, plan.features, plan.units
@@ -475,7 +479,7 @@
     sign = jnp.where(grid_index((1, 2 * states), 1) < states, 1.0, -1.0)
     full_ref[...] = dot(act_ref[...], unit_grad_ref[...], 0, 0)
     out_grad = dot(lru_grad_ref[...], low_ref[...], 0, 0) * sign
-    out_ref[...] = dot(out_grad.astype(BF16), regroup_matrix(states, plan.tensor), 1, 1)
+    out_ref[...] = dot(out_grad.astype(BF16), regroup_ref[...], 1, 1)
     targets = [
         (0, pair, out_ref, 0),
         (pair, units, full_ref, 0),
@@ -489,6 +493,7 @@
 def leave_kernel(
     plan, me_ref, x_ref, stats_ref, normed_ref, source_ref, ends_ref, hold_ref, carry_ref, hidden_ref,
     state_grad_ref, lru_grad_ref, input_map_ref, vec_ref, params_ref, masks_ref, sums_ref,
+    turn_ref, regroup_ref,
     keep_ref, send_ref, normed_grad_ref,
     drive_grad_ref, low_ref, full_ref,
 ):
@@ -534,7 +539,7 @@
     vectors = read_vectors(vec_ref)
     skip = vectors[2:3]
     gain_sum = jnp.zeros((8, features), F32)
-    turn = turn_matrix().astype(BF16)
+    turn = turn_ref[...]
 
     def rows_step(index, sums):
         gain_sum, shift_sum = sums
@@ -548,7 +553,7 @@
 
     gain_sum, shift_sum = lax.fori_loop(0, plan.blocks, rows_step, (gain_sum, gain_sum))
     into = dot(normed_ref[...], low_ref[...], 0, 0)
-    full_ref[...] = dot(into.astype(BF16), regroup_matrix(states, plan.tensor), 1, 1)
+    full_ref[...] = dot(into.astype(BF16), regroup_ref[...], 1, 1)
     distribute(
         plan, me_ref[0], plan.down, (keep_ref, send_ref), 0, plan.own_rows, 0,
         [(0, 2 * plan.own_states, full_ref, 0)],
@@ -757,10 +762,15 @@
         me, *matrices, *lines,
         far_in=14,
     )
-    stats, masks = call(
+    stats, masks, turn, regroup = call(
         token_kernel,
         plan,
-        [shape((2, rows, LANES)), shape((4, rows, LANES))],
+        [
+            shape((2, rows, LANES)),
+            shape((4, rows, LANES)),
+            shape((TILE, TILE), BF16),
+            shape((2 * states, 2 * states), BF16),
+        ],
         [pltpu.VMEM((3, plan.group_rows // LANES, LANES), F32)],
         8,
         2,
@@ -785,7 +795,7 @@
         [pltpu.VMEM((features, 2 * states), pack_type)],
         8,
         0.3,
-        me, block_input, stats, b0, b1, vectors, masks,
+        me, block_input, stats, b0, b1, vectors, masks, turn, regroup,
     )
 
     left = carry
@@ -817,7 +827,7 @@
         24,
         10,
         me, block_input, out_grad, normed, source, ends, hold, carry,
-        held, came, held_other, came_other, vectors, params, masks,
+        held, came, held_other, came_other, vectors, params, masks, turn, regroup,
     )
     half_rows = plan.count // 2 * long
     pieces = plan.halves
@@ -831,7 +841,7 @@
         ],
         10,
         2.5,
-        me, act, unit_grad, lru_grad, low,
+        me, act, unit_grad, lru_grad, low, regroup,
     )
     w_keeps, w_sends = outs[::2], outs[1::2]
     w_others = [flip(send, 0, plan.count) for send in w_sends]
@@ -866,7 +876,7 @@
         14,
         4.5,
         me, block_input, stats, normed, source, back_ends, back_hold, back, hidden,
-        state_grad, lru_grad, input_map, vectors, params, masks, sums,
+        state_grad, lru_grad, input_map, vectors, params, masks, sums, turn, regroup,
     )
     w_others = [after(other, b_keep) for other in w_others]
     halves = [cut(added(half[0], other)) for half, other in zip(halves, w_others)]

time: 71.7 us -> 71.5 us (level)
  transfers between devices with their start and end apart: 28 -> 28, of which waited for: 19 -> 18; matrix products, arithmetic and copies ran while one was open for 1% -> 1% of each run, Pallas kernels for 13% -> 13%
where the time goes in v8:
time: 71.5 us; the launch traced here: 71.3 us
  starting transfers between devices  28.7 us (40%)
  Pallas kernels  20.7 us (29%)
  waiting for transfers between devices  19.5 us (27%)
  between operations  1.25 us (2%)
  other arithmetic  0.73 us (1%)
    ppermute x28, starting transfers between devices, flip(): return lax.ppermute(value, AXES, [(i, i ^ 1 << bit) for i in range(count)])  28.7 us
    pallas_call x9, Pallas kernels, call(): pl.pallas_call(functools.partial(kernel, plan), out_shape=outs, in_specs=...  20.7 us
    ppermute x28, waiting for transfers between devices, flip(): return lax.ppermute(value, AXES, [(i, i ^ 1 << bit) for i in range(count)])  19.5 us
  transfers between devices with their start and end apart: 28, of which 18 were waited for; matrix products, arithmetic and copies ran while one was open for 1% of the time, Pallas kernels for 13%

profile of v8, /device:TPU:0, one launch (start us, length us, event | category | flops | bytes accessed | tf_op | source)
XLA Modules:
  0.0 71.3 jit_solution(3222185619514559902)
XLA Ops:
  0.7 1.1 %shard_map.289 = (bf16[96,128]{1,0:T(8,128)(2,1)S(1)}, bf16[64,384]{1,0:T(8,128)(2,1)S(1)}) custom-call(s32[1]{0:T(128)} %bitcast.me_ref, bf16[64,64]{1,0:T(8,128)(2,1)} %refs_0_.1, bf16[64,64]{1,0:T(8,128)(2,1)} %refs_1_.1, bf16[64,64]{1,0:T(8,128)(2,1)} %refs_2_.1, bf16[64,64]{1,0:T(8,128)(2,1)} %refs_3_.1, bf16[64,128]{1,0:T(8,128)(2,1)} %refs_4_.1, ...), custom_call_target="tpu_custom_call" | custom-call | flops 1500000000 | bytes 5250000 | tf_op jit(solution)/shard_map/pallas_call | solution.py:637
  1.8 4.1 %collective-permute-start = (bf16[96,128]{1,0:T(8,128)(2,1)S(1)}, bf16[96,128]{1,0:T(8,128)(2,1)S(1)}, u32[]{:S(2)}, u32[]{:S(2)}) collective-permute-start(bf16[96,128]{1,0:T(8,128)(2,1)S(1)} %get-tuple-element.80), channel_id=1, source_target_pairs={{0,16},{1,17},{2,18},{3,19},{4,20},{5,21},{6,22},{7,23},{8,24},{9,... | collective-permute-start | bytes 73736 | tf_op jit(solution)/shard_map/ppermute | solution.py:30
  6.0 1.2 %shard_map.288 = (f32[2,1024,128]{2,1,0:T(8,128)S(1)}, f32[4,1024,128]{2,1,0:T(8,128)S(1)}, bf16[256,256]{1,0:T(8,128)(2,1)S(1)}, bf16[512,512]{1,0:T(8,128)(2,1)S(1)}) custom-call(s32[1]{0:T(128)} %bitcast.me_ref, bf16[1024,512]{1,0:T(8,128)(2,1)S(1)} %copy-done, s32[32,128]{1,0:T(8,128)S(1)} %bitcast.26), custom_call_target="tpu_custom_call" | custom-call | flops 2000000000 | bytes 7000000 | tf_op jit(solution)/shard_map/pallas_call | solution.py:637
  7.2 0.5 collective-permute-done
  7.7 3.3 %collective-permute-done.1 = bf16[64,384]{1,0:T(8,128)(2,1)S(1)} collective-permute-done((bf16[64,384]{1,0:T(8,128)(2,1)S(1)}, bf16[64,384]{1,0:T(8,128)(2,1)S(1)}, u32[]{:S(2)}, u32[]{:S(2)}) %collective-permute-start.1) | collective-permute-done | bytes 49184 | tf_op jit(solution)/shard_map/ppermute | solution.py:30
  11.0 1.5 %collective-permute-start.2 = (bf16[160,128]{1,0:T(8,128)(2,1)S(1)}, bf16[160,128]{1,0:T(8,128)(2,1)S(1)}, u32[]{:S(2)}, u32[]{:S(2)}) collective-permute-start(bf16[160,128]{1,0:T(8,128)(2,1)S(1)} %pad_maximum_fusion.9), channel_id=1, source_target_pairs={{0,8},{1,9},{2,10},{3,11},{4,12},{5,13},{6,14},{7,15},{8,0},{9,1},... | collective-permute-start | bytes 122888 | tf_op jit(solution)/shard_map/ppermute | solution.py:30
  12.6 1.6 %collective-permute-start.7 = (bf16[128,384]{1,0:T(8,128)(2,1)S(1)}, bf16[128,384]{1,0:T(8,128)(2,1)S(1)}, u32[]{:S(2)}, u32[]{:S(2)}) collective-permute-start(bf16[128,384]{1,0:T(8,128)(2,1)S(1)} %pad_maximum_fusion.5), channel_id=1, source_target_pairs={{0,2},{1,3},{2,0},{3,1},{4,6},{5,7},{6,4},{7,5},{8,10},{9,11},{10,... | collective-permute-start | bytes 294920 | tf_op jit(solution)/shard_map/ppermute | solution.py:30
  14.1 1.0 %collective-permute-done.2 = bf16[160,128]{1,0:T(8,128)(2,1)S(1)} collective-permute-done((bf16[160,128]{1,0:T(8,128)(2,1)S(1)}, bf16[160,128]{1,0:T(8,128)(2,1)S(1)}, u32[]{:S(2)}, u32[]{:S(2)}) %collective-permute-start.2) | collective-permute-done | bytes 40992 | tf_op jit(solution)/shard_map/ppermute | solution.py:30
  15.1 1.6 %collective-permute-start.3 = (bf16[288,128]{1,0:T(8,128)(2,1)S(1)}, bf16[288,128]{1,0:T(8,128)(2,1)S(1)}, u32[]{:S(2)}, u32[]{:S(2)}) collective-permute-start(bf16[288,128]{1,0:T(8,128)(2,1)S(1)} %pad_maximum_fusion.7), channel_id=1, source_target_pairs={{0,4},{1,5},{2,6},{3,7},{4,0},{5,1},{6,2},{7,3},{8,12},{9,13},{10,... | collective-permute-start | bytes 221192 | tf_op jit(solution)/shard_map/ppermute | solution.py:30
  16.7 0.5 collective-permute-done.7
  17.3 1.6 %collective-permute-start.9 = (bf16[128,384]{1,0:T(8,128)(2,1)S(1)}, bf16[128,384]{1,0:T(8,128)(2,1)S(1)}, u32[]{:S(2)}, u32[]{:S(2)}) collective-permute-start(bf16[128,384]{1,0:T(8,128)(2,1)S(1)} %bitcast.27), channel_id=1, source_target_pairs={{0,4},{1,5},{2,6},{3,7},{4,0},{5,1},{6,2},{7,3},{8,12},{9,13},{10,... | collective-permute-start | bytes 294920 | tf_op jit(solution)/shard_map/ppermute | solution.py:30
  18.9 0.6 collective-permute-start.8
  19.6 1.6 %collective-permute-start.4 = (bf16[512,128]{1,0:T(8,128)(2,1)S(1)}, bf16[512,128]{1,0:T(8,128)(2,1)S(1)}, u32[]{:S(2)}, u32[]{:S(2)}) collective-permute-start(bf16[512,128]{1,0:T(8,128)(2,1)S(1)} %pad_maximum_fusion.4), channel_id=1, source_target_pairs={{0,2},{1,3},{2,0},{3,1},{4,6},{5,7},{6,4},{7,5},{8,10},{9,11},{10,... | collective-permute-start | bytes 393224 | tf_op jit(solution)/shard_map/ppermute | solution.py:30
  21.2 0.8 %collective-permute-done.9 = bf16[128,384]{1,0:T(8,128)(2,1)S(1)} collective-permute-done((bf16[128,384]{1,0:T(8,128)(2,1)S(1)}, bf16[128,384]{1,0:T(8,128)(2,1)S(1)}, u32[]{:S(2)}, u32[]{:S(2)}) %collective-permute-start.9) | collective-permute-done | bytes 98336 | tf_op jit(solution)/shard_map/ppermute | solution.py:30
  22.0 1.6 %collective-permute-start.11 = (bf16[256,384]{1,0:T(8,128)(2,1)S(1)}, bf16[256,384]{1,0:T(8,128)(2,1)S(1)}, u32[]{:S(2)}, u32[]{:S(2)}) collective-permute-start(bf16[256,384]{1,0:T(8,128)(2,1)S(1)} %pad_maximum_fusion.2), channel_id=1, source_target_pairs={{0,8},{1,9},{2,10},{3,11},{4,12},{5,13},{6,14},{7,15},{8,0},{9,1},... | collective-permute-start | bytes 589832 | tf_op jit(solution)/shard_map/ppermute | solution.py:30
  23.7 1.5 %collective-permute-start.10 = (bf16[256,384]{1,0:T(8,128)(2,1)S(1)}, bf16[256,384]{1,0:T(8,128)(2,1)S(1)}, u32[]{:S(2)}, u32[]{:S(2)}) collective-permute-start(bf16[256,384]{1,0:T(8,128)(2,1)S(1)} %pad_maximum_fusion.1), channel_id=1, source_target_pairs={{0,4},{1,5},{2,6},{3,7},{4,0},{5,1},{6,2},{7,3},{8,12},{9,13},{10,... | collective-permute-start | bytes 589832 | tf_op jit(solution)/shard_map/ppermute | solution.py:30
  25.3 0.6 collective-permute-start.12
  25.9 0.9 %collective-permute-done.5.b1_ref = bf16[1024,128]{1,0:T(8,128)(2,1)S(1)} collective-permute-done((bf16[1024,128]{1,0:T(8,128)(2,1)S(1)}, bf16[1024,128]{1,0:T(8,128)(2,1)S(1)}, u32[]{:S(2)}, u32[]{:S(2)}) %collective-permute-start.5) | collective-permute-done | bytes 262176 | tf_op jit(solution)/shard_map/ppermute | solution.py:30
  26.8 1.9 %shard_map.290 = (bf16[1024,512]{1,0:T(8,128)(2,1)S(1)}, f32[1024,512]{1,0:T(8,128)S(1)}, f32[64,512]{1,0:T(8,128)S(1)}, f32[64,128]{1,0:T(8,128)S(1)}, f32[8,51...) custom-call(s32[1]{0:T(128)} %bitcast.me_ref, bf16[1024,512]{1,0:T(8,128)(2,1)S(1)} %copy-done, ...), custom_call_target="tpu_custom_call" | custom-call | flops 300000000 | bytes 1050000 | tf_op jit(solution)/shard_map/pallas_call | solution.py:637
  28.7 0.7 %collective-permute-done.10 = bf16[256,384]{1,0:T(8,128)(2,1)S(1)} collective-permute-done((bf16[256,384]{1,0:T(8,128)(2,1)S(1)}, bf16[256,384]{1,0:T(8,128)(2,1)S(1)}, u32[]{:S(2)}, u32[]{:S(2)}) %collective-permute-start.10) | collective-permute-done | bytes 196640 | tf_op jit(solution)/shard_map/ppermute | solution.py:30
  29.6 0.5 collective-permute-start.6
  30.1 1.2 %collective-permute-done.6.carry_ref = f32[8,512]{1,0:T(8,128)S(1)} collective-permute-done((f32[8,512]{1,0:T(8,128)S(1)}, f32[8,512]{1,0:T(8,128)S(1)}, u32[]{:S(2)}, u32[]{:S(2)}) %collective-permute-start.6) | collective-permute-done | bytes 16416 | tf_op jit(solution)/shard_map/ppermute | solution.py:30
  31.3 6.4 %shard_map.291 = (bf16[1024,512]{1,0:T(8,128)(2,1)}, f32[1024,512]{1,0:T(8,128)S(1)}, bf16[1024,512]{1,0:T(8,128)(2,1)S(1)}, f32[1024,512]{1,0:T(8,128)S(1)}, bf...) custom-call(s32[1]{0:T(128)} %bitcast.me_ref, ...), custom_call_target="tpu_custom_call" | custom-call | flops 10000000000 | bytes 35000000 | tf_op jit(solution)/shard_map/pallas_call | solution.py:637
  37.8 2.7 %shard_map.292 = (bf16[512,384]{1,0:T(8,128)(2,1)S(1)}, bf16[512,384]{1,0:T(8,128)(2,1)S(1)}, bf16[512,384]{1,0:T(8,128)(2,1)S(1)}, bf16[512,384]{1,0:T(8,128)(2,1)S(1)}) custom-call(s32[1]{0:T(128)} %bitcast.me_ref, bf16[1024,512]{1,0:T(8,128)(2,1)S(1)} %get-tuple-element.99.act_ref, bf16[1024,1024]{1,0:T(8,128)(2,1)S(1)} %get-tuple-element.100.unit_grad_ref, ...), custom_call_target="tpu_custom_call" | custom-call | flops 2500000000 | bytes 8750000 | tf_op jit(solution)/shard_map/pallas_call | solution.py:637
  40.4 0.2 collective-permute-start.14
  40.6 0.4 collective-permute-start.15
  41.0 0.5 shard_map.293
  41.5 0.2 collective-permute-start.16
  41.7 0.5 collective-permute-done.14
  42.4 1.5 %collective-permute-start.18 = (bf16[256,384]{1,0:T(8,128)(2,1)S(1)}, bf16[256,384]{1,0:T(8,128)(2,1)S(1)}, u32[]{:S(2)}, u32[]{:S(2)}) collective-permute-start(bf16[256,384]{1,0:T(8,128)(2,1)S(1)} %slice.201), channel_id=1, source_target_pairs={{0,4},{1,5},{2,6},{3,7},{4,0},{5,1},{6,2},{7,3},{8,12},{9,13},{10,... | collective-permute-start | bytes 589832 | tf_op jit(solution)/shard_map/ppermute | solution.py:30
  44.0 1.4 %collective-permute-start.19 = (bf16[256,384]{1,0:T(8,128)(2,1)S(1)}, bf16[256,384]{1,0:T(8,128)(2,1)S(1)}, u32[]{:S(2)}, u32[]{:S(2)}) collective-permute-start(bf16[256,384]{1,0:T(8,128)(2,1)S(1)} %slice.202), channel_id=1, source_target_pairs={{0,8},{1,9},{2,10},{3,11},{4,12},{5,13},{6,14},{7,15},{8,0},{9,1},... | collective-permute-start | bytes 589832 | tf_op jit(solution)/shard_map/ppermute | solution.py:30
  45.3 3.4 %shard_map.294 = (bf16[1024,128]{1,0:T(8,128)(2,1)S(1)}, bf16[1056,128]{1,0:T(8,128)(2,1)S(1)}, f32[1024,512]{1,0:T(8,128)S(1)}) custom-call(s32[1]{0:T(128)} %bitcast.me_ref, bf16[1024,512]{1,0:T(8,128)(2,1)S(1)} %copy-done, f32[2,1024,128]{2,1,0:T(8,128)S(1)} %get-tuple-element.79.stats_ref, bf16[1024,512]{1,0:T(8,128)(2,1)S(1)} %get-tuple-element.86.normed_ref, ...), custom_call_target="tpu_custom_call" | custom-call | flops 4499999744 | bytes 15750000 | tf_op jit(solution)/shard_map/pallas_call | solution.py:637
  48.9 0.5 collective-permute-done.18
  49.5 1.2 %collective-permute-done.19 = bf16[256,384]{1,0:T(8,128)(2,1)S(1)} collective-permute-done((bf16[256,384]{1,0:T(8,128)(2,1)S(1)}, bf16[256,384]{1,0:T(8,128)(2,1)S(1)}, u32[]{:S(2)}, u32[]{:S(2)}) %collective-permute-start.19) | collective-permute-done | bytes 196640 | tf_op jit(solution)/shard_map/ppermute | solution.py:30
  50.9 1.6 %collective-permute-start.20 = (bf16[544,128]{1,0:T(8,128)(2,1)S(1)}, bf16[544,128]{1,0:T(8,128)(2,1)S(1)}, u32[]{:S(2)}, u32[]{:S(2)}) collective-permute-start(bf16[544,128]{1,0:T(8,128)(2,1)S(1)} %pad_maximum_fusion.3), channel_id=1, source_target_pairs={{0,2},{1,3},{2,0},{3,1},{4,6},{5,7},{6,4},{7,5},{8,10},{9,11},{10,... | collective-permute-start | bytes 417800 | tf_op jit(solution)/shard_map/ppermute | solution.py:30
  52.5 1.6 %collective-permute-start.24 = (bf16[128,384]{1,0:T(8,128)(2,1)S(1)}, bf16[128,384]{1,0:T(8,128)(2,1)S(1)}, u32[]{:S(2)}, u32[]{:S(2)}) collective-permute-start(bf16[128,384]{1,0:T(8,128)(2,1)S(1)} %slice.204), channel_id=1, source_target_pairs={{0,8},{1,9},{2,10},{3,11},{4,12},{5,13},{6,14},{7,15},{8,0},{9,1},... | collective-permute-start | bytes 294920 | tf_op jit(solution)/shard_map/ppermute | solution.py:30
  54.1 0.6 collective-permute-start.25
  54.7 1.6 %collective-permute-done.20 = bf16[544,128]{1,0:T(8,128)(2,1)S(1)} collective-permute-done((bf16[544,128]{1,0:T(8,128)(2,1)S(1)}, bf16[544,128]{1,0:T(8,128)(2,1)S(1)}, u32[]{:S(2)}, u32[]{:S(2)}) %collective-permute-start.20) | collective-permute-done | bytes 139296 | tf_op jit(solution)/shard_map/ppermute | solution.py:30
  56.4 0.4 collective-permute-start.21
  56.9 2.6 %collective-permute-done.25 = bf16[128,384]{1,0:T(8,128)(2,1)S(1)} collective-permute-done((bf16[128,384]{1,0:T(8,128)(2,1)S(1)}, bf16[128,384]{1,0:T(8,128)(2,1)S(1)}, u32[]{:S(2)}, u32[]{:S(2)}) %collective-permute-start.25) | collective-permute-done | bytes 98336 | tf_op jit(solution)/shard_map/ppermute | solution.py:30
  59.7 1.2 %collective-permute-done.21 = bf16[288,128]{1,0:T(8,128)(2,1)S(1)} collective-permute-done((bf16[288,128]{1,0:T(8,128)(2,1)S(1)}, bf16[288,128]{1,0:T(8,128)(2,1)S(1)}, u32[]{:S(2)}, u32[]{:S(2)}) %collective-permute-start.21) | collective-permute-done | bytes 73760 | tf_op jit(solution)/shard_map/ppermute | solution.py:30
  60.9 1.1 %collective-permute-start.22 = (bf16[160,128]{1,0:T(8,128)(2,1)S(1)}, bf16[160,128]{1,0:T(8,128)(2,1)S(1)}, u32[]{:S(2)}, u32[]{:S(2)}) collective-permute-start(bf16[160,128]{1,0:T(8,128)(2,1)S(1)} %pad_maximum_fusion.10), channel_id=1, source_target_pairs={{0,8},{1,9},{2,10},{3,11},{4,12},{5,13},{6,14},{7,15},{8,0},{9,1},... | collective-permute-start | bytes 122888 | tf_op jit(solution)/shard_map/ppermute | solution.py:30
  62.0 2.3 %collective-permute-done.26 = bf16[128,384]{1,0:T(8,128)(2,1)S(1)} collective-permute-done((bf16[128,384]{1,0:T(8,128)(2,1)S(1)}, bf16[128,384]{1,0:T(8,128)(2,1)S(1)}, u32[]{:S(2)}, u32[]{:S(2)}) %collective-permute-start.26) | collective-permute-done | bytes 98336 | tf_op jit(solution)/shard_map/ppermute | solution.py:30
  64.3 0.4 collective-permute-start.27
  64.7 0.3 collective-permute-done.22
  65.0 2.4 %collective-permute-start.23 = (bf16[96,128]{1,0:T(8,128)(2,1)S(1)}, bf16[96,128]{1,0:T(8,128)(2,1)S(1)}, u32[]{:S(2)}, u32[]{:S(2)}) collective-permute-start(bf16[96,128]{1,0:T(8,128)(2,1)S(1)} %pad_maximum_fusion.11), channel_id=1, source_target_pairs={{0,16},{1,17},{2,18},{3,19},{4,20},{5,21},{6,22},{7,23},{8,24},{9,... | collective-permute-start | bytes 73736 | tf_op jit(solution)/shard_map/ppermute | solution.py:30
  67.5 2.4 %shard_map.295 = f32[1024,512]{1,0:T(8,128)} custom-call(s32[1]{0:T(128)} %bitcast.me_ref, bf16[1024,512]{1,0:T(8,128)(2,1)S(1)} %copy-done, f32[2,1024,128]{2,1,0:T(8,128)S(1)} %get-tuple-element.79.stats_ref, bf16[1024,512]{1,0:T(8,128)(2,1)S(1)} %copy-done.1, f32[1024,512]{1,0:T(8,128)S(1)} %get-tuple-element.123.normed_grad_ref, ...), custom_call_target="tpu_custom_call" | custom-call | flops 2500000000 | bytes 8750000 | tf_op jit(solution)/shard_map/pallas_call | solution.py:637
  70.0 1.1 %shard_map.296 = (f32[64,64]{1,0:T(8,128)}, f32[64,64]{1,0:T(8,128)}, f32[64,64]{1,0:T(8,128)}, f32[64,64]{1,0:T(8,128)}, f32[64,128]{1,0:T(8,128)}, /*index=5*/...) custom-call(s32[1]{0:T(128)} %bitcast.me_ref, ...), custom_call_target="tpu_custom_call" | custom-call | flops 2000000000 | bytes 7000000 | tf_op jit(solution)/shard_map/pallas_call | solution.py:637
  (79 shorter events, 1.8 us)
Async XLA Ops:
  0.7 5.3 %copy-start = (bf16[1024,512]{1,0:T(8,128)(2,1)S(1)}, bf16[1024,512]{1,0:T(8,128)(2,1)}, u32[]{:S(2)}) copy-start(bf16[1024,512]{1,0:T(8,128)(2,1)} %x_ref.9) | copy-start | bytes 3145732
  0.7 5.3 %copy-start.2 = (s32[4096]{0:T(1024)S(1)}, s32[4096]{0:T(1024)}, u32[]{:S(2)}) copy-start(s32[4096]{0:T(1024)} %param.18) | copy-start | bytes 49156
  1.8 5.9 %collective-permute-start = (bf16[96,128]{1,0:T(8,128)(2,1)S(1)}, bf16[96,128]{1,0:T(8,128)(2,1)S(1)}, u32[]{:S(2)}, u32[]{:S(2)}) collective-permute-start(bf16[96,128]{1,0:T(8,128)(2,1)S(1)} %get-tuple-element.80), channel_id=1, source_target_pairs={{0,16},{1,17},{2,18},{3,19},{4,20},{5,21},{6,22},{7,23},{8,24},{9,... | collective-permute-start | bytes 73736 | tf_op jit(solution)/shard_map/ppermute | solution.py:30
  5.9 5.1 %collective-permute-start.1 = (bf16[64,384]{1,0:T(8,128)(2,1)S(1)}, bf16[64,384]{1,0:T(8,128)(2,1)S(1)}, u32[]{:S(2)}, u32[]{:S(2)}) collective-permute-start(bf16[64,384]{1,0:T(8,128)(2,1)S(1)} %get-tuple-element.82), channel_id=1, source_target_pairs={{0,16},{1,17},{2,18},{3,19},{4,20},{5,21},{6,22},{7,23},{8,24},{9,... | collective-permute-start | bytes 147464 | tf_op jit(solution)/shard_map/ppermute | solution.py:30
  11.0 4.1 %collective-permute-start.2 = (bf16[160,128]{1,0:T(8,128)(2,1)S(1)}, bf16[160,128]{1,0:T(8,128)(2,1)S(1)}, u32[]{:S(2)}, u32[]{:S(2)}) collective-permute-start(bf16[160,128]{1,0:T(8,128)(2,1)S(1)} %pad_maximum_fusion.9), channel_id=1, source_target_pairs={{0,8},{1,9},{2,10},{3,11},{4,12},{5,13},{6,14},{7,15},{8,0},{9,1},... | collective-permute-start | bytes 122888 | tf_op jit(solution)/shard_map/ppermute | solution.py:30
  12.6 4.7 %collective-permute-start.7 = (bf16[128,384]{1,0:T(8,128)(2,1)S(1)}, bf16[128,384]{1,0:T(8,128)(2,1)S(1)}, u32[]{:S(2)}, u32[]{:S(2)}) collective-permute-start(bf16[128,384]{1,0:T(8,128)(2,1)S(1)} %pad_maximum_fusion.5), channel_id=1, source_target_pairs={{0,2},{1,3},{2,0},{3,1},{4,6},{5,7},{6,4},{7,5},{8,10},{9,11},{10,... | collective-permute-start | bytes 294920 | tf_op jit(solution)/shard_map/ppermute | solution.py:30
  15.1 4.4 %collective-permute-start.3 = (bf16[288,128]{1,0:T(8,128)(2,1)S(1)}, bf16[288,128]{1,0:T(8,128)(2,1)S(1)}, u32[]{:S(2)}, u32[]{:S(2)}) collective-permute-start(bf16[288,128]{1,0:T(8,128)(2,1)S(1)} %pad_maximum_fusion.7), channel_id=1, source_target_pairs={{0,4},{1,5},{2,6},{3,7},{4,0},{5,1},{6,2},{7,3},{8,12},{9,13},{10,... | collective-permute-start | bytes 221192 | tf_op jit(solution)/shard_map/ppermute | solution.py:30
  17.3 4.7 %collective-permute-start.9 = (bf16[128,384]{1,0:T(8,128)(2,1)S(1)}, bf16[128,384]{1,0:T(8,128)(2,1)S(1)}, u32[]{:S(2)}, u32[]{:S(2)}) collective-permute-start(bf16[128,384]{1,0:T(8,128)(2,1)S(1)} %bitcast.27), channel_id=1, source_target_pairs={{0,4},{1,5},{2,6},{3,7},{4,0},{5,1},{6,2},{7,3},{8,12},{9,13},{10,... | collective-permute-start | bytes 294920 | tf_op jit(solution)/shard_map/ppermute | solution.py:30
  18.9 4.8 %collective-permute-start.8 = (bf16[128,384]{1,0:T(8,128)(2,1)S(1)}, bf16[128,384]{1,0:T(8,128)(2,1)S(1)}, u32[]{:S(2)}, u32[]{:S(2)}) collective-permute-start(bf16[128,384]{1,0:T(8,128)(2,1)S(1)} %bitcast.30), channel_id=1, source_target_pairs={{0,8},{1,9},{2,10},{3,11},{4,12},{5,13},{6,14},{7,15},{8,0},{9,1},... | collective-permute-start | bytes 294920 | tf_op jit(solution)/shard_map/ppermute | solution.py:30
  19.6 5.6 %collective-permute-start.4 = (bf16[512,128]{1,0:T(8,128)(2,1)S(1)}, bf16[512,128]{1,0:T(8,128)(2,1)S(1)}, u32[]{:S(2)}, u32[]{:S(2)}) collective-permute-start(bf16[512,128]{1,0:T(8,128)(2,1)S(1)} %pad_maximum_fusion.4), channel_id=1, source_target_pairs={{0,2},{1,3},{2,0},{3,1},{4,6},{5,7},{6,4},{7,5},{8,10},{9,11},{10,... | collective-permute-start | bytes 393224 | tf_op jit(solution)/shard_map/ppermute | solution.py:30
  22.0 6.7 %collective-permute-start.11 = (bf16[256,384]{1,0:T(8,128)(2,1)S(1)}, bf16[256,384]{1,0:T(8,128)(2,1)S(1)}, u32[]{:S(2)}, u32[]{:S(2)}) collective-permute-start(bf16[256,384]{1,0:T(8,128)(2,1)S(1)} %pad_maximum_fusion.2), channel_id=1, source_target_pairs={{0,8},{1,9},{2,10},{3,11},{4,12},{5,13},{6,14},{7,15},{8,0},{9,1},... | collective-permute-start | bytes 589832 | tf_op jit(solution)/shard_map/ppermute | solution.py:30
  23.7 5.7 %collective-permute-start.10 = (bf16[256,384]{1,0:T(8,128)(2,1)S(1)}, bf16[256,384]{1,0:T(8,128)(2,1)S(1)}, u32[]{:S(2)}, u32[]{:S(2)}) collective-permute-start(bf16[256,384]{1,0:T(8,128)(2,1)S(1)} %pad_maximum_fusion.1), channel_id=1, source_target_pairs={{0,4},{1,5},{2,6},{3,7},{4,0},{5,1},{6,2},{7,3},{8,12},{9,13},{10,... | collective-permute-start | bytes 589832 | tf_op jit(solution)/shard_map/ppermute | solution.py:30
  25.2 1.6 %collective-permute-start.5 = (bf16[1024,128]{1,0:T(8,128)(2,1)S(1)}, bf16[1024,128]{1,0:T(8,128)(2,1)S(1)}, u32[]{:S(2)}, u32[]{:S(2)}) collective-permute-start(bf16[1024,128]{1,0:T(8,128)(2,1)S(1)} %constant_dynamic-update-slice_fusion.b0_ref), channel_id=1, source_target_pairs={{0,1},{1,0},{2,3},{3,2},{4,5},{5,4},{6,7},{7,6},{8,9},{9,8},{10,11... | collective-permute-start | bytes 786440 | tf_op jit(solution)/shard_map/ppermute | solution.py:30
  25.3 6.0 %collective-permute-start.12 = (bf16[512,384]{1,0:T(8,128)(2,1)S(1)}, bf16[512,384]{1,0:T(8,128)(2,1)S(1)}, u32[]{:S(2)}, u32[]{:S(2)}) collective-permute-start(bf16[512,384]{1,0:T(8,128)(2,1)S(1)} %constant_dynamic-update-slice_fusion.5.g0_ref), channel_id=1, source_target_pairs={{0,1},{1,0},{2,3},{3,2},{4,5},{5,4},{6,7},{7,6},{8,9},{9,8},{10,11... | collective-permute-start | bytes 1179656 | tf_op jit(solution)/shard_map/ppermute | solution.py:30
  26.8 4.5 %copy-start.1 = (bf16[1024,512]{1,0:T(8,128)(2,1)S(1)}, bf16[1024,512]{1,0:T(8,128)(2,1)}, u32[]{:S(2)}) copy-start(bf16[1024,512]{1,0:T(8,128)(2,1)} %grad_ref.3) | copy-start | bytes 3145732
  29.5 1.8 %collective-permute-start.13 = (bf16[512,384]{1,0:T(8,128)(2,1)S(1)}, bf16[512,384]{1,0:T(8,128)(2,1)S(1)}, u32[]{:S(2)}, u32[]{:S(2)}) collective-permute-start(bf16[512,384]{1,0:T(8,128)(2,1)S(1)} %constant_dynamic-update-slice_fusion.9.g1_ref), channel_id=1, source_target_pairs={{0,1},{1,0},{2,3},{3,2},{4,5},{5,4},{6,7},{7,6},{8,9},{9,8},{10,11... | collective-permute-start | bytes 1179656 | tf_op jit(solution)/shard_map/ppermute | solution.py:30
  29.6 1.7 %collective-permute-start.6 = (f32[8,512]{1,0:T(8,128)S(1)}, f32[8,512]{1,0:T(8,128)S(1)}, u32[]{:S(2)}, u32[]{:S(2)}) collective-permute-start(f32[8,512]{1,0:T(8,128)S(1)} %get-tuple-element.90), channel_id=1, source_target_pairs={{0,1},{1,0},{2,3},{3,2},{4,5},{5,4},{6,7},{7,6},{8,9},{9,8},{10,11... | collective-permute-start | bytes 49160 | tf_op jit(solution)/shard_map/ppermute | solution.py:30
  40.4 1.8 %collective-permute-start.14 = (bf16[512,384]{1,0:T(8,128)(2,1)S(1)}, bf16[512,384]{1,0:T(8,128)(2,1)S(1)}, u32[]{:S(2)}, u32[]{:S(2)}) collective-permute-start(bf16[512,384]{1,0:T(8,128)(2,1)S(1)} %get-tuple-element.103), channel_id=1, source_target_pairs={{0,1},{1,0},{2,3},{3,2},{4,5},{5,4},{6,7},{7,6},{8,9},{9,8},{10,11... | collective-permute-start | bytes 1179656 | tf_op jit(solution)/shard_map/ppermute | solution.py:30
  40.6 3.2 %collective-permute-start.15 = (bf16[512,384]{1,0:T(8,128)(2,1)S(1)}, bf16[512,384]{1,0:T(8,128)(2,1)S(1)}, u32[]{:S(2)}, u32[]{:S(2)}) collective-permute-start(bf16[512,384]{1,0:T(8,128)(2,1)S(1)} %get-tuple-element.104), channel_id=1, source_target_pairs={{0,1},{1,0},{2,3},{3,2},{4,5},{5,4},{6,7},{7,6},{8,9},{9,8},{10,11... | collective-permute-start | bytes 1179656 | tf_op jit(solution)/shard_map/ppermute | solution.py:30
  41.5 3.8 %collective-permute-start.16 = (f32[8,512]{1,0:T(8,128)S(1)}, f32[8,512]{1,0:T(8,128)S(1)}, u32[]{:S(2)}, u32[]{:S(2)}) collective-permute-start(f32[8,512]{1,0:T(8,128)S(1)} %get-tuple-element.113), channel_id=1, source_target_pairs={{0,1},{1,0},{2,3},{3,2},{4,5},{5,4},{6,7},{7,6},{8,9},{9,8},{10,11... | collective-permute-start | bytes 49160 | tf_op jit(solution)/shard_map/ppermute | solution.py:30
  42.4 7.0 %collective-permute-start.18 = (bf16[256,384]{1,0:T(8,128)(2,1)S(1)}, bf16[256,384]{1,0:T(8,128)(2,1)S(1)}, u32[]{:S(2)}, u32[]{:S(2)}) collective-permute-start(bf16[256,384]{1,0:T(8,128)(2,1)S(1)} %slice.201), channel_id=1, source_target_pairs={{0,4},{1,5},{2,6},{3,7},{4,0},{5,1},{6,2},{7,3},{8,12},{9,13},{10,... | collective-permute-start | bytes 589832 | tf_op jit(solution)/shard_map/ppermute | solution.py:30
  44.0 6.7 %collective-permute-start.19 = (bf16[256,384]{1,0:T(8,128)(2,1)S(1)}, bf16[256,384]{1,0:T(8,128)(2,1)S(1)}, u32[]{:S(2)}, u32[]{:S(2)}) collective-permute-start(bf16[256,384]{1,0:T(8,128)(2,1)S(1)} %slice.202), channel_id=1, source_target_pairs={{0,8},{1,9},{2,10},{3,11},{4,12},{5,13},{6,14},{7,15},{8,0},{9,1},... | collective-permute-start | bytes 589832 | tf_op jit(solution)/shard_map/ppermute | solution.py:30
  48.8 2.0 %collective-permute-start.17 = (bf16[1056,128]{1,0:T(8,128)(2,1)S(1)}, bf16[1056,128]{1,0:T(8,128)(2,1)S(1)}, u32[]{:S(2)}, u32[]{:S(2)}) collective-permute-start(bf16[1056,128]{1,0:T(8,128)(2,1)S(1)} %get-tuple-element.119), channel_id=1, source_target_pairs={{0,1},{1,0},{2,3},{3,2},{4,5},{5,4},{6,7},{7,6},{8,9},{9,8},{10,11... | collective-permute-start | bytes 811016 | tf_op jit(solution)/shard_map/ppermute | solution.py:30
  50.9 5.4 %collective-permute-start.20 = (bf16[544,128]{1,0:T(8,128)(2,1)S(1)}, bf16[544,128]{1,0:T(8,128)(2,1)S(1)}, u32[]{:S(2)}, u32[]{:S(2)}) collective-permute-start(bf16[544,128]{1,0:T(8,128)(2,1)S(1)} %pad_maximum_fusion.3), channel_id=1, source_target_pairs={{0,2},{1,3},{2,0},{3,1},{4,6},{5,7},{6,4},{7,5},{8,10},{9,11},{10,... | collective-permute-start | bytes 417800 | tf_op jit(solution)/shard_map/ppermute | solution.py:30
  52.5 7.1 %collective-permute-start.24 = (bf16[128,384]{1,0:T(8,128)(2,1)S(1)}, bf16[128,384]{1,0:T(8,128)(2,1)S(1)}, u32[]{:S(2)}, u32[]{:S(2)}) collective-permute-start(bf16[128,384]{1,0:T(8,128)(2,1)S(1)} %slice.204), channel_id=1, source_target_pairs={{0,8},{1,9},{2,10},{3,11},{4,12},{5,13},{6,14},{7,15},{8,0},{9,1},... | collective-permute-start | bytes 294920 | tf_op jit(solution)/shard_map/ppermute | solution.py:30
  54.1 5.4 %collective-permute-start.25 = (bf16[128,384]{1,0:T(8,128)(2,1)S(1)}, bf16[128,384]{1,0:T(8,128)(2,1)S(1)}, u32[]{:S(2)}, u32[]{:S(2)}) collective-permute-start(bf16[128,384]{1,0:T(8,128)(2,1)S(1)} %slice.206), channel_id=1, source_target_pairs={{0,4},{1,5},{2,6},{3,7},{4,0},{5,1},{6,2},{7,3},{8,12},{9,13},{10,... | collective-permute-start | bytes 294920 | tf_op jit(solution)/shard_map/ppermute | solution.py:30
  56.4 4.4 %collective-permute-start.21 = (bf16[288,128]{1,0:T(8,128)(2,1)S(1)}, bf16[288,128]{1,0:T(8,128)(2,1)S(1)}, u32[]{:S(2)}, u32[]{:S(2)}) collective-permute-start(bf16[288,128]{1,0:T(8,128)(2,1)S(1)} %pad_maximum_fusion.8), channel_id=1, source_target_pairs={{0,4},{1,5},{2,6},{3,7},{4,0},{5,1},{6,2},{7,3},{8,12},{9,13},{10,... | collective-permute-start | bytes 221192 | tf_op jit(solution)/shard_map/ppermute | solution.py:30
  59.6 4.7 %collective-permute-start.26 = (bf16[128,384]{1,0:T(8,128)(2,1)S(1)}, bf16[128,384]{1,0:T(8,128)(2,1)S(1)}, u32[]{:S(2)}, u32[]{:S(2)}) collective-permute-start(bf16[128,384]{1,0:T(8,128)(2,1)S(1)} %pad_maximum_fusion.6), channel_id=1, source_target_pairs={{0,2},{1,3},{2,0},{3,1},{4,6},{5,7},{6,4},{7,5},{8,10},{9,11},{10,... | collective-permute-start | bytes 294920 | tf_op jit(solution)/shard_map/ppermute | solution.py:30
  60.9 4.1 %collective-permute-start.22 = (bf16[160,128]{1,0:T(8,128)(2,1)S(1)}, bf16[160,128]{1,0:T(8,128)(2,1)S(1)}, u32[]{:S(2)}, u32[]{:S(2)}) collective-permute-start(bf16[160,128]{1,0:T(8,128)(2,1)S(1)} %pad_maximum_fusion.10), channel_id=1, source_target_pairs={{0,8},{1,9},{2,10},{3,11},{4,12},{5,13},{6,14},{7,15},{8,0},{9,1},... | collective-permute-start | bytes 122888 | tf_op jit(solution)/shard_map/ppermute | solution.py:30
  64.3 5.5 %collective-permute-start.27 = (bf16[64,384]{1,0:T(8,128)(2,1)S(1)}, bf16[64,384]{1,0:T(8,128)(2,1)S(1)}, u32[]{:S(2)}, u32[]{:S(2)}) collective-permute-start(bf16[64,384]{1,0:T(8,128)(2,1)S(1)} %bitcast.35), channel_id=1, source_target_pairs={{0,16},{1,17},{2,18},{3,19},{4,20},{5,21},{6,22},{7,23},{8,24},{9,... | collective-permute-start | bytes 147464 | tf_op jit(solution)/shard_map/ppermute | solution.py:30
  65.0 5.0 %collective-permute-start.23 = (bf16[96,128]{1,0:T(8,128)(2,1)S(1)}, bf16[96,128]{1,0:T(8,128)(2,1)S(1)}, u32[]{:S(2)}, u32[]{:S(2)}) collective-permute-start(bf16[96,128]{1,0:T(8,128)(2,1)S(1)} %pad_maximum_fusion.11), channel_id=1, source_target_pairs={{0,16},{1,17},{2,18},{3,19},{4,20},{5,21},{6,22},{7,23},{8,24},{9,... | collective-permute-start | bytes 73736 | tf_op jit(solution)/shard_map/ppermute | solution.py:30

commit v9 on v8

--- a/solution.py
+++ b/solution.py
@@ -262,7 +262,8 @@
 
 
 def token_kernel(
-    plan, me_ref, x_ref, segments_ref, stats_ref, masks_ref, turn_ref, regroup_ref, flags_ref
+    plan, me_ref, x_ref, segments_ref, stats_ref, masks_ref, turn_ref, regroup_ref, standard_ref,
+    flags_ref,
 ):
     shard = me_ref[0] & (plan.tensor - 1)
     ids = segments_ref[...]
@@ -298,17 +299,15 @@
         mean = jnp.mean(values, axis=1, keepdims=True)
         centred = values - mean
         inverse = lax.rsqrt(jnp.mean(centred * centred, axis=1, keepdims=True) + norm_epsilon)
-        stats_ref[0, at, :] = jnp.broadcast_to(mean, (plan.block, LANES))
-        stats_ref[1, at, :] = jnp.broadcast_to(inverse, (plan.block, LANES))
+        standard_ref[at, :] = centred * inverse
+        stats_ref[0, at, :] = jnp.broadcast_to(inverse, (plan.block, LANES))
         return 0
 
     lax.fori_loop(0, plan.blocks, rows_step, 0)
 
 
-def standard_rows(plan, x_ref, stats_ref, at):
-    mean = wide(stats_ref[0, at, :], plan.features)
-    inverse = wide(stats_ref[1, at, :], plan.features)
-    return (x_ref[at, :].astype(F32) - mean) * inverse, inverse
+def standard_rows(plan, standard_ref, stats_ref, at):
+    return standard_ref[at, :], wide(stats_ref[0, at, :], plan.features)
 
 
 def read_vectors(vec_ref):
@@ -762,14 +761,15 @@
         me, *matrices, *lines,
         far_in=14,
     )
-    stats, masks, turn, regroup = call(
+    stats, masks, turn, regroup, standard = call(
         token_kernel,
         plan,
         [
-            shape((2, rows, LANES)),
+            shape((1, rows, LANES)),
             shape((4, rows, LANES)),
             shape((TILE, TILE), BF16),
             shape((2 * states, 2 * states), BF16),
+            shape((rows, features)),
         ],
         [pltpu.VMEM((3, plan.group_rows // LANES, LANES), F32)],
         8,
@@ -795,7 +795,7 @@
         [pltpu.VMEM((features, 2 * states), pack_type)],
         8,
         0.3,
-        me, block_input, stats, b0, b1, vectors, masks, turn, regroup,
+        me, standard, stats, b0, b1, vectors, masks, turn, regroup,
     )
 
     left = carry
@@ -875,7 +875,7 @@
         ],
         14,
         4.5,
-        me, block_input, stats, normed, source, back_ends, back_hold, back, hidden,
+        me, standard, stats, normed, source, back_ends, back_hold, back, hidden,
         state_grad, lru_grad, input_map, vectors, params, masks, sums, turn, regroup,
     )
     w_others = [after(other, b_keep) for other in w_others]
@@ -906,7 +906,7 @@
         [],
         8,
         2.5,
-        me, block_input, stats, out_grad, after(normed_grad, b_send), vectors,
+        me, standard, stats, out_grad, after(normed_grad, b_send), vectors,
     )
     w_mine = added(w_keep, w_other)
     b_other = after(flip(b_send, plan.bits - 1, plan.count), w_mine, input_grad)

time: 71.5 us -> 71.4 us (level)
  no operation moved by 1% of the time
where the time goes in v9:
time: 71.4 us; the launch traced here: 71.2 us
  starting transfers between devices  29 us (41%)
  Pallas kernels  20.6 us (29%)
  waiting for transfers between devices  19.3 us (27%)
  between operations  1.25 us (2%)
  other arithmetic  0.73 us (1%)
    ppermute x28, starting transfers between devices, flip(): return lax.ppermute(value, AXES, [(i, i ^ 1 << bit) for i in range(count)])  29 us
    pallas_call x9, Pallas kernels, call(): pl.pallas_call(functools.partial(kernel, plan), out_shape=outs, in_specs=...  20.6 us
    ppermute x28, waiting for transfers between devices, flip(): return lax.ppermute(value, AXES, [(i, i ^ 1 << bit) for i in range(count)])  19.3 us
  transfers between devices with their start and end apart: 28, of which 18 were waited for; matrix products, arithmetic and copies ran while one was open for 1% of the time, Pallas kernels for 13%

profile of v9, /device:TPU:0, one launch (start us, length us, event | category | flops | bytes accessed | tf_op | source)
XLA Modules:
  0.0 71.2 jit_solution(9601606351754041182)
XLA Ops:
  0.7 1.1 %shard_map.289 = (bf16[96,128]{1,0:T(8,128)(2,1)S(1)}, bf16[64,384]{1,0:T(8,128)(2,1)S(1)}) custom-call(s32[1]{0:T(128)} %bitcast.me_ref, bf16[64,64]{1,0:T(8,128)(2,1)} %refs_0_.1, bf16[64,64]{1,0:T(8,128)(2,1)} %refs_1_.1, bf16[64,64]{1,0:T(8,128)(2,1)} %refs_2_.1, bf16[64,64]{1,0:T(8,128)(2,1)} %refs_3_.1, bf16[64,128]{1,0:T(8,128)(2,1)} %refs_4_.1, ...), custom_call_target="tpu_custom_call" | custom-call | flops 1500000000 | bytes 5250000 | tf_op jit(solution)/shard_map/pallas_call | solution.py:636
  1.8 4.1 %collective-permute-start = (bf16[96,128]{1,0:T(8,128)(2,1)S(1)}, bf16[96,128]{1,0:T(8,128)(2,1)S(1)}, u32[]{:S(2)}, u32[]{:S(2)}) collective-permute-start(bf16[96,128]{1,0:T(8,128)(2,1)S(1)} %get-tuple-element.82), channel_id=1, source_target_pairs={{0,16},{1,17},{2,18},{3,19},{4,20},{5,21},{6,22},{7,23},{8,24},{9,... | collective-permute-start | bytes 73736 | tf_op jit(solution)/shard_map/ppermute | solution.py:30
  6.0 1.4 %shard_map.288 = (f32[1,1024,128]{2,1,0:T(8,128)S(1)}, f32[4,1024,128]{2,1,0:T(8,128)S(1)}, bf16[256,256]{1,0:T(8,128)(2,1)S(1)}, bf16[512,512]{1,0:T(8,128)(2,1)S(1)}, f32[1024,512]{1,0:T(8,128)S(1)}) custom-call(s32[1]{0:T(128)} %bitcast.me_ref, bf16[1024,512]{1,0:T(8,128)(2,1)S(1)} %copy-done, s32[32,128]{1,0:T(8,128)S(1)} %bitcast.26), custom_call_target="tpu_custom_call" | custom-call | flops 2000000000 | bytes 7000000 | tf_op jit(solution)/shard_map/pallas_call | solution.py:636
  7.4 0.3 collective-permute-done
  7.7 3.3 %collective-permute-done.1 = bf16[64,384]{1,0:T(8,128)(2,1)S(1)} collective-permute-done((bf16[64,384]{1,0:T(8,128)(2,1)S(1)}, bf16[64,384]{1,0:T(8,128)(2,1)S(1)}, u32[]{:S(2)}, u32[]{:S(2)}) %collective-permute-start.1) | collective-permute-done | bytes 49184 | tf_op jit(solution)/shard_map/ppermute | solution.py:30
  11.0 1.5 %collective-permute-start.2 = (bf16[160,128]{1,0:T(8,128)(2,1)S(1)}, bf16[160,128]{1,0:T(8,128)(2,1)S(1)}, u32[]{:S(2)}, u32[]{:S(2)}) collective-permute-start(bf16[160,128]{1,0:T(8,128)(2,1)S(1)} %pad_maximum_fusion.9), channel_id=1, source_target_pairs={{0,8},{1,9},{2,10},{3,11},{4,12},{5,13},{6,14},{7,15},{8,0},{9,1},... | collective-permute-start | bytes 122888 | tf_op jit(solution)/shard_map/ppermute | solution.py:30
  12.6 1.6 %collective-permute-start.7 = (bf16[128,384]{1,0:T(8,128)(2,1)S(1)}, bf16[128,384]{1,0:T(8,128)(2,1)S(1)}, u32[]{:S(2)}, u32[]{:S(2)}) collective-permute-start(bf16[128,384]{1,0:T(8,128)(2,1)S(1)} %pad_maximum_fusion.5), channel_id=1, source_target_pairs={{0,2},{1,3},{2,0},{3,1},{4,6},{5,7},{6,4},{7,5},{8,10},{9,11},{10,... | collective-permute-start | bytes 294920 | tf_op jit(solution)/shard_map/ppermute | solution.py:30
  14.1 1.0 %collective-permute-done.2 = bf16[160,128]{1,0:T(8,128)(2,1)S(1)} collective-permute-done((bf16[160,128]{1,0:T(8,128)(2,1)S(1)}, bf16[160,128]{1,0:T(8,128)(2,1)S(1)}, u32[]{:S(2)}, u32[]{:S(2)}) %collective-permute-start.2) | collective-permute-done | bytes 40992 | tf_op jit(solution)/shard_map/ppermute | solution.py:30
  15.1 1.6 %collective-permute-start.3 = (bf16[288,128]{1,0:T(8,128)(2,1)S(1)}, bf16[288,128]{1,0:T(8,128)(2,1)S(1)}, u32[]{:S(2)}, u32[]{:S(2)}) collective-permute-start(bf16[288,128]{1,0:T(8,128)(2,1)S(1)} %pad_maximum_fusion.7), channel_id=1, source_target_pairs={{0,4},{1,5},{2,6},{3,7},{4,0},{5,1},{6,2},{7,3},{8,12},{9,13},{10,... | collective-permute-start | bytes 221192 | tf_op jit(solution)/shard_map/ppermute | solution.py:30
  16.7 0.5 collective-permute-done.7
  17.3 1.6 %collective-permute-start.9 = (bf16[128,384]{1,0:T(8,128)(2,1)S(1)}, bf16[128,384]{1,0:T(8,128)(2,1)S(1)}, u32[]{:S(2)}, u32[]{:S(2)}) collective-permute-start(bf16[128,384]{1,0:T(8,128)(2,1)S(1)} %bitcast.27), channel_id=1, source_target_pairs={{0,4},{1,5},{2,6},{3,7},{4,0},{5,1},{6,2},{7,3},{8,12},{9,13},{10,... | collective-permute-start | bytes 294920 | tf_op jit(solution)/shard_map/ppermute | solution.py:30
  18.9 0.6 collective-permute-start.8
  19.6 1.6 %collective-permute-start.4 = (bf16[512,128]{1,0:T(8,128)(2,1)S(1)}, bf16[512,128]{1,0:T(8,128)(2,1)S(1)}, u32[]{:S(2)}, u32[]{:S(2)}) collective-permute-start(bf16[512,128]{1,0:T(8,128)(2,1)S(1)} %pad_maximum_fusion.4), channel_id=1, source_target_pairs={{0,2},{1,3},{2,0},{3,1},{4,6},{5,7},{6,4},{7,5},{8,10},{9,11},{10,... | collective-permute-start | bytes 393224 | tf_op jit(solution)/shard_map/ppermute | solution.py:30
  21.2 0.8 %collective-permute-done.9 = bf16[128,384]{1,0:T(8,128)(2,1)S(1)} collective-permute-done((bf16[128,384]{1,0:T(8,128)(2,1)S(1)}, bf16[128,384]{1,0:T(8,128)(2,1)S(1)}, u32[]{:S(2)}, u32[]{:S(2)}) %collective-permute-start.9) | collective-permute-done | bytes 98336 | tf_op jit(solution)/shard_map/ppermute | solution.py:30
  22.0 1.6 %collective-permute-start.11 = (bf16[256,384]{1,0:T(8,128)(2,1)S(1)}, bf16[256,384]{1,0:T(8,128)(2,1)S(1)}, u32[]{:S(2)}, u32[]{:S(2)}) collective-permute-start(bf16[256,384]{1,0:T(8,128)(2,1)S(1)} %pad_maximum_fusion.2), channel_id=1, source_target_pairs={{0,8},{1,9},{2,10},{3,11},{4,12},{5,13},{6,14},{7,15},{8,0},{9,1},... | collective-permute-start | bytes 589832 | tf_op jit(solution)/shard_map/ppermute | solution.py:30
  23.7 1.5 %collective-permute-start.10 = (bf16[256,384]{1,0:T(8,128)(2,1)S(1)}, bf16[256,384]{1,0:T(8,128)(2,1)S(1)}, u32[]{:S(2)}, u32[]{:S(2)}) collective-permute-start(bf16[256,384]{1,0:T(8,128)(2,1)S(1)} %pad_maximum_fusion.1), channel_id=1, source_target_pairs={{0,4},{1,5},{2,6},{3,7},{4,0},{5,1},{6,2},{7,3},{8,12},{9,13},{10,... | collective-permute-start | bytes 589832 | tf_op jit(solution)/shard_map/ppermute | solution.py:30
  25.3 0.6 collective-permute-start.12
  25.9 0.9 %collective-permute-done.5.b1_ref = bf16[1024,128]{1,0:T(8,128)(2,1)S(1)} collective-permute-done((bf16[1024,128]{1,0:T(8,128)(2,1)S(1)}, bf16[1024,128]{1,0:T(8,128)(2,1)S(1)}, u32[]{:S(2)}, u32[]{:S(2)}) %collective-permute-start.5) | collective-permute-done | bytes 262176 | tf_op jit(solution)/shard_map/ppermute | solution.py:30
  26.8 1.8 %shard_map.290 = (bf16[1024,512]{1,0:T(8,128)(2,1)S(1)}, f32[1024,512]{1,0:T(8,128)S(1)}, f32[64,512]{1,0:T(8,128)S(1)}, f32[64,128]{1,0:T(8,128)S(1)}, f32[8,51...) custom-call(s32[1]{0:T(128)} %bitcast.me_ref, f32[1024,512]{1,0:T(8,128)S(1)} %get-tuple-element.80.x_ref, ...), custom_call_target="tpu_custom_call" | custom-call | flops 300000000 | bytes 1050000 | tf_op jit(solution)/shard_map/pallas_call | solution.py:636
  28.6 0.8 %collective-permute-done.10 = bf16[256,384]{1,0:T(8,128)(2,1)S(1)} collective-permute-done((bf16[256,384]{1,0:T(8,128)(2,1)S(1)}, bf16[256,384]{1,0:T(8,128)(2,1)S(1)}, u32[]{:S(2)}, u32[]{:S(2)}) %collective-permute-start.10) | collective-permute-done | bytes 196640 | tf_op jit(solution)/shard_map/ppermute | solution.py:30
  29.6 0.5 collective-permute-start.6
  30.1 1.2 %collective-permute-done.6.carry_ref = f32[8,512]{1,0:T(8,128)S(1)} collective-permute-done((f32[8,512]{1,0:T(8,128)S(1)}, f32[8,512]{1,0:T(8,128)S(1)}, u32[]{:S(2)}, u32[]{:S(2)}) %collective-permute-start.6) | collective-permute-done | bytes 16416 | tf_op jit(solution)/shard_map/ppermute | solution.py:30
  31.3 6.4 %shard_map.291 = (bf16[1024,512]{1,0:T(8,128)(2,1)}, f32[1024,512]{1,0:T(8,128)S(1)}, bf16[1024,512]{1,0:T(8,128)(2,1)S(1)}, f32[1024,512]{1,0:T(8,128)S(1)}, bf...) custom-call(s32[1]{0:T(128)} %bitcast.me_ref, ...), custom_call_target="tpu_custom_call" | custom-call | flops 10000000000 | bytes 35000000 | tf_op jit(solution)/shard_map/pallas_call | solution.py:636
  37.8 2.7 %shard_map.292 = (bf16[512,384]{1,0:T(8,128)(2,1)S(1)}, bf16[512,384]{1,0:T(8,128)(2,1)S(1)}, bf16[512,384]{1,0:T(8,128)(2,1)S(1)}, bf16[512,384]{1,0:T(8,128)(2,1)S(1)}) custom-call(s32[1]{0:T(128)} %bitcast.me_ref, bf16[1024,512]{1,0:T(8,128)(2,1)S(1)} %get-tuple-element.101.act_ref, bf16[1024,1024]{1,0:T(8,128)(2,1)S(1)} %get-tuple-element.102.unit_grad_ref, ...), custom_call_target="tpu_custom_call" | custom-call | flops 2500000000 | bytes 8750000 | tf_op jit(solution)/shard_map/pallas_call | solution.py:636
  40.5 0.2 collective-permute-start.14
  40.7 0.4 collective-permute-start.15
  41.0 0.5 shard_map.293
  41.5 0.2 collective-permute-start.16
  41.7 0.5 collective-permute-done.14
  42.4 1.5 %collective-permute-start.18 = (bf16[256,384]{1,0:T(8,128)(2,1)S(1)}, bf16[256,384]{1,0:T(8,128)(2,1)S(1)}, u32[]{:S(2)}, u32[]{:S(2)}) collective-permute-start(bf16[256,384]{1,0:T(8,128)(2,1)S(1)} %slice.201), channel_id=1, source_target_pairs={{0,4},{1,5},{2,6},{3,7},{4,0},{5,1},{6,2},{7,3},{8,12},{9,13},{10,... | collective-permute-start | bytes 589832 | tf_op jit(solution)/shard_map/ppermute | solution.py:30
  44.0 1.4 %collective-permute-start.19 = (bf16[256,384]{1,0:T(8,128)(2,1)S(1)}, bf16[256,384]{1,0:T(8,128)(2,1)S(1)}, u32[]{:S(2)}, u32[]{:S(2)}) collective-permute-start(bf16[256,384]{1,0:T(8,128)(2,1)S(1)} %slice.202), channel_id=1, source_target_pairs={{0,8},{1,9},{2,10},{3,11},{4,12},{5,13},{6,14},{7,15},{8,0},{9,1},... | collective-permute-start | bytes 589832 | tf_op jit(solution)/shard_map/ppermute | solution.py:30
  45.4 3.3 %shard_map.294 = (bf16[1024,128]{1,0:T(8,128)(2,1)S(1)}, bf16[1056,128]{1,0:T(8,128)(2,1)S(1)}, f32[1024,512]{1,0:T(8,128)S(1)}) custom-call(s32[1]{0:T(128)} %bitcast.me_ref, f32[1024,512]{1,0:T(8,128)S(1)} %get-tuple-element.80.x_ref, f32[1,1024,128]{2,1,0:T(8,128)S(1)} %get-tuple-element.81.stats_ref, bf16[1024,512]{1,0:T(8,128)(2,1)S(1)} %get-tuple-element.88.normed_ref, ...), custom_call_target="tpu_custom_call" | custom-call | flops 4499999744 | bytes 15750000 | tf_op jit(solution)/shard_map/pallas_call | solution.py:636
  48.8 0.6 collective-permute-done.18
  49.5 1.2 %collective-permute-done.19 = bf16[256,384]{1,0:T(8,128)(2,1)S(1)} collective-permute-done((bf16[256,384]{1,0:T(8,128)(2,1)S(1)}, bf16[256,384]{1,0:T(8,128)(2,1)S(1)}, u32[]{:S(2)}, u32[]{:S(2)}) %collective-permute-start.19) | collective-permute-done | bytes 196640 | tf_op jit(solution)/shard_map/ppermute | solution.py:30
  50.9 1.6 %collective-permute-start.20 = (bf16[544,128]{1,0:T(8,128)(2,1)S(1)}, bf16[544,128]{1,0:T(8,128)(2,1)S(1)}, u32[]{:S(2)}, u32[]{:S(2)}) collective-permute-start(bf16[544,128]{1,0:T(8,128)(2,1)S(1)} %pad_maximum_fusion.3), channel_id=1, source_target_pairs={{0,2},{1,3},{2,0},{3,1},{4,6},{5,7},{6,4},{7,5},{8,10},{9,11},{10,... | collective-permute-start | bytes 417800 | tf_op jit(solution)/shard_map/ppermute | solution.py:30
  52.5 1.6 %collective-permute-start.24 = (bf16[128,384]{1,0:T(8,128)(2,1)S(1)}, bf16[128,384]{1,0:T(8,128)(2,1)S(1)}, u32[]{:S(2)}, u32[]{:S(2)}) collective-permute-start(bf16[128,384]{1,0:T(8,128)(2,1)S(1)} %slice.204), channel_id=1, source_target_pairs={{0,8},{1,9},{2,10},{3,11},{4,12},{5,13},{6,14},{7,15},{8,0},{9,1},... | collective-permute-start | bytes 294920 | tf_op jit(solution)/shard_map/ppermute | solution.py:30
  54.1 0.6 collective-permute-start.25
  54.7 1.5 %collective-permute-done.20 = bf16[544,128]{1,0:T(8,128)(2,1)S(1)} collective-permute-done((bf16[544,128]{1,0:T(8,128)(2,1)S(1)}, bf16[544,128]{1,0:T(8,128)(2,1)S(1)}, u32[]{:S(2)}, u32[]{:S(2)}) %collective-permute-start.20) | collective-permute-done | bytes 139296 | tf_op jit(solution)/shard_map/ppermute | solution.py:30
  56.3 0.5 collective-permute-start.21
  56.8 2.7 %collective-permute-done.25 = bf16[128,384]{1,0:T(8,128)(2,1)S(1)} collective-permute-done((bf16[128,384]{1,0:T(8,128)(2,1)S(1)}, bf16[128,384]{1,0:T(8,128)(2,1)S(1)}, u32[]{:S(2)}, u32[]{:S(2)}) %collective-permute-start.25) | collective-permute-done | bytes 98336 | tf_op jit(solution)/shard_map/ppermute | solution.py:30
  59.7 1.0 %collective-permute-done.21 = bf16[288,128]{1,0:T(8,128)(2,1)S(1)} collective-permute-done((bf16[288,128]{1,0:T(8,128)(2,1)S(1)}, bf16[288,128]{1,0:T(8,128)(2,1)S(1)}, u32[]{:S(2)}, u32[]{:S(2)}) %collective-permute-start.21) | collective-permute-done | bytes 73760 | tf_op jit(solution)/shard_map/ppermute | solution.py:30
  60.8 1.2 %collective-permute-start.22 = (bf16[160,128]{1,0:T(8,128)(2,1)S(1)}, bf16[160,128]{1,0:T(8,128)(2,1)S(1)}, u32[]{:S(2)}, u32[]{:S(2)}) collective-permute-start(bf16[160,128]{1,0:T(8,128)(2,1)S(1)} %pad_maximum_fusion.10), channel_id=1, source_target_pairs={{0,8},{1,9},{2,10},{3,11},{4,12},{5,13},{6,14},{7,15},{8,0},{9,1},... | collective-permute-start | bytes 122888 | tf_op jit(solution)/shard_map/ppermute | solution.py:30
  62.0 2.3 %collective-permute-done.26 = bf16[128,384]{1,0:T(8,128)(2,1)S(1)} collective-permute-done((bf16[128,384]{1,0:T(8,128)(2,1)S(1)}, bf16[128,384]{1,0:T(8,128)(2,1)S(1)}, u32[]{:S(2)}, u32[]{:S(2)}) %collective-permute-start.26) | collective-permute-done | bytes 98336 | tf_op jit(solution)/shard_map/ppermute | solution.py:30
  64.4 0.4 collective-permute-start.27
  64.9 2.6 %collective-permute-start.23 = (bf16[96,128]{1,0:T(8,128)(2,1)S(1)}, bf16[96,128]{1,0:T(8,128)(2,1)S(1)}, u32[]{:S(2)}, u32[]{:S(2)}) collective-permute-start(bf16[96,128]{1,0:T(8,128)(2,1)S(1)} %pad_maximum_fusion.11), channel_id=1, source_target_pairs={{0,16},{1,17},{2,18},{3,19},{4,20},{5,21},{6,22},{7,23},{8,24},{9,... | collective-permute-start | bytes 73736 | tf_op jit(solution)/shard_map/ppermute | solution.py:30
  67.5 2.2 %shard_map.295 = f32[1024,512]{1,0:T(8,128)} custom-call(s32[1]{0:T(128)} %bitcast.me_ref, f32[1024,512]{1,0:T(8,128)S(1)} %get-tuple-element.80.x_ref, f32[1,1024,128]{2,1,0:T(8,128)S(1)} %get-tuple-element.81.stats_ref, bf16[1024,512]{1,0:T(8,128)(2,1)S(1)} %copy-done.1, f32[1024,512]{1,0:T(8,128)S(1)} %get-tuple-element.125.normed_grad_ref, ...), custom_call_target="tpu_custom_call" | custom-call | flops 2500000000 | bytes 8750000 | tf_op jit(solution)/shard_map/pallas_call | solution.py:636
  69.8 0.2 collective-permute-done.23
  70.0 1.1 %shard_map.296 = (f32[64,64]{1,0:T(8,128)}, f32[64,64]{1,0:T(8,128)}, f32[64,64]{1,0:T(8,128)}, f32[64,64]{1,0:T(8,128)}, f32[64,128]{1,0:T(8,128)}, /*index=5*/...) custom-call(s32[1]{0:T(128)} %bitcast.me_ref, ...), custom_call_target="tpu_custom_call" | custom-call | flops 2000000000 | bytes 7000000 | tf_op jit(solution)/shard_map/pallas_call | solution.py:636
  (79 shorter events, 1.7 us)
Async XLA Ops:
  0.7 5.3 %copy-start = (bf16[1024,512]{1,0:T(8,128)(2,1)S(1)}, bf16[1024,512]{1,0:T(8,128)(2,1)}, u32[]{:S(2)}) copy-start(bf16[1024,512]{1,0:T(8,128)(2,1)} %x_ref.3) | copy-start | bytes 3145732
  0.7 5.3 %copy-start.2 = (s32[4096]{0:T(1024)S(1)}, s32[4096]{0:T(1024)}, u32[]{:S(2)}) copy-start(s32[4096]{0:T(1024)} %param.18) | copy-start | bytes 49156
  1.8 5.9 %collective-permute-start = (bf16[96,128]{1,0:T(8,128)(2,1)S(1)}, bf16[96,128]{1,0:T(8,128)(2,1)S(1)}, u32[]{:S(2)}, u32[]{:S(2)}) collective-permute-start(bf16[96,128]{1,0:T(8,128)(2,1)S(1)} %get-tuple-element.82), channel_id=1, source_target_pairs={{0,16},{1,17},{2,18},{3,19},{4,20},{5,21},{6,22},{7,23},{8,24},{9,... | collective-permute-start | bytes 73736 | tf_op jit(solution)/shard_map/ppermute | solution.py:30
  5.9 5.1 %collective-permute-start.1 = (bf16[64,384]{1,0:T(8,128)(2,1)S(1)}, bf16[64,384]{1,0:T(8,128)(2,1)S(1)}, u32[]{:S(2)}, u32[]{:S(2)}) collective-permute-start(bf16[64,384]{1,0:T(8,128)(2,1)S(1)} %get-tuple-element.84), channel_id=1, source_target_pairs={{0,16},{1,17},{2,18},{3,19},{4,20},{5,21},{6,22},{7,23},{8,24},{9,... | collective-permute-start | bytes 147464 | tf_op jit(solution)/shard_map/ppermute | solution.py:30
  11.0 4.1 %collective-permute-start.2 = (bf16[160,128]{1,0:T(8,128)(2,1)S(1)}, bf16[160,128]{1,0:T(8,128)(2,1)S(1)}, u32[]{:S(2)}, u32[]{:S(2)}) collective-permute-start(bf16[160,128]{1,0:T(8,128)(2,1)S(1)} %pad_maximum_fusion.9), channel_id=1, source_target_pairs={{0,8},{1,9},{2,10},{3,11},{4,12},{5,13},{6,14},{7,15},{8,0},{9,1},... | collective-permute-start | bytes 122888 | tf_op jit(solution)/shard_map/ppermute | solution.py:30
  12.6 4.7 %collective-permute-start.7 = (bf16[128,384]{1,0:T(8,128)(2,1)S(1)}, bf16[128,384]{1,0:T(8,128)(2,1)S(1)}, u32[]{:S(2)}, u32[]{:S(2)}) collective-permute-start(bf16[128,384]{1,0:T(8,128)(2,1)S(1)} %pad_maximum_fusion.5), channel_id=1, source_target_pairs={{0,2},{1,3},{2,0},{3,1},{4,6},{5,7},{6,4},{7,5},{8,10},{9,11},{10,... | collective-permute-start | bytes 294920 | tf_op jit(solution)/shard_map/ppermute | solution.py:30
  15.1 4.4 %collective-permute-start.3 = (bf16[288,128]{1,0:T(8,128)(2,1)S(1)}, bf16[288,128]{1,0:T(8,128)(2,1)S(1)}, u32[]{:S(2)}, u32[]{:S(2)}) collective-permute-start(bf16[288,128]{1,0:T(8,128)(2,1)S(1)} %pad_maximum_fusion.7), channel_id=1, source_target_pairs={{0,4},{1,5},{2,6},{3,7},{4,0},{5,1},{6,2},{7,3},{8,12},{9,13},{10,... | collective-permute-start | bytes 221192 | tf_op jit(solution)/shard_map/ppermute | solution.py:30
  17.3 4.7 %collective-permute-start.9 = (bf16[128,384]{1,0:T(8,128)(2,1)S(1)}, bf16[128,384]{1,0:T(8,128)(2,1)S(1)}, u32[]{:S(2)}, u32[]{:S(2)}) collective-permute-start(bf16[128,384]{1,0:T(8,128)(2,1)S(1)} %bitcast.27), channel_id=1, source_target_pairs={{0,4},{1,5},{2,6},{3,7},{4,0},{5,1},{6,2},{7,3},{8,12},{9,13},{10,... | collective-permute-start | bytes 294920 | tf_op jit(solution)/shard_map/ppermute | solution.py:30
  18.9 4.8 %collective-permute-start.8 = (bf16[128,384]{1,0:T(8,128)(2,1)S(1)}, bf16[128,384]{1,0:T(8,128)(2,1)S(1)}, u32[]{:S(2)}, u32[]{:S(2)}) collective-permute-start(bf16[128,384]{1,0:T(8,128)(2,1)S(1)} %bitcast.30), channel_id=1, source_target_pairs={{0,8},{1,9},{2,10},{3,11},{4,12},{5,13},{6,14},{7,15},{8,0},{9,1},... | collective-permute-start | bytes 294920 | tf_op jit(solution)/shard_map/ppermute | solution.py:30
  19.6 5.6 %collective-permute-start.4 = (bf16[512,128]{1,0:T(8,128)(2,1)S(1)}, bf16[512,128]{1,0:T(8,128)(2,1)S(1)}, u32[]{:S(2)}, u32[]{:S(2)}) collective-permute-start(bf16[512,128]{1,0:T(8,128)(2,1)S(1)} %pad_maximum_fusion.4), channel_id=1, source_target_pairs={{0,2},{1,3},{2,0},{3,1},{4,6},{5,7},{6,4},{7,5},{8,10},{9,11},{10,... | collective-permute-start | bytes 393224 | tf_op jit(solution)/shard_map/ppermute | solution.py:30
  22.0 6.6 %collective-permute-start.11 = (bf16[256,384]{1,0:T(8,128)(2,1)S(1)}, bf16[256,384]{1,0:T(8,128)(2,1)S(1)}, u32[]{:S(2)}, u32[]{:S(2)}) collective-permute-start(bf16[256,384]{1,0:T(8,128)(2,1)S(1)} %pad_maximum_fusion.2), channel_id=1, source_target_pairs={{0,8},{1,9},{2,10},{3,11},{4,12},{5,13},{6,14},{7,15},{8,0},{9,1},... | collective-permute-start | bytes 589832 | tf_op jit(solution)/shard_map/ppermute | solution.py:30
  23.7 5.7 %collective-permute-start.10 = (bf16[256,384]{1,0:T(8,128)(2,1)S(1)}, bf16[256,384]{1,0:T(8,128)(2,1)S(1)}, u32[]{:S(2)}, u32[]{:S(2)}) collective-permute-start(bf16[256,384]{1,0:T(8,128)(2,1)S(1)} %pad_maximum_fusion.1), channel_id=1, source_target_pairs={{0,4},{1,5},{2,6},{3,7},{4,0},{5,1},{6,2},{7,3},{8,12},{9,13},{10,... | collective-permute-start | bytes 589832 | tf_op jit(solution)/shard_map/ppermute | solution.py:30
  25.2 1.6 %collective-permute-start.5 = (bf16[1024,128]{1,0:T(8,128)(2,1)S(1)}, bf16[1024,128]{1,0:T(8,128)(2,1)S(1)}, u32[]{:S(2)}, u32[]{:S(2)}) collective-permute-start(bf16[1024,128]{1,0:T(8,128)(2,1)S(1)} %constant_dynamic-update-slice_fusion.b0_ref), channel_id=1, source_target_pairs={{0,1},{1,0},{2,3},{3,2},{4,5},{5,4},{6,7},{7,6},{8,9},{9,8},{10,11... | collective-permute-start | bytes 786440 | tf_op jit(solution)/shard_map/ppermute | solution.py:30
  25.3 6.0 %collective-permute-start.12 = (bf16[512,384]{1,0:T(8,128)(2,1)S(1)}, bf16[512,384]{1,0:T(8,128)(2,1)S(1)}, u32[]{:S(2)}, u32[]{:S(2)}) collective-permute-start(bf16[512,384]{1,0:T(8,128)(2,1)S(1)} %constant_dynamic-update-slice_fusion.5.g0_ref), channel_id=1, source_target_pairs={{0,1},{1,0},{2,3},{3,2},{4,5},{5,4},{6,7},{7,6},{8,9},{9,8},{10,11... | collective-permute-start | bytes 1179656 | tf_op jit(solution)/shard_map/ppermute | solution.py:30
  26.8 4.5 %copy-start.1 = (bf16[1024,512]{1,0:T(8,128)(2,1)S(1)}, bf16[1024,512]{1,0:T(8,128)(2,1)}, u32[]{:S(2)}) copy-start(bf16[1024,512]{1,0:T(8,128)(2,1)} %grad_ref.3) | copy-start | bytes 3145732
  29.5 1.8 %collective-permute-start.13 = (bf16[512,384]{1,0:T(8,128)(2,1)S(1)}, bf16[512,384]{1,0:T(8,128)(2,1)S(1)}, u32[]{:S(2)}, u32[]{:S(2)}) collective-permute-start(bf16[512,384]{1,0:T(8,128)(2,1)S(1)} %constant_dynamic-update-slice_fusion.9.g1_ref), channel_id=1, source_target_pairs={{0,1},{1,0},{2,3},{3,2},{4,5},{5,4},{6,7},{7,6},{8,9},{9,8},{10,11... | collective-permute-start | bytes 1179656 | tf_op jit(solution)/shard_map/ppermute | solution.py:30
  29.6 1.7 %collective-permute-start.6 = (f32[8,512]{1,0:T(8,128)S(1)}, f32[8,512]{1,0:T(8,128)S(1)}, u32[]{:S(2)}, u32[]{:S(2)}) collective-permute-start(f32[8,512]{1,0:T(8,128)S(1)} %get-tuple-element.92), channel_id=1, source_target_pairs={{0,1},{1,0},{2,3},{3,2},{4,5},{5,4},{6,7},{7,6},{8,9},{9,8},{10,11... | collective-permute-start | bytes 49160 | tf_op jit(solution)/shard_map/ppermute | solution.py:30
  40.5 1.8 %collective-permute-start.14 = (bf16[512,384]{1,0:T(8,128)(2,1)S(1)}, bf16[512,384]{1,0:T(8,128)(2,1)S(1)}, u32[]{:S(2)}, u32[]{:S(2)}) collective-permute-start(bf16[512,384]{1,0:T(8,128)(2,1)S(1)} %get-tuple-element.105), channel_id=1, source_target_pairs={{0,1},{1,0},{2,3},{3,2},{4,5},{5,4},{6,7},{7,6},{8,9},{9,8},{10,11... | collective-permute-start | bytes 1179656 | tf_op jit(solution)/shard_map/ppermute | solution.py:30
  40.7 3.2 %collective-permute-start.15 = (bf16[512,384]{1,0:T(8,128)(2,1)S(1)}, bf16[512,384]{1,0:T(8,128)(2,1)S(1)}, u32[]{:S(2)}, u32[]{:S(2)}) collective-permute-start(bf16[512,384]{1,0:T(8,128)(2,1)S(1)} %get-tuple-element.106), channel_id=1, source_target_pairs={{0,1},{1,0},{2,3},{3,2},{4,5},{5,4},{6,7},{7,6},{8,9},{9,8},{10,11... | collective-permute-start | bytes 1179656 | tf_op jit(solution)/shard_map/ppermute | solution.py:30
  41.5 3.8 %collective-permute-start.16 = (f32[8,512]{1,0:T(8,128)S(1)}, f32[8,512]{1,0:T(8,128)S(1)}, u32[]{:S(2)}, u32[]{:S(2)}) collective-permute-start(f32[8,512]{1,0:T(8,128)S(1)} %get-tuple-element.115), channel_id=1, source_target_pairs={{0,1},{1,0},{2,3},{3,2},{4,5},{5,4},{6,7},{7,6},{8,9},{9,8},{10,11... | collective-permute-start | bytes 49160 | tf_op jit(solution)/shard_map/ppermute | solution.py:30
  42.4 7.0 %collective-permute-start.18 = (bf16[256,384]{1,0:T(8,128)(2,1)S(1)}, bf16[256,384]{1,0:T(8,128)(2,1)S(1)}, u32[]{:S(2)}, u32[]{:S(2)}) collective-permute-start(bf16[256,384]{1,0:T(8,128)(2,1)S(1)} %slice.201), channel_id=1, source_target_pairs={{0,4},{1,5},{2,6},{3,7},{4,0},{5,1},{6,2},{7,3},{8,12},{9,13},{10,... | collective-permute-start | bytes 589832 | tf_op jit(solution)/shard_map/ppermute | solution.py:30
  44.0 6.7 %collective-permute-start.19 = (bf16[256,384]{1,0:T(8,128)(2,1)S(1)}, bf16[256,384]{1,0:T(8,128)(2,1)S(1)}, u32[]{:S(2)}, u32[]{:S(2)}) collective-permute-start(bf16[256,384]{1,0:T(8,128)(2,1)S(1)} %slice.202), channel_id=1, source_target_pairs={{0,8},{1,9},{2,10},{3,11},{4,12},{5,13},{6,14},{7,15},{8,0},{9,1},... | collective-permute-start | bytes 589832 | tf_op jit(solution)/shard_map/ppermute | solution.py:30
  48.7 2.1 %collective-permute-start.17 = (bf16[1056,128]{1,0:T(8,128)(2,1)S(1)}, bf16[1056,128]{1,0:T(8,128)(2,1)S(1)}, u32[]{:S(2)}, u32[]{:S(2)}) collective-permute-start(bf16[1056,128]{1,0:T(8,128)(2,1)S(1)} %get-tuple-element.121), channel_id=1, source_target_pairs={{0,1},{1,0},{2,3},{3,2},{4,5},{5,4},{6,7},{7,6},{8,9},{9,8},{10,11... | collective-permute-start | bytes 811016 | tf_op jit(solution)/shard_map/ppermute | solution.py:30
  50.9 5.3 %collective-permute-start.20 = (bf16[544,128]{1,0:T(8,128)(2,1)S(1)}, bf16[544,128]{1,0:T(8,128)(2,1)S(1)}, u32[]{:S(2)}, u32[]{:S(2)}) collective-permute-start(bf16[544,128]{1,0:T(8,128)(2,1)S(1)} %pad_maximum_fusion.3), channel_id=1, source_target_pairs={{0,2},{1,3},{2,0},{3,1},{4,6},{5,7},{6,4},{7,5},{8,10},{9,11},{10,... | collective-permute-start | bytes 417800 | tf_op jit(solution)/shard_map/ppermute | solution.py:30
  52.5 7.1 %collective-permute-start.24 = (bf16[128,384]{1,0:T(8,128)(2,1)S(1)}, bf16[128,384]{1,0:T(8,128)(2,1)S(1)}, u32[]{:S(2)}, u32[]{:S(2)}) collective-permute-start(bf16[128,384]{1,0:T(8,128)(2,1)S(1)} %slice.204), channel_id=1, source_target_pairs={{0,8},{1,9},{2,10},{3,11},{4,12},{5,13},{6,14},{7,15},{8,0},{9,1},... | collective-permute-start | bytes 294920 | tf_op jit(solution)/shard_map/ppermute | solution.py:30
  54.1 5.4 %collective-permute-start.25 = (bf16[128,384]{1,0:T(8,128)(2,1)S(1)}, bf16[128,384]{1,0:T(8,128)(2,1)S(1)}, u32[]{:S(2)}, u32[]{:S(2)}) collective-permute-start(bf16[128,384]{1,0:T(8,128)(2,1)S(1)} %slice.206), channel_id=1, source_target_pairs={{0,4},{1,5},{2,6},{3,7},{4,0},{5,1},{6,2},{7,3},{8,12},{9,13},{10,... | collective-permute-start | bytes 294920 | tf_op jit(solution)/shard_map/ppermute | solution.py:30
  56.3 4.4 %collective-permute-start.21 = (bf16[288,128]{1,0:T(8,128)(2,1)S(1)}, bf16[288,128]{1,0:T(8,128)(2,1)S(1)}, u32[]{:S(2)}, u32[]{:S(2)}) collective-permute-start(bf16[288,128]{1,0:T(8,128)(2,1)S(1)} %pad_maximum_fusion.8), channel_id=1, source_target_pairs={{0,4},{1,5},{2,6},{3,7},{4,0},{5,1},{6,2},{7,3},{8,12},{9,13},{10,... | collective-permute-start | bytes 221192 | tf_op jit(solution)/shard_map/ppermute | solution.py:30
  59.6 4.7 %collective-permute-start.26 = (bf16[128,384]{1,0:T(8,128)(2,1)S(1)}, bf16[128,384]{1,0:T(8,128)(2,1)S(1)}, u32[]{:S(2)}, u32[]{:S(2)}) collective-permute-start(bf16[128,384]{1,0:T(8,128)(2,1)S(1)} %pad_maximum_fusion.6), channel_id=1, source_target_pairs={{0,2},{1,3},{2,0},{3,1},{4,6},{5,7},{6,4},{7,5},{8,10},{9,11},{10,... | collective-permute-start | bytes 294920 | tf_op jit(solution)/shard_map/ppermute | solution.py:30
  60.8 4.1 %collective-permute-start.22 = (bf16[160,128]{1,0:T(8,128)(2,1)S(1)}, bf16[160,128]{1,0:T(8,128)(2,1)S(1)}, u32[]{:S(2)}, u32[]{:S(2)}) collective-permute-start(bf16[160,128]{1,0:T(8,128)(2,1)S(1)} %pad_maximum_fusion.10), channel_id=1, source_target_pairs={{0,8},{1,9},{2,10},{3,11},{4,12},{5,13},{6,14},{7,15},{8,0},{9,1},... | collective-permute-start | bytes 122888 | tf_op jit(solution)/shard_map/ppermute | solution.py:30
  64.4 5.4 %collective-permute-start.27 = (bf16[64,384]{1,0:T(8,128)(2,1)S(1)}, bf16[64,384]{1,0:T(8,128)(2,1)S(1)}, u32[]{:S(2)}, u32[]{:S(2)}) collective-permute-start(bf16[64,384]{1,0:T(8,128)(2,1)S(1)} %bitcast.35), channel_id=1, source_target_pairs={{0,16},{1,17},{2,18},{3,19},{4,20},{5,21},{6,22},{7,23},{8,24},{9,... | collective-permute-start | bytes 147464 | tf_op jit(solution)/shard_map/ppermute | solution.py:30
  64.9 5.1 %collective-permute-start.23 = (bf16[96,128]{1,0:T(8,128)(2,1)S(1)}, bf16[96,128]{1,0:T(8,128)(2,1)S(1)}, u32[]{:S(2)}, u32[]{:S(2)}) collective-permute-start(bf16[96,128]{1,0:T(8,128)(2,1)S(1)} %pad_maximum_fusion.11), channel_id=1, source_target_pairs={{0,16},{1,17},{2,18},{3,19},{4,20},{5,21},{6,22},{7,23},{8,24},{9,... | collective-permute-start | bytes 73736 | tf_op jit(solution)/shard_map/ppermute | solution.py:30
